TPU v7x, 32 devices: a whole 2x2x4 slice. The times are simulated.
32 devices in a mesh: dp: 8 (over z, core), tensor: 4 (over y, x).
Axes of the slice: x: 2, y: 2, z: 4, core: 2. Of those that a mesh axis runs over, the one named last changes fastest.
Arguments:
- layer_in: bfloat16 [8192, 2304], P(('dp', 'tensor')), may hold values from -6 to 6
- cotangent: bfloat16 [8192, 2304], P(('dp', 'tensor')), may hold values from -6 to 6
- lengths: int32 [8], P('dp'), may hold values from 256 to 1024, as said below
- adapter_ids: int32 [8, 1], P('dp'), may hold values from 0 to 7
- norm_gains: float32 [4, 2304], replicated, may hold values from 0.1 to 1.9
- query_weight: bfloat16 [2304, 2048], P('dp', 'tensor'), may hold values from -0.125 to 0.125
- key_weight: bfloat16 [2304, 1024], P('dp'), may hold values from -0.125 to 0.125
- value_weight: bfloat16 [2304, 1024], P('dp'), may hold values from -0.125 to 0.125
- out_weight: bfloat16 [2048, 2304], P('tensor', 'dp'), may hold values from -0.125 to 0.125
- gate_weight: bfloat16 [2304, 9216], P('dp', 'tensor'), may hold values from -0.125 to 0.125
- up_weight: bfloat16 [2304, 9216], P('dp', 'tensor'), may hold values from -0.125 to 0.125
- down_weight: bfloat16 [9216, 2304], P('tensor', 'dp'), may hold values from -0.0625 to 0.0625
- adapt_in: bfloat16 [8, 2304, 80], P(None, ('dp', 'tensor')), may hold values from -0.125 to 0.125
- adapt_heads: bfloat16 [8, 2048, 16], P(None, ('dp', 'tensor')), may hold values from -0.125 to 0.125
- adapt_hidden: bfloat16 [8, 9216, 16], P(None, ('dp', 'tensor')), may hold values from -0.0625 to 0.0625
- lift_query: bfloat16 [8, 16, 2048], P(None, None, ('dp', 'tensor')), may hold values from -0.75 to 0.75
- lift_keyval: bfloat16 [8, 2, 16, 1024], P(None, None, None, ('dp', 'tensor')), may hold values from -0.75 to 0.75
- lift_gateup: bfloat16 [8, 2, 16, 9216], P(None, None, None, ('dp', 'tensor')), may hold values from -0.75 to 0.75
- lift_resid: bfloat16 [8, 2, 16, 2304], P(None, None, None, ('dp', 'tensor')), may hold values from -0.75 to 0.75
Outputs:
- layer_out: bfloat16 [8192, 2304], P(('dp', 'tensor'))
- input_grad: bfloat16 [8192, 2304], P(('dp', 'tensor'))
- adapt_in_grad: float32 [8, 2304, 80], P(None, ('dp', 'tensor'))
- adapt_heads_grad: float32 [8, 2048, 16], P(None, ('dp', 'tensor'))
- adapt_hidden_grad: float32 [8, 9216, 16], P(None, ('dp', 'tensor'))
- lift_query_grad: float32 [8, 16, 2048], P(None, None, ('dp', 'tensor'))
- lift_keyval_grad: float32 [8, 2, 16, 1024], P(None, None, None, ('dp', 'tensor'))
- lift_gateup_grad: float32 [8, 2, 16, 9216], P(None, None, None, ('dp', 'tensor'))
- lift_resid_grad: float32 [8, 2, 16, 2304], P(None, None, None, ('dp', 'tensor'))
Inputs may be any that keep to these rules, and one draw needn't show every extreme that they name: `lengths`: a sequence's real tokens stand at its start and the rest of its 1024 slots are padding; at least one sequence is full. `adapter_ids`: one adapter per sequence; every one of the 8 adapters serves some sequence.
All inputs are finite; a program needn't handle non-finite values.
Results may differ from a plain program's by a relative error of at most 0.025.
Values may be sent and summed in bfloat16 or wider, within the bound.
A program may use at most 320 MiB of HBM per device.

v0:
```python
import jax
import jax.numpy as jnp
from jax import lax
from jax.sharding import PartitionSpec as P

D = 2304
HQ = 8
KV = 4
HD = 256
FF = 9216
NA = 8
ADAPTER_RANK = 16
LEN = 1024


EPSILON = 1e-06
SOFT_CAP = 50.0
MASKED = -1e30
FULL_PRECISION = lax.Precision.HIGHEST


def rms_norm(values, gain_row):
    return (
        values * lax.rsqrt(jnp.mean(values * values, axis=-1, keepdims=True) + EPSILON) * gain_row
    )


def norm_back(values, gain_row, gradient):
    unused, pullback = jax.vjp(lambda inner_value: rms_norm(inner_value, gain_row), values)
    return pullback(gradient)[0]


def gated_gelu(gate_in, up_in):
    return jax.nn.gelu(gate_in, approximate=True) * up_in


def tables(length, size):
    half_size = size // 2
    frequency = 10000.0 ** (-2.0 * jnp.arange(half_size, dtype=jnp.float32) / size)
    angles = jnp.arange(length, dtype=jnp.float32)[:, None] * frequency[None, :]
    return (jnp.cos(angles)[:, None, :], jnp.sin(angles)[:, None, :])


def rotate(values, cosine, sine):
    half_size = values.shape[-1] // 2
    first_half = values[..., :half_size]
    second_half = values[..., half_size:]
    return jnp.concatenate(
        [first_half * cosine - second_half * sine, second_half * cosine + first_half * sine],
        axis=-1,
    )


def pick_adapter(onehot, table_in):
    flat_table = table_in.reshape(table_in.shape[0], -1)
    chosen = jnp.dot(onehot, flat_table, preferred_element_type=jnp.float32)
    return chosen.astype(jnp.bfloat16).reshape((onehot.shape[0],) + table_in.shape[1:])


def to_adapters(seq_hot_wide, stacked):
    return jnp.einsum("sa,s...->a...", seq_hot_wide, stacked, precision=FULL_PRECISION)


def spread(row_values, row_select):
    return (row_select[:, :, None] * row_values[:, None, :]).reshape(row_values.shape[0], -1)


def lift_rows(row_values, row_select, lift_table):
    flat_table = lift_table.reshape(-1, lift_table.shape[-1])
    return jnp.dot(spread(row_values, row_select), flat_table, preferred_element_type=jnp.float32)


def lift_back(gradient, row_select, lift_table):
    flat_table = lift_table.reshape(-1, lift_table.shape[-1])
    every_one = jnp.einsum("te,ke->tk", gradient, flat_table, preferred_element_type=jnp.float32)
    every_one = every_one.reshape(gradient.shape[0], row_select.shape[1], -1)
    return jnp.sum(every_one * row_select[:, :, None].astype(jnp.float32), axis=1)


def lift_grad(row_values, row_select, gradient):
    stacked = jnp.einsum(
        "tk,te->ke", spread(row_values, row_select), gradient, preferred_element_type=jnp.float32
    )
    return stacked.reshape(row_select.shape[1], row_values.shape[1], gradient.shape[1])


def down_back(grad_rows, row_select, table_in):
    flat_table = jnp.transpose(table_in, (0, 2, 1)).reshape(-1, table_in.shape[1])
    return jnp.dot(spread(grad_rows, row_select), flat_table, preferred_element_type=jnp.float32)


def down_grad(inputs, row_select, grad_rows):
    stacked = jnp.einsum(
        "te,tk->ek", inputs, spread(grad_rows, row_select), preferred_element_type=jnp.float32
    )
    stacked = stacked.reshape(inputs.shape[1], row_select.shape[1], grad_rows.shape[1])
    return jnp.transpose(stacked, (1, 0, 2))


def place_into(term_part, first_index, axis_number, full_shape):
    return lax.dynamic_update_slice_in_dim(
        jnp.zeros(full_shape, jnp.float32), term_part, first_index, axis_number
    )


def per_device(
    layer_in,
    cotangent,
    lengths,
    adapter_ids,
    norm_gains,
    query_weight,
    key_weight,
    value_weight,
    out_weight,
    gate_weight,
    up_weight,
    down_weight,
    adapt_in,
    adapt_heads,
    adapt_hidden,
    lift_query,
    lift_keyval,
    lift_gateup,
    lift_resid,
):
    tensor_count = lax.axis_size("tensor")
    tensor_index = lax.axis_index("tensor")
    rows_here = layer_in.shape[0]
    seq_count = lengths.shape[0]
    group_rows = seq_count * LEN
    heads_here = HQ // tensor_count
    hidden_here = FF // tensor_count
    ratio_group = HQ // KV
    head_width = heads_here * HD
    row_start = tensor_index * rows_here
    full_in, full_heads, full_hidden, full_query, full_keyval, full_gateup, full_resid = (
        lax.all_gather(adapt_in, ("dp", "tensor"), axis=1, tiled=True),
        lax.all_gather(adapt_heads, ("dp", "tensor"), axis=1, tiled=True),
        lax.all_gather(adapt_hidden, ("dp", "tensor"), axis=1, tiled=True),
        lax.all_gather(lift_query, ("dp", "tensor"), axis=2, tiled=True),
        lax.all_gather(lift_keyval, ("dp", "tensor"), axis=3, tiled=True),
        lax.all_gather(lift_gateup, ("dp", "tensor"), axis=3, tiled=True),
        lax.all_gather(lift_resid, ("dp", "tensor"), axis=3, tiled=True),
    )

    def head_columns(weight_matrix):
        pieces = []
        for head_slot in range(heads_here):
            source = (tensor_index * heads_here + head_slot) // ratio_group
            pieces.append(
                lax.dynamic_slice_in_dim(weight_matrix, source * HD, HD, weight_matrix.ndim - 1)
            )
        return jnp.concatenate(pieces, axis=-1)

    def attention_weights():
        gathered = (
            lax.all_gather(query_weight, "dp", axis=0, tiled=True),
            lax.all_gather(key_weight, "dp", axis=0, tiled=True),
            lax.all_gather(value_weight, "dp", axis=0, tiled=True),
            lax.all_gather(out_weight, "dp", axis=1, tiled=True),
        )
        whole_out = gathered[3]
        return (gathered[0], head_columns(gathered[1]), head_columns(gathered[2]), whole_out)

    def mlp_weights():
        return (
            lax.all_gather(gate_weight, "dp", axis=0, tiled=True),
            lax.all_gather(up_weight, "dp", axis=0, tiled=True),
            lax.all_gather(down_weight, "dp", axis=1, tiled=True),
        )

    def gather_forward(values):
        return lax.all_gather(values, "tensor", axis=0, tiled=True)

    def gather_backward(first_part, second_part):
        return (
            lax.all_gather(first_part, "tensor", axis=0, tiled=True),
            lax.all_gather(second_part, "tensor", axis=0, tiled=True),
        )

    def scatter_forward(term_fn):
        return lax.psum_scatter(
            term_fn(jnp.int32(0), lax.axis_size("tensor") * rows_here).astype(jnp.bfloat16),
            "tensor",
            scatter_dimension=0,
            tiled=True,
        ).astype(jnp.float32)

    def scatter_backward(term_fn):
        return lax.psum_scatter(
            term_fn(jnp.int32(0), lax.axis_size("tensor") * rows_here).astype(jnp.bfloat16),
            "tensor",
            scatter_dimension=0,
            tiled=True,
        ).astype(jnp.float32)

    def rank_sum(values):
        return lax.psum(values.astype(jnp.bfloat16), "tensor").astype(jnp.float32)

    def own_rows(values):
        return lax.dynamic_slice_in_dim(values.reshape(group_rows, -1), row_start, rows_here, 0)

    adapter_range = jnp.arange(NA, dtype=jnp.int32)
    seq_adapter = adapter_ids[:, 0]
    seq_hot = seq_adapter[:, None] == adapter_range[None, :]
    seq_hot_low = seq_hot.astype(jnp.bfloat16)
    seq_hot_wide = seq_hot.astype(jnp.float32)
    row_global = row_start + jnp.arange(rows_here, dtype=jnp.int32)
    row_match = (
        (row_global // LEN)[:, None] == jnp.arange(seq_count, dtype=jnp.int32)[None, :]
    ).astype(jnp.int32)
    row_length = jnp.sum(row_match * lengths[None, :], axis=1)
    row_adapter = jnp.sum(row_match * seq_adapter[None, :], axis=1)
    row_hot = (row_adapter[:, None] == adapter_range[None, :]).astype(jnp.bfloat16)
    row_valid = (row_global % LEN < row_length).astype(jnp.float32)[:, None]
    key_ok = jnp.arange(LEN, dtype=jnp.int32)[None, :] < lengths[:, None]
    cosine, sine = tables(LEN, HD)
    causal = jnp.arange(LEN)[:, None] >= jnp.arange(LEN)[None, :]
    head_shape = (seq_count, LEN, heads_here, HD)

    def scores_of(query_seq, key_seq, ok_seq):
        raw_scores = jnp.einsum(
            "qhd,khd->hqk", query_seq, key_seq, preferred_element_type=jnp.float32
        )
        capped = SOFT_CAP * jnp.tanh(raw_scores / SOFT_CAP)
        allowed = causal[None] & ok_seq[None, None, :]
        return (raw_scores, jnp.where(allowed, capped, MASKED))

    def attend(inputs):
        query_seq, key_seq, value_seq, ok_seq = inputs
        raw_scores, capped = scores_of(query_seq, key_seq, ok_seq)
        row_max = jnp.max(capped, axis=-1, keepdims=True)
        exp_scores = jnp.exp(capped - row_max)
        row_total = jnp.sum(exp_scores, axis=-1, keepdims=True)
        softmax_out = (exp_scores / row_total).astype(jnp.bfloat16)
        mixed = jnp.einsum(
            "hqk,khd->qhd", softmax_out, value_seq, preferred_element_type=jnp.float32
        )
        return (mixed.astype(jnp.bfloat16), (row_max + jnp.log(row_total))[..., 0])

    def attend_back(inputs):
        query_seq, key_seq, value_seq, ok_seq, total_seq, grad_seq = inputs
        raw_scores, capped = scores_of(query_seq, key_seq, ok_seq)
        softmax_out = jnp.exp(capped - total_seq[..., None])
        softmax_low = softmax_out.astype(jnp.bfloat16)
        grad_probs = jnp.einsum(
            "qhd,khd->hqk", grad_seq, value_seq, preferred_element_type=jnp.float32
        )
        grad_value = jnp.einsum(
            "hqk,qhd->khd", softmax_low, grad_seq, preferred_element_type=jnp.float32
        )
        grad_capped = softmax_out * (
            grad_probs - jnp.sum(softmax_out * grad_probs, axis=-1, keepdims=True)
        )
        squash = jnp.tanh(raw_scores / SOFT_CAP)
        grad_raw = (grad_capped * (1.0 - squash * squash)).astype(jnp.bfloat16)
        grad_query = jnp.einsum(
            "hqk,khd->qhd", grad_raw, key_seq, preferred_element_type=jnp.float32
        )
        grad_key = jnp.einsum(
            "hqk,qhd->khd", grad_raw, query_seq, preferred_element_type=jnp.float32
        )
        return (grad_query, grad_key, grad_value)

    w_query, key_cols, value_cols, output_matrix = attention_weights()
    resid_in = layer_in.astype(jnp.float32)
    attention_input_normed = rms_norm(resid_in, norm_gains[0]).astype(jnp.bfloat16)
    sequence_attention = gather_forward(attention_input_normed).reshape(seq_count, LEN, D)
    select_input_adapter = pick_adapter(seq_hot_low, full_in)
    rank_query_key_value = jnp.einsum(
        "xpt,xtv->xpv",
        sequence_attention,
        select_input_adapter[:, :, : 3 * ADAPTER_RANK],
        preferred_element_type=jnp.float32,
    ).astype(jnp.bfloat16)
    pick_query = pick_adapter(seq_hot_low, full_query)
    local_query = lax.dynamic_slice_in_dim(pick_query, tensor_index * head_width, head_width, 2)
    pick_keyval = pick_adapter(seq_hot_low, full_keyval)
    local_key = head_columns(pick_keyval[:, 0])
    local_value = head_columns(pick_keyval[:, 1])

    def project(weight_matrix, lift_table, low_rows):
        dense_portion = jnp.einsum(
            "rti,iv->rtv", sequence_attention, weight_matrix, preferred_element_type=jnp.float32
        )
        return dense_portion + jnp.einsum(
            "slr,sre->sle", low_rows, lift_table, preferred_element_type=jnp.float32
        )

    query_pre = project(w_query, local_query, rank_query_key_value[..., :ADAPTER_RANK]).reshape(
        head_shape
    )
    key_pre = project(
        key_cols, local_key, rank_query_key_value[..., ADAPTER_RANK : 2 * ADAPTER_RANK]
    ).reshape(head_shape)
    value_pre = project(
        value_cols, local_value, rank_query_key_value[..., 2 * ADAPTER_RANK :]
    ).reshape(head_shape)
    queries = (rotate(query_pre, cosine, sine) * HD ** (-0.5)).astype(jnp.bfloat16)
    keys = rotate(key_pre, cosine, sine).astype(jnp.bfloat16)
    values = value_pre.astype(jnp.bfloat16)
    attention_output, log_total = lax.map(attend, (queries, keys, values, key_ok))
    head_rows = attention_output.reshape(group_rows, head_width)
    pick_heads = pick_adapter(seq_hot_low, full_heads)
    local_heads = lax.dynamic_slice_in_dim(pick_heads, tensor_index * head_width, head_width, 1)
    low_out_part = jnp.einsum(
        "sle,ser->slr",
        attention_output.reshape(seq_count, LEN, head_width),
        local_heads,
        preferred_element_type=jnp.float32,
    )
    low_out_rows = own_rows(rank_sum(low_out_part).astype(jnp.bfloat16))

    def out_term(first_row, row_count):
        return jnp.dot(head_rows, output_matrix, preferred_element_type=jnp.float32)

    attn_main = scatter_forward(out_term)
    attention_total = attn_main + lift_rows(low_out_rows, row_hot, full_resid[:, 0])
    resid_mid = resid_in + rms_norm(attention_total, norm_gains[1])
    feedforward_input_normed = rms_norm(resid_mid, norm_gains[2]).astype(jnp.bfloat16)
    gate_matrix, up_matrix, down_matrix = mlp_weights()
    sequence_feedforward = gather_forward(feedforward_input_normed).reshape(seq_count, LEN, D)
    rank_gate_up_projection = jnp.einsum(
        "xpt,xtv->xpv",
        sequence_feedforward,
        select_input_adapter[:, :, 3 * ADAPTER_RANK :],
        preferred_element_type=jnp.float32,
    ).astype(jnp.bfloat16)
    pick_gu = pick_adapter(seq_hot_low, full_gateup)
    local_gu = lax.dynamic_slice_in_dim(pick_gu, tensor_index * hidden_here, hidden_here, 3)
    gate_preactivation = jnp.einsum(
        "zvp,pj->zvj", sequence_feedforward, gate_matrix, preferred_element_type=jnp.float32
    )
    gate_preactivation = gate_preactivation + jnp.einsum(
        "slr,srf->slf",
        rank_gate_up_projection[..., :ADAPTER_RANK],
        local_gu[:, 0],
        preferred_element_type=jnp.float32,
    )
    up_preactivation = jnp.einsum(
        "zvp,pj->zvj", sequence_feedforward, up_matrix, preferred_element_type=jnp.float32
    )
    up_preactivation = up_preactivation + jnp.einsum(
        "slr,srf->slf",
        rank_gate_up_projection[..., ADAPTER_RANK:],
        local_gu[:, 1],
        preferred_element_type=jnp.float32,
    )
    hidden_state = gated_gelu(gate_preactivation, up_preactivation).astype(jnp.bfloat16)
    pick_hidden = pick_adapter(seq_hot_low, full_hidden)
    local_hidden = lax.dynamic_slice_in_dim(pick_hidden, tensor_index * hidden_here, hidden_here, 1)
    low_down_part = jnp.einsum(
        "slf,sfr->slr", hidden_state, local_hidden, preferred_element_type=jnp.float32
    )
    low_down_rows = own_rows(rank_sum(low_down_part).astype(jnp.bfloat16))
    hidden_rows = hidden_state.reshape(group_rows, hidden_here)

    def down_term(first_row, row_count):
        return jnp.dot(hidden_rows, down_matrix, preferred_element_type=jnp.float32)

    feedforward_total = scatter_forward(down_term) + lift_rows(
        low_down_rows, row_hot, full_resid[:, 1]
    )
    layer_out = (row_valid * (resid_mid + rms_norm(feedforward_total, norm_gains[3]))).astype(
        jnp.bfloat16
    )
    grad_out = cotangent.astype(jnp.float32) * row_valid
    grad_mlp = norm_back(feedforward_total, norm_gains[3], grad_out).astype(jnp.bfloat16)
    grad_lift_down = lift_grad(low_down_rows, row_hot, grad_mlp)
    grad_low_down = lift_back(grad_mlp, row_hot, full_resid[:, 1]).astype(jnp.bfloat16)
    group_grad_mlp, group_low_down = gather_backward(grad_mlp, grad_low_down)
    gate_matrix, up_matrix, down_matrix = mlp_weights()
    sequence_feedforward_gradient = group_grad_mlp.reshape(seq_count, LEN, D)
    seq_low_down = group_low_down.reshape(seq_count, LEN, ADAPTER_RANK)
    grad_hidden = jnp.einsum(
        "iza,qa->izq",
        sequence_feedforward_gradient,
        down_matrix,
        preferred_element_type=jnp.float32,
    )
    grad_hidden = grad_hidden + jnp.einsum(
        "slr,sfr->slf", seq_low_down, local_hidden, preferred_element_type=jnp.float32
    )
    hidden_local = to_adapters(
        seq_hot_wide,
        jnp.einsum("slf,slr->sfr", hidden_state, seq_low_down, preferred_element_type=jnp.float32),
    )
    unused, gelu_pull = jax.vjp(gated_gelu, gate_preactivation, up_preactivation)
    grad_gate, grad_up = gelu_pull(grad_hidden)
    grad_gate = grad_gate.astype(jnp.bfloat16)
    grad_up = grad_up.astype(jnp.bfloat16)
    gateup_local = to_adapters(
        seq_hot_wide,
        jnp.stack(
            [
                jnp.einsum(
                    "slr,slf->srf",
                    rank_gate_up_projection[..., :ADAPTER_RANK],
                    grad_gate,
                    preferred_element_type=jnp.float32,
                ),
                jnp.einsum(
                    "slr,slf->srf",
                    rank_gate_up_projection[..., ADAPTER_RANK:],
                    grad_up,
                    preferred_element_type=jnp.float32,
                ),
            ],
            axis=1,
        ),
    )
    low_gu_part = jnp.concatenate(
        [
            jnp.einsum(
                "slf,srf->slr", grad_gate, local_gu[:, 0], preferred_element_type=jnp.float32
            ),
            jnp.einsum("slf,srf->slr", grad_up, local_gu[:, 1], preferred_element_type=jnp.float32),
        ],
        axis=-1,
    )
    low_gu_grad = own_rows(rank_sum(low_gu_part).astype(jnp.bfloat16))
    gate_grad_rows = grad_gate.reshape(group_rows, hidden_here)
    up_grad_rows = grad_up.reshape(group_rows, hidden_here)

    def mlp_back_term(first_row, row_count):
        gate_back = jnp.einsum(
            "tf,df->td", gate_grad_rows, gate_matrix, preferred_element_type=jnp.float32
        )
        return gate_back + jnp.einsum(
            "tf,df->td", up_grad_rows, up_matrix, preferred_element_type=jnp.float32
        )

    grad_normed_mlp = scatter_backward(mlp_back_term) + down_back(
        low_gu_grad, row_hot, full_in[:, :, 3 * ADAPTER_RANK :]
    )
    grad_mid = grad_out + norm_back(resid_mid, norm_gains[2], grad_normed_mlp)
    grad_attn = norm_back(attention_total, norm_gains[1], grad_mid).astype(jnp.bfloat16)
    grad_lift_out = lift_grad(low_out_rows, row_hot, grad_attn)
    grad_low_out = lift_back(grad_attn, row_hot, full_resid[:, 0]).astype(jnp.bfloat16)
    w_query, key_cols, value_cols, output_matrix = attention_weights()
    group_grad_attn, group_low_out = gather_backward(grad_attn, grad_low_out)
    seq_low_out = group_low_out.reshape(seq_count, LEN, ADAPTER_RANK)
    grad_heads = jnp.einsum(
        "td,ed->te", group_grad_attn, output_matrix, preferred_element_type=jnp.float32
    )
    grad_heads = grad_heads.reshape(seq_count, LEN, head_width)
    grad_heads = grad_heads + jnp.einsum(
        "slr,ser->sle", seq_low_out, local_heads, preferred_element_type=jnp.float32
    )
    grad_heads = grad_heads.astype(jnp.bfloat16)
    heads_term = jnp.einsum(
        "sle,slr->ser",
        attention_output.reshape(seq_count, LEN, head_width),
        seq_low_out,
        preferred_element_type=jnp.float32,
    )
    heads_term = place_into(
        to_adapters(seq_hot_wide, heads_term),
        tensor_index * head_width,
        1,
        (NA, HQ * HD, ADAPTER_RANK),
    )
    grad_query, grad_key, grad_value = lax.map(
        attend_back, (queries, keys, values, key_ok, log_total, grad_heads.reshape(head_shape))
    )
    grad_q_pre = (
        rotate(grad_query * HD ** (-0.5), cosine, -sine)
        .astype(jnp.bfloat16)
        .reshape(seq_count, LEN, head_width)
    )
    grad_k_pre = (
        rotate(grad_key, cosine, -sine).astype(jnp.bfloat16).reshape(seq_count, LEN, head_width)
    )
    grad_v_pre = grad_value.astype(jnp.bfloat16).reshape(seq_count, LEN, head_width)
    query_local = to_adapters(
        seq_hot_wide,
        jnp.einsum(
            "slr,sle->sre",
            rank_query_key_value[..., :ADAPTER_RANK],
            grad_q_pre,
            preferred_element_type=jnp.float32,
        ),
    )
    keyval_parts = to_adapters(
        seq_hot_wide,
        jnp.stack(
            [
                jnp.einsum(
                    "slr,sle->sre",
                    rank_query_key_value[..., ADAPTER_RANK : 2 * ADAPTER_RANK],
                    grad_k_pre,
                    preferred_element_type=jnp.float32,
                ),
                jnp.einsum(
                    "slr,sle->sre",
                    rank_query_key_value[..., 2 * ADAPTER_RANK :],
                    grad_v_pre,
                    preferred_element_type=jnp.float32,
                ),
            ],
            axis=1,
        ),
    )
    keyval_term = jnp.zeros((NA, 2, ADAPTER_RANK, KV * HD), jnp.float32)
    for head_slot in range(heads_here):
        source = (tensor_index * heads_here + head_slot) // ratio_group
        current = lax.dynamic_slice_in_dim(keyval_term, source * HD, HD, 3)
        addition = keyval_parts[:, :, :, head_slot * HD : (head_slot + 1) * HD]
        keyval_term = lax.dynamic_update_slice_in_dim(
            keyval_term, current + addition, source * HD, 3
        )
    low_qkv_part = jnp.concatenate(
        [
            jnp.einsum("sle,sre->slr", grad_q_pre, local_query, preferred_element_type=jnp.float32),
            jnp.einsum("sle,sre->slr", grad_k_pre, local_key, preferred_element_type=jnp.float32),
            jnp.einsum("sle,sre->slr", grad_v_pre, local_value, preferred_element_type=jnp.float32),
        ],
        axis=-1,
    )
    low_qkv_grad = own_rows(rank_sum(low_qkv_part).astype(jnp.bfloat16))
    q_grad_rows = grad_q_pre.reshape(group_rows, head_width)
    k_grad_rows = grad_k_pre.reshape(group_rows, head_width)
    v_grad_rows = grad_v_pre.reshape(group_rows, head_width)

    def attn_back_term(first_row, row_count):
        summed_back = jnp.einsum(
            "te,de->td", q_grad_rows, w_query, preferred_element_type=jnp.float32
        )
        summed_back = summed_back + jnp.einsum(
            "te,de->td", k_grad_rows, key_cols, preferred_element_type=jnp.float32
        )
        return summed_back + jnp.einsum(
            "te,de->td", v_grad_rows, value_cols, preferred_element_type=jnp.float32
        )

    grad_normed_attn = scatter_backward(attn_back_term) + down_back(
        low_qkv_grad, row_hot, full_in[:, :, : 3 * ADAPTER_RANK]
    )
    input_grad = (grad_mid + norm_back(resid_in, norm_gains[0], grad_normed_attn)).astype(
        jnp.bfloat16
    )
    in_term = jnp.concatenate(
        [
            down_grad(attention_input_normed, row_hot, low_qkv_grad),
            down_grad(feedforward_input_normed, row_hot, low_gu_grad),
        ],
        axis=2,
    )
    resid_term = jnp.stack([grad_lift_out, grad_lift_down], axis=1)
    hidden_term = place_into(hidden_local, tensor_index * hidden_here, 1, (NA, FF, ADAPTER_RANK))
    query_term = place_into(query_local, tensor_index * head_width, 2, (NA, ADAPTER_RANK, HQ * HD))
    gateup_term = place_into(gateup_local, tensor_index * hidden_here, 3, (NA, 2, ADAPTER_RANK, FF))
    summed = (
        lax.psum_scatter(in_term, ("dp", "tensor"), scatter_dimension=1, tiled=True),
        lax.psum_scatter(heads_term, ("dp", "tensor"), scatter_dimension=1, tiled=True),
        lax.psum_scatter(hidden_term, ("dp", "tensor"), scatter_dimension=1, tiled=True),
        lax.psum_scatter(query_term, ("dp", "tensor"), scatter_dimension=2, tiled=True),
        lax.psum_scatter(keyval_term, ("dp", "tensor"), scatter_dimension=3, tiled=True),
        lax.psum_scatter(gateup_term, ("dp", "tensor"), scatter_dimension=3, tiled=True),
        lax.psum_scatter(resid_term, ("dp", "tensor"), scatter_dimension=3, tiled=True),
    )
    in_grad, heads_grad, hidden_grad, query_grad = (summed[0], summed[1], summed[2], summed[3])
    keyval_grad, gateup_grad, resid_grad = (summed[4], summed[5], summed[6])
    return (
        layer_out,
        input_grad,
        in_grad,
        heads_grad,
        hidden_grad,
        query_grad,
        keyval_grad,
        gateup_grad,
        resid_grad,
    )


def solution(mesh):
    return jax.shard_map(
        per_device,
        mesh=mesh,
        in_specs=(
            P(("dp", "tensor"), None),
            P(("dp", "tensor"), None),
            P("dp"),
            P("dp", None),
            P(),
            P("dp", "tensor"),
            P("dp", None),
            P("dp", None),
            P("tensor", "dp"),
            P("dp", "tensor"),
            P("dp", "tensor"),
            P("tensor", "dp"),
            P(None, ("dp", "tensor"), None),
            P(None, ("dp", "tensor"), None),
            P(None, ("dp", "tensor"), None),
            P(None, None, ("dp", "tensor")),
            P(None, None, None, ("dp", "tensor")),
            P(None, None, None, ("dp", "tensor")),
            P(None, None, None, ("dp", "tensor")),
        ),
        out_specs=(
            P(("dp", "tensor"), None),
            P(("dp", "tensor"), None),
            P(None, ("dp", "tensor"), None),
            P(None, ("dp", "tensor"), None),
            P(None, ("dp", "tensor"), None),
            P(None, None, ("dp", "tensor")),
            P(None, None, None, ("dp", "tensor")),
            P(None, None, None, ("dp", "tensor")),
            P(None, None, None, ("dp", "tensor")),
        ),
        check_vma=False,
    )
```

profile of v0, /device:TPU:0, one launch (start us, length us, event | category | flops | bytes accessed | tf_op | source)
XLA Modules:
  0.0 2672.5 jit_solution(12070095615943462474)
XLA Ops:
  24.3 139.3 %all_gather.70 = bf16[8,2,16,1024]{2,0,1,3:T(8,128)(2,1)} all-gather(bf16[8,2,16,32]{2,0,1,3:T(8,128)(2,1)S(1)} %copy.104), channel_id=1, replica_groups=mesh['dp'=8,'tensor'=4] {'dp','tensor'}, dimensions={3}, use_global_device_ids=true | all-gather | bytes 540672 | tf_op jit(solution)/shard_map/all_gather | solution.py:142
  170.2 147.1 %all_gather.72 = bf16[8,16,2048]{1,0,2:T(8,128)(2,1)} all-gather(bf16[8,16,64]{1,0,2:T(8,128)(2,1)S(1)} %copy.106), channel_id=1, replica_groups=mesh['dp'=8,'tensor'=4] {'dp','tensor'}, dimensions={2}, use_global_device_ids=true | all-gather | bytes 540672 | tf_op jit(solution)/shard_map/all_gather | solution.py:141
  397.5 147.3 %all_gather.75 = bf16[8,2048,16]{2,0,1:T(8,128)(2,1)S(1)} all-gather(bf16[8,64,16]{2,0,1:T(8,128)(2,1)S(1)} %copy.113), channel_id=1, replica_groups=mesh['dp'=8,'tensor'=4] {'dp','tensor'}, dimensions={1}, use_global_device_ids=true | all-gather | bytes 540672 | tf_op jit(solution)/shard_map/all_gather | solution.py:139
  574.4 18.5 psum.28
  602.2 174.4 %all-gather.34.cloned.1.call-done = bf16[8,2,16,9216]{2,0,1,3:T(8,128)(2,1)} async-done(((bf16[8,2,16,288]{2,0,1,3:T(8,128)(2,1)}), bf16[8,2,16,9216]{2,0,1,3:T(8,128)(2,1)}) %all-gather.34.cloned.1.call-update) | async-done | bytes 4718608 | tf_op jit(solution)/shard_map/all_gather | solution.py:143
  776.6 33.6 %copy.118 = bf16[8,2,16,9216]{3,2,1,0:T(8,128)(2,1)} copy(bf16[8,2,16,9216]{2,0,1,3:T(8,128)(2,1)} %all-gather.34.cloned.1.call-done) | data formatting | bytes 9437184 | tf_op jit(solution)/shard_map/all_gather | solution.py:143
  816.9 59.9 %all-gather.36.cloned.1.call-done = bf16[2304,2304]{1,0:T(8,128)(2,1)} async-done(((bf16[288,2304]{1,0:T(8,128)(2,1)}), bf16[2304,2304]{1,0:T(8,128)(2,1)}) %all-gather.36.cloned.1.call-update) | async-done | bytes 10616848 | tf_op jit(solution)/shard_map/all_gather | solution.py:169
  876.8 57.3 %all-gather.30.cloned.1.call-done = bf16[1024,2304]{1,0:T(8,128)(2,1)} async-done(((bf16[256,2304]{1,0:T(8,128)(2,1)}), bf16[1024,2304]{1,0:T(8,128)(2,1)}) %all-gather.30.cloned.1.call-update) | async-done | bytes 4718608 | tf_op jit(solution)/shard_map/all_gather | solution.py:174
  950.8 85.3 %all-gather.32.cloned.1.call-done = bf16[2304,2304]{1,0:T(8,128)(2,1)} async-done(((bf16[288,2304]{1,0:T(8,128)(2,1)}), bf16[2304,2304]{1,0:T(8,128)(2,1)}) %all-gather.32.cloned.1.call-update) | async-done | bytes 10616848 | tf_op jit(solution)/shard_map/all_gather | solution.py:168
  1036.1 17.7 fusion.191
  1071.4 65.2 %all-gather.38.cloned.1.call-done = bf16[2304,2304]{0,1:T(8,128)(2,1)} async-done(((bf16[2304,288]{0,1:T(8,128)(2,1)}), bf16[2304,2304]{0,1:T(8,128)(2,1)}) %all-gather.38.cloned.1.call-update) | async-done | bytes 10616848 | tf_op jit(solution)/shard_map/all_gather | solution.py:170
  1158.9 103.6 %all-gather.40.cloned.1.call-done = bf16[8,9216,16]{2,0,1:T(8,128)(2,1)} async-done(((bf16[8,288,16]{2,0,1:T(8,128)(2,1)}), bf16[8,9216,16]{2,0,1:T(8,128)(2,1)}) %all-gather.40.cloned.1.call-update) | async-done | bytes 2359312 | tf_op jit(solution)/shard_map/all_gather | solution.py:140
  1262.4 18.3 copy.120
  1280.8 21.3 reshape.1016
  1315.6 16.8 psum.29
  1349.6 45.6 %all-gather.42.cloned.1.call-done = bf16[1024,2304]{1,0:T(8,128)(2,1)} async-done(((bf16[256,2304]{1,0:T(8,128)(2,1)}), bf16[1024,2304]{1,0:T(8,128)(2,1)}) %all-gather.42.cloned.1.call-update) | async-done | bytes 4718608 | tf_op jit(solution)/shard_map/all_gather | solution.py:178
  1430.6 17.2 fusion.194
  1447.8 18.9 add_convert_fusion.1
  1480.7 51.7 %reduce-scatter.28.cloned.1.call-done = bf16[256,2304]{1,0:T(8,128)(2,1)} async-done(((bf16[1024,2304]{1,0:T(8,128)(2,1)}), bf16[256,2304]{1,0:T(8,128)(2,1)}) %reduce-scatter.28.cloned.1.call-update) | async-done | bytes 1179664 | tf_op jit(solution)/shard_map/reduce_scatter | solution.py:191
  1552.3 44.8 %all-gather.44.cloned.1.call-done = bf16[1024,2304]{1,0:T(8,128)(2,1)} async-done(((bf16[256,2304]{1,0:T(8,128)(2,1)}), bf16[1024,2304]{1,0:T(8,128)(2,1)}) %all-gather.44.cloned.1.call-update) | async-done | bytes 4718608 | tf_op jit(solution)/shard_map/all_gather | solution.py:178
  1615.4 17.0 convolution_bitcast_fusion.8
  1632.5 17.5 multiply_bitcast_fusion
  1666.1 18.8 copy.150
  1684.8 24.0 reshape.1000
  1760.1 82.8 %copy.156 = f32[8,2,16,9216]{2,1,0,3:T(2,128)} copy(f32[8,2,16,9216]{3,2,1,0:T(8,128)} %multiply_dynamic-update-slice_fusion) | data formatting | bytes 18874368
  1843.0 101.4 %reshape.1006 = f32[9216,256]{1,0:T(8,128)} reshape(f32[9216,8,2,16]{3,2,1,0:T(2,128)} %bitcast.112) | data formatting | bytes 18874368
  2025.8 27.1 %reduce-scatter.44.cloned.1.call-done = f32[72,256]{1,0:T(8,128)} async-done(((f32[2304,256]{1,0:T(8,128)}), f32[72,256]{1,0:T(8,128)}) %reduce-scatter.44.cloned.1.call-update) | async-done | bytes 73744
  2054.9 139.4 %reduce-scatter.42.cloned.1.call-done = f32[288,256]{1,0:T(8,128)} async-done(((f32[9216,256]{1,0:T(8,128)}), f32[288,256]{1,0:T(8,128)}) %reduce-scatter.42.cloned.1.call-update) | async-done | bytes 294928
  2200.9 129.9 %reduce-scatter.40.cloned.1.call-done = f32[32,256]{1,0:T(8,128)} async-done(((f32[1024,256]{1,0:T(8,128)}), f32[32,256]{1,0:T(8,128)}) %reduce-scatter.40.cloned.1.call-update) | async-done | bytes 32784
  2332.8 131.1 %reduce-scatter.38.cloned.1.call-done = f32[64,128]{1,0:T(8,128)} async-done(((f32[2048,128]{1,0:T(8,128)}), f32[64,128]{1,0:T(8,128)}) %reduce-scatter.38.cloned.1.call-update) | async-done | bytes 32784
  2465.5 135.9 %reduce-scatter.32.cloned.1.call-done = f32[8,72,80]{2,0,1:T(8,128)} async-done(((f32[8,2304,80]{2,0,1:T(8,128)}), f32[8,72,80]{2,0,1:T(8,128)}) %reduce-scatter.32.cloned.1.call-update) | async-done | bytes 184336 | tf_op jit(solution)/shard_map/reduce_scatter | solution.py:555
  2603.2 57.7 %reduce-scatter.30.cloned.1.call-done = bf16[256,2304]{1,0:T(8,128)(2,1)} async-done(((bf16[1024,2304]{1,0:T(8,128)(2,1)}), bf16[256,2304]{1,0:T(8,128)(2,1)}) %reduce-scatter.30.cloned.1.call-update) | async-done | bytes 1179664 | tf_op jit(solution)/shard_map/reduce_scatter | solution.py:191
  (468 shorter events, 488.4 us)
Async XLA Ops:
  7.2 315.2 %all-gather.20.cloned.1.call-start = ((), (), s32[]{:S(2)}) async-start(), calls=%async_computation.13 | async-start | bytes 4866048 | tf_op jit(solution)/shard_map/all_gather | solution.py:138
  8.9 333.8 %all-gather.22.cloned.1.call-start = ((), (), s32[]{:S(2)}) async-start(), calls=%async_computation.14 | async-start | bytes 2654208 | tf_op jit(solution)/shard_map/all_gather | solution.py:158
  9.7 333.0 %all-gather.16.cloned.1.call-start = ((), (), s32[]{:S(2)}) async-start(), calls=%async_computation.11 | async-start | bytes 5898240 | tf_op jit(solution)/shard_map/all_gather | solution.py:174
  15.6 337.5 %all-gather.24.cloned.1.call-start = ((), (), s32[]{:S(2)}) async-start(), calls=%async_computation.15 | async-start | bytes 5308416 | tf_op jit(solution)/shard_map/all_gather | solution.py:159
  16.2 358.3 %all-gather.18.cloned.1.call-start = ((), (), s32[]{:S(2)}) async-start(), calls=%async_computation.12 | async-start | bytes 5308416 | tf_op jit(solution)/shard_map/all_gather | solution.py:160
  16.8 370.6 %all-gather.26.cloned.1.call-start = ((), (), s32[]{:S(2)}) async-start(), calls=%async_computation.16 | async-start | bytes 2654208 | tf_op jit(solution)/shard_map/all_gather | solution.py:161
  17.4 542.3 %all-gather.28.cloned.1.call-start = ((), (), s32[]{:S(2)}) async-start(), calls=%async_computation.18 | async-start | bytes 9732096 | tf_op jit(solution)/shard_map/all_gather | solution.py:144
  18.4 574.6 %reduce-scatter.24.cloned.1.call-start = ((), (), s32[]{:S(2)}) async-start(), calls=%async_computation.17 | async-start | bytes 5898240 | tf_op jit(solution)/shard_map/reduce_scatter | solution.py:183
  393.7 382.9 %all-gather.34.cloned.1.call-start = ((), (), s32[]{:S(2)}) async-start(), calls=%async_computation.21 | async-start | bytes 38928384 | tf_op jit(solution)/shard_map/all_gather | solution.py:143
  396.7 480.1 %all-gather.36.cloned.1.call-start = ((), (), s32[]{:S(2)}) async-start(), calls=%async_computation.22 | async-start | bytes 11943936 | tf_op jit(solution)/shard_map/all_gather | solution.py:169
  397.3 536.8 %all-gather.30.cloned.1.call-start = ((), (), s32[]{:S(2)}) async-start(), calls=%async_computation.19 | async-start | bytes 5898240 | tf_op jit(solution)/shard_map/all_gather | solution.py:174
  559.7 972.7 %copy-start.53 = (bf16[256,8]{0,1:T(8,128)(2,1)}, bf16[256,8]{0,1:T(8,128)(2,1)S(1)}, u32[]{:S(2)}) copy-start(bf16[256,8]{0,1:T(8,128)(2,1)S(1)} %get-tuple-element.145) | copy-start | bytes 12292
  596.9 739.9 %copy-start.3 = (f32[256,2304]{1,0:T(8,128)}, f32[256,2304]{1,0:T(8,128)S(1)}, u32[]{:S(2)}) copy-start(f32[256,2304]{1,0:T(8,128)S(1)} %get-tuple-element.111) | copy-start | bytes 7077892
  599.6 436.5 %all-gather.32.cloned.1.call-start = ((), (), s32[]{:S(2)}) async-start(), calls=%async_computation.20 | async-start | bytes 11943936 | tf_op jit(solution)/shard_map/all_gather | solution.py:168
  600.2 536.4 %all-gather.38.cloned.1.call-start = ((), (), s32[]{:S(2)}) async-start(), calls=%async_computation.23 | async-start | bytes 11943936 | tf_op jit(solution)/shard_map/all_gather | solution.py:170
  600.9 661.5 %all-gather.40.cloned.1.call-start = ((), (), s32[]{:S(2)}) async-start(), calls=%async_computation.25 | async-start | bytes 19464192 | tf_op jit(solution)/shard_map/all_gather | solution.py:140
  602.2 732.1 %reduce-scatter.26.cloned.1.call-start = ((), (), s32[]{:S(2)}) async-start(), calls=%async_computation.24 | async-start | bytes 5898240 | tf_op jit(solution)/shard_map/reduce_scatter | solution.py:183
  1152.8 242.3 %all-gather.42.cloned.1.call-start = ((), (), s32[]{:S(2)}) async-start(), calls=%async_computation.26 | async-start | bytes 5898240 | tf_op jit(solution)/shard_map/all_gather | solution.py:178
  1339.3 139.9 %all-reduce.3.cloned.1.call-start = ((), (), s32[]{:S(2)}) async-start(), calls=%async_computation.28 | async-start | bytes 131072 | tf_op jit(solution)/shard_map/psum | solution.py:199
  1430.5 101.9 %reduce-scatter.28.cloned.1.call-start = ((), (), s32[]{:S(2)}) async-start(), calls=%async_computation.27 | async-start | bytes 5898240 | tf_op jit(solution)/shard_map/reduce_scatter | solution.py:191
  1466.7 130.3 %all-gather.44.cloned.1.call-start = ((), (), s32[]{:S(2)}) async-start(), calls=%async_computation.29 | async-start | bytes 5898240 | tf_op jit(solution)/shard_map/all_gather | solution.py:178
  1539.8 444.0 %all-reduce.5.cloned.1.call-start = ((), (), s32[]{:S(2)}) async-start(), calls=%async_computation.31 | async-start | bytes 196608 | tf_op jit(solution)/shard_map/psum | solution.py:199
  1661.5 360.1 %reduce-scatter.36.cloned.1.call-start = ((), (), s32[]{:S(2)}) async-start(), calls=%async_computation.34 | async-start | bytes 4866048
  1708.8 315.2 %reduce-scatter.34.cloned.1.call-start = ((), (), s32[]{:S(2)}) async-start(), calls=%async_computation.33 | async-start | bytes 1081344
  1722.1 330.8 %reduce-scatter.44.cloned.1.call-start = ((), (), s32[]{:S(2)}) async-start(), calls=%async_computation.38 | async-start | bytes 2433024
  1747.3 447.0 %reduce-scatter.42.cloned.1.call-start = ((), (), s32[]{:S(2)}) async-start(), calls=%async_computation.37 | async-start | bytes 9732096
  1944.4 386.4 %reduce-scatter.40.cloned.1.call-start = ((), (), s32[]{:S(2)}) async-start(), calls=%async_computation.36 | async-start | bytes 1081344
  1968.5 495.4 %reduce-scatter.38.cloned.1.call-start = ((), (), s32[]{:S(2)}) async-start(), calls=%async_computation.35 | async-start | bytes 1081344
  1980.4 621.1 %reduce-scatter.32.cloned.1.call-start = ((), (), s32[]{:S(2)}) async-start(), calls=%async_computation.32 | async-start | bytes 9732096 | tf_op jit(solution)/shard_map/reduce_scatter | solution.py:555
  1997.0 663.9 %reduce-scatter.30.cloned.1.call-start = ((), (), s32[]{:S(2)}) async-start(), calls=%async_computation.30 | async-start | bytes 5898240 | tf_op jit(solution)/shard_map/reduce_scatter | solution.py:191
  2024.1 636.8 %copy-start.10 = (bf16[256,2304]{1,0:T(8,128)(2,1)S(1)}, bf16[256,2304]{1,0:T(8,128)(2,1)}, u32[]{:S(2)}) copy-start(bf16[256,2304]{1,0:T(8,128)(2,1)} %param.19) | copy-start | bytes 3538948
  2024.1 636.8 %copy-start.76 = (f32[2304]{0:T(1024)S(1)}, f32[2304]{0:T(1024)}, u32[]{:S(2)}) copy-start(f32[2304]{0:T(1024)} %copy-done.75) | copy-start | bytes 27652
  (104 other events, 2531.4 us)
Sparse Core Ops, SparseCore 0:
  11.5 77.0 all-gather.19
  90.2 34.2 all-gather.21
  126.9 80.6 all-gather.15
  209.1 62.6 all-gather.23
  273.3 55.9 all-gather.17
  330.8 31.7 all-gather.25
  366.1 98.4 all-gather.27
  467.5 87.9 reduce-scatter.23
  559.0 217.5 all-gather.33
  778.1 98.6 all-gather.35
  878.6 55.4 all-gather.29
  935.6 100.4 all-gather.31
  1037.7 98.8 all-gather.37
  1139.4 123.0 all-gather.39
  1265.3 55.2 reduce-scatter.25
  1339.5 55.6 all-gather.41
  1430.6 41.4 all-reduce.2
  1475.3 57.0 reduce-scatter.27
  1539.9 57.0 all-gather.43
  1661.6 41.8 all-reduce.4
  1709.0 106.9 reduce-scatter.35
  1818.4 134.0 reduce-scatter.33
  1957.8 95.0 reduce-scatter.43
  2059.7 134.5 reduce-scatter.41
  2196.5 134.2 reduce-scatter.39
  2333.0 130.7 reduce-scatter.37
  2469.6 131.8 reduce-scatter.31
  2604.8 56.0 reduce-scatter.29
where the time goes:
time: 2690 us; the launch traced here: 2670 us
  waiting for transfers between devices  1310 us (49%)
  local copies, waits for them, and re-layouts  538 us (20%)
  blocking collectives  485 us (18%)
  matrix products  279 us (10%)
  other arithmetic  37.4 us (1%)
    unnamed x34, waiting for transfers between devices  432 us
    unnamed x261, local copies, waits for them, and re-layouts  402 us
    all_gather x1, waiting for transfers between devices, per_device(): lax.all_gather(lift_gateup, ('dp', 'tensor'), axis=3, tiled=True)  174 us
    all_gather x1, blocking collectives, per_device(): lax.all_gather(adapt_heads, ('dp', 'tensor'), axis=1, tiled=True)  147 us
    all_gather x1, blocking collectives, per_device(): lax.all_gather(lift_query, ('dp', 'tensor'), axis=2, tiled=True)  147 us
    all_gather x1, blocking collectives, per_device(): lax.all_gather(lift_keyval, ('dp', 'tensor'), axis=3, tiled=True)  139 us
    reduce_scatter x1, waiting for transfers between devices, per_device(): lax.psum_scatter(in_term, ('dp', 'tensor'), scatter_dimension=1, tiled=True)  136 us
    reduce_scatter x2, waiting for transfers between devices, scatter_backward(): lax.psum_scatter(term_fn(jnp.int32(0), lax.axis_size('tensor') * rows_her...  109 us
  transfers between devices with their start and end apart: 28, of which 15 were waited for; matrix products, arithmetic and copies ran while one was open for 27% of the time, Pallas kernels for 0%

commit v1 on v0

v1 whole, which is shorter than its diff:
```python
import functools

import jax
import jax.numpy as jnp
from jax import lax
from jax.experimental import pallas as pl
from jax.experimental.pallas import tpu as pltpu
from jax.sharding import PartitionSpec as P

D = 2304
HQ = 8
KV = 4
HD = 256
FF = 9216
NA = 8
RANK = 16
LEN = 1024
LANES = 128

EPSILON = 1e-06
SOFT_CAP = 50.0
MESH = pl.DeviceIdType.MESH
BF16 = jnp.bfloat16
F32 = jnp.float32
VMEM_LIMIT = 48 * 1024 * 1024


def rms_norm(values, gain_row):
    return (
        values * lax.rsqrt(jnp.mean(values * values, axis=-1, keepdims=True) + EPSILON) * gain_row
    )


def norm_back(values, gain_row, gradient):
    inverse = lax.rsqrt(jnp.mean(values * values, axis=-1, keepdims=True) + EPSILON)
    scaled = gradient * gain_row
    normed = values * inverse
    return inverse * (scaled - normed * jnp.mean(scaled * normed, axis=-1, keepdims=True))


def gated_gelu(gate_in, up_in):
    return jax.nn.gelu(gate_in, approximate=True) * up_in


def tables(length, size):
    half_size = size // 2
    frequency = 10000.0 ** (-2.0 * jnp.arange(half_size, dtype=F32) / size)
    angles = jnp.arange(length, dtype=F32)[:, None] * frequency[None, :]
    return (jnp.cos(angles)[:, None, :], jnp.sin(angles)[:, None, :])


def rotate(values, cosine, sine):
    half_size = values.shape[-1] // 2
    first_half = values[..., :half_size]
    second_half = values[..., half_size:]
    return jnp.concatenate(
        [first_half * cosine - second_half * sine, second_half * cosine + first_half * sine],
        axis=-1,
    )


def nn(a, b):
    return lax.dot_general(a, b, (((1,), (0,)), ((), ())), preferred_element_type=F32)


def nt(a, b):
    return lax.dot_general(a, b, (((1,), (1,)), ((), ())), preferred_element_type=F32)


def tn(a, b):
    return lax.dot_general(a, b, (((0,), (0,)), ((), ())), preferred_element_type=F32)


def pad_lanes(values):
    return jnp.pad(values, [(0, 0)] * (values.ndim - 1) + [(0, LANES - values.shape[-1])])


def greet(peers):
    barrier = pltpu.get_barrier_semaphore()
    for peer in peers:
        pl.semaphore_signal(barrier, inc=1, device_id=peer, device_id_type=MESH)
    pl.semaphore_wait(barrier, len(peers))


def square_peers(index):
    return index + 1 - 2 * lax.rem(index, 2), lax.rem(index + 2, 4), 3 - index


def remote(source, target, send_sem, recv_sem, peer):
    return pltpu.make_async_remote_copy(
        src_ref=source,
        dst_ref=target,
        send_sem=send_sem,
        recv_sem=recv_sem,
        device_id={"tensor": peer},
        device_id_type=MESH,
    )


def gather_kernel(count, rows, x_ref, o_ref, local_sem, send_sem, recv_sem):
    me = lax.axis_index("tensor")
    if count == 4:
        across, down, _ = square_peers(me)
        greet([{"tensor": across}, {"tensor": down}])
        own = pltpu.make_async_copy(x_ref, o_ref.at[pl.ds(me * rows, rows)], local_sem)
        own.start()
        half = rows // 2
        links = (across, down)
        first = [[None, None], [None, None]]
        for order in range(2):
            for link in range(2):
                part = order if link == 0 else 1 - order
                target = o_ref.at[pl.ds(me * rows + part * half, half)]
                copy = remote(
                    x_ref.at[pl.ds(part * half, half)],
                    target,
                    send_sem.at[link, part],
                    recv_sem.at[link, part],
                    links[link],
                )
                copy.start()
                first[link][part] = copy
        second = []
        for link in range(2):
            first[link][link].wait_recv()
            block = o_ref.at[pl.ds(links[link] * rows + link * half, half)]
            copy = remote(
                block, block, send_sem.at[2, link], recv_sem.at[2, link], links[1 - link]
            )
            copy.start()
            second.append(copy)
        for link in range(2):
            first[link][1 - link].wait_recv()
        for copy in second:
            copy.wait_recv()
        own.wait()
        for link in range(2):
            for part in range(2):
                first[link][part].wait_send()
        for copy in second:
            copy.wait_send()
    else:
        peers = [lax.rem(me + step, count) for step in range(1, count)]
        greet([{"tensor": peer} for peer in peers])
        own = pltpu.make_async_copy(x_ref, o_ref.at[pl.ds(me * rows, rows)], local_sem)
        own.start()
        copies = []
        for step, peer in enumerate(peers):
            copy = remote(
                x_ref,
                o_ref.at[pl.ds(me * rows, rows)],
                send_sem.at[0, step],
                recv_sem.at[0, step],
                peer,
            )
            copy.start()
            copies.append(copy)
        own.wait()
        for copy in copies:
            copy.wait()


def tensor_gather(values, count):
    rows, width = values.shape
    slots = max(2, count - 1)
    return pl.pallas_call(
        functools.partial(gather_kernel, count, rows),
        out_shape=jax.ShapeDtypeStruct((count * rows, width), values.dtype),
        in_specs=[pl.BlockSpec(memory_space=pl.ANY)],
        out_specs=pl.BlockSpec(memory_space=pl.ANY),
        scratch_shapes=[
            pltpu.SemaphoreType.DMA,
            pltpu.SemaphoreType.DMA((3, slots)),
            pltpu.SemaphoreType.DMA((3, slots)),
        ],
        compiler_params=pltpu.CompilerParams(
            collective_id=1, has_side_effects=True, vmem_limit_bytes=VMEM_LIMIT
        ),
        name="tensor_gather",
    )(values)


def scatter_kernel(count, rows, p_ref, q_ref, o_ref, l_ref, *scratch):
    me = lax.axis_index("tensor")
    payload = ((p_ref, o_ref), (q_ref, l_ref))
    if count == 4:
        across, down, far = square_peers(me)
        greet([{"tensor": across}, {"tensor": down}])
        half = rows // 2
        first = scratch[0:2]
        sums = scratch[2:4]
        second = scratch[4:6]
        send_sem, recv_sem = scratch[6], scratch[7]
        links = (across, down)
        copies = {}
        for which in (1, 0):
            for link in range(2):
                block = far if which == 1 else links[link]
                for item in range(2):
                    copy = remote(
                        payload[item][0].at[pl.ds(block * rows + link * half, half)],
                        first[item].at[link, which],
                        send_sem.at[item, link, which],
                        recv_sem.at[item, link, which],
                        links[link],
                    )
                    copy.start()
                    copies[item, link, which] = copy
        for link in range(2):
            block = links[1 - link]
            for item in range(2):
                copies[item, link, 1].wait_recv()
                mine = payload[item][0][pl.ds(block * rows + link * half, half), :]
                sums[item][link] = (
                    mine.astype(F32) + first[item][link, 1].astype(F32)
                ).astype(BF16)
                copy = remote(
                    sums[item].at[link],
                    second[item].at[link],
                    send_sem.at[item, link, 2],
                    recv_sem.at[item, link, 2],
                    links[1 - link],
                )
                copy.start()
                copies[item, link, 2] = copy
        for link in range(2):
            for item in range(2):
                copies[item, link, 0].wait_recv()
                mine = payload[item][0][pl.ds(me * rows + link * half, half), :]
                payload[item][1][pl.ds(link * half, half), :] = mine.astype(F32) + first[item][
                    link, 0
                ].astype(F32)
        for link in range(2):
            for item in range(2):
                copies[item, link, 2].wait_recv()
                payload[item][1][pl.ds(link * half, half), :] += second[item][link].astype(F32)
        for copy in copies.values():
            copy.wait_send()
    else:
        peers = [lax.rem(me + step, count) for step in range(1, count)]
        greet([{"tensor": peer} for peer in peers])
        first = scratch[0:2]
        send_sem, recv_sem = scratch[2], scratch[3]
        copies = []
        for step, peer in enumerate(peers):
            for item in range(2):
                copy = remote(
                    payload[item][0].at[pl.ds(peer * rows, rows)],
                    first[item].at[step],
                    send_sem.at[item, step],
                    recv_sem.at[item, step],
                    peer,
                )
                copy.start()
                copies.append((item, step, copy))
        for item in range(2):
            payload[item][1][...] = payload[item][0][pl.ds(me * rows, rows), :].astype(F32)
        for item, step, copy in copies:
            copy.wait()
            payload[item][1][...] += first[item][step].astype(F32)


def tensor_scatter(values, narrow, count):
    rows = values.shape[0] // count
    widths = (values.shape[1], narrow.shape[1])
    if count == 4:
        half = rows // 2
        scratch = [pltpu.VMEM((2, 2, half, width), BF16) for width in widths]
        scratch += [pltpu.VMEM((2, half, width), BF16) for width in widths]
        scratch += [pltpu.VMEM((2, half, width), BF16) for width in widths]
        scratch += [pltpu.SemaphoreType.DMA((2, 2, 3)), pltpu.SemaphoreType.DMA((2, 2, 3))]
    else:
        scratch = [pltpu.VMEM((count - 1, rows, width), BF16) for width in widths]
        scratch += [pltpu.SemaphoreType.DMA((2, count - 1))] * 2
    vmem = pl.BlockSpec(memory_space=pltpu.VMEM)
    return pl.pallas_call(
        functools.partial(scatter_kernel, count, rows),
        out_shape=tuple(jax.ShapeDtypeStruct((rows, width), F32) for width in widths),
        in_specs=[vmem, vmem],
        out_specs=(vmem, vmem),
        scratch_shapes=scratch,
        compiler_params=pltpu.CompilerParams(
            collective_id=2, has_side_effects=True, vmem_limit_bytes=VMEM_LIMIT
        ),
        name="tensor_scatter",
    )(values, narrow)


class Layout:
    def __init__(self):
        self.dp = lax.axis_size("dp")
        self.tensor = lax.axis_size("tensor")
        self.total = self.dp * self.tensor
        self.d = lax.axis_index("dp")
        self.t = lax.axis_index("tensor")
        self.me = self.d * self.tensor + self.t
        self.heads_here = HQ // self.tensor
        self.ratio = HQ // KV
        self.share = max(1, self.tensor // KV)
        self.kv_owners = self.total // KV
        self.kv_head = self.t * self.heads_here // self.ratio
        self.user = self.me // self.dp
        self.kv_slice_head = self.me // self.kv_owners

    def device(self, flat):
        return {"dp": flat // self.tensor, "tensor": lax.rem(flat, self.tensor)}


def greet_all(lay):
    barrier = pltpu.get_barrier_semaphore()

    def signal(step, unused):
        peer = lax.rem(lay.me + step, lay.total)
        pl.semaphore_signal(
            barrier, inc=1, device_id=lay.device(peer), device_id_type=MESH
        )
        return unused

    lax.fori_loop(1, lay.total, signal, 0)
    pl.semaphore_wait(barrier, lay.total - 1)


def send_or_keep(lay, sends, source, target, send_sem, recv_sem, flat, maybe_own):
    def far():
        return pltpu.make_async_remote_copy(
            src_ref=source,
            dst_ref=target,
            send_sem=send_sem,
            recv_sem=recv_sem,
            device_id=lay.device(flat),
            device_id_type=MESH,
        )

    if maybe_own is None:
        copy = far()
        copy.start()
        sends.append((None, copy))
        return

    @pl.when(maybe_own)
    def _():
        pltpu.make_async_copy(source, target, recv_sem).start()

    @pl.when(jnp.logical_not(maybe_own))
    def _():
        far().start()

    sends.append((maybe_own, far()))


def finish(sends, received):
    for own, copy in sends:
        if own is None:
            copy.wait_send()
        else:

            @pl.when(jnp.logical_not(own))
            def _(copy=copy):
                copy.wait_send()

    for target, sem in received:
        pltpu.make_async_copy(target, target, sem).wait()


def tables_kernel(d_ref, f_ref, h_ref, k_ref, do_ref, fo_ref, ho_ref, ko_ref, *sems):
    lay = Layout()
    send_sems, recv_sem = sems[:4], sems[4]
    greet_all(lay)
    sends = []
    for step in range(lay.dp):
        group = lax.rem(lay.d + step, lay.dp)
        flat = group * lay.tensor + lay.user
        own = (lay.user == lay.t) if step == 0 else None
        for item, (source, target) in enumerate(((f_ref, fo_ref), (h_ref, ho_ref))):
            send_or_keep(
                lay,
                sends,
                source.at[group],
                target.at[lax.rem(lay.me, lay.dp)],
                send_sems[item].at[step],
                recv_sem.at[item],
                flat,
                own,
            )
        for extra in range(lay.share):
            user = lay.kv_slice_head * lay.share + extra
            flat = group * lay.tensor + user
            send_or_keep(
                lay,
                sends,
                k_ref.at[group],
                ko_ref.at[lax.rem(lay.me, lay.kv_owners)],
                send_sems[2].at[step, extra],
                recv_sem.at[2],
                flat,
                (user == lay.t) if step == 0 else None,
            )
    pltpu.make_async_copy(d_ref.at[lay.d], do_ref.at[lay.me], recv_sem.at[3]).start()
    for step in range(1, lay.total):
        flat = lax.rem(lay.me + step, lay.total)
        send_or_keep(
            lay,
            sends,
            d_ref.at[flat // lay.tensor],
            do_ref.at[lay.me],
            send_sems[3].at[step],
            recv_sem.at[3],
            flat,
            None,
        )
    finish(
        sends,
        (
            (fo_ref, recv_sem.at[0]),
            (ho_ref, recv_sem.at[1]),
            (ko_ref, recv_sem.at[2]),
            (do_ref, recv_sem.at[3]),
        ),
    )


def grads_kernel(d_ref, f_ref, h_ref, k_ref, do_ref, fo_ref, ho_ref, ko_ref, *sems):
    lay = Layout()
    send_sems, recv_sem = sems[:4], sems[4]
    greet_all(lay)
    sends = []
    for step in range(lay.dp):
        slot = lax.rem(lay.d + step, lay.dp)
        flat = lay.t * lay.dp + slot
        for item, (source, target) in enumerate(((f_ref, fo_ref), (h_ref, ho_ref))):
            send_or_keep(
                lay,
                sends,
                source.at[slot],
                target.at[lay.d],
                send_sems[item].at[step],
                recv_sem.at[item],
                flat,
                flat == lay.me,
            )
    for step in range(lay.kv_owners):
        slot = lax.rem(lay.d + step, lay.kv_owners)
        flat = lay.kv_head * lay.kv_owners + slot
        send_or_keep(
            lay,
            sends,
            k_ref.at[slot],
            ko_ref.at[lay.d * lay.share + lax.rem(lay.t, lay.share)],
            send_sems[2].at[step // lay.share, step % lay.share],
            recv_sem.at[2],
            flat,
            flat == lay.me,
        )
    pltpu.make_async_copy(d_ref.at[lay.me], do_ref.at[lay.me], recv_sem.at[3]).start()
    for step in range(1, lay.total):
        flat = lax.rem(lay.me + step, lay.total)
        send_or_keep(
            lay,
            sends,
            d_ref.at[flat],
            do_ref.at[lay.me],
            send_sems[3].at[step],
            recv_sem.at[3],
            flat,
            None,
        )
    finish(
        sends,
        (
            (fo_ref, recv_sem.at[0]),
            (ho_ref, recv_sem.at[1]),
            (ko_ref, recv_sem.at[2]),
            (do_ref, recv_sem.at[3]),
        ),
    )


def exchange(kernel, name, number, arrays, outs, dp, total, share):
    anywhere = pl.BlockSpec(memory_space=pl.ANY)
    return pl.pallas_call(
        kernel,
        out_shape=tuple(jax.ShapeDtypeStruct(shape, BF16) for shape in outs),
        in_specs=[anywhere] * 4,
        out_specs=(anywhere,) * 4,
        scratch_shapes=[
            pltpu.SemaphoreType.DMA((dp,)),
            pltpu.SemaphoreType.DMA((dp,)),
            pltpu.SemaphoreType.DMA((dp, share)),
            pltpu.SemaphoreType.DMA((total,)),
            pltpu.SemaphoreType.DMA((4,)),
        ],
        compiler_params=pltpu.CompilerParams(
            collective_id=number, has_side_effects=True, vmem_limit_bytes=VMEM_LIMIT
        ),
        name=name,
    )(*arrays)


def per_device(
    layer_in,
    cotangent,
    lengths,
    adapter_ids,
    norm_gains,
    query_weight,
    key_weight,
    value_weight,
    out_weight,
    gate_weight,
    up_weight,
    down_weight,
    adapt_in,
    adapt_heads,
    adapt_hidden,
    lift_query,
    lift_keyval,
    lift_gateup,
    lift_resid,
):
    lay = Layout()
    count = lay.tensor
    rows = layer_in.shape[0]
    group_rows = rows * count
    assert lengths.shape[0] == 1 and group_rows == LEN
    heads_here = lay.heads_here
    head_width = heads_here * HD
    hidden_here = FF // count
    assert lay.ratio % heads_here == 0

    key_cols = lax.dynamic_slice_in_dim(key_weight, lay.kv_head * HD, HD, 1)
    value_cols = lax.dynamic_slice_in_dim(value_weight, lay.kv_head * HD, HD, 1)
    attn_shard = jnp.concatenate([query_weight, key_cols, value_cols, out_weight.T], axis=1)
    attn_w = lax.all_gather(attn_shard, "dp", axis=0, tiled=True)
    gate_up_shard = jnp.concatenate([gate_weight, up_weight], axis=1)
    down_shard = down_weight.T
    attn_shard, gate_up_shard, down_shard = lax.optimization_barrier(
        (attn_shard, gate_up_shard, down_shard)
    )
    gate_up_w = lax.all_gather(gate_up_shard, "dp", axis=0, tiled=True)
    down_w = lax.all_gather(down_shard, "dp", axis=0, tiled=True)
    qkv_width = head_width + 2 * HD

    all_ids = lax.all_gather(adapter_ids[:, 0], "dp", axis=0, tiled=True)
    group_hot = (all_ids[:, None] == jnp.arange(NA, dtype=jnp.int32)[None, :]).astype(BF16)

    def rows_of(table):
        moved = jnp.moveaxis(table, -1, 1)
        return moved.reshape(NA, moved.shape[1], -1)

    def choose(*parts):
        packed = pad_lanes(jnp.concatenate(parts, axis=-1))
        return lax.dot_general(
            group_hot, packed, (((1,), (0,)), ((), ())), preferred_element_type=F32
        ).astype(BF16)

    d_send = choose(adapt_in, rows_of(lift_resid))
    f_send = choose(adapt_hidden, rows_of(lift_gateup))
    h_send = choose(adapt_heads, rows_of(lift_query))
    k_send = choose(rows_of(lift_keyval))
    d_rows, f_rows, h_rows, k_rows = (item.shape[1] for item in (d_send, f_send, h_send, k_send))
    d_tab, f_tab, h_tab, k_tab = exchange(
        tables_kernel,
        "adapter_tables",
        3,
        (d_send, f_send, h_send, k_send),
        (
            (lay.total, d_rows, LANES),
            (lay.dp, f_rows, LANES),
            (lay.dp, h_rows, LANES),
            (lay.kv_owners, k_rows, LANES),
        ),
        lay.dp,
        lay.total,
        lay.share,
    )
    d_tab = d_tab.reshape(D, LANES)
    f_tab = f_tab.reshape(hidden_here, LANES)
    h_tab = h_tab.reshape(head_width, LANES)
    k_tab = k_tab.reshape(HD, LANES)
    in_qkv, in_gu = d_tab[:, : 3 * RANK], d_tab[:, 3 * RANK : 5 * RANK]
    lift_out, lift_down = d_tab[:, 5 * RANK : 6 * RANK], d_tab[:, 6 * RANK : 7 * RANK]
    map_hidden, lift_gate, lift_up = (f_tab[:, i * RANK : (i + 1) * RANK] for i in range(3))
    map_heads, lift_q = h_tab[:, :RANK], h_tab[:, RANK : 2 * RANK]
    lift_k, lift_v = k_tab[:, :RANK], k_tab[:, RANK : 2 * RANK]

    row_start = lay.t * rows
    length = lengths[0]
    row_valid = ((row_start + jnp.arange(rows, dtype=jnp.int32)) < length).astype(F32)[:, None]
    cosine, sine = tables(LEN, HD)
    place = jnp.arange(LEN, dtype=jnp.int32)
    allowed = (place[:, None] >= place[None, :]) & (place[None, :] < length)

    resid_in = layer_in.astype(F32)
    normed_attn = rms_norm(resid_in, norm_gains[0]).astype(BF16)
    seq_attn = tensor_gather(normed_attn, count)
    low_qkv = nn(seq_attn, in_qkv).astype(BF16)
    low_q, low_k, low_v = (low_qkv[:, i * RANK : (i + 1) * RANK] for i in range(3))
    qkv = nn(seq_attn, attn_w[:, :qkv_width])
    query_pre = (qkv[:, :head_width] + nt(low_q, lift_q)).reshape(LEN, heads_here, HD)
    key_pre = (qkv[:, head_width : head_width + HD] + nt(low_k, lift_k)).reshape(LEN, 1, HD)
    value_pre = qkv[:, head_width + HD :] + nt(low_v, lift_v)
    queries = (rotate(query_pre, cosine, sine) * HD ** (-0.5)).astype(BF16)
    keys = rotate(key_pre, cosine, sine).astype(BF16).reshape(LEN, HD)
    values = value_pre.astype(BF16)

    def scores_of():
        raw = jnp.einsum("qhd,kd->hqk", queries, keys, preferred_element_type=F32)
        squash = jnp.tanh(raw / SOFT_CAP)
        return squash, jnp.where(allowed[None], jnp.exp(SOFT_CAP * squash), 0.0)

    squash, weights = scores_of()
    inverse_total = 1.0 / jnp.sum(weights, axis=-1, keepdims=True)
    attended = jnp.einsum(
        "hqk,kd->qhd", (weights * inverse_total).astype(BF16), values, preferred_element_type=F32
    )
    attended = attended.astype(BF16).reshape(LEN, head_width)
    w_out = attn_w[:, qkv_width:]
    out_part = nt(attended, w_out).astype(BF16)
    low_out_part = pad_lanes(nn(attended, map_heads).astype(BF16))
    attn_main, low_out = tensor_scatter(out_part, low_out_part, count)
    low_out = low_out[:, :RANK].astype(BF16)
    attn_total = attn_main + nt(low_out, lift_out)
    resid_mid = resid_in + rms_norm(attn_total, norm_gains[1])

    normed_mlp = rms_norm(resid_mid, norm_gains[2]).astype(BF16)
    seq_mlp = tensor_gather(normed_mlp, count)
    low_gu = nn(seq_mlp, in_gu).astype(BF16)
    low_g, low_u = low_gu[:, :RANK], low_gu[:, RANK:]
    w_gate, w_up = gate_up_w[:, :hidden_here], gate_up_w[:, hidden_here:]
    gate = nn(seq_mlp, w_gate) + nt(low_g, lift_gate)
    up = nn(seq_mlp, w_up) + nt(low_u, lift_up)
    hidden = gated_gelu(gate, up).astype(BF16)
    down_part = nt(hidden, down_w).astype(BF16)
    low_down_part = pad_lanes(nn(hidden, map_hidden).astype(BF16))
    mlp_main, low_down = tensor_scatter(down_part, low_down_part, count)
    low_down = low_down[:, :RANK].astype(BF16)
    mlp_total = mlp_main + nt(low_down, lift_down)
    layer_out = (row_valid * (resid_mid + rms_norm(mlp_total, norm_gains[3]))).astype(BF16)

    grad_out = cotangent.astype(F32) * row_valid
    grad_mlp = norm_back(mlp_total, norm_gains[3], grad_out).astype(BF16)
    seq_grad_mlp = tensor_gather(grad_mlp, count)
    grad_low_down = nn(seq_grad_mlp, lift_down).astype(BF16)
    grad_hidden = nn(seq_grad_mlp, down_w) + nt(grad_low_down, map_hidden)
    unused, pull = jax.vjp(gated_gelu, gate, up)
    grad_gate, grad_up = pull(grad_hidden)
    grad_gate, grad_up = grad_gate.astype(BF16), grad_up.astype(BF16)
    low_gu_part = pad_lanes(
        jnp.concatenate([nn(grad_gate, lift_gate), nn(grad_up, lift_up)], axis=1).astype(BF16)
    )
    mlp_back_part = (nt(grad_gate, w_gate) + nt(grad_up, w_up)).astype(BF16)
    mlp_back, grad_low_gu = tensor_scatter(mlp_back_part, low_gu_part, count)
    grad_low_gu = grad_low_gu[:, : 2 * RANK].astype(BF16)
    grad_normed_mlp = mlp_back + nt(grad_low_gu, in_gu)
    grad_mid = grad_out + norm_back(resid_mid, norm_gains[2], grad_normed_mlp)

    grad_attn = norm_back(attn_total, norm_gains[1], grad_mid).astype(BF16)
    seq_grad_attn = tensor_gather(grad_attn, count)
    grad_low_out = nn(seq_grad_attn, lift_out).astype(BF16)
    grad_attended = (nn(seq_grad_attn, w_out) + nt(grad_low_out, map_heads)).astype(BF16)
    grad_heads = grad_attended.reshape(LEN, heads_here, HD)
    probs = weights * inverse_total
    probs_low = probs.astype(BF16)
    grad_probs = jnp.einsum("qhd,kd->hqk", grad_heads, values, preferred_element_type=F32)
    grad_value = jnp.einsum("hqk,qhd->kd", probs_low, grad_heads, preferred_element_type=F32)
    grad_capped = probs * (grad_probs - jnp.sum(probs * grad_probs, axis=-1, keepdims=True))
    grad_raw = (grad_capped * (1.0 - squash * squash)).astype(BF16)
    grad_query = jnp.einsum("hqk,kd->qhd", grad_raw, keys, preferred_element_type=F32)
    grad_key = jnp.einsum("hqk,qhd->kd", grad_raw, queries, preferred_element_type=F32)
    grad_q_pre = rotate(grad_query * HD ** (-0.5), cosine, -sine).astype(BF16)
    grad_q_pre = grad_q_pre.reshape(LEN, head_width)
    grad_k_pre = rotate(grad_key.reshape(LEN, 1, HD), cosine, -sine).astype(BF16)
    grad_k_pre = grad_k_pre.reshape(LEN, HD)
    grad_v_pre = grad_value.astype(BF16)
    low_qkv_part = pad_lanes(
        jnp.concatenate(
            [nn(grad_q_pre, lift_q), nn(grad_k_pre, lift_k), nn(grad_v_pre, lift_v)], axis=1
        ).astype(BF16)
    )
    grad_qkv = jnp.concatenate([grad_q_pre, grad_k_pre, grad_v_pre], axis=1)
    attn_back_part = nt(grad_qkv, attn_w[:, :qkv_width]).astype(BF16)
    attn_back, grad_low_qkv = tensor_scatter(attn_back_part, low_qkv_part, count)
    grad_low_qkv = grad_low_qkv[:, : 3 * RANK].astype(BF16)
    grad_normed_attn = attn_back + nt(grad_low_qkv, in_qkv)
    input_grad = (grad_mid + norm_back(resid_in, norm_gains[0], grad_normed_attn)).astype(BF16)

    def packed(parts, blocks):
        return pad_lanes(jnp.concatenate(parts, axis=1).astype(BF16)).reshape(
            blocks, -1, LANES
        )

    d_grad = packed(
        [
            tn(normed_attn, grad_low_qkv),
            tn(normed_mlp, grad_low_gu),
            tn(grad_attn, low_out),
            tn(grad_mlp, low_down),
        ],
        lay.total,
    )
    f_grad = packed(
        [tn(hidden, grad_low_down), tn(grad_gate, low_g), tn(grad_up, low_u)], lay.dp
    )
    h_grad = packed([tn(attended, grad_low_out), tn(grad_q_pre, low_q)], lay.dp)
    k_grad = packed([tn(grad_k_pre, low_k), tn(grad_v_pre, low_v)], lay.kv_owners)
    d_all, f_all, h_all, k_all = exchange(
        grads_kernel,
        "adapter_grads",
        4,
        (d_grad, f_grad, h_grad, k_grad),
        (
            (lay.total, d_rows, LANES),
            (lay.dp, f_rows, LANES),
            (lay.dp, h_rows, LANES),
            (lay.dp * lay.share, k_rows, LANES),
        ),
        lay.dp,
        lay.total,
        lay.share,
    )

    def collect(received):
        repeats = received.shape[0] // lay.dp
        hot = jnp.repeat(group_hot, repeats, axis=0)
        return lax.dot_general(
            hot, received, (((0,), (0,)), ((), ())), preferred_element_type=F32
        )

    d_all, f_all, h_all, k_all = (collect(item) for item in (d_all, f_all, h_all, k_all))

    def lift_form(values, shape):
        return jnp.moveaxis(values, 1, 2).reshape(shape)

    return (
        layer_out,
        input_grad,
        d_all[:, :, : 5 * RANK],
        h_all[:, :, :RANK],
        f_all[:, :, :RANK],
        lift_form(h_all[:, :, RANK : 2 * RANK], lift_query.shape),
        lift_form(k_all[:, :, : 2 * RANK], lift_keyval.shape),
        lift_form(f_all[:, :, RANK : 3 * RANK], lift_gateup.shape),
        lift_form(d_all[:, :, 5 * RANK : 7 * RANK], lift_resid.shape),
    )


def solution(mesh):
    return jax.shard_map(
        per_device,
        mesh=mesh,
        in_specs=(
            P(("dp", "tensor"), None),
            P(("dp", "tensor"), None),
            P("dp"),
            P("dp", None),
            P(),
            P("dp", "tensor"),
            P("dp", None),
            P("dp", None),
            P("tensor", "dp"),
            P("dp", "tensor"),
            P("dp", "tensor"),
            P("tensor", "dp"),
            P(None, ("dp", "tensor"), None),
            P(None, ("dp", "tensor"), None),
            P(None, ("dp", "tensor"), None),
            P(None, None, ("dp", "tensor")),
            P(None, None, None, ("dp", "tensor")),
            P(None, None, None, ("dp", "tensor")),
            P(None, None, None, ("dp", "tensor")),
        ),
        out_specs=(
            P(("dp", "tensor"), None),
            P(("dp", "tensor"), None),
            P(None, ("dp", "tensor"), None),
            P(None, ("dp", "tensor"), None),
            P(None, ("dp", "tensor"), None),
            P(None, None, ("dp", "tensor")),
            P(None, None, None, ("dp", "tensor")),
            P(None, None, None, ("dp", "tensor")),
            P(None, None, None, ("dp", "tensor")),
        ),
        check_vma=False,
    )
```

time: 2690 us -> 861 us (0.32)
  waiting for transfers between devices: 1310 us -> 102 us
  local copies, waits for them, and re-layouts: 538 us -> 35.6 us
  blocking collectives: 485 us -> 12.2 us
  Pallas kernels: 0 us -> 426 us
  matrix products: 279 us -> 235 us
    all_gather x15 -> x3, waiting for transfers between devices: 636 us -> 102 us  [the longest x1 54.3 us: per_device(): down_w = lax.all_gather(down_shard, 'dp', axis=0, tiled=True)]
    all_gather x5 -> x0, blocking collectives: 450 us -> none  [the longest x1 147 us: per_device(): lax.all_gather(adapt_heads, ('dp', 'tensor'), axis=1, tiled=True)]
    unnamed x34 -> x3, waiting for transfers between devices: 432 us -> 0.05 us
    pallas_call x0 -> x10, Pallas kernels: none -> 426 us  [the longest x4 173 us: tensor_scatter(): pl.pallas_call(functools.partial(scatter_kernel, count, rows), out_shape=...]
    unnamed x261 -> x203, local copies, waits for them, and re-layouts: 402 us -> 23.8 us
    reduce_scatter x5 -> x0, waiting for transfers between devices: 245 us -> none  [the longest x1 136 us: per_device(): lax.psum_scatter(in_term, ('dp', 'tensor'), scatter_dimension=1, tiled=True)]
    all_gather x6 -> x0, local copies, waits for them, and re-layouts: 68.8 us -> none  [the longest x1 33.6 us: per_device(): lax.all_gather(lift_gateup, ('dp', 'tensor'), axis=3, tiled=True)]
    dot_general x59 -> x57, matrix products: 279 us -> 235 us  [the longest x16 100 us: nt(): lax.dot_general(a, b, (((1,), (1,)), ((), ())), preferred_element_type=F32)]
  transfers between devices with their start and end apart: 28 -> 3, of which waited for: 15 -> 2; matrix products, arithmetic and copies ran while one was open for 27% -> 12% of each run, Pallas kernels for 0% -> 18%
where the time goes in v1:
time: 861 us; the launch traced here: 856 us
  Pallas kernels  426 us (49%)
  matrix products  235 us (27%)
  waiting for transfers between devices  102 us (12%)
  local copies, waits for them, and re-layouts  35.6 us (4%)
  other arithmetic  27.9 us (3%)
  between operations  17 us (2%)
  blocking collectives  12.2 us (1%)
    pallas_call x4, Pallas kernels, tensor_scatter(): pl.pallas_call(functools.partial(scatter_kernel, count, rows), out_shape=...  173 us
    pallas_call x4, Pallas kernels, tensor_gather(): pl.pallas_call(functools.partial(gather_kernel, count, rows), out_shape=j...  153 us
    dot_general x16, matrix products, nt(): lax.dot_general(a, b, (((1,), (1,)), ((), ())), preferred_element_type=F32)  100 us
    pallas_call x2, Pallas kernels, exchange(): pl.pallas_call(kernel, out_shape=tuple((jax.ShapeDtypeStruct(shape, BF16)...  99.3 us
    dot_general x16, matrix products, nn(): lax.dot_general(a, b, (((1,), (0,)), ((), ())), preferred_element_type=F32)  74.2 us
    all_gather x1, waiting for transfers between devices, per_device(): down_w = lax.all_gather(down_shard, 'dp', axis=0, tiled=True)  54.3 us
    all_gather x1, waiting for transfers between devices, per_device(): gate_up_w = lax.all_gather(gate_up_shard, 'dp', axis=0, tiled=True)  47.9 us
    unnamed x203, local copies, waits for them, and re-layouts  23.8 us
  transfers between devices with their start and end apart: 3, of which 2 were waited for; matrix products, arithmetic and copies ran while one was open for 12% of the time, Pallas kernels for 18%

profile of v1, /device:TPU:0, one launch (start us, length us, event | category | flops | bytes accessed | tf_op | source)
XLA Modules:
  0.0 856.0 jit_solution(2585271993703372732)
XLA Ops:
  16.0 12.2 %all-reduce.12 = s32[8]{0:T(128)S(1)} all-reduce(s32[8]{0:T(128)S(1)} %bitcast_dynamic-update-slice_fusion), channel_id=2, replica_groups=mesh['dp'=8,'tensor'=4] {'dp'}, use_global_device_ids=true, to_apply=%add.12 | all-reduce | flops 8 | bytes 64
  33.2 38.8 %tensor_gather.4 = bf16[1024,2304]{1,0:T(8,128)(2,1)S(1)} custom-call(bf16[256,2304]{1,0:T(8,128)(2,1)S(1)} %fusion.30.x_ref), custom_call_target="tpu_custom_call" | custom-call | tf_op jit(solution)/shard_map/tensor_gather/pallas_call | solution.py:166
  73.0 37.0 %adapter_tables.1 = (bf16[32,72,128]{2,1,0:T(8,128)(2,1)S(1)}, bf16[8,288,128]{2,1,0:T(8,128)(2,1)S(1)}, bf16[8,64,128]{2,1,0:T(8,128)(2,1)S(1)}, bf16[8,32,128]{2,1,0:T(8,128)(2,1)S(1)}) custom-call(bf16[8,72,128]{2,1,0:T(8,128)(2,1)S(1)} %copy.269.d_ref, bf16[8,288,128]{2,1,0:T(8,128)(2,1)S(1)} %copy.268.f_ref, bf16[8,64,128]{2,1,0:T(8,128)(2,1)S(1)} %copy.270.h_ref, ...), custom_call_target="tpu_custom_call" | custom-call | tf_op jit(solution)/shard_map/adapter_tables/pallas_call | solution.py:480
  115.9 8.6 fusion.25
  141.8 4.0 convolution_convert_fusion.10
  147.4 6.9 convolution_convert_fusion.p_ref
  154.3 40.3 %tensor_scatter.4 = (f32[256,2304]{1,0:T(8,128)S(1)}, f32[256,128]{1,0:T(8,128)S(1)}) custom-call(bf16[1024,2304]{1,0:T(8,128)(2,1)} %convolution_convert_fusion.p_ref, bf16[1024,128]{1,0:T(8,128)(2,1)S(1)} %pad.51.q_ref), custom_call_target="tpu_custom_call" | custom-call | tf_op jit(solution)/shard_map/tensor_scatter/pallas_call | solution.py:276
  197.8 35.3 %tensor_gather.5 = bf16[1024,2304]{1,0:T(8,128)(2,1)S(1)} custom-call(bf16[256,2304]{1,0:T(8,128)(2,1)S(1)} %multiply_convert_fusion.6.x_ref), custom_call_target="tpu_custom_call" | custom-call | tf_op jit(solution)/shard_map/tensor_gather/pallas_call | solution.py:166
  237.8 47.9 %all-gather.7.cloned.1.call-done = bf16[2304,4608]{1,0:T(8,128)(2,1)} async-done(((bf16[288,4608]{1,0:T(8,128)(2,1)}), bf16[2304,4608]{1,0:T(8,128)(2,1)}) %all-gather.7.cloned.1.call-update) | async-done | bytes 21233680 | tf_op jit(solution)/shard_map/all_gather | solution.py:539
  285.8 15.0 %fusion.14 = f32[1024,2304]{1,0:T(8,128)S(1)} fusion(bf16[1024,2304]{1,0:T(8,128)(2,1)} %copy-done.1, bf16[2304,4608]{1,0:T(8,128)(2,1)} %all-gather.7.cloned.1.call-done), kind=kOutput, calls=%fused_computation.19 | convolution fusion | flops 10871635968 | bytes 24772608 | tf_op jit(solution)/shard_map/dot_general | solution.py:63
  303.1 18.2 %fusion.10 = f32[1024,2304]{1,0:T(8,128)} fusion(bf16[1024,2304]{1,0:T(8,128)(2,1)S(1)} %copy-done.2, bf16[2304,4608]{1,0:T(8,128)(2,1)} %all-gather.7.cloned.1.call-done), kind=kOutput, calls=%fused_computation.15 | convolution fusion | flops 10871635968 | bytes 24772608 | tf_op jit(solution)/shard_map/dot_general | solution.py:63
  321.3 8.8 %multiply_convert_fusion.1 = (bf16[1024,2304]{1,0:T(8,128)(2,1)S(1)}, f32[1024,2304]{1,0:T(8,128)}) fusion(f32[1024,2304]{1,0:T(8,128)S(1)} %convolution_add_fusion.2, f32[1024,2304]{1,0:T(8,128)} %fusion.10, bf16[2304,128]{1,0:T(8,128)(2,1)S(1)} %bitcast.188, bf16[1024,32]{0,1:T(8,128)(2,1)S(1)} %convolution_convert_fusion.12), kind=kOutput, calls=%fused_computation.12 | convolution fusion | flops 101449728 | bytes 33652736 | tf_op jit(solution)/shard_map/dot_general | solution.py:67
  333.8 54.3 %all-gather.9.cloned.1.call-done = bf16[2304,2304]{1,0:T(8,128)(2,1)} async-done(((bf16[288,2304]{1,0:T(8,128)(2,1)}), bf16[2304,2304]{1,0:T(8,128)(2,1)}) %all-gather.9.cloned.1.call-update) | async-done | bytes 10616848 | tf_op jit(solution)/shard_map/all_gather | solution.py:540
  388.1 16.2 %convolution_convert_fusion.2.p_ref = bf16[1024,2304]{1,0:T(8,128)(2,1)} fusion(bf16[1024,2304]{1,0:T(8,128)(2,1)} %copy-done.13, bf16[2304,2304]{1,0:T(8,128)(2,1)} %all-gather.9.cloned.1.call-done), kind=kOutput, calls=%fused_computation.35 | convolution fusion | flops 10873995264 | bytes 20054016 | tf_op jit(solution)/shard_map/dot_general | solution.py:67
  404.3 46.6 %tensor_scatter.5 = (f32[256,2304]{1,0:T(8,128)S(1)}, f32[256,128]{1,0:T(8,128)S(1)}) custom-call(bf16[1024,2304]{1,0:T(8,128)(2,1)} %convolution_convert_fusion.2.p_ref, bf16[1024,128]{1,0:T(8,128)(2,1)S(1)} %pad.52.q_ref), custom_call_target="tpu_custom_call" | custom-call | tf_op jit(solution)/shard_map/tensor_scatter/pallas_call | solution.py:276
  455.5 40.6 %tensor_gather.6 = bf16[1024,2304]{1,0:T(8,128)(2,1)S(1)} custom-call(bf16[256,2304]{1,0:T(8,128)(2,1)S(1)} %get-tuple-element.95.x_ref), custom_call_target="tpu_custom_call" | custom-call | tf_op jit(solution)/shard_map/tensor_gather/pallas_call | solution.py:166
  499.7 15.2 %fusion.188 = f32[1024,2304]{1,0:T(8,128)} fusion(bf16[1024,2304]{1,0:T(8,128)(2,1)S(1)} %tensor_gather.6, bf16[2304,2304]{1,0:T(8,128)(2,1)} %all-gather.9.cloned.1.call-done), kind=kOutput, calls=%fused_computation.290 | convolution fusion | flops 10871635968 | bytes 24772608 | tf_op jit(solution)/shard_map/dot_general | solution.py:63
  514.8 12.9 %fusion.7 = (bf16[1024,2304]{1,0:T(8,128)(2,1)S(1)}, bf16[1024,2304]{1,0:T(8,128)(2,1)S(1)}) fusion(f32[1024,2304]{1,0:T(8,128)} %copy-done.16, f32[1024,2304]{1,0:T(8,128)} %get-tuple-element.113, f32[1024,2304]{1,0:T(8,128)} %fusion.188, bf16[1024,16]{0,1:T(8,128)(2,1)S(1)} %convolution_convert_fusion.17, bf16[2304,128]{1,0:T(8,128)(2,1)S(1)} %bitcast.190), kind=kOutput, calls=%fused_computation.9 | convolution fusion | flops 134479872 | bytes 38371328 | tf_op jit(solution)/shard_map/dot_general | solution.py:67
  534.2 16.7 %fusion.8 = f32[1024,2304]{1,0:T(8,128)} fusion(bf16[1024,2304]{1,0:T(8,128)(2,1)} %copy-done.20, bf16[2304,4608]{1,0:T(8,128)(2,1)} %all-gather.7.cloned.1.call-done), kind=kOutput, calls=%fused_computation.13 | convolution fusion | flops 10871635968 | bytes 24772608 | tf_op jit(solution)/shard_map/dot_general | solution.py:67
  550.9 19.2 %add_convert_fusion.p_ref = bf16[1024,2304]{1,0:T(8,128)(2,1)} fusion(f32[1024,2304]{1,0:T(8,128)} %fusion.8, bf16[1024,2304]{1,0:T(8,128)(2,1)} %copy-done.19, bf16[2304,4608]{1,0:T(8,128)(2,1)} %all-gather.7.cloned.1.call-done), kind=kOutput, calls=%fused_computation.10 | convolution fusion | flops 10876354560 | bytes 29491200 | tf_op jit(solution)/shard_map/dot_general | solution.py:67
  570.1 43.9 %tensor_scatter.6 = (f32[256,2304]{1,0:T(8,128)S(1)}, f32[256,128]{1,0:T(8,128)S(1)}) custom-call(bf16[1024,2304]{1,0:T(8,128)(2,1)} %add_convert_fusion.p_ref, bf16[1024,128]{1,0:T(8,128)(2,1)S(1)} %pad.53.q_ref), custom_call_target="tpu_custom_call" | custom-call | tf_op jit(solution)/shard_map/tensor_scatter/pallas_call | solution.py:276
  619.1 38.5 %tensor_gather.7 = bf16[1024,2304]{1,0:T(8,128)(2,1)S(1)} custom-call(bf16[256,2304]{1,0:T(8,128)(2,1)S(1)} %multiply_convert_fusion.3.x_ref), custom_call_target="tpu_custom_call" | custom-call | tf_op jit(solution)/shard_map/tensor_gather/pallas_call | solution.py:166
  659.5 4.5 fusion.46
  664.5 3.7 fusion.51
  670.0 4.6 fusion.189
  674.6 16.1 %convolution_bitcast_fusion.1 = f32[1024,1,256]{0,2,1:T(8,128)} fusion(f32[1024,1024,2]{1,0,2:T(8,128)} %fusion.189, f32[1024,1024,2]{1,0,2:T(8,128)} %copy-done.88, f32[2,1024]{1,0:T(2,128)S(1)} %copy-done.83, pred[1024,1024]{0,1:T(8,128)(4,1)} %fusion.23, f32[1024,2,128]{2,0,1:T(8,128)S(1)} %copy-done.43, f32[1024,2,128]{2,0,1:T(8,128)S(1)} %copy-done.41), kind=kOutput, calls=%fused_computation.102 | convolution fusion | flops 1106775040 | bytes 20979712 | tf_op jit(solution)/shard_map/hqk,qhd->kd/dot_general | solution.py:669
  690.7 15.8 %multiply_bitcast_fusion = f32[1024,2,256]{2,0,1:T(8,128)S(1)} fusion(bf16[1024,128]{0,1:T(8,128)(2,1)} %copy-done.55, bf16[1024,128]{0,1:T(8,128)(2,1)} %copy-done.54, f32[1024,1024,2]{1,0,2:T(8,128)} %fusion.189, f32[1024,1024,2]{1,0,2:T(8,128)} %copy-done.88, f32[2,1024]{1,0:T(2,128)S(1)} %copy-done.83, pred[1024,1024]{0,1:T(8,128)(4,1)} %fusion.23), kind=kOutput, calls=%fused_computation.92 | convolution fusion | flops 1106775040 | bytes 20455424 | tf_op jit(solution)/shard_map/hqk,kd->qhd/dot_general | solution.py:668
  706.5 3.7 fusion.93
  718.1 9.5 %convolution_convert_fusion.1.p_ref = bf16[1024,2304]{1,0:T(8,128)(2,1)} fusion(bf16[2304,1536]{1,0:T(8,128)(2,1)} %all-gather.5.cloned.1.call-done, bf16[1024,256]{0,1:T(8,128)(2,1)S(1)} %copy-done.37, bf16[1024,128]{0,1:T(8,128)(2,1)} %copy-done.57, bf16[1024,128]{0,1:T(8,128)(2,1)} %copy-done.56, bf16[1024,512]{0,1:T(8,128)(2,1)S(1)} %bitcast.210), kind=kOutput, calls=%fused_computation.34 | convolution fusion | flops 4842586112 | bytes 11534336 | tf_op jit(solution)/shard_map/dot_general | solution.py:67
  727.6 42.2 %tensor_scatter.7 = (f32[256,2304]{1,0:T(8,128)S(1)}, f32[256,128]{1,0:T(8,128)S(1)}) custom-call(bf16[1024,2304]{1,0:T(8,128)(2,1)} %convolution_convert_fusion.1.p_ref, bf16[1024,128]{1,0:T(8,128)(2,1)S(1)} %pad.54.q_ref), custom_call_target="tpu_custom_call" | custom-call | tf_op jit(solution)/shard_map/tensor_scatter/pallas_call | solution.py:276
  772.8 62.3 %adapter_grads.1 = (bf16[32,72,128]{2,1,0:T(8,128)(2,1)S(1)}, bf16[8,288,128]{2,1,0:T(8,128)(2,1)S(1)}, bf16[8,64,128]{2,1,0:T(8,128)(2,1)S(1)}, bf16[8,32,128]{2,1,0:T(8,128)(2,1)S(1)}) custom-call(bf16[32,72,128]{2,1,0:T(8,128)(2,1)S(1)} %bitcast.194, bf16[8,288,128]{2,1,0:T(8,128)(2,1)S(1)} %bitcast.193, bf16[8,64,128]{2,1,0:T(8,128)(2,1)S(1)} %bitcast.203, ...), custom_call_target="tpu_custom_call" | custom-call | tf_op jit(solution)/shard_map/adapter_grads/pallas_call | solution.py:480
  845.3 4.0 fusion.35
  (319 shorter events, 95.6 us)
Async XLA Ops:
  7.2 108.7 %all-gather.5.cloned.1.call-start = ((), (), s32[]{:S(2)}) async-start(), calls=%async_computation | async-start | bytes 7962624 | tf_op jit(solution)/shard_map/all_gather | solution.py:533
  10.3 20.2 %copy-start.61 = (bf16[8,72,80]{2,1,0:T(8,128)(2,1)S(1)}, bf16[8,72,80]{2,1,0:T(8,128)(2,1)}, u32[]{:S(2)}) copy-start(bf16[8,72,80]{2,1,0:T(8,128)(2,1)} %param.31) | copy-start | bytes 276484
  10.4 20.2 %copy-start.68 = (bf16[8,2,16,72]{3,2,1,0:T(8,128)(2,1)S(1)}, bf16[8,2,16,72]{3,2,1,0:T(8,128)(2,1)}, u32[]{:S(2)}) copy-start(bf16[8,2,16,72]{3,2,1,0:T(8,128)(2,1)} %param.37) | copy-start | bytes 110596
  10.4 275.4 %all-gather.7.cloned.1.call-start = ((), (), s32[]{:S(2)}) async-start(), calls=%async_computation.1 | async-start | bytes 23887872 | tf_op jit(solution)/shard_map/all_gather | solution.py:539
  13.9 18.5 %copy-start.69 = (f32[4,2304]{1,0:T(4,128)S(1)}, f32[4,2304]{1,0:T(4,128)}, u32[]{:S(2)}) copy-start(f32[4,2304]{1,0:T(4,128)} %param.23) | copy-start | bytes 110596
  13.9 18.6 %copy-start.21 = (bf16[256,2304]{1,0:T(8,128)(2,1)S(1)}, bf16[256,2304]{1,0:T(8,128)(2,1)}, u32[]{:S(2)}) copy-start(bf16[256,2304]{1,0:T(8,128)(2,1)} %param.19) | copy-start | bytes 3538948
  13.9 374.2 %all-gather.9.cloned.1.call-start = ((), (), s32[]{:S(2)}) async-start(), calls=%async_computation.2 | async-start | bytes 11943936 | tf_op jit(solution)/shard_map/all_gather | solution.py:540
  32.5 39.5 %copy-start.64 = (f32[2304]{0:T(1024)}, f32[2304]{0:T(1024)S(1)}, u32[]{:S(2)}) copy-start(f32[2304]{0:T(1024)S(1)} %get-tuple-element.83) | copy-start | bytes 27652
  32.5 162.7 %copy-start.59 = (f32[2304]{0:T(1024)}, f32[2304]{0:T(1024)S(1)}, u32[]{:S(2)}) copy-start(f32[2304]{0:T(1024)S(1)} %get-tuple-element.82) | copy-start | bytes 27652
  32.5 164.1 %copy-start.62 = (f32[2304]{0:T(1024)}, f32[2304]{0:T(1024)S(1)}, u32[]{:S(2)}) copy-start(f32[2304]{0:T(1024)S(1)} %get-tuple-element.84) | copy-start | bytes 27652
  32.8 80.1 %copy-start.77 = (f32[256]{0:T(256)}, f32[256]{0:T(256)S(1)}, u32[]{:S(2)}) copy-start(f32[256]{0:T(256)S(1)} %add_rsqrt_fusion.3) | copy-start | bytes 3076
  73.0 41.3 %copy-start = (bf16[1024,2304]{1,0:T(8,128)(2,1)}, bf16[1024,2304]{1,0:T(8,128)(2,1)S(1)}, u32[]{:S(2)}) copy-start(bf16[1024,2304]{1,0:T(8,128)(2,1)S(1)} %tensor_gather.4) | copy-start | bytes 14155780
  110.0 23.8 %copy-start.9 = (bf16[8,32,128]{2,1,0:T(8,128)(2,1)}, bf16[8,32,128]{2,1,0:T(8,128)(2,1)S(1)}, u32[]{:S(2)}) copy-start(bf16[8,32,128]{2,1,0:T(8,128)(2,1)S(1)} %get-tuple-element.28) | copy-start | bytes 196612
  110.0 35.8 %copy-start.7 = (bf16[8,64,128]{2,1,0:T(8,128)(2,1)}, bf16[8,64,128]{2,1,0:T(8,128)(2,1)S(1)}, u32[]{:S(2)}) copy-start(bf16[8,64,128]{2,1,0:T(8,128)(2,1)S(1)} %get-tuple-element.29) | copy-start | bytes 393220
  110.1 25.5 %copy-start.85 = (f32[128]{0:T(128)}, f32[128]{0:T(128)S(1)}, u32[]{:S(2)}) copy-start(f32[128]{0:T(128)S(1)} %multiply_power_fusion) | copy-start | bytes 1540
  112.9 25.0 %copy-start.26 = (f32[1024,128]{1,0:T(8,128)}, f32[1024,128]{1,0:T(8,128)S(1)}, u32[]{:S(2)}) copy-start(f32[1024,128]{1,0:T(8,128)S(1)} %get-tuple-element.107) | copy-start | bytes 1572868
  195.9 37.2 %copy-start.75 = (f32[256]{0:T(256)}, f32[256]{0:T(256)S(1)}, u32[]{:S(2)}) copy-start(f32[256]{0:T(256)S(1)} %add_rsqrt_fusion.1) | copy-start | bytes 3076
  237.8 83.4 %copy-start.46 = (bf16[1024,32]{0,1:T(8,128)(2,1)}, bf16[1024,32]{0,1:T(8,128)(2,1)S(1)}, u32[]{:S(2)}) copy-start(bf16[1024,32]{0,1:T(8,128)(2,1)S(1)} %convolution_convert_fusion.12) | copy-start | bytes 196612
  303.1 18.2 %copy-start.16 = (f32[1024,2304]{1,0:T(8,128)}, f32[1024,2304]{1,0:T(8,128)S(1)}, u32[]{:S(2)}) copy-start(f32[1024,2304]{1,0:T(8,128)S(1)} %convolution_add_fusion.2) | copy-start | bytes 28311556
  404.3 47.2 %copy-start.24 = (bf16[256,2304]{1,0:T(8,128)(2,1)S(1)}, bf16[256,2304]{1,0:T(8,128)(2,1)}, u32[]{:S(2)}) copy-start(bf16[256,2304]{1,0:T(8,128)(2,1)} %param.20) | copy-start | bytes 3538948
  455.5 42.0 %slice-start = ((s8[4718592]{0:T(1024)(128)(4,1)}), s8[524288]{0:T(1024)(128)(4,1)S(1)}, s32[]{:S(2)}) async-start(s8[4718592]{0:T(1024)(128)(4,1)} %bitcast.205), calls=%async_computation.3 | async-start | bytes 1048576
  570.1 44.0 %copy-start.4 = (bf16[256,2304]{1,0:T(8,128)(2,1)S(1)}, bf16[256,2304]{1,0:T(8,128)(2,1)}, u32[]{:S(2)}) copy-start(bf16[256,2304]{1,0:T(8,128)(2,1)} %copy-done.3) | copy-start | bytes 3538948
  570.1 45.0 %copy-start.63 = (f32[2304]{0:T(1024)S(1)}, f32[2304]{0:T(1024)}, u32[]{:S(2)}) copy-start(f32[2304]{0:T(1024)} %copy-done.62) | copy-start | bytes 27652
  570.1 45.0 %copy-start.76 = (f32[256]{0:T(256)S(1)}, f32[256]{0:T(256)}, u32[]{:S(2)}) copy-start(f32[256]{0:T(256)} %copy-done.75) | copy-start | bytes 3076
  617.1 40.6 %copy-start.23 = (f32[256,2304]{1,0:T(8,128)}, f32[256,2304]{1,0:T(8,128)S(1)}, u32[]{:S(2)}) copy-start(f32[256,2304]{1,0:T(8,128)S(1)} %get-tuple-element.86) | copy-start | bytes 7077892
  690.7 21.3 %copy-start.27 = (f32[1024,128]{1,0:T(8,128)S(1)}, f32[1024,128]{1,0:T(8,128)}, u32[]{:S(2)}) copy-start(f32[1024,128]{1,0:T(8,128)} %copy-done.26) | copy-start | bytes 1572868
  727.6 42.2 %copy-start.6 = (bf16[256,2304]{1,0:T(8,128)(2,1)S(1)}, bf16[256,2304]{1,0:T(8,128)(2,1)}, u32[]{:S(2)}) copy-start(bf16[256,2304]{1,0:T(8,128)(2,1)} %copy-done.5) | copy-start | bytes 3538948
  727.6 42.6 %copy-start.22 = (bf16[256,2304]{1,0:T(8,128)(2,1)S(1)}, bf16[256,2304]{1,0:T(8,128)(2,1)}, u32[]{:S(2)}) copy-start(bf16[256,2304]{1,0:T(8,128)(2,1)} %param.19) | copy-start | bytes 3538948
  727.6 42.6 %copy-start.65 = (f32[2304]{0:T(1024)S(1)}, f32[2304]{0:T(1024)}, u32[]{:S(2)}) copy-start(f32[2304]{0:T(1024)} %copy-done.64) | copy-start | bytes 27652
  727.6 42.6 %copy-start.78 = (f32[256]{0:T(256)S(1)}, f32[256]{0:T(256)}, u32[]{:S(2)}) copy-start(f32[256]{0:T(256)} %copy-done.77) | copy-start | bytes 3076
  770.2 65.0 %copy-start.80 = (s32[8]{0:T(128)S(1)}, s32[8]{0:T(128)}, u32[]{:S(2)}) copy-start(s32[8]{0:T(128)} %copy-done.79) | copy-start | bytes 100
  772.2 65.7 %copy-start.81 = (bf16[8,8]{1,0:T(8,128)(2,1)S(1)}, bf16[8,8]{1,0:T(8,128)(2,1)}, u32[]{:S(2)}) copy-start(bf16[8,8]{1,0:T(8,128)(2,1)} %copy.213) | copy-start | bytes 388
  (64 other events, 308.0 us)
Sparse Core Ops, SparseCore 0:
  10.4 84.7 all-gather.4
  96.9 188.8 all-gather.6
  287.4 100.6 all-gather.8

commit v2 on v1

--- a/solution.py
+++ b/solution.py
@@ -38,8 +38,14 @@
     return inverse * (scaled - normed * jnp.mean(scaled * normed, axis=-1, keepdims=True))
 
 
-def gated_gelu(gate_in, up_in):
-    return jax.nn.gelu(gate_in, approximate=True) * up_in
+def gelu_parts(gate, up):
+    scale = (2.0 / jnp.pi) ** 0.5
+    square = gate * gate
+    bend = jnp.tanh(scale * gate * (1.0 + 0.044715 * square))
+    low = 0.5 * (1.0 + bend)
+    gelu = gate * low
+    slope = low + 0.5 * gate * (1.0 - bend * bend) * (scale * (1.0 + 3.0 * 0.044715 * square))
+    return (gelu * up).astype(BF16), (slope * up).astype(BF16), gelu.astype(BF16)
 
 
 def tables(length, size):
@@ -286,6 +292,324 @@
     )(values, narrow)
 
 
+class Square:
+    def __init__(self, rows):
+        self.rows = rows
+        self.half = rows // 2
+        self.me = lax.axis_index("tensor")
+        self.across, self.down, self.far = square_peers(self.me)
+        self.links = (self.across, self.down)
+
+    def greet(self):
+        greet([{"tensor": self.across}, {"tensor": self.down}])
+
+    def pieces(self, chunk):
+        block = {0: self.me, 3: self.far}.get(chunk)
+        if block is not None:
+            starts = (block * self.rows, block * self.rows + self.half)
+        elif chunk == 1:
+            starts = (self.across * self.rows, self.down * self.rows + self.half)
+        else:
+            starts = (self.across * self.rows + self.half, self.down * self.rows)
+        return tuple((start, part * self.half) for part, start in enumerate(starts))
+
+
+class ChunkGather:
+    def __init__(self, sq, source, buf, send_sem, recv_sem):
+        half = sq.half
+        self.first, self.second, self.onward = [], [], []
+        for link in range(2):
+            for order in range(2):
+                part = link if order == 0 else 1 - link
+                copy = remote(
+                    source.at[pl.ds(part * half, half)],
+                    buf.at[1 + order, pl.ds(link * half, half)],
+                    send_sem.at[2 * order + link],
+                    recv_sem.at[2 * order + link],
+                    sq.links[link],
+                )
+                (self.first if order == 0 else self.second).append(copy)
+            self.onward.append(
+                remote(
+                    buf.at[1, pl.ds(link * half, half)],
+                    buf.at[3, pl.ds(link * half, half)],
+                    send_sem.at[4 + link],
+                    recv_sem.at[4 + link],
+                    sq.links[1 - link],
+                )
+            )
+
+    def start(self):
+        for copy in self.first + self.second:
+            copy.start()
+
+    def wait_chunk(self, chunk):
+        if chunk == 1:
+            for copy in self.first:
+                copy.wait_recv()
+            for copy in self.onward:
+                copy.start()
+        if chunk == 2:
+            for copy in self.second:
+                copy.wait_recv()
+        if chunk == 3:
+            for copy in self.onward:
+                copy.wait_recv()
+
+    def finish(self):
+        for copy in self.first + self.second + self.onward:
+            copy.wait_send()
+
+
+class ChunkScatter:
+    def __init__(self, sq, part, landing, passed, send_sem, recv_sem):
+        half = sq.half
+        self.half, self.part, self.landing, self.passed = half, part, landing, passed
+        self.own, self.far, self.last = [], [], []
+        for link in range(2):
+            rows = pl.ds(link * half, half)
+            for kind, chunk, group in ((0, 1, self.own), (1, 3, self.far)):
+                slot = 2 * kind + link
+                group.append(
+                    remote(
+                        part.at[chunk, rows],
+                        landing.at[slot],
+                        send_sem.at[slot],
+                        recv_sem.at[slot],
+                        sq.links[link],
+                    )
+                )
+            self.last.append(
+                remote(
+                    passed.at[link],
+                    landing.at[4 + link],
+                    send_sem.at[4 + link],
+                    recv_sem.at[4 + link],
+                    sq.links[1 - link],
+                )
+            )
+
+    def send_own(self):
+        for copy in self.own:
+            copy.start()
+
+    def send_far(self):
+        for copy in self.far:
+            copy.start()
+
+    def pass_on(self, link):
+        self.far[link].wait_recv()
+        rows = pl.ds((1 - link) * self.half, self.half)
+        mine = self.part[2, rows, :].astype(F32)
+        self.passed[link] = (mine + self.landing[2 + link].astype(F32)).astype(BF16)
+        self.last[link].start()
+
+    def collect(self, out_ref):
+        for link in range(2):
+            self.own[link].wait_recv()
+            self.last[link].wait_recv()
+            rows = pl.ds(link * self.half, self.half)
+            out_ref[rows, :] = (
+                self.part[0, rows, :].astype(F32)
+                + self.landing[link].astype(F32)
+                + self.landing[4 + link].astype(F32)
+            )
+
+    def finish(self):
+        for copy in self.own + self.far + self.last:
+            copy.wait_send()
+
+
+def scatter_scratch(rows, width):
+    half = rows // 2
+    return [
+        pltpu.VMEM((4, rows, width), BF16),
+        pltpu.VMEM((6, half, width), BF16),
+        pltpu.VMEM((2, half, width), BF16),
+        pltpu.SemaphoreType.DMA((6,)),
+        pltpu.SemaphoreType.DMA((6,)),
+    ]
+
+
+def tile_of(width):
+    return 768 if width % 768 == 0 else 384
+
+
+def columns(step, tile, base=0):
+    return pl.ds(pl.multiple_of(base + step * tile, LANES), tile)
+
+
+def mlp_back_kernel(
+    rows,
+    g_ref,
+    down_hbm,
+    gu_hbm,
+    slope_hbm,
+    gelu_hbm,
+    hidden_hbm,
+    low_hbm,
+    lift_down_ref,
+    map_ref,
+    lift_gu_ref,
+    o_ref,
+    l_ref,
+    f_ref,
+    down_w,
+    gu_w,
+    buf,
+    slope,
+    gelu,
+    hidden,
+    low,
+    grads,
+    weight_sem,
+    load_sem,
+    own_sem,
+    gather_send,
+    gather_recv,
+    *scratch,
+):
+    sq = Square(rows)
+    half = sq.half
+    width = hidden.shape[-1]
+    model = o_ref.shape[-1]
+    down_load = pltpu.make_async_copy(down_hbm, down_w, weight_sem.at[0])
+    gu_load = pltpu.make_async_copy(gu_hbm, gu_w, weight_sem.at[1])
+    own_load = pltpu.make_async_copy(g_ref, buf.at[0], own_sem)
+
+    def loads(chunk):
+        slot = chunk % 2
+        copies = []
+        for part, (start, place) in enumerate(sq.pieces(chunk)):
+            for item, (source, target) in enumerate(
+                ((slope_hbm, slope), (gelu_hbm, gelu), (hidden_hbm, hidden), (low_hbm, low))
+            ):
+                copies.append(
+                    pltpu.make_async_copy(
+                        source.at[pl.ds(start, half)],
+                        target.at[slot, pl.ds(place, half)],
+                        load_sem.at[slot, item, part],
+                    )
+                )
+        return copies
+
+    down_load.start()
+    own_load.start()
+    for copy in loads(0):
+        copy.start()
+    sq.greet()
+    gather = ChunkGather(sq, g_ref, buf, gather_send, gather_recv)
+    gather.start()
+    gu_load.start()
+    part, part_low = scratch[0], scratch[5]
+    scatters = (ChunkScatter(sq, *scratch[:5]), ChunkScatter(sq, *scratch[5:10]))
+    f_ref[...] = jnp.zeros_like(f_ref)
+    own_load.wait()
+    down_load.wait()
+
+    @pl.loop(0, 4)
+    def _(chunk):
+        slot = lax.rem(chunk, 2)
+        for step in range(4):
+
+            @pl.when(chunk == step)
+            def _(step=step):
+                gather.wait_chunk(step)
+                for copy in loads(step):
+                    copy.wait()
+                if step < 3:
+                    for copy in loads(step + 1):
+                        copy.start()
+
+        incoming = buf.at[chunk]
+        low_down = nn(incoming[...], lift_down_ref[...]).astype(BF16)
+        tile = tile_of(width)
+
+        @pl.loop(0, width // tile)
+        def _(step):
+            here = columns(step, tile)
+            grad = nn(incoming[...], down_w[:, here]) + nt(low_down, map_ref[here, :])
+            grads[:, here] = (grad * slope[slot, :, here].astype(F32)).astype(BF16)
+            grads[:, columns(step, tile, width)] = (
+                grad * gelu[slot, :, here].astype(F32)
+            ).astype(BF16)
+
+        @pl.when(chunk == 0)
+        def _():
+            gu_load.wait()
+
+        part_low[chunk] = nn(grads[...], lift_gu_ref[...]).astype(BF16)
+        wide = tile_of(model)
+
+        @pl.loop(0, model // wide)
+        def _(step):
+            here = columns(step, wide)
+            part[chunk, :, here] = nt(grads[...], gu_w[here, :]).astype(BF16)
+
+        @pl.when(chunk == 1)
+        def _():
+            for scatter in scatters:
+                scatter.send_own()
+
+        @pl.when(chunk == 3)
+        def _():
+            for scatter in scatters:
+                scatter.send_far()
+
+        low_turned = low_down.astype(F32).T[:RANK].astype(BF16)
+        gu_turned = low[slot].astype(F32).T.astype(BF16)
+        f_ref[:RANK, :] += nn(low_turned, hidden[slot])
+        f_ref[RANK : 2 * RANK, :] += nn(gu_turned[:RANK], grads[:, :width])
+        f_ref[2 * RANK : 3 * RANK, :] += nn(gu_turned[RANK : 2 * RANK], grads[:, width:])
+
+    for link in range(2):
+        for scatter in scatters:
+            scatter.pass_on(link)
+    gather.finish()
+    scatters[0].collect(o_ref)
+    scatters[1].collect(l_ref)
+    for scatter in scatters:
+        scatter.finish()
+
+
+def mlp_back_fused(grad, down_w, gu_w, slope, gelu, hidden, low, lift_down, map_hidden, lift_gu):
+    rows, model = grad.shape
+    width = hidden.shape[1]
+    anywhere = pl.BlockSpec(memory_space=pl.ANY)
+    vmem = pl.BlockSpec(memory_space=pltpu.VMEM)
+    return pl.pallas_call(
+        functools.partial(mlp_back_kernel, rows),
+        out_shape=(
+            jax.ShapeDtypeStruct((rows, model), F32),
+            jax.ShapeDtypeStruct((rows, LANES), F32),
+            jax.ShapeDtypeStruct((3 * RANK, width), F32),
+        ),
+        in_specs=[vmem] + [anywhere] * 6 + [vmem] * 3,
+        out_specs=(vmem,) * 3,
+        scratch_shapes=[
+            pltpu.VMEM((model, width), BF16),
+            pltpu.VMEM((model, 2 * width), BF16),
+            pltpu.VMEM((4, rows, model), BF16),
+            pltpu.VMEM((2, rows, width), BF16),
+            pltpu.VMEM((2, rows, width), BF16),
+            pltpu.VMEM((2, rows, width), BF16),
+            pltpu.VMEM((2, rows, LANES), BF16),
+            pltpu.VMEM((rows, 2 * width), BF16),
+            pltpu.SemaphoreType.DMA((2,)),
+            pltpu.SemaphoreType.DMA((2, 4, 2)),
+            pltpu.SemaphoreType.DMA,
+            pltpu.SemaphoreType.DMA((6,)),
+            pltpu.SemaphoreType.DMA((6,)),
+        ]
+        + scatter_scratch(rows, model)
+        + scatter_scratch(rows, LANES),
+        compiler_params=pltpu.CompilerParams(
+            collective_id=5, has_side_effects=True, vmem_limit_bytes=62 * 1024 * 1024
+        ),
+        name="mlp_back",
+    )(grad, down_w, gu_w, slope, gelu, hidden, low, lift_down, map_hidden, lift_gu)
+
+
 class Layout:
     def __init__(self):
         self.dp = lax.axis_size("dp")
@@ -629,7 +953,7 @@
     w_gate, w_up = gate_up_w[:, :hidden_here], gate_up_w[:, hidden_here:]
     gate = nn(seq_mlp, w_gate) + nt(low_g, lift_gate)
     up = nn(seq_mlp, w_up) + nt(low_u, lift_up)
-    hidden = gated_gelu(gate, up).astype(BF16)
+    hidden, slope, gelu = gelu_parts(gate, up)
     down_part = nt(hidden, down_w).astype(BF16)
     low_down_part = pad_lanes(nn(hidden, map_hidden).astype(BF16))
     mlp_main, low_down = tensor_scatter(down_part, low_down_part, count)
@@ -639,17 +963,35 @@
 
     grad_out = cotangent.astype(F32) * row_valid
     grad_mlp = norm_back(mlp_total, norm_gains[3], grad_out).astype(BF16)
-    seq_grad_mlp = tensor_gather(grad_mlp, count)
-    grad_low_down = nn(seq_grad_mlp, lift_down).astype(BF16)
-    grad_hidden = nn(seq_grad_mlp, down_w) + nt(grad_low_down, map_hidden)
-    unused, pull = jax.vjp(gated_gelu, gate, up)
-    grad_gate, grad_up = pull(grad_hidden)
-    grad_gate, grad_up = grad_gate.astype(BF16), grad_up.astype(BF16)
-    low_gu_part = pad_lanes(
-        jnp.concatenate([nn(grad_gate, lift_gate), nn(grad_up, lift_up)], axis=1).astype(BF16)
-    )
-    mlp_back_part = (nt(grad_gate, w_gate) + nt(grad_up, w_up)).astype(BF16)
-    mlp_back, grad_low_gu = tensor_scatter(mlp_back_part, low_gu_part, count)
+    if count == 4:
+        lift_gu = jnp.concatenate(
+            [pad_lanes(lift_gate), jnp.pad(lift_up, ((0, 0), (RANK, LANES - 2 * RANK)))], axis=0
+        )
+        mlp_back, grad_low_gu, f_turned = mlp_back_fused(
+            grad_mlp,
+            down_w,
+            gate_up_w,
+            slope,
+            gelu,
+            hidden,
+            pad_lanes(low_gu),
+            pad_lanes(lift_down),
+            pad_lanes(map_hidden),
+            lift_gu,
+        )
+        f_parts = [f_turned.T]
+    else:
+        seq_grad_mlp = tensor_gather(grad_mlp, count)
+        grad_low_down = nn(seq_grad_mlp, lift_down).astype(BF16)
+        grad_hidden = nn(seq_grad_mlp, down_w) + nt(grad_low_down, map_hidden)
+        grad_gate = (grad_hidden * slope.astype(F32)).astype(BF16)
+        grad_up = (grad_hidden * gelu.astype(F32)).astype(BF16)
+        low_gu_part = pad_lanes(
+            jnp.concatenate([nn(grad_gate, lift_gate), nn(grad_up, lift_up)], axis=1).astype(BF16)
+        )
+        mlp_back_part = (nt(grad_gate, w_gate) + nt(grad_up, w_up)).astype(BF16)
+        mlp_back, grad_low_gu = tensor_scatter(mlp_back_part, low_gu_part, count)
+        f_parts = [tn(hidden, grad_low_down), tn(grad_gate, low_g), tn(grad_up, low_u)]
     grad_low_gu = grad_low_gu[:, : 2 * RANK].astype(BF16)
     grad_normed_mlp = mlp_back + nt(grad_low_gu, in_gu)
     grad_mid = grad_out + norm_back(resid_mid, norm_gains[2], grad_normed_mlp)
@@ -698,9 +1040,7 @@
         ],
         lay.total,
     )
-    f_grad = packed(
-        [tn(hidden, grad_low_down), tn(grad_gate, low_g), tn(grad_up, low_u)], lay.dp
-    )
+    f_grad = packed(f_parts, lay.dp)
     h_grad = packed([tn(attended, grad_low_out), tn(grad_q_pre, low_q)], lay.dp)
     k_grad = packed([tn(grad_k_pre, low_k), tn(grad_v_pre, low_v)], lay.kv_owners)
     d_all, f_all, h_all, k_all = exchange(

time: 861 us -> 816 us (0.948)
  matrix products: 235 us -> 182 us
  waiting for transfers between devices: 102 us -> 59.6 us
  Pallas kernels: 426 us -> 455 us
  local copies, waits for them, and re-layouts: 35.6 us -> 58.4 us
    pallas_call x0 -> x1, Pallas kernels: none -> 86 us  [mlp_back_fused(): pl.pallas_call(functools.partial(mlp_back_kernel, rows), out_shape=(jax.S...]
    all_gather x1, waiting for transfers between devices: 47.9 us -> 14.4 us  [per_device(): gate_up_w = lax.all_gather(gate_up_shard, 'dp', axis=0, tiled=True)]
    dot_general x16 -> x13, matrix products: 100 us -> 67.3 us  [nt(): lax.dot_general(a, b, (((1,), (1,)), ((), ())), preferred_element_type=F32)]
    pallas_call x4 -> x3, Pallas kernels: 173 us -> 141 us  [tensor_scatter(): pl.pallas_call(functools.partial(scatter_kernel, count, rows), out_shape=...]
    pallas_call x4 -> x3, Pallas kernels: 153 us -> 122 us  [tensor_gather(): pl.pallas_call(functools.partial(gather_kernel, count, rows), out_shape=j...]
    dot_general x16 -> x12, matrix products: 74.2 us -> 53.4 us  [nn(): lax.dot_general(a, b, (((1,), (0,)), ((), ())), preferred_element_type=F32)]
    unnamed x203, local copies, waits for them, and re-layouts: 23.8 us -> 37.2 us
    all_gather x1, waiting for transfers between devices: 54.3 us -> 44.5 us  [per_device(): down_w = lax.all_gather(down_shard, 'dp', axis=0, tiled=True)]
  transfers between devices with their start and end apart: 3 -> 3, of which waited for: 2 -> 2; matrix products, arithmetic and copies ran while one was open for 12% -> 15% of each run, Pallas kernels for 18% -> 22%
where the time goes in v2:
time: 816 us; the launch traced here: 810 us
  Pallas kernels  455 us (56%)
  matrix products  182 us (22%)
  waiting for transfers between devices  59.6 us (7%)
  local copies, waits for them, and re-layouts  58.4 us (7%)
  other arithmetic  28.7 us (4%)
  between operations  16.6 us (2%)
  blocking collectives  9.45 us (1%)
    pallas_call x3, Pallas kernels, tensor_scatter(): pl.pallas_call(functools.partial(scatter_kernel, count, rows), out_shape=...  141 us
    pallas_call x3, Pallas kernels, tensor_gather(): pl.pallas_call(functools.partial(gather_kernel, count, rows), out_shape=j...  122 us
    pallas_call x2, Pallas kernels, exchange(): pl.pallas_call(kernel, out_shape=tuple((jax.ShapeDtypeStruct(shape, BF16)...  107 us
    pallas_call x1, Pallas kernels, mlp_back_fused(): pl.pallas_call(functools.partial(mlp_back_kernel, rows), out_shape=(jax.S...  86 us
    dot_general x13, matrix products, nt(): lax.dot_general(a, b, (((1,), (1,)), ((), ())), preferred_element_type=F32)  67.3 us
    dot_general x12, matrix products, nn(): lax.dot_general(a, b, (((1,), (0,)), ((), ())), preferred_element_type=F32)  53.4 us
    all_gather x1, waiting for transfers between devices, per_device(): down_w = lax.all_gather(down_shard, 'dp', axis=0, tiled=True)  44.5 us
    unnamed x203, local copies, waits for them, and re-layouts  37.2 us
  transfers between devices with their start and end apart: 3, of which 2 were waited for; matrix products, arithmetic and copies ran while one was open for 15% of the time, Pallas kernels for 22%

profile of v2, /device:TPU:0, one launch (start us, length us, event | category | flops | bytes accessed | tf_op | source)
XLA Modules:
  0.0 810.1 jit_solution(7645340082585698415)
XLA Ops:
  10.5 3.1 pad_maximum_fusion
  18.3 43.2 %tensor_gather.3 = bf16[1024,2304]{1,0:T(8,128)(2,1)S(1)} custom-call(bf16[256,2304]{1,0:T(8,128)(2,1)S(1)} %fusion.19.x_ref), custom_call_target="tpu_custom_call" | custom-call | tf_op jit(solution)/shard_map/tensor_gather/pallas_call | solution.py:172
  64.8 9.4 %all-reduce.15 = s32[8]{0:T(128)S(1)} all-reduce(s32[8]{0:T(128)S(1)} %bitcast_dynamic-update-slice_fusion), channel_id=2, replica_groups=mesh['dp'=8,'tensor'=4] {'dp'}, use_global_device_ids=true, to_apply=%add.15 | all-reduce | flops 8 | bytes 64
  81.1 44.8 %adapter_tables.1 = (bf16[32,72,128]{2,1,0:T(8,128)(2,1)S(1)}, bf16[8,288,128]{2,1,0:T(8,128)(2,1)S(1)}, bf16[8,64,128]{2,1,0:T(8,128)(2,1)S(1)}, bf16[8,32,128]{2,1,0:T(8,128)(2,1)S(1)}) custom-call(bf16[8,72,128]{2,1,0:T(8,128)(2,1)S(1)} %copy.268.d_ref, bf16[8,288,128]{2,1,0:T(8,128)(2,1)S(1)} %copy.267.f_ref, bf16[8,64,128]{2,1,0:T(8,128)(2,1)S(1)} %copy.269.h_ref, ...), custom_call_target="tpu_custom_call" | custom-call | tf_op jit(solution)/shard_map/adapter_tables/pallas_call | solution.py:804
  126.2 3.9 convolution_convert_fusion.9
  133.7 2.8 fusion.82
  139.1 8.4 %fusion.14 = f32[1024,1024]{0,1:T(8,128)S(1)} fusion(bf16[1024,2304]{1,0:T(8,128)(2,1)} %copy-done, bf16[2304,1536]{1,0:T(8,128)(2,1)} %all-gather.5.cloned.1.call-done), kind=kOutput, calls=%fused_computation.34 | convolution fusion | flops 4831838208 | bytes 13631488 | tf_op jit(solution)/shard_map/dot_general | solution.py:69
  161.4 3.5 fusion.8
  165.0 3.7 convolution_convert_fusion.7
  170.3 6.9 convolution_convert_fusion.p_ref
  177.2 51.3 %tensor_scatter.3 = (f32[256,2304]{1,0:T(8,128)S(1)}, f32[256,128]{1,0:T(8,128)S(1)}) custom-call(bf16[1024,2304]{1,0:T(8,128)(2,1)} %convolution_convert_fusion.p_ref, bf16[1024,128]{1,0:T(8,128)(2,1)S(1)} %pad.65.q_ref), custom_call_target="tpu_custom_call" | custom-call | tf_op jit(solution)/shard_map/tensor_scatter/pallas_call | solution.py:282
  231.7 39.2 %tensor_gather.4 = bf16[1024,2304]{1,0:T(8,128)(2,1)S(1)} custom-call(bf16[256,2304]{1,0:T(8,128)(2,1)S(1)} %multiply_convert_fusion.6.x_ref), custom_call_target="tpu_custom_call" | custom-call | tf_op jit(solution)/shard_map/tensor_gather/pallas_call | solution.py:172
  275.4 14.4 %all-gather.7.cloned.1.call-done.gu_hbm = bf16[2304,4608]{1,0:T(8,128)(2,1)} async-done(((bf16[288,4608]{1,0:T(8,128)(2,1)}), bf16[2304,4608]{1,0:T(8,128)(2,1)}) %all-gather.7.cloned.1.call-update) | async-done | bytes 21233680 | tf_op jit(solution)/shard_map/all_gather | solution.py:863
  289.8 17.8 %fusion.3 = f32[1024,2304]{1,0:T(8,128)} fusion(bf16[1024,2304]{1,0:T(8,128)(2,1)} %copy-done.3, bf16[2304,4608]{1,0:T(8,128)(2,1)} %all-gather.7.cloned.1.call-done.gu_hbm), kind=kOutput, calls=%fused_computation.3 | convolution fusion | flops 10871635968 | bytes 24772608 | tf_op jit(solution)/shard_map/dot_general | solution.py:69
  307.7 9.0 %convolution_add_fusion.1 = f32[1024,2304]{1,0:T(8,128)} fusion(f32[1024,2304]{1,0:T(8,128)} %fusion.3, bf16[1024,32]{1,0:T(8,128)(2,1)S(1)} %convolution_convert_fusion.8, bf16[2304,128]{1,0:T(8,128)(2,1)S(1)} %bitcast.179), kind=kOutput, calls=%fused_computation.19 | convolution fusion | flops 77856768 | bytes 19529728 | tf_op jit(solution)/shard_map/dot_general | solution.py:73
  316.8 13.5 %fusion.1 = f32[1024,2304]{1,0:T(8,128)} fusion(bf16[1024,2304]{1,0:T(8,128)(2,1)S(1)} %copy-done.4, bf16[2304,4608]{1,0:T(8,128)(2,1)S(1)} %bitcast.195), kind=kOutput, calls=%fused_computation.1 | convolution fusion | flops 10871635968 | bytes 24772608 | tf_op jit(solution)/shard_map/dot_general | solution.py:69
  330.2 14.9 %multiply_convert_fusion = (bf16[1024,2304]{1,0:T(8,128)(2,1)}, bf16[1024,2304]{1,0:T(8,128)(2,1)S(1)}, bf16[1024,2304]{1,0:T(8,128)(2,1)}) fusion(f32[1024,2304]{1,0:T(8,128)} %convolution_add_fusion.1, f32[1024,2304]{1,0:T(8,128)} %fusion.1, bf16[2304,128]{1,0:T(8,128)(2,1)S(1)} %bitcast.180, bf16[1024,32]{1,0:T(8,128)(2,1)S(1)} %convolution_convert_fusion.8), kind=kOutput, calls=%fused_computation.5 | convolution fusion | flops 129761280 | bytes 33685504 | tf_op jit(solution)/shard_map/dot_general | solution.py:73
  348.9 44.5 %all-gather.9.cloned.1.call-done.down_hbm = bf16[2304,2304]{1,0:T(8,128)(2,1)} async-done(((bf16[288,2304]{1,0:T(8,128)(2,1)}), bf16[2304,2304]{1,0:T(8,128)(2,1)}) %all-gather.9.cloned.1.call-update) | async-done | bytes 10616848 | tf_op jit(solution)/shard_map/all_gather | solution.py:864
  393.4 16.4 %convolution_convert_fusion.2.p_ref = bf16[1024,2304]{1,0:T(8,128)(2,1)} fusion(bf16[1024,2304]{1,0:T(8,128)(2,1)} %copy-done.21, bf16[2304,2304]{1,0:T(8,128)(2,1)} %all-gather.9.cloned.1.call-done.down_hbm), kind=kOutput, calls=%fused_computation.22 | convolution fusion | flops 10873995264 | bytes 20054016 | tf_op jit(solution)/shard_map/dot_general | solution.py:73
  409.8 46.6 %tensor_scatter.4 = (f32[256,2304]{1,0:T(8,128)S(1)}, f32[256,128]{1,0:T(8,128)S(1)}) custom-call(bf16[1024,2304]{1,0:T(8,128)(2,1)} %convolution_convert_fusion.2.p_ref, bf16[1024,128]{1,0:T(8,128)(2,1)S(1)} %pad.66.q_ref), custom_call_target="tpu_custom_call" | custom-call | tf_op jit(solution)/shard_map/tensor_scatter/pallas_call | solution.py:282
  460.5 86.0 %mlp_back.1 = (f32[256,2304]{1,0:T(8,128)}, f32[256,128]{1,0:T(8,128)}, f32[48,2304]{1,0:T(8,128)}) custom-call(bf16[256,2304]{1,0:T(8,128)(2,1)} %get-tuple-element.98.g_ref, bf16[2304,2304]{1,0:T(8,128)(2,1)} %all-gather.9.cloned.1.call-done.down_hbm, bf16[2304,4608]{1,0:T(8,128)(2,1)} %all-gather.7.cloned.1.call-done.gu_hbm, ...), custom_call_target="tpu_custom_call" | custom-call | tf_op jit(solution)/shard_map/mlp_back/pallas_call | solution.py:580
  546.6 3.4 multiply_reduce_fusion.1
  553.7 39.3 %tensor_gather.5 = bf16[1024,2304]{1,0:T(8,128)(2,1)S(1)} custom-call(bf16[256,2304]{1,0:T(8,128)(2,1)S(1)} %multiply_convert_fusion.3.x_ref), custom_call_target="tpu_custom_call" | custom-call | tf_op jit(solution)/shard_map/tensor_gather/pallas_call | solution.py:172
  594.4 4.5 fusion.37
  599.3 4.7 fusion.175
  604.0 4.2 fusion.42
  608.6 17.3 %convolution_bitcast_fusion.1 = f32[1024,1,256]{0,2,1:T(8,128)} fusion(f32[1024,1024,2]{1,0,2:T(8,128)} %fusion.175, f32[1024,1024,2]{1,0,2:T(8,128)} %copy-done.84, f32[2,1024]{1,0:T(2,128)S(1)} %copy-done.79, pred[1024,1024]{0,1:T(8,128)(4,1)} %fusion.12, f32[1024,2,128]{2,0,1:T(8,128)} %copy-done.47, f32[1024,2,128]{2,0,1:T(8,128)} %copy-done.46), kind=kOutput, calls=%fused_computation.91 | convolution fusion | flops 1106775040 | bytes 20979712 | tf_op jit(solution)/shard_map/hqk,qhd->kd/dot_general | solution.py:1011
  625.9 17.0 %multiply_bitcast_fusion = f32[1024,2,256]{2,0,1:T(8,128)} fusion(bf16[1024,128]{0,1:T(8,128)(2,1)} %copy-done.54, bf16[1024,128]{0,1:T(8,128)(2,1)} %copy-done.53, f32[1024,1024,2]{1,0,2:T(8,128)} %fusion.175, f32[1024,1024,2]{1,0,2:T(8,128)} %copy-done.84, f32[2,1024]{1,0:T(2,128)S(1)} %copy-done.79, pred[1024,1024]{0,1:T(8,128)(4,1)} %fusion.12), kind=kOutput, calls=%fused_computation.81 | convolution fusion | flops 1106775040 | bytes 20455424 | tf_op jit(solution)/shard_map/hqk,kd->qhd/dot_general | solution.py:1010
  648.3 3.7 fusion.80
  654.9 9.1 %convolution_convert_fusion.1.p_ref = bf16[1024,2304]{1,0:T(8,128)(2,1)} fusion(bf16[2304,1536]{1,0:T(8,128)(2,1)} %all-gather.5.cloned.1.call-done, bf16[1024,256]{0,1:T(8,128)(2,1)S(1)} %copy-done.41, bf16[1024,128]{0,1:T(8,128)(2,1)S(1)} %get-tuple-element.103, bf16[1024,128]{0,1:T(8,128)(2,1)S(1)} %get-tuple-element.102, bf16[1024,512]{0,1:T(8,128)(2,1)S(1)} %bitcast.199), kind=kOutput, calls=%fused_computation.21 | convolution fusion | flops 4842586112 | bytes 11534336 | tf_op jit(solution)/shard_map/dot_general | solution.py:73
  664.0 42.6 %tensor_scatter.5 = (f32[256,2304]{1,0:T(8,128)S(1)}, f32[256,128]{1,0:T(8,128)S(1)}) custom-call(bf16[1024,2304]{1,0:T(8,128)(2,1)} %convolution_convert_fusion.1.p_ref, bf16[1024,128]{1,0:T(8,128)(2,1)S(1)} %pad.72.q_ref), custom_call_target="tpu_custom_call" | custom-call | tf_op jit(solution)/shard_map/tensor_scatter/pallas_call | solution.py:282
  716.2 62.2 %adapter_grads.1 = (bf16[32,72,128]{2,1,0:T(8,128)(2,1)S(1)}, bf16[8,288,128]{2,1,0:T(8,128)(2,1)S(1)}, bf16[8,64,128]{2,1,0:T(8,128)(2,1)S(1)}, bf16[8,32,128]{2,1,0:T(8,128)(2,1)S(1)}) custom-call(bf16[32,72,128]{2,1,0:T(8,128)(2,1)S(1)} %bitcast.182, bf16[8,288,128]{2,1,0:T(8,128)(2,1)S(1)} %bitcast.183, bf16[8,64,128]{2,1,0:T(8,128)(2,1)S(1)} %bitcast.192, ...), custom_call_target="tpu_custom_call" | custom-call | tf_op jit(solution)/shard_map/adapter_grads/pallas_call | solution.py:804
  (311 shorter events, 102.1 us)
Async XLA Ops:
  7.2 131.9 %all-gather.5.cloned.1.call-start = ((), (), s32[]{:S(2)}) async-start(), calls=%async_computation | async-start | bytes 7962624 | tf_op jit(solution)/shard_map/all_gather | solution.py:857
  10.4 279.4 %all-gather.7.cloned.1.call-start = ((), (), s32[]{:S(2)}) async-start(), calls=%async_computation.1 | async-start | bytes 23887872 | tf_op jit(solution)/shard_map/all_gather | solution.py:863
  13.6 379.8 %all-gather.9.cloned.1.call-start = ((), (), s32[]{:S(2)}) async-start(), calls=%async_computation.2 | async-start | bytes 11943936 | tf_op jit(solution)/shard_map/all_gather | solution.py:864
  15.6 45.9 %copy-start.60 = (f32[2304]{0:T(1024)}, f32[2304]{0:T(1024)S(1)}, u32[]{:S(2)}) copy-start(f32[2304]{0:T(1024)S(1)} %get-tuple-element.85) | copy-start | bytes 27652
  15.9 58.3 %copy-start.63 = (bf16[8,288,16]{1,2,0:T(8,128)(2,1)S(1)}, bf16[8,288,16]{1,2,0:T(8,128)(2,1)}, u32[]{:S(2)}) copy-start(bf16[8,288,16]{1,2,0:T(8,128)(2,1)} %param.33) | copy-start | bytes 221188
  15.9 58.7 %copy-start.71 = (f32[256]{0:T(256)}, f32[256]{0:T(256)S(1)}, u32[]{:S(2)}) copy-start(f32[256]{0:T(256)S(1)} %add_rsqrt_fusion.3) | copy-start | bytes 3076
  16.6 58.0 %copy-start.55 = (bf16[8,2,16,288]{3,2,1,0:T(8,128)(2,1)S(1)}, bf16[8,2,16,288]{3,2,1,0:T(8,128)(2,1)}, u32[]{:S(2)}) copy-start(bf16[8,2,16,288]{3,2,1,0:T(8,128)(2,1)} %param.36) | copy-start | bytes 442372
  18.2 57.9 %copy-start.58 = (bf16[8,72,80]{2,1,0:T(8,128)(2,1)S(1)}, bf16[8,72,80]{2,1,0:T(8,128)(2,1)}, u32[]{:S(2)}) copy-start(bf16[8,72,80]{2,1,0:T(8,128)(2,1)} %param.31) | copy-start | bytes 276484
  18.2 58.0 %copy-start.64 = (bf16[8,2,16,72]{3,2,1,0:T(8,128)(2,1)S(1)}, bf16[8,2,16,72]{3,2,1,0:T(8,128)(2,1)}, u32[]{:S(2)}) copy-start(bf16[8,2,16,72]{3,2,1,0:T(8,128)(2,1)} %param.37) | copy-start | bytes 110596
  64.8 12.5 %copy-start.66 = (bf16[8,16,64]{2,1,0:T(8,128)(2,1)S(1)}, bf16[8,16,64]{2,1,0:T(8,128)(2,1)}, u32[]{:S(2)}) copy-start(bf16[8,16,64]{2,1,0:T(8,128)(2,1)} %param.34) | copy-start | bytes 49156
  125.9 31.2 %copy-start.5 = (bf16[8,32,128]{2,1,0:T(8,128)(2,1)}, bf16[8,32,128]{2,1,0:T(8,128)(2,1)S(1)}, u32[]{:S(2)}) copy-start(bf16[8,32,128]{2,1,0:T(8,128)(2,1)S(1)} %get-tuple-element.29) | copy-start | bytes 196612
  130.0 27.1 %copy-start.44 = (bf16[1024,48]{0,1:T(8,128)(2,1)}, bf16[1024,48]{0,1:T(8,128)(2,1)S(1)}, u32[]{:S(2)}) copy-start(bf16[1024,48]{0,1:T(8,128)(2,1)S(1)} %convolution_convert_fusion.9) | copy-start | bytes 294916
  132.7 325.0 %copy-start.73 = (f32[256]{0:T(256)}, f32[256]{0:T(256)S(1)}, u32[]{:S(2)}) copy-start(f32[256]{0:T(256)S(1)} %compare_convert_fusion) | copy-start | bytes 3076
  136.5 24.7 %copy-start.29 = (f32[1024,128]{1,0:T(8,128)}, f32[1024,128]{1,0:T(8,128)S(1)}, u32[]{:S(2)}) copy-start(f32[1024,128]{1,0:T(8,128)S(1)} %get-tuple-element.112) | copy-start | bytes 1572868
  177.2 52.0 %copy-start.56 = (f32[2304]{0:T(1024)S(1)}, f32[2304]{0:T(1024)}, u32[]{:S(2)}) copy-start(f32[2304]{0:T(1024)} %get-tuple-element.84) | copy-start | bytes 27652
  289.8 26.9 %slice-start = ((s8[21233664]{0:T(1024)(128)(4,1)}), s8[4194304]{0:T(1024)(128)(4,1)S(1)}, s32[]{:S(2)}) async-start(s8[21233664]{0:T(1024)(128)(4,1)} %bitcast.194), calls=%async_computation.3 | async-start | bytes 8388608
  289.8 26.9 %slice-start.1 = ((s8[21233664]{0:T(1024)(128)(4,1)}), s8[4194304]{0:T(1024)(128)(4,1)S(1)}, s32[]{:S(2)}) async-start(s8[21233664]{0:T(1024)(128)(4,1)} %bitcast.194), calls=%async_computation.4 | async-start | bytes 8388608
  289.8 26.9 %slice-start.2 = ((s8[21233664]{0:T(1024)(128)(4,1)}), s8[4194304]{0:T(1024)(128)(4,1)S(1)}, s32[]{:S(2)}) async-start(s8[21233664]{0:T(1024)(128)(4,1)} %bitcast.194), calls=%async_computation.5 | async-start | bytes 8388608
  289.8 26.9 %slice-start.3 = ((s8[21233664]{0:T(1024)(128)(4,1)}), s8[4194304]{0:T(1024)(128)(4,1)S(1)}, s32[]{:S(2)}) async-start(s8[21233664]{0:T(1024)(128)(4,1)} %bitcast.194), calls=%async_computation.6 | async-start | bytes 8388608
  289.8 26.9 %slice-start.4 = ((s8[21233664]{0:T(1024)(128)(4,1)}), s8[4194304]{0:T(1024)(128)(4,1)S(1)}, s32[]{:S(2)}) async-start(s8[21233664]{0:T(1024)(128)(4,1)} %bitcast.194), calls=%async_computation.7 | async-start | bytes 8388608
  409.8 47.3 %copy-start.27 = (bf16[256,2304]{1,0:T(8,128)(2,1)S(1)}, bf16[256,2304]{1,0:T(8,128)(2,1)}, u32[]{:S(2)}) copy-start(bf16[256,2304]{1,0:T(8,128)(2,1)} %param.20) | copy-start | bytes 3538948
  409.8 47.3 %copy-start.62 = (f32[2304]{0:T(1024)S(1)}, f32[2304]{0:T(1024)}, u32[]{:S(2)}) copy-start(f32[2304]{0:T(1024)} %get-tuple-element.83) | copy-start | bytes 27652
  593.0 11.0 %slice-start.6 = ((s8[8388608]{0:T(1024)(128)(4,1)}), s8[4194304]{0:T(1024)(128)(4,1)S(1)}, s32[]{:S(2)}) async-start(s8[8388608]{0:T(1024)(128)(4,1)} %bitcast.217), calls=%async_computation.9 | async-start | bytes 8388608
  625.9 17.0 %copy-start.51 = (f32[256,128]{1,0:T(8,128)S(1)}, f32[256,128]{1,0:T(8,128)}, u32[]{:S(2)}) copy-start(f32[256,128]{1,0:T(8,128)} %get-tuple-element.39) | copy-start | bytes 393220
  625.9 18.4 %copy-start.11 = (f32[256,128]{1,0:T(8,128)S(1)}, f32[256,128]{1,0:T(8,128)}, u32[]{:S(2)}) copy-start(f32[256,128]{1,0:T(8,128)} %copy-done.10) | copy-start | bytes 393220
  664.0 42.6 %copy-start.2 = (bf16[256,2304]{1,0:T(8,128)(2,1)S(1)}, bf16[256,2304]{1,0:T(8,128)(2,1)}, u32[]{:S(2)}) copy-start(bf16[256,2304]{1,0:T(8,128)(2,1)} %copy-done.1) | copy-start | bytes 3538948
  664.0 43.3 %copy-start.50 = (bf16[2304,32]{0,1:T(8,128)(2,1)S(1)}, bf16[2304,32]{0,1:T(8,128)(2,1)}, u32[]{:S(2)}) copy-start(bf16[2304,32]{0,1:T(8,128)(2,1)} %convolution_convert_fusion.4) | copy-start | bytes 442372
  664.0 43.3 %copy-start.52 = (bf16[2304,16]{0,1:T(8,128)(2,1)S(1)}, bf16[2304,16]{0,1:T(8,128)(2,1)}, u32[]{:S(2)}) copy-start(bf16[2304,16]{0,1:T(8,128)(2,1)} %convolution_convert_fusion.5) | copy-start | bytes 221188
  706.7 72.6 %copy-start.76 = (s32[8]{0:T(128)S(1)}, s32[8]{0:T(128)}, u32[]{:S(2)}) copy-start(s32[8]{0:T(128)} %copy-done.75) | copy-start | bytes 100
  779.3 14.0 %copy-start.8 = (bf16[32,72,128]{2,1,0:T(8,128)(2,1)S(1)}, bf16[32,72,128]{2,1,0:T(8,128)(2,1)}, u32[]{:S(2)}) copy-start(bf16[32,72,128]{2,1,0:T(8,128)(2,1)} %copy-done.7) | copy-start | bytes 1769476
  782.4 17.0 %copy-start.61 = (f32[2304]{0:T(1024)S(1)}, f32[2304]{0:T(1024)}, u32[]{:S(2)}) copy-start(f32[2304]{0:T(1024)} %copy-done.60) | copy-start | bytes 27652
  782.4 17.0 %copy-start.72 = (f32[256]{0:T(256)S(1)}, f32[256]{0:T(256)}, u32[]{:S(2)}) copy-start(f32[256]{0:T(256)} %copy-done.71) | copy-start | bytes 3076
  (64 other events, 223.6 us)
Sparse Core Ops, SparseCore 0:
  10.5 74.0 all-gather.4
  86.3 203.4 all-gather.6
  291.5 101.9 all-gather.8

commit v3 on v2

--- a/solution.py
+++ b/solution.py
@@ -453,6 +453,7 @@
     lift_gu_ref,
     o_ref,
     l_ref,
+    f_out,
     f_ref,
     down_w,
     gu_w,
@@ -562,6 +563,13 @@
         f_ref[RANK : 2 * RANK, :] += nn(gu_turned[:RANK], grads[:, :width])
         f_ref[2 * RANK : 3 * RANK, :] += nn(gu_turned[RANK : 2 * RANK], grads[:, width:])
 
+    @pl.loop(0, width // LANES)
+    def _(step):
+        here = columns(step, LANES)
+        f_out[here, :] = jnp.concatenate(
+            [f_ref[:, here], jnp.zeros((LANES - 4 * RANK, LANES), F32)], axis=0
+        ).T.astype(BF16)
+
     for link in range(2):
         for scatter in scatters:
             scatter.pass_on(link)
@@ -582,11 +590,12 @@
         out_shape=(
             jax.ShapeDtypeStruct((rows, model), F32),
             jax.ShapeDtypeStruct((rows, LANES), F32),
-            jax.ShapeDtypeStruct((3 * RANK, width), F32),
+            jax.ShapeDtypeStruct((width, LANES), BF16),
         ),
         in_specs=[vmem] + [anywhere] * 6 + [vmem] * 3,
         out_specs=(vmem,) * 3,
         scratch_shapes=[
+            pltpu.VMEM((4 * RANK, width), F32),
             pltpu.VMEM((model, width), BF16),
             pltpu.VMEM((model, 2 * width), BF16),
             pltpu.VMEM((4, rows, model), BF16),
@@ -820,6 +829,387 @@
     )(*arrays)
 
 
+def chunk_start(sq, chunk, part):
+    is_own = (3 - chunk) // 3
+    is_far = chunk // 3
+    near = 1 - is_own - is_far
+    neighbour = sq.down if part == 1 else sq.across
+    block = sq.me * is_own + sq.far * is_far + neighbour * near
+    other_half = chunk // 2 - is_far
+    half = 1 - other_half if part == 1 else other_half
+    return pl.multiple_of(block * sq.rows + half * sq.half, sq.half)
+
+
+def rotate_back(values, cosine, sine):
+    first, second = values[:, : HD // 2], values[:, HD // 2 :]
+    return jnp.concatenate([first * cosine + second * sine, second * cosine - first * sine], axis=1)
+
+
+def attn_back_kernel(
+    rows,
+    ids_ref,
+    length_ref,
+    g_ref,
+    weight_hbm,
+    seq_hbm,
+    q_ref,
+    k_ref,
+    kt_ref,
+    v_ref,
+    attended_ref,
+    inverse_ref,
+    cos_ref,
+    sin_ref,
+    low_ref,
+    lift_out_ref,
+    map_ref,
+    lift_qkv_ref,
+    normed_ref,
+    grad_gu_ref,
+    low_out_ref,
+    grad_mlp_ref,
+    low_down_ref,
+    f_hbm,
+    o_ref,
+    l_ref,
+    in_out,
+    heads_out,
+    hidden_out,
+    query_out,
+    keyval_out,
+    gateup_out,
+    resid_out,
+    weight,
+    seq,
+    buf,
+    att,
+    q_grad,
+    k_sum,
+    v_sum,
+    kv_grad,
+    joined,
+    d_turned,
+    h_turned,
+    k_turned,
+    d_send,
+    h_send,
+    k_send,
+    d_recv,
+    f_recv,
+    h_recv,
+    k_recv,
+    load_sem,
+    own_sem,
+    gather_send,
+    gather_recv,
+    d_sem,
+    f_sem,
+    h_sem,
+    k_sem,
+    recv_sem,
+    *scratch,
+):
+    sq = Square(rows)
+    lay = Layout()
+    half = sq.half
+    model = o_ref.shape[-1]
+    weight_load = pltpu.make_async_copy(weight_hbm, weight, load_sem.at[0])
+    seq_load = pltpu.make_async_copy(seq_hbm, seq, load_sem.at[1])
+    own_load = pltpu.make_async_copy(g_ref, buf.at[0], own_sem)
+    weight_load.start()
+    own_load.start()
+    greet_all(lay)
+    gather = ChunkGather(sq, g_ref, buf, gather_send, gather_recv)
+    gather.start()
+    seq_load.start()
+    sends = []
+    for step in range(lay.dp):
+        slot = lax.rem(lay.d + step, lay.dp)
+        flat = lay.t * lay.dp + slot
+        send_or_keep(
+            lay,
+            sends,
+            f_hbm.at[slot],
+            f_recv.at[lay.d],
+            f_sem.at[step],
+            recv_sem.at[0],
+            flat,
+            flat == lay.me,
+        )
+    part, part_low = scratch[0], scratch[5]
+    scatters = (ChunkScatter(sq, *scratch[:5]), ChunkScatter(sq, *scratch[5:10]))
+
+    def turned(values):
+        return values.astype(F32).T.astype(BF16)
+
+    d_turned[...] = jnp.zeros_like(d_turned)
+    wide = tile_of(model)
+    low_grads = (
+        (turned(grad_gu_ref[...]), normed_ref, 3 * RANK, 2 * RANK),
+        (turned(low_out_ref[...]), g_ref, 5 * RANK, RANK),
+        (turned(low_down_ref[...]), grad_mlp_ref, 6 * RANK, RANK),
+    )
+
+    @pl.loop(0, model // wide)
+    def _(step):
+        here = columns(step, wide)
+        for low, source, first, count in low_grads:
+            d_turned[pl.ds(first, count), here] = nn(low[:count], source[:, here])
+
+    h_turned[...] = jnp.zeros_like(h_turned)
+    k_turned[...] = jnp.zeros_like(k_turned)
+    k_sum[...] = jnp.zeros_like(k_sum)
+    v_sum[...] = jnp.zeros_like(v_sum)
+    own_load.wait()
+    weight_load.wait()
+    q_width = q_ref.shape[1]
+    qkv_width = q_width + 2 * HD
+    heads = q_width // HD
+    stacked = heads * half
+
+    @pl.loop(0, 4)
+    def _(chunk):
+        for step in range(4):
+
+            @pl.when(chunk == step)
+            def _(step=step):
+                gather.wait_chunk(step)
+
+        incoming = buf.at[chunk]
+        low_out = nn(incoming[...], lift_out_ref[...]).astype(BF16)
+        att[...] = (
+            nn(incoming[...], weight[:, qkv_width:]) + nt(low_out, map_ref[...])
+        ).astype(BF16)
+        low_turned = turned(low_out)[:RANK]
+        for side in range(2):
+            start = chunk_start(sq, chunk, side)
+            here = pl.ds(start, half)
+            place = pl.ds(side * half, half)
+            h_turned[:RANK, :] += nn(
+                low_turned[:, side * half : (side + 1) * half], attended_ref[here, :]
+            )
+            queries = jnp.concatenate(
+                [q_ref[here, h * HD : (h + 1) * HD] for h in range(heads)], axis=0
+            )
+            grads = jnp.concatenate(
+                [att[place, h * HD : (h + 1) * HD] for h in range(heads)], axis=0
+            )
+            inverse = jnp.concatenate([inverse_ref[h : h + 1, here] for h in range(heads)], axis=1)
+            key_at = lax.broadcasted_iota(jnp.int32, (LEN, stacked), 0)
+            query_at = lax.rem(lax.broadcasted_iota(jnp.int32, (LEN, stacked), 1), half) + start
+            allowed = (key_at <= query_at) & (key_at < length_ref[0])
+            squash = jnp.tanh(nt(k_ref[...], queries) * (1.0 / SOFT_CAP))
+            probs = jnp.where(allowed, jnp.exp(SOFT_CAP * squash) * inverse, 0.0)
+            grad_probs = nt(v_ref[...], grads)
+            mean = jnp.sum(probs * grad_probs, axis=0, keepdims=True)
+            grad_raw = (probs * (grad_probs - mean) * (1.0 - squash * squash)).astype(BF16)
+            k_sum[...] += nn(grad_raw, queries)
+            v_sum[...] += nn(probs.astype(BF16), grads)
+            q_back = nn(kt_ref[...], grad_raw).T * HD ** (-0.5)
+            for h in range(heads):
+                q_grad[chunk, place, h * HD : (h + 1) * HD] = rotate_back(
+                    q_back[h * half : (h + 1) * half], cos_ref[here, :], sin_ref[here, :]
+                ).astype(BF16)
+
+    kv_grad[:, :HD] = rotate_back(k_sum[...], cos_ref[...], sin_ref[...]).astype(BF16)
+    kv_grad[:, HD:] = v_sum[...].astype(BF16)
+
+    @pl.loop(0, 4)
+    def _(step):
+        chunk = step + 3 * ((3 - step) // 3) - 3 * (step // 3)
+        joined[chunk, :, :q_width] = q_grad[chunk]
+        for side in range(2):
+            here = pl.ds(chunk_start(sq, chunk, side), half)
+            joined[chunk, pl.ds(side * half, half), q_width:] = kv_grad[here, :]
+        part_low[chunk] = nn(joined[chunk], lift_qkv_ref[...]).astype(BF16)
+
+        @pl.loop(0, model // wide)
+        def _(tile):
+            here = columns(tile, wide)
+            part[chunk, :, here] = nt(joined[chunk], weight[here, :qkv_width]).astype(BF16)
+
+        @pl.when(step == 0)
+        def _():
+            for scatter in scatters:
+                scatter.send_far()
+
+        @pl.when(step == 1)
+        def _():
+            for scatter in scatters:
+                scatter.send_own()
+
+    seq_load.wait()
+
+    @pl.loop(0, 4)
+    def _(chunk):
+        grad_turned = turned(part_low[chunk])[: 3 * RANK]
+        for side in range(2):
+            here = pl.ds(chunk_start(sq, chunk, side), half)
+            place = slice(side * half, (side + 1) * half)
+            low_turned = turned(low_ref[here, :])
+            mine = joined.at[chunk, pl.ds(side * half, half)]
+            h_turned[RANK : 2 * RANK, :] += nn(low_turned[:RANK], mine[:, :q_width])
+            k_turned[:RANK, :] += nn(
+                low_turned[RANK : 2 * RANK], mine[:, q_width : q_width + HD]
+            )
+            k_turned[RANK : 2 * RANK, :] += nn(
+                low_turned[2 * RANK : 3 * RANK], mine[:, q_width + HD :]
+            )
+
+            @pl.loop(0, model // wide)
+            def _(tile):
+                where = columns(tile, wide)
+                d_turned[: 3 * RANK, where] += nn(grad_turned[:, place], seq[here, where])
+
+    @pl.loop(0, model // LANES)
+    def _(step):
+        here = columns(step, LANES)
+        d_send[here, :] = d_turned[:, here].T.astype(BF16)
+
+    h_send[...] = h_turned[...].T.astype(BF16)
+    k_send[...] = k_turned[...].T.astype(BF16)
+    d_rows, h_rows, k_rows = d_recv.shape[1], h_recv.shape[1], k_recv.shape[1]
+    for step in range(lay.dp):
+        slot = lax.rem(lay.d + step, lay.dp)
+        flat = lay.t * lay.dp + slot
+        for item, (source, size, target, sem) in enumerate(
+            ((h_send, h_rows, h_recv, h_sem), (k_send, k_rows, k_recv, k_sem))
+        ):
+            send_or_keep(
+                lay,
+                sends,
+                source.at[pl.ds(pl.multiple_of(slot * size, size), size)],
+                target.at[lay.d],
+                sem.at[step],
+                recv_sem.at[1 + item],
+                flat,
+                flat == lay.me,
+            )
+    pltpu.make_async_copy(
+        d_send.at[pl.ds(pl.multiple_of(lay.me * d_rows, 8), d_rows)],
+        d_recv.at[lay.me],
+        recv_sem.at[3],
+    ).start()
+    for step in range(1, lay.total):
+        flat = lax.rem(lay.me + step, lay.total)
+        send_or_keep(
+            lay,
+            sends,
+            d_send.at[pl.ds(pl.multiple_of(flat * d_rows, 8), d_rows)],
+            d_recv.at[lay.me],
+            d_sem.at[step],
+            recv_sem.at[3],
+            flat,
+            None,
+        )
+    for link in range(2):
+        for scatter in scatters:
+            scatter.pass_on(link)
+    scatters[0].collect(o_ref)
+    scatters[1].collect(l_ref)
+    finish(
+        sends,
+        (
+            (f_recv, recv_sem.at[0]),
+            (h_recv, recv_sem.at[1]),
+            (k_recv, recv_sem.at[2]),
+            (d_recv, recv_sem.at[3]),
+        ),
+    )
+
+    @pl.loop(0, NA)
+    def _(adapter):
+        def pick(parts):
+            total = None
+            for group in range(lay.dp):
+                mine = jnp.where(ids_ref[group] == adapter, parts(group), 0.0)
+                total = mine if total is None else total + mine
+            return total
+
+        def d_part(group):
+            return sum(
+                d_recv[group * lay.tensor + t].astype(F32) for t in range(lay.tensor)
+            )
+
+        d_all = pick(d_part)
+        in_out[adapter] = d_all[:, : 5 * RANK]
+        d_flip = d_all.T
+        f_all = pick(lambda group: f_recv[group].astype(F32))
+        hidden_out[adapter] = f_all[:, :RANK]
+        f_flip = f_all.T
+        h_all = pick(lambda group: h_recv[group].astype(F32))
+        heads_out[adapter] = h_all[:, :RANK]
+        query_out[adapter] = h_all.T[RANK : 2 * RANK]
+        k_flip = pick(lambda group: k_recv[group].astype(F32)).T
+        for which in range(2):
+            band = slice(which * RANK, (which + 1) * RANK)
+            keyval_out[adapter, which] = k_flip[band]
+            gateup_out[adapter, which] = f_flip[RANK:][band]
+            resid_out[adapter, which] = d_flip[5 * RANK :][band]
+
+    gather.finish()
+    for scatter in scatters:
+        scatter.finish()
+
+
+def attn_back_fused(scalars, arrays, grad_shapes, dp, total):
+    (g, weight, seq, q) = arrays[:4]
+    rows, model = g.shape
+    f_send = arrays[-1]
+    anywhere = pl.BlockSpec(memory_space=pl.ANY)
+    vmem = pl.BlockSpec(memory_space=pltpu.VMEM)
+    smem = pl.BlockSpec(memory_space=pltpu.SMEM)
+    q_width = q.shape[1]
+    specs = [smem, smem] + [vmem] * len(arrays)
+    specs[3] = specs[4] = specs[-1] = anywhere
+    outs = [jax.ShapeDtypeStruct((rows, model), F32), jax.ShapeDtypeStruct((rows, LANES), F32)]
+    outs += [jax.ShapeDtypeStruct(shape, F32) for shape in grad_shapes]
+    d_rows, h_rows = model // total, q_width // dp
+    k_rows = HD // dp
+    return pl.pallas_call(
+        functools.partial(attn_back_kernel, rows),
+        out_shape=tuple(outs),
+        in_specs=specs,
+        out_specs=(vmem,) * len(outs),
+        scratch_shapes=[
+            pltpu.VMEM(weight.shape, BF16),
+            pltpu.VMEM(seq.shape, BF16),
+            pltpu.VMEM((4, rows, model), BF16),
+            pltpu.VMEM((rows, q_width), BF16),
+            pltpu.VMEM((4, rows, q_width), BF16),
+            pltpu.VMEM((LEN, HD), F32),
+            pltpu.VMEM((LEN, HD), F32),
+            pltpu.VMEM((LEN, 2 * HD), BF16),
+            pltpu.VMEM((4, rows, q_width + 2 * HD), BF16),
+            pltpu.VMEM((LANES, model), F32),
+            pltpu.VMEM((LANES, q_width), F32),
+            pltpu.VMEM((LANES, HD), F32),
+            pltpu.VMEM((model, LANES), BF16),
+            pltpu.VMEM((q_width, LANES), BF16),
+            pltpu.VMEM((HD, LANES), BF16),
+            pltpu.VMEM((total, d_rows, LANES), BF16),
+            pltpu.VMEM(f_send.shape, BF16),
+            pltpu.VMEM((dp, h_rows, LANES), BF16),
+            pltpu.VMEM((dp, k_rows, LANES), BF16),
+            pltpu.SemaphoreType.DMA((2,)),
+            pltpu.SemaphoreType.DMA,
+            pltpu.SemaphoreType.DMA((6,)),
+            pltpu.SemaphoreType.DMA((6,)),
+            pltpu.SemaphoreType.DMA((total,)),
+            pltpu.SemaphoreType.DMA((dp,)),
+            pltpu.SemaphoreType.DMA((dp,)),
+            pltpu.SemaphoreType.DMA((dp,)),
+            pltpu.SemaphoreType.DMA((4,)),
+        ]
+        + scatter_scratch(rows, model)
+        + scatter_scratch(rows, LANES),
+        compiler_params=pltpu.CompilerParams(
+            collective_id=6, has_side_effects=True, vmem_limit_bytes=62 * 1024 * 1024
+        ),
+        name="attn_back",
+    )(*scalars, *arrays)
+
+
 def per_device(
     layer_in,
     cotangent,
@@ -967,7 +1357,7 @@
         lift_gu = jnp.concatenate(
             [pad_lanes(lift_gate), jnp.pad(lift_up, ((0, 0), (RANK, LANES - 2 * RANK)))], axis=0
         )
-        mlp_back, grad_low_gu, f_turned = mlp_back_fused(
+        mlp_back, grad_low_gu, f_grad = mlp_back_fused(
             grad_mlp,
             down_w,
             gate_up_w,
@@ -979,7 +1369,6 @@
             pad_lanes(map_hidden),
             lift_gu,
         )
-        f_parts = [f_turned.T]
     else:
         seq_grad_mlp = tensor_gather(grad_mlp, count)
         grad_low_down = nn(seq_grad_mlp, lift_down).astype(BF16)
@@ -997,34 +1386,88 @@
     grad_mid = grad_out + norm_back(resid_mid, norm_gains[2], grad_normed_mlp)
 
     grad_attn = norm_back(attn_total, norm_gains[1], grad_mid).astype(BF16)
-    seq_grad_attn = tensor_gather(grad_attn, count)
-    grad_low_out = nn(seq_grad_attn, lift_out).astype(BF16)
-    grad_attended = (nn(seq_grad_attn, w_out) + nt(grad_low_out, map_heads)).astype(BF16)
-    grad_heads = grad_attended.reshape(LEN, heads_here, HD)
-    probs = weights * inverse_total
-    probs_low = probs.astype(BF16)
-    grad_probs = jnp.einsum("qhd,kd->hqk", grad_heads, values, preferred_element_type=F32)
-    grad_value = jnp.einsum("hqk,qhd->kd", probs_low, grad_heads, preferred_element_type=F32)
-    grad_capped = probs * (grad_probs - jnp.sum(probs * grad_probs, axis=-1, keepdims=True))
-    grad_raw = (grad_capped * (1.0 - squash * squash)).astype(BF16)
-    grad_query = jnp.einsum("hqk,kd->qhd", grad_raw, keys, preferred_element_type=F32)
-    grad_key = jnp.einsum("hqk,qhd->kd", grad_raw, queries, preferred_element_type=F32)
-    grad_q_pre = rotate(grad_query * HD ** (-0.5), cosine, -sine).astype(BF16)
-    grad_q_pre = grad_q_pre.reshape(LEN, head_width)
-    grad_k_pre = rotate(grad_key.reshape(LEN, 1, HD), cosine, -sine).astype(BF16)
-    grad_k_pre = grad_k_pre.reshape(LEN, HD)
-    grad_v_pre = grad_value.astype(BF16)
-    low_qkv_part = pad_lanes(
-        jnp.concatenate(
-            [nn(grad_q_pre, lift_q), nn(grad_k_pre, lift_k), nn(grad_v_pre, lift_v)], axis=1
-        ).astype(BF16)
+    grad_shapes = tuple(
+        table.shape
+        for table in (
+            adapt_in,
+            adapt_heads,
+            adapt_hidden,
+            lift_query,
+            lift_keyval,
+            lift_gateup,
+            lift_resid,
+        )
     )
-    grad_qkv = jnp.concatenate([grad_q_pre, grad_k_pre, grad_v_pre], axis=1)
-    attn_back_part = nt(grad_qkv, attn_w[:, :qkv_width]).astype(BF16)
-    attn_back, grad_low_qkv = tensor_scatter(attn_back_part, low_qkv_part, count)
+    if count == 4:
+        lift_qkv = jnp.concatenate(
+            [
+                pad_lanes(lift_q),
+                jnp.pad(lift_k, ((0, 0), (RANK, LANES - 2 * RANK))),
+                jnp.pad(lift_v, ((0, 0), (2 * RANK, LANES - 3 * RANK))),
+            ],
+            axis=0,
+        )
+        attn_back, grad_low_qkv, *adapter_grads = attn_back_fused(
+            (all_ids, lengths),
+            (
+                grad_attn,
+                attn_w,
+                seq_attn,
+                queries.reshape(LEN, head_width),
+                keys,
+                keys.T,
+                values,
+                attended,
+                inverse_total.reshape(heads_here, LEN),
+                cosine.reshape(LEN, HD // 2),
+                sine.reshape(LEN, HD // 2),
+                pad_lanes(low_qkv),
+                pad_lanes(lift_out),
+                pad_lanes(map_heads),
+                lift_qkv,
+                normed_mlp,
+                pad_lanes(grad_low_gu),
+                pad_lanes(low_out),
+                grad_mlp,
+                pad_lanes(low_down),
+                f_grad.reshape(lay.dp, -1, LANES),
+            ),
+            grad_shapes,
+            lay.dp,
+            lay.total,
+        )
+    else:
+        seq_grad_attn = tensor_gather(grad_attn, count)
+        grad_low_out = nn(seq_grad_attn, lift_out).astype(BF16)
+        grad_attended = (nn(seq_grad_attn, w_out) + nt(grad_low_out, map_heads)).astype(BF16)
+        grad_heads = grad_attended.reshape(LEN, heads_here, HD)
+        probs = weights * inverse_total
+        probs_low = probs.astype(BF16)
+        grad_probs = jnp.einsum("qhd,kd->hqk", grad_heads, values, preferred_element_type=F32)
+        grad_value = jnp.einsum("hqk,qhd->kd", probs_low, grad_heads, preferred_element_type=F32)
+        grad_capped = probs * (grad_probs - jnp.sum(probs * grad_probs, axis=-1, keepdims=True))
+        grad_raw = (grad_capped * (1.0 - squash * squash)).astype(BF16)
+        grad_query = jnp.einsum("hqk,kd->qhd", grad_raw, keys, preferred_element_type=F32)
+        grad_key = jnp.einsum("hqk,qhd->kd", grad_raw, queries, preferred_element_type=F32)
+        grad_q_pre = rotate(grad_query * HD ** (-0.5), cosine, -sine).astype(BF16)
+        grad_q_pre = grad_q_pre.reshape(LEN, head_width)
+        grad_k_pre = rotate(grad_key.reshape(LEN, 1, HD), cosine, -sine).astype(BF16)
+        grad_k_pre = grad_k_pre.reshape(LEN, HD)
+        grad_v_pre = grad_value.astype(BF16)
+        low_qkv_part = pad_lanes(
+            jnp.concatenate(
+                [nn(grad_q_pre, lift_q), nn(grad_k_pre, lift_k), nn(grad_v_pre, lift_v)], axis=1
+            ).astype(BF16)
+        )
+        grad_qkv = jnp.concatenate([grad_q_pre, grad_k_pre, grad_v_pre], axis=1)
+        attn_back_part = nt(grad_qkv, attn_w[:, :qkv_width]).astype(BF16)
+        attn_back, grad_low_qkv = tensor_scatter(attn_back_part, low_qkv_part, count)
     grad_low_qkv = grad_low_qkv[:, : 3 * RANK].astype(BF16)
     grad_normed_attn = attn_back + nt(grad_low_qkv, in_qkv)
     input_grad = (grad_mid + norm_back(resid_in, norm_gains[0], grad_normed_attn)).astype(BF16)
+
+    if count == 4:
+        return (layer_out, input_grad, *adapter_grads)
 
     def packed(parts, blocks):
         return pad_lanes(jnp.concatenate(parts, axis=1).astype(BF16)).reshape(

time: 816 us -> 707 us (0.87)
  matrix products: 182 us -> 116 us
  Pallas kernels: 455 us -> 427 us
  local copies, waits for them, and re-layouts: 58.4 us -> 39.3 us
    pallas_call x0 -> x1, Pallas kernels: none -> 130 us  [attn_back_fused(): pl.pallas_call(functools.partial(attn_back_kernel, rows), out_shape=tuple...]
    pallas_call x2 -> x1, Pallas kernels: 107 us -> 34.9 us  [exchange(): pl.pallas_call(kernel, out_shape=tuple((jax.ShapeDtypeStruct(shape, BF16)...]
    dot_general x16 -> x0, matrix products: 50.8 us -> none  [the longest x1 17.3 us: per_device(): jnp.einsum('hqk,qhd->kd', grad_raw, queries, preferred_element_type=F32)]
    pallas_call x3 -> x2, Pallas kernels: 141 us -> 91.5 us  [tensor_scatter(): pl.pallas_call(functools.partial(scatter_kernel, count, rows), out_shape=...]
    pallas_call x3 -> x2, Pallas kernels: 122 us -> 85.3 us  [tensor_gather(): pl.pallas_call(functools.partial(gather_kernel, count, rows), out_shape=j...]
    unnamed x203 -> x141, local copies, waits for them, and re-layouts: 37.2 us -> 25.3 us
    all_gather x0 -> x1, blocking collectives: none -> 10.2 us  [per_device(): all_ids = lax.all_gather(adapter_ids[:, 0], 'dp', axis=0, tiled=True)]
    unnamed x1 -> x0, blocking collectives: 9.45 us -> none
  transfers between devices with their start and end apart: 3 -> 3, of which waited for: 2 -> 2; matrix products, arithmetic and copies ran while one was open for 15% -> 19% of each run, Pallas kernels for 22% -> 24%
where the time goes in v3:
time: 707 us; the launch traced here: 700 us
  Pallas kernels  427 us (60%)
  matrix products  116 us (16%)
  waiting for transfers between devices  59.7 us (8%)
  local copies, waits for them, and re-layouts  39.3 us (6%)
  other arithmetic  31.3 us (4%)
  between operations  16.2 us (2%)
  blocking collectives  10.2 us (1%)
    pallas_call x1, Pallas kernels, attn_back_fused(): pl.pallas_call(functools.partial(attn_back_kernel, rows), out_shape=tuple...  130 us
    pallas_call x2, Pallas kernels, tensor_scatter(): pl.pallas_call(functools.partial(scatter_kernel, count, rows), out_shape=...  91.5 us
    pallas_call x1, Pallas kernels, mlp_back_fused(): pl.pallas_call(functools.partial(mlp_back_kernel, rows), out_shape=(jax.S...  86.1 us
    pallas_call x2, Pallas kernels, tensor_gather(): pl.pallas_call(functools.partial(gather_kernel, count, rows), out_shape=j...  85.3 us
    dot_general x11, matrix products, nt(): lax.dot_general(a, b, (((1,), (1,)), ((), ())), preferred_element_type=F32)  58.2 us
    dot_general x7, matrix products, nn(): lax.dot_general(a, b, (((1,), (0,)), ((), ())), preferred_element_type=F32)  48.8 us
    all_gather x1, waiting for transfers between devices, per_device(): down_w = lax.all_gather(down_shard, 'dp', axis=0, tiled=True)  42.1 us
    pallas_call x1, Pallas kernels, exchange(): pl.pallas_call(kernel, out_shape=tuple((jax.ShapeDtypeStruct(shape, BF16)...  34.9 us
  transfers between devices with their start and end apart: 3, of which 2 were waited for; matrix products, arithmetic and copies ran while one was open for 19% of the time, Pallas kernels for 24%

profile of v3, /device:TPU:0, one launch (start us, length us, event | category | flops | bytes accessed | tf_op | source)
XLA Modules:
  0.0 700.0 jit_solution(11149467251596309705)
XLA Ops:
  16.2 43.2 %tensor_gather.2.seq_hbm = bf16[1024,2304]{1,0:T(8,128)(2,1)S(1)} custom-call(bf16[256,2304]{1,0:T(8,128)(2,1)S(1)} %fusion.17.x_ref), custom_call_target="tpu_custom_call" | custom-call | tf_op jit(solution)/shard_map/tensor_gather/pallas_call | solution.py:172
  59.4 2.1 copy-done
  61.6 10.2 %all-reduce.15.ids_ref = s32[8]{0:T(128)S(1)} all-reduce(s32[8]{0:T(128)S(1)} %bitcast_dynamic-update-slice_fusion), channel_id=2, replica_groups=mesh['dp'=8,'tensor'=4] {'dp'}, use_global_device_ids=true, to_apply=%add.15 | all-reduce | flops 8 | bytes 64 | tf_op jit(solution)/shard_map/all_gather | solution.py:1257
  74.6 34.9 %adapter_tables.1 = (bf16[32,72,128]{2,1,0:T(8,128)(2,1)S(1)}, bf16[8,288,128]{2,1,0:T(8,128)(2,1)S(1)}, bf16[8,64,128]{2,1,0:T(8,128)(2,1)S(1)}, bf16[8,32,128]{2,1,0:T(8,128)(2,1)S(1)}) custom-call(bf16[8,72,128]{2,1,0:T(8,128)(2,1)S(1)} %copy.113.d_ref, bf16[8,288,128]{2,1,0:T(8,128)(2,1)S(1)} %copy.112.f_ref, bf16[8,64,128]{2,1,0:T(8,128)(2,1)S(1)} %copy.114.h_ref, ...), custom_call_target="tpu_custom_call" | custom-call | tf_op jit(solution)/shard_map/adapter_tables/pallas_call | solution.py:813
  109.9 3.8 convolution_convert_fusion.3
  113.7 2.7 fusion.47
  125.5 8.4 %fusion.6 = f32[1024,1024]{0,1:T(8,128)S(1)} fusion(bf16[1024,2304]{1,0:T(8,128)(2,1)} %copy-done, bf16[2304,1536]{1,0:T(8,128)(2,1)} %all-gather.5.cloned.1.call-done.weight_hbm), kind=kOutput, calls=%fused_computation.16 | convolution fusion | flops 4831838208 | bytes 13631488 | tf_op jit(solution)/shard_map/dot_general | solution.py:69
  137.8 2.6 copy.105
  140.3 2.6 copy.106
  142.9 2.5 copy.104
  147.3 2.5 fusion.70
  151.8 3.5 fusion.5
  155.7 4.3 fusion.29
  160.1 2.3 copy.103.attended_ref
  164.1 6.9 convolution_convert_fusion.p_ref
  171.0 45.0 %tensor_scatter.2 = (f32[256,2304]{1,0:T(8,128)S(1)}, f32[256,128]{1,0:T(8,128)S(1)}) custom-call(bf16[1024,2304]{1,0:T(8,128)(2,1)} %convolution_convert_fusion.p_ref, bf16[1024,128]{1,0:T(8,128)(2,1)S(1)} %pad.78.q_ref), custom_call_target="tpu_custom_call" | custom-call | tf_op jit(solution)/shard_map/tensor_scatter/pallas_call | solution.py:282
  219.1 42.0 %tensor_gather.3 = bf16[1024,2304]{1,0:T(8,128)(2,1)S(1)} custom-call(bf16[256,2304]{1,0:T(8,128)(2,1)S(1)} %multiply_convert_fusion.7.x_ref.normed_ref), custom_call_target="tpu_custom_call" | custom-call | tf_op jit(solution)/shard_map/tensor_gather/pallas_call | solution.py:172
  268.7 16.9 %all-gather.7.cloned.1.call-done.gu_hbm = bf16[2304,4608]{1,0:T(8,128)(2,1)} async-done(((bf16[288,4608]{1,0:T(8,128)(2,1)}), bf16[2304,4608]{1,0:T(8,128)(2,1)}) %all-gather.7.cloned.1.call-update) | async-done | bytes 21233680 | tf_op jit(solution)/shard_map/all_gather | solution.py:1253
  285.7 17.6 %fusion.2 = f32[1024,2304]{1,0:T(8,128)} fusion(bf16[1024,2304]{1,0:T(8,128)(2,1)} %copy-done.2, bf16[2304,4608]{1,0:T(8,128)(2,1)} %all-gather.7.cloned.1.call-done.gu_hbm), kind=kOutput, calls=%fused_computation.2 | convolution fusion | flops 10871635968 | bytes 24772608 | tf_op jit(solution)/shard_map/dot_general | solution.py:69
  303.3 8.9 %convolution_add_fusion.1 = f32[1024,2304]{1,0:T(8,128)} fusion(f32[1024,2304]{1,0:T(8,128)} %fusion.2, bf16[1024,32]{1,0:T(8,128)(2,1)S(1)} %convolution_convert_fusion.2, bf16[2304,128]{1,0:T(8,128)(2,1)S(1)} %bitcast.81), kind=kOutput, calls=%fused_computation.12 | convolution fusion | flops 77856768 | bytes 19529728 | tf_op jit(solution)/shard_map/dot_general | solution.py:73
  312.2 14.7 %fusion = f32[1024,2304]{1,0:T(8,128)} fusion(bf16[1024,2304]{1,0:T(8,128)(2,1)} %copy-done.2, bf16[2304,4608]{1,0:T(8,128)(2,1)S(1)} %bitcast.91), kind=kOutput, calls=%fused_computation | convolution fusion | flops 10871635968 | bytes 24772608 | tf_op jit(solution)/shard_map/dot_general | solution.py:69
  326.9 15.0 %multiply_convert_fusion = (bf16[1024,2304]{1,0:T(8,128)(2,1)}, bf16[1024,2304]{1,0:T(8,128)(2,1)S(1)}, bf16[1024,2304]{1,0:T(8,128)(2,1)}) fusion(f32[1024,2304]{1,0:T(8,128)} %convolution_add_fusion.1, f32[1024,2304]{1,0:T(8,128)} %fusion, bf16[2304,128]{1,0:T(8,128)(2,1)S(1)} %bitcast.82, bf16[1024,32]{1,0:T(8,128)(2,1)S(1)} %convolution_convert_fusion.2), kind=kOutput, calls=%fused_computation.4 | convolution fusion | flops 129761280 | bytes 33685504 | tf_op jit(solution)/shard_map/dot_general | solution.py:73
  341.9 2.2 copy-done.8
  345.7 42.1 %all-gather.9.cloned.1.call-done.down_hbm = bf16[2304,2304]{1,0:T(8,128)(2,1)} async-done(((bf16[288,2304]{1,0:T(8,128)(2,1)}), bf16[2304,2304]{1,0:T(8,128)(2,1)}) %all-gather.9.cloned.1.call-update) | async-done | bytes 10616848 | tf_op jit(solution)/shard_map/all_gather | solution.py:1254
  387.8 16.2 %convolution_convert_fusion.1.p_ref = bf16[1024,2304]{1,0:T(8,128)(2,1)} fusion(bf16[1024,2304]{1,0:T(8,128)(2,1)} %copy-done.8, bf16[2304,2304]{1,0:T(8,128)(2,1)} %all-gather.9.cloned.1.call-done.down_hbm), kind=kOutput, calls=%fused_computation.15 | convolution fusion | flops 10873995264 | bytes 20054016 | tf_op jit(solution)/shard_map/dot_general | solution.py:73
  404.0 46.5 %tensor_scatter.3 = (f32[256,2304]{1,0:T(8,128)S(1)}, f32[256,128]{1,0:T(8,128)S(1)}) custom-call(bf16[1024,2304]{1,0:T(8,128)(2,1)} %convolution_convert_fusion.1.p_ref, bf16[1024,128]{1,0:T(8,128)(2,1)S(1)} %pad.79.q_ref), custom_call_target="tpu_custom_call" | custom-call | tf_op jit(solution)/shard_map/tensor_scatter/pallas_call | solution.py:282
  453.5 2.5 multiply_convert_fusion.5
  455.9 86.1 %mlp_back.1 = (f32[256,2304]{1,0:T(8,128)}, f32[256,128]{1,0:T(8,128)}, bf16[2304,128]{1,0:T(8,128)(2,1)}) custom-call(bf16[256,2304]{1,0:T(8,128)(2,1)} %get-tuple-element.99.g_ref.grad_mlp_ref, bf16[2304,2304]{1,0:T(8,128)(2,1)} %all-gather.9.cloned.1.call-done.down_hbm, bf16[2304,4608]{1,0:T(8,128)(2,1)} %all-gather.7.cloned.1.call-done.gu_hbm, ...), custom_call_target="tpu_custom_call" | custom-call | tf_op jit(solution)/shard_map/mlp_back/pallas_call | solution.py:588
  543.6 3.3 multiply_reduce_fusion.1
  550.5 129.5 %attn_back.1 = (f32[256,2304]{1,0:T(8,128)}, f32[256,128]{1,0:T(8,128)}, f32[8,72,80]{2,1,0:T(8,128)}, f32[8,64,16]{2,1,0:T(8,128)}, f32[8,288,16]{2,1,0:T(8,128...) custom-call(s32[8]{0:T(128)} %copy-done.53, ...), custom_call_target="tpu_custom_call" | custom-call | tf_op jit(solution)/shard_map/attn_back/pallas_call | solution.py:1169
  680.0 3.9 fusion.18
  685.8 4.0 fusion.22
  (213 shorter events, 54.8 us)
Async XLA Ops:
  7.2 118.3 %all-gather.5.cloned.1.call-start = ((), (), s32[]{:S(2)}) async-start(), calls=%async_computation | async-start | bytes 7962624 | tf_op jit(solution)/shard_map/all_gather | solution.py:1247
  10.5 275.2 %all-gather.7.cloned.1.call-start = ((), (), s32[]{:S(2)}) async-start(), calls=%async_computation.1 | async-start | bytes 23887872 | tf_op jit(solution)/shard_map/all_gather | solution.py:1253
  12.3 375.5 %all-gather.9.cloned.1.call-start = ((), (), s32[]{:S(2)}) async-start(), calls=%async_computation.2 | async-start | bytes 11943936 | tf_op jit(solution)/shard_map/all_gather | solution.py:1254
  13.5 45.9 %copy-start.40 = (f32[2304]{0:T(1024)}, f32[2304]{0:T(1024)S(1)}, u32[]{:S(2)}) copy-start(f32[2304]{0:T(1024)S(1)} %get-tuple-element.82) | copy-start | bytes 27652
  13.9 45.6 %copy-start.50 = (f32[256]{0:T(256)}, f32[256]{0:T(256)S(1)}, u32[]{:S(2)}) copy-start(f32[256]{0:T(256)S(1)} %add_rsqrt_fusion.3) | copy-start | bytes 3076
  16.1 55.7 %copy-start.42 = (bf16[8,288,16]{1,2,0:T(8,128)(2,1)S(1)}, bf16[8,288,16]{1,2,0:T(8,128)(2,1)}, u32[]{:S(2)}) copy-start(bf16[8,288,16]{1,2,0:T(8,128)(2,1)} %param.33) | copy-start | bytes 221188
  16.2 56.0 %copy-start.36 = (bf16[8,2,16,288]{3,2,1,0:T(8,128)(2,1)S(1)}, bf16[8,2,16,288]{3,2,1,0:T(8,128)(2,1)}, u32[]{:S(2)}) copy-start(bf16[8,2,16,288]{3,2,1,0:T(8,128)(2,1)} %param.36) | copy-start | bytes 442372
  113.7 4.9 copy-start.21
  116.4 33.4 %copy-start.13 = (f32[1024,128]{1,0:T(8,128)}, f32[1024,128]{1,0:T(8,128)S(1)}, u32[]{:S(2)}) copy-start(f32[1024,128]{1,0:T(8,128)S(1)} %get-tuple-element.113.cos_ref) | copy-start | bytes 1572868
  125.5 9.6 %copy-start.22 = (bf16[1024,48]{1,0:T(8,128)(2,1)S(1)}, bf16[1024,48]{1,0:T(8,128)(2,1)}, u32[]{:S(2)}) copy-start(bf16[1024,48]{1,0:T(8,128)(2,1)} %copy-done.21) | copy-start | bytes 294916
  145.5 4.4 copy-start.14
  145.5 4.4 copy-start.17
  145.5 4.4 copy-start.18
  150.1 5.1 copy-start.15
  150.1 5.1 copy-start.16
  155.3 4.7 copy-start.47
  218.8 43.9 %copy-start.3 = (f32[256,2304]{1,0:T(8,128)}, f32[256,2304]{1,0:T(8,128)S(1)}, u32[]{:S(2)}) copy-start(f32[256,2304]{1,0:T(8,128)S(1)} %get-tuple-element.93) | copy-start | bytes 7077892
  219.0 42.0 %copy-start.1 = (bf16[256,2304]{1,0:T(8,128)(2,1)}, bf16[256,2304]{1,0:T(8,128)(2,1)S(1)}, u32[]{:S(2)}) copy-start(bf16[256,2304]{1,0:T(8,128)(2,1)S(1)} %multiply_convert_fusion.7.x_ref.normed_ref) | copy-start | bytes 3538948
  285.6 26.5 %slice-start = ((s8[21233664]{0:T(1024)(128)(4,1)}), s8[4194304]{0:T(1024)(128)(4,1)S(1)}, s32[]{:S(2)}) async-start(s8[21233664]{0:T(1024)(128)(4,1)} %bitcast.90), calls=%async_computation.3 | async-start | bytes 8388608
  285.6 26.5 %slice-start.1 = ((s8[21233664]{0:T(1024)(128)(4,1)}), s8[4194304]{0:T(1024)(128)(4,1)S(1)}, s32[]{:S(2)}) async-start(s8[21233664]{0:T(1024)(128)(4,1)} %bitcast.90), calls=%async_computation.4 | async-start | bytes 8388608
  285.6 26.5 %slice-start.2 = ((s8[21233664]{0:T(1024)(128)(4,1)}), s8[4194304]{0:T(1024)(128)(4,1)S(1)}, s32[]{:S(2)}) async-start(s8[21233664]{0:T(1024)(128)(4,1)} %bitcast.90), calls=%async_computation.5 | async-start | bytes 8388608
  285.6 26.5 %slice-start.3 = ((s8[21233664]{0:T(1024)(128)(4,1)}), s8[4194304]{0:T(1024)(128)(4,1)S(1)}, s32[]{:S(2)}) async-start(s8[21233664]{0:T(1024)(128)(4,1)} %bitcast.90), calls=%async_computation.6 | async-start | bytes 8388608
  285.6 26.5 %slice-start.4 = ((s8[21233664]{0:T(1024)(128)(4,1)}), s8[4194304]{0:T(1024)(128)(4,1)S(1)}, s32[]{:S(2)}) async-start(s8[21233664]{0:T(1024)(128)(4,1)} %bitcast.90), calls=%async_computation.7 | async-start | bytes 8388608
  303.2 8.9 %slice-start.5 = ((s8[21233664]{0:T(1024)(128)(4,1)}), s8[262144]{0:T(1024)(128)(4,1)S(1)}, s32[]{:S(2)}) async-start(s8[21233664]{0:T(1024)(128)(4,1)} %bitcast.90), calls=%async_computation.8 | async-start | bytes 524288
  455.9 86.1 %copy-start.54 = (pred[128]{0:T(512)(128)(4,1)S(1)}, pred[128]{0:T(512)(128)(4,1)}, u32[]{:S(2)}) copy-start(pred[128]{0:T(512)(128)(4,1)} %constant.70.clone.1) | copy-start | bytes 388
  550.5 129.5 %copy-start.41 = (f32[2304]{0:T(1024)S(1)}, f32[2304]{0:T(1024)}, u32[]{:S(2)}) copy-start(f32[2304]{0:T(1024)} %copy-done.40) | copy-start | bytes 27652
  550.5 129.5 %copy-start.51 = (f32[256]{0:T(256)S(1)}, f32[256]{0:T(256)}, u32[]{:S(2)}) copy-start(f32[256]{0:T(256)} %copy-done.50) | copy-start | bytes 3076
  680.0 5.0 copy-start.35
  685.8 4.8 copy-start.45
  685.8 5.4 copy-start.39
  685.8 6.1 copy-start.33
  685.8 6.8 copy-start.38
  (33 other events, 77.8 us)
Sparse Core Ops, SparseCore 0:
  10.6 84.1 all-gather.4
  96.4 189.1 all-gather.6
  287.3 100.4 all-gather.8

commit v4 on v3

--- a/solution.py
+++ b/solution.py
@@ -303,16 +303,6 @@
     def greet(self):
         greet([{"tensor": self.across}, {"tensor": self.down}])
 
-    def pieces(self, chunk):
-        block = {0: self.me, 3: self.far}.get(chunk)
-        if block is not None:
-            starts = (block * self.rows, block * self.rows + self.half)
-        elif chunk == 1:
-            starts = (self.across * self.rows, self.down * self.rows + self.half)
-        else:
-            starts = (self.across * self.rows + self.half, self.down * self.rows)
-        return tuple((start, part * self.half) for part, start in enumerate(starts))
-
 
 class ChunkGather:
     def __init__(self, sq, source, buf, send_sem, recv_sem):
@@ -363,61 +353,54 @@
 
 class ChunkScatter:
     def __init__(self, sq, part, landing, passed, send_sem, recv_sem):
-        half = sq.half
-        self.half, self.part, self.landing, self.passed = half, part, landing, passed
-        self.own, self.far, self.last = [], [], []
+        self.sq, self.half = sq, sq.half
+        self.part, self.landing, self.passed = part, landing, passed
+        self.send_sem, self.recv_sem = send_sem, recv_sem
+
+    def copy(self, kind, link):
+        rows = pl.ds(link * self.half, self.half)
+        source = (
+            self.passed.at[link] if kind == 2 else self.part.at[1 + 2 * kind, rows]
+        )
+        slot = 2 * kind + link
+        return remote(
+            source,
+            self.landing.at[slot],
+            self.send_sem.at[slot],
+            self.recv_sem.at[slot],
+            self.sq.links[1 - link if kind == 2 else link],
+        )
+
+    def send_own(self):
         for link in range(2):
-            rows = pl.ds(link * half, half)
-            for kind, chunk, group in ((0, 1, self.own), (1, 3, self.far)):
-                slot = 2 * kind + link
-                group.append(
-                    remote(
-                        part.at[chunk, rows],
-                        landing.at[slot],
-                        send_sem.at[slot],
-                        recv_sem.at[slot],
-                        sq.links[link],
-                    )
-                )
-            self.last.append(
-                remote(
-                    passed.at[link],
-                    landing.at[4 + link],
-                    send_sem.at[4 + link],
-                    recv_sem.at[4 + link],
-                    sq.links[1 - link],
-                )
-            )
-
-    def send_own(self):
-        for copy in self.own:
-            copy.start()
+            self.copy(0, link).start()
 
     def send_far(self):
-        for copy in self.far:
-            copy.start()
+        for link in range(2):
+            self.copy(1, link).start()
 
     def pass_on(self, link):
-        self.far[link].wait_recv()
+        self.copy(1, link).wait_recv()
         rows = pl.ds((1 - link) * self.half, self.half)
         mine = self.part[2, rows, :].astype(F32)
         self.passed[link] = (mine + self.landing[2 + link].astype(F32)).astype(BF16)
-        self.last[link].start()
-
-    def collect(self, out_ref):
+        self.copy(2, link).start()
+
+    def collect(self, out_ref, first=0):
         for link in range(2):
-            self.own[link].wait_recv()
-            self.last[link].wait_recv()
+            self.copy(0, link).wait_recv()
+            self.copy(2, link).wait_recv()
             rows = pl.ds(link * self.half, self.half)
-            out_ref[rows, :] = (
+            out_ref[rows, first : first + self.part.shape[-1]] = (
                 self.part[0, rows, :].astype(F32)
                 + self.landing[link].astype(F32)
                 + self.landing[4 + link].astype(F32)
             )
 
     def finish(self):
-        for copy in self.own + self.far + self.last:
-            copy.wait_send()
+        for kind in range(3):
+            for link in range(2):
+                self.copy(kind, link).wait_send()
 
 
 def scatter_scratch(rows, width):
@@ -471,7 +454,6 @@
     *scratch,
 ):
     sq = Square(rows)
-    half = sq.half
     width = hidden.shape[-1]
     model = o_ref.shape[-1]
     down_load = pltpu.make_async_copy(down_hbm, down_w, weight_sem.at[0])
@@ -480,19 +462,12 @@
 
     def loads(chunk):
         slot = chunk % 2
-        copies = []
-        for part, (start, place) in enumerate(sq.pieces(chunk)):
+        return [
+            pltpu.make_async_copy(source.at[chunk], target.at[slot], load_sem.at[slot, item])
             for item, (source, target) in enumerate(
                 ((slope_hbm, slope), (gelu_hbm, gelu), (hidden_hbm, hidden), (low_hbm, low))
-            ):
-                copies.append(
-                    pltpu.make_async_copy(
-                        source.at[pl.ds(start, half)],
-                        target.at[slot, pl.ds(place, half)],
-                        load_sem.at[slot, item, part],
-                    )
-                )
-        return copies
+            )
+        ]
 
     down_load.start()
     own_load.start()
@@ -582,7 +557,7 @@
 
 def mlp_back_fused(grad, down_w, gu_w, slope, gelu, hidden, low, lift_down, map_hidden, lift_gu):
     rows, model = grad.shape
-    width = hidden.shape[1]
+    width = hidden.shape[2]
     anywhere = pl.BlockSpec(memory_space=pl.ANY)
     vmem = pl.BlockSpec(memory_space=pltpu.VMEM)
     return pl.pallas_call(
@@ -605,7 +580,7 @@
             pltpu.VMEM((2, rows, LANES), BF16),
             pltpu.VMEM((rows, 2 * width), BF16),
             pltpu.SemaphoreType.DMA((2,)),
-            pltpu.SemaphoreType.DMA((2, 4, 2)),
+            pltpu.SemaphoreType.DMA((2, 4)),
             pltpu.SemaphoreType.DMA,
             pltpu.SemaphoreType.DMA((6,)),
             pltpu.SemaphoreType.DMA((6,)),
@@ -617,6 +592,362 @@
         ),
         name="mlp_back",
     )(grad, down_w, gu_w, slope, gelu, hidden, low, lift_down, map_hidden, lift_gu)
+
+
+class Line:
+    def __init__(self, slots, send_sem, recv_sem):
+        self.d = lax.axis_index("dp")
+        self.places = lax.axis_size("dp") // 2
+        self.core = lax.rem(self.d, 2)
+        self.z = self.d // 2
+        self.sibling = self.d + 1 - 2 * self.core
+        self.slots, self.send_sem, self.recv_sem = slots, send_sem, recv_sem
+
+    def greet(self, others):
+        barrier = pltpu.get_barrier_semaphore()
+        for peer in others + [{"dp": self.sibling}]:
+            pl.semaphore_signal(barrier, inc=1, device_id=peer, device_id_type=MESH)
+
+        @pl.when(self.z > 0)
+        def _():
+            pl.semaphore_signal(
+                barrier, inc=1, device_id={"dp": self.d - 2}, device_id_type=MESH
+            )
+
+        @pl.when(self.z < self.places - 1)
+        def _():
+            pl.semaphore_signal(
+                barrier, inc=1, device_id={"dp": self.d + 2}, device_id_type=MESH
+            )
+
+        last = self.places - 1
+        ends = (last - self.z) // last + self.z // last
+        pl.semaphore_wait(barrier, len(others) + 3 - ends)
+
+    def copy(self, place, kind):
+        target = (self.d + 2, self.d - 2, self.sibling)[kind]
+        slot = 2 * place + self.core
+        return pltpu.make_async_remote_copy(
+            src_ref=self.slots.at[slot],
+            dst_ref=self.slots.at[slot],
+            send_sem=self.send_sem.at[kind, place],
+            recv_sem=self.recv_sem.at[slot],
+            device_id={"dp": target},
+            device_id_type=MESH,
+        )
+
+    def send_up(self, place):
+        @pl.when(self.z < self.places - 1)
+        def _():
+            self.copy(place, 0).start()
+
+    def send_down(self, place):
+        @pl.when(self.z > 0)
+        def _():
+            self.copy(place, 1).start()
+
+    def start(self):
+        self.send_up(self.z)
+        self.send_down(self.z)
+        self.copy(self.z, 2).start()
+
+    def arrive(self, distance):
+        @pl.when(self.z >= distance)
+        def _():
+            place = self.z - distance
+            self.copy(place, 2).wait_recv()
+            self.send_up(place)
+            self.copy(place, 2).start()
+
+        @pl.when(self.z + distance < self.places)
+        def _():
+            place = self.z + distance
+            self.copy(place, 2).wait_recv()
+            self.send_down(place)
+            self.copy(place, 2).start()
+
+    def wait_sibling(self, place):
+        slot = self.slots.at[2 * place + 1 - self.core]
+        pltpu.make_async_copy(
+            slot, slot, self.recv_sem.at[2 * place + 1 - self.core]
+        ).wait()
+
+    def finish(self):
+        for place in range(self.places):
+
+            @pl.when((self.z >= place) & (self.z < self.places - 1))
+            def _(place=place):
+                self.copy(place, 0).wait_send()
+
+            @pl.when((self.z <= place) & (self.z > 0))
+            def _(place=place):
+                self.copy(place, 1).wait_send()
+
+            self.copy(place, 2).wait_send()
+
+
+ARRIVALS = ((0, 1, 2, 3), (1, 0, 2, 3), (2, 1, 3, 0), (3, 2, 1, 0))
+
+
+def mlp_kernel(
+    rows,
+    x_hbm,
+    gu_hbm,
+    shard_hbm,
+    low_ref,
+    lift_gu_ref,
+    map_ref,
+    o_ref,
+    l_ref,
+    hidden_out,
+    slope_out,
+    gelu_out,
+    down_out,
+    seq,
+    tiles,
+    hidden,
+    slope,
+    gelu,
+    down,
+    load_sem,
+    tile_sem,
+    store_sem,
+    keep_sem,
+    line_send,
+    line_recv,
+    part,
+    landing,
+    passed,
+    part_send,
+    part_recv,
+    *low_scratch,
+):
+    sq = Square(rows)
+    line = Line(down, line_send, line_recv)
+    width = hidden.shape[-1]
+    tile = tiles.shape[-1] // 2
+    steps = width // tile
+    own_shard = pltpu.make_async_copy(shard_hbm, down.at[line.d], load_sem.at[0])
+    seq_load = pltpu.make_async_copy(x_hbm, seq, load_sem.at[1])
+
+    def tile_loads(step, slot):
+        return [
+            pltpu.make_async_copy(
+                gu_hbm.at[:, columns(step, tile, which * width)],
+                tiles.at[slot, :, pl.ds(which * tile, tile)],
+                tile_sem.at[slot, which],
+            )
+            for which in range(2)
+        ]
+
+    def stores(step, slot):
+        here = columns(step, tile)
+        return [
+            pltpu.make_async_copy(
+                source.at[slot], target.at[:, :, here], store_sem.at[slot, which]
+            )
+            for which, (source, target) in enumerate(((slope, slope_out), (gelu, gelu_out)))
+        ]
+
+    own_shard.start()
+    seq_load.start()
+    for copy in tile_loads(0, 0):
+        copy.start()
+    line.greet([{"tensor": sq.across}, {"tensor": sq.down}])
+    own_shard.wait()
+    line.start()
+    seq_load.wait()
+
+    @pl.loop(0, steps)
+    def _(step):
+        slot = lax.rem(step, 2)
+        for copy in tile_loads(step, slot):
+            copy.wait()
+
+        @pl.when(step + 1 < steps)
+        def _():
+            for copy in tile_loads(step + 1, 1 - slot):
+                copy.start()
+
+        @pl.when(step >= 2)
+        def _():
+            for copy in stores(step - 2, slot):
+                copy.wait()
+
+        here = columns(step, tile)
+
+        @pl.loop(0, 4)
+        def _(chunk):
+            both = nn(seq[chunk], tiles[slot])
+            gate = both[:, :tile] + nt(low_ref[chunk], lift_gu_ref[here, :])
+            up = both[:, tile:] + nt(low_ref[chunk], lift_gu_ref[columns(step, tile, width), :])
+            hidden[chunk, :, here], slope[slot, chunk], gelu[slot, chunk] = gelu_parts(gate, up)
+
+        for copy in stores(step, slot):
+            copy.start()
+
+        @pl.when(step == steps - 2)
+        def _():
+            line.arrive(1)
+
+    keep_hidden = pltpu.make_async_copy(hidden, hidden_out, keep_sem.at[0])
+    keep_hidden.start()
+    last = line.places - 1
+    is_first, is_last = (last - line.z) // last, line.z // last
+    is_third = line.z // 2 - is_last
+    is_here = (is_first, 1 - is_first - is_third - is_last, is_third, is_last)
+    order = [sum(flag * ARRIVALS[z][i] for z, flag in enumerate(is_here)) for i in range(4)]
+
+    def scatter_at(place):
+        return ChunkScatter(
+            sq,
+            part.at[place],
+            landing.at[place],
+            passed.at[place],
+            part_send.at[place],
+            part_recv.at[place],
+        )
+
+    low_scatter = ChunkScatter(sq, *low_scratch)
+
+    @pl.loop(0, 4)
+    def _(chunk):
+        low_scratch[0][chunk] = nn(hidden[chunk], map_ref[...]).astype(BF16)
+
+    low_scatter.send_far()
+    low_scatter.send_own()
+    keeps = []
+    for step in range(4):
+        if step >= 2:
+            line.arrive(step)
+        place = order[step]
+        line.wait_sibling(place)
+        pair = pl.ds(2 * place, 2)
+        keep = pltpu.make_async_copy(down.at[pair], down_out.at[pair], keep_sem.at[1 + step])
+        keep.start()
+        keeps.append(keep)
+        scatter = scatter_at(place)
+        shard_rows = down.shape[1]
+
+        @pl.loop(0, 4)
+        def _(turn, place=place, scatter=scatter):
+            chunk = turn + 3 * ((3 - turn) // 3) - 3 * (turn // 3)
+            for core in range(2):
+                part[place, chunk, :, core * shard_rows : (core + 1) * shard_rows] = nt(
+                    hidden[chunk], down[2 * place + core]
+                ).astype(BF16)
+
+            @pl.when(turn == 0)
+            def _():
+                scatter.send_far()
+
+            @pl.when(turn == 1)
+            def _():
+                scatter.send_own()
+
+        if step > 0:
+            for link in range(2):
+                scatter_at(order[step - 1]).pass_on(link)
+        else:
+            for link in range(2):
+                low_scatter.pass_on(link)
+    for link in range(2):
+        scatter_at(order[3]).pass_on(link)
+    wide = part.shape[-1]
+    low_scatter.collect(l_ref)
+    for place in range(4):
+        scatter_at(place).collect(o_ref, place * wide)
+    for place in range(4):
+        scatter_at(place).finish()
+    low_scatter.finish()
+    line.finish()
+    for step in (steps - 2, steps - 1):
+        for copy in stores(step, step % 2):
+            copy.wait()
+    keep_hidden.wait()
+    for keep in keeps:
+        keep.wait()
+
+
+def mlp_fused(seq, gu_w, shard, low, lift_gu, map_hidden, dp):
+    chunks, rows, model = seq.shape
+    width = shard.shape[1]
+    tile = 384
+    wide = model // (dp // 2)
+    half = rows // 2
+    anywhere = pl.BlockSpec(memory_space=pl.ANY)
+    vmem = pl.BlockSpec(memory_space=pltpu.VMEM)
+    saved = jax.ShapeDtypeStruct((4, rows, width), BF16)
+    return pl.pallas_call(
+        functools.partial(mlp_kernel, rows),
+        out_shape=(
+            jax.ShapeDtypeStruct((rows, model), F32),
+            jax.ShapeDtypeStruct((rows, LANES), F32),
+            saved,
+            saved,
+            saved,
+            jax.ShapeDtypeStruct((dp,) + shard.shape, BF16),
+        ),
+        in_specs=[anywhere] * 3 + [vmem] * 3,
+        out_specs=(vmem, vmem) + (anywhere,) * 4,
+        scratch_shapes=[
+            pltpu.VMEM((4, rows, model), BF16),
+            pltpu.VMEM((2, model, 2 * tile), BF16),
+            pltpu.VMEM((4, rows, width), BF16),
+            pltpu.VMEM((2, 4, rows, tile), BF16),
+            pltpu.VMEM((2, 4, rows, tile), BF16),
+            pltpu.VMEM((dp,) + shard.shape, BF16),
+            pltpu.SemaphoreType.DMA((2,)),
+            pltpu.SemaphoreType.DMA((2, 2)),
+            pltpu.SemaphoreType.DMA((2, 2)),
+            pltpu.SemaphoreType.DMA((5,)),
+            pltpu.SemaphoreType.DMA((3, dp // 2)),
+            pltpu.SemaphoreType.DMA((dp,)),
+            pltpu.VMEM((4, 4, rows, wide), BF16),
+            pltpu.VMEM((4, 6, half, wide), BF16),
+            pltpu.VMEM((4, 2, half, wide), BF16),
+            pltpu.SemaphoreType.DMA((4, 6)),
+            pltpu.SemaphoreType.DMA((4, 6)),
+        ]
+        + scatter_scratch(rows, LANES),
+        compiler_params=pltpu.CompilerParams(
+            collective_id=7, has_side_effects=True, vmem_limit_bytes=62 * 1024 * 1024
+        ),
+        name="mlp",
+    )(seq, gu_w, shard, low, lift_gu, map_hidden)
+
+
+def chunk_gather_kernel(rows, x_ref, o_ref, own_sem, send_sem, recv_sem):
+    sq = Square(rows)
+    sq.greet()
+    gather = ChunkGather(sq, x_ref, o_ref, send_sem, recv_sem)
+    gather.start()
+    own = pltpu.make_async_copy(x_ref, o_ref.at[0], own_sem)
+    own.start()
+    for chunk in range(1, 4):
+        gather.wait_chunk(chunk)
+    own.wait()
+    gather.finish()
+
+
+def chunk_gather(values):
+    rows, width = values.shape
+    anywhere = pl.BlockSpec(memory_space=pl.ANY)
+    return pl.pallas_call(
+        functools.partial(chunk_gather_kernel, rows),
+        out_shape=jax.ShapeDtypeStruct((4, rows, width), values.dtype),
+        in_specs=[anywhere],
+        out_specs=anywhere,
+        scratch_shapes=[
+            pltpu.SemaphoreType.DMA,
+            pltpu.SemaphoreType.DMA((6,)),
+            pltpu.SemaphoreType.DMA((6,)),
+        ],
+        compiler_params=pltpu.CompilerParams(
+            collective_id=8, has_side_effects=True, vmem_limit_bytes=VMEM_LIMIT
+        ),
+        name="chunk_gather",
+    )(values)
 
 
 class Layout:
@@ -1251,7 +1582,6 @@
         (attn_shard, gate_up_shard, down_shard)
     )
     gate_up_w = lax.all_gather(gate_up_shard, "dp", axis=0, tiled=True)
-    down_w = lax.all_gather(down_shard, "dp", axis=0, tiled=True)
     qkv_width = head_width + 2 * HD
 
     all_ids = lax.all_gather(adapter_ids[:, 0], "dp", axis=0, tiled=True)
@@ -1337,26 +1667,36 @@
     resid_mid = resid_in + rms_norm(attn_total, norm_gains[1])
 
     normed_mlp = rms_norm(resid_mid, norm_gains[2]).astype(BF16)
-    seq_mlp = tensor_gather(normed_mlp, count)
-    low_gu = nn(seq_mlp, in_gu).astype(BF16)
-    low_g, low_u = low_gu[:, :RANK], low_gu[:, RANK:]
-    w_gate, w_up = gate_up_w[:, :hidden_here], gate_up_w[:, hidden_here:]
-    gate = nn(seq_mlp, w_gate) + nt(low_g, lift_gate)
-    up = nn(seq_mlp, w_up) + nt(low_u, lift_up)
-    hidden, slope, gelu = gelu_parts(gate, up)
-    down_part = nt(hidden, down_w).astype(BF16)
-    low_down_part = pad_lanes(nn(hidden, map_hidden).astype(BF16))
-    mlp_main, low_down = tensor_scatter(down_part, low_down_part, count)
+    line_of_four = count == 4 and lay.dp == 8
+    if line_of_four:
+        seq_mlp = chunk_gather(normed_mlp)
+        low_gu = pad_lanes(nn(seq_mlp.reshape(LEN, D), in_gu).astype(BF16)).reshape(4, rows, LANES)
+        lift_gu = jnp.concatenate(
+            [pad_lanes(lift_gate), jnp.pad(lift_up, ((0, 0), (RANK, LANES - 2 * RANK)))], axis=0
+        )
+        mlp_main, low_down, hidden, slope, gelu, down_w = mlp_fused(
+            seq_mlp, gate_up_w, down_shard, low_gu, lift_gu, pad_lanes(map_hidden), lay.dp
+        )
+        down_w = down_w.reshape(D, hidden_here)
+    else:
+        seq_mlp = tensor_gather(normed_mlp, count)
+        low_gu = nn(seq_mlp, in_gu).astype(BF16)
+        low_g, low_u = low_gu[:, :RANK], low_gu[:, RANK:]
+        w_gate, w_up = gate_up_w[:, :hidden_here], gate_up_w[:, hidden_here:]
+        gate = nn(seq_mlp, w_gate) + nt(low_g, lift_gate)
+        up = nn(seq_mlp, w_up) + nt(low_u, lift_up)
+        hidden, slope, gelu = gelu_parts(gate, up)
+        down_w = lax.all_gather(down_shard, "dp", axis=0, tiled=True)
+        down_part = nt(hidden, down_w).astype(BF16)
+        low_down_part = pad_lanes(nn(hidden, map_hidden).astype(BF16))
+        mlp_main, low_down = tensor_scatter(down_part, low_down_part, count)
     low_down = low_down[:, :RANK].astype(BF16)
     mlp_total = mlp_main + nt(low_down, lift_down)
     layer_out = (row_valid * (resid_mid + rms_norm(mlp_total, norm_gains[3]))).astype(BF16)
 
     grad_out = cotangent.astype(F32) * row_valid
     grad_mlp = norm_back(mlp_total, norm_gains[3], grad_out).astype(BF16)
-    if count == 4:
-        lift_gu = jnp.concatenate(
-            [pad_lanes(lift_gate), jnp.pad(lift_up, ((0, 0), (RANK, LANES - 2 * RANK)))], axis=0
-        )
+    if line_of_four:
         mlp_back, grad_low_gu, f_grad = mlp_back_fused(
             grad_mlp,
             down_w,
@@ -1364,7 +1704,7 @@
             slope,
             gelu,
             hidden,
-            pad_lanes(low_gu),
+            low_gu,
             pad_lanes(lift_down),
             pad_lanes(map_hidden),
             lift_gu,
@@ -1398,7 +1738,7 @@
             lift_resid,
         )
     )
-    if count == 4:
+    if line_of_four:
         lift_qkv = jnp.concatenate(
             [
                 pad_lanes(lift_q),
@@ -1466,7 +1806,7 @@
     grad_normed_attn = attn_back + nt(grad_low_qkv, in_qkv)
     input_grad = (grad_mid + norm_back(resid_in, norm_gains[0], grad_normed_attn)).astype(BF16)
 
-    if count == 4:
+    if line_of_four:
         return (layer_out, input_grad, *adapter_grads)
 
     def packed(parts, blocks):

time: 707 us -> 665 us (0.941)
  matrix products: 116 us -> 38.7 us
  Pallas kernels: 427 us -> 503 us
  waiting for transfers between devices: 59.7 us -> 18.5 us
    pallas_call x0 -> x2, Pallas kernels: none -> 158 us  [the longest x1 117 us: mlp_fused(): pl.pallas_call(functools.partial(mlp_kernel, rows), out_shape=(jax.ShapeD...]
    pallas_call x2 -> x1, Pallas kernels: 85.3 us -> 40.1 us  [tensor_gather(): pl.pallas_call(functools.partial(gather_kernel, count, rows), out_shape=j...]
    pallas_call x2 -> x1, Pallas kernels: 91.5 us -> 47.8 us  [tensor_scatter(): pl.pallas_call(functools.partial(scatter_kernel, count, rows), out_shape=...]
    all_gather x1 -> x0, waiting for transfers between devices: 42.1 us -> none  [per_device(): down_w = lax.all_gather(down_shard, 'dp', axis=0, tiled=True)]
    dot_general x11 -> x8, matrix products: 58.2 us -> 19 us  [nt(): lax.dot_general(a, b, (((1,), (1,)), ((), ())), preferred_element_type=F32)]
    dot_general x7 -> x4, matrix products: 48.8 us -> 11.6 us  [nn(): lax.dot_general(a, b, (((1,), (0,)), ((), ())), preferred_element_type=F32)]
    unnamed x141 -> x114, local copies, waits for them, and re-layouts: 25.3 us -> 25.9 us
  transfers between devices with their start and end apart: 3 -> 2, of which waited for: 2 -> 1; matrix products, arithmetic and copies ran while one was open for 19% -> 10% of each run, Pallas kernels for 24% -> 25%
where the time goes in v4:
time: 665 us; the launch traced here: 658 us
  Pallas kernels  503 us (76%)
  matrix products  38.7 us (6%)
  local copies, waits for them, and re-layouts  38.5 us (6%)
  other arithmetic  32.5 us (5%)
  waiting for transfers between devices  18.5 us (3%)
  between operations  16.5 us (2%)
  blocking collectives  10.7 us (2%)
    pallas_call x1, Pallas kernels, attn_back_fused(): pl.pallas_call(functools.partial(attn_back_kernel, rows), out_shape=tuple...  130 us
    pallas_call x1, Pallas kernels, mlp_fused(): pl.pallas_call(functools.partial(mlp_kernel, rows), out_shape=(jax.ShapeD...  117 us
    pallas_call x1, Pallas kernels, mlp_back_fused(): pl.pallas_call(functools.partial(mlp_back_kernel, rows), out_shape=(jax.S...  88.6 us
    pallas_call x1, Pallas kernels, tensor_scatter(): pl.pallas_call(functools.partial(scatter_kernel, count, rows), out_shape=...  47.8 us
    pallas_call x1, Pallas kernels, chunk_gather(): pl.pallas_call(functools.partial(chunk_gather_kernel, rows), out_shape=ja...  41 us
    pallas_call x1, Pallas kernels, tensor_gather(): pl.pallas_call(functools.partial(gather_kernel, count, rows), out_shape=j...  40.1 us
    pallas_call x1, Pallas kernels, exchange(): pl.pallas_call(kernel, out_shape=tuple((jax.ShapeDtypeStruct(shape, BF16)...  38.2 us
    unnamed x114, local copies, waits for them, and re-layouts  25.9 us
  transfers between devices with their start and end apart: 2, of which 1 were waited for; matrix products, arithmetic and copies ran while one was open for 10% of the time, Pallas kernels for 25%

profile of v4, /device:TPU:0, one launch (start us, length us, event | category | flops | bytes accessed | tf_op | source)
XLA Modules:
  0.0 658.4 jit_solution(15512457909885095452)
XLA Ops:
  8.4 2.1 pad_maximum_fusion.1
  10.6 1.7 pad_maximum_fusion
  14.3 10.7 %all-reduce.14.ids_ref = s32[8]{0:T(128)S(1)} all-reduce(s32[8]{0:T(128)S(1)} %bitcast_dynamic-update-slice_fusion), channel_id=2, replica_groups=mesh['dp'=8,'tensor'=4] {'dp'}, use_global_device_ids=true, to_apply=%add.14 | all-reduce | flops 8 | bytes 64 | tf_op jit(solution)/shard_map/all_gather | solution.py:1587
  25.9 40.1 %tensor_gather.1.seq_hbm = bf16[1024,2304]{1,0:T(8,128)(2,1)S(1)} custom-call(bf16[256,2304]{1,0:T(8,128)(2,1)S(1)} %fusion.11.x_ref), custom_call_target="tpu_custom_call" | custom-call | tf_op jit(solution)/shard_map/tensor_gather/pallas_call | solution.py:172
  66.0 2.2 copy-done.1
  71.7 38.2 %adapter_tables.1 = (bf16[32,72,128]{2,1,0:T(8,128)(2,1)S(1)}, bf16[8,288,128]{2,1,0:T(8,128)(2,1)S(1)}, bf16[8,64,128]{2,1,0:T(8,128)(2,1)S(1)}, bf16[8,32,128]{2,1,0:T(8,128)(2,1)S(1)}) custom-call(bf16[8,72,128]{2,1,0:T(8,128)(2,1)S(1)} %copy.110.d_ref, bf16[8,288,128]{2,1,0:T(8,128)(2,1)S(1)} %copy.109.f_ref, bf16[8,64,128]{2,1,0:T(8,128)(2,1)S(1)} %copy.111.h_ref, ...), custom_call_target="tpu_custom_call" | custom-call | tf_op jit(solution)/shard_map/adapter_tables/pallas_call | solution.py:1144
  116.0 1.9 fusion.40
  121.9 8.4 %fusion.1 = f32[1024,1024]{0,1:T(8,128)S(1)} fusion(bf16[1024,2304]{1,0:T(8,128)(2,1)} %copy-done.1, bf16[2304,1536]{1,0:T(8,128)(2,1)} %all-gather.4.cloned.1.call-done.weight_hbm), kind=kOutput, calls=%fused_computation.4 | convolution fusion | flops 4831838208 | bytes 13631488 | tf_op jit(solution)/shard_map/dot_general | solution.py:69
  134.1 2.6 copy.101
  136.7 2.5 copy.102
  139.2 2.5 copy.100
  141.7 1.7 fusion.24
  143.5 2.9 fusion.61
  148.3 3.5 fusion
  152.2 3.5 fusion.23
  157.6 6.1 convolution_convert_fusion.p_ref
  163.7 47.8 %tensor_scatter.1 = (f32[256,2304]{1,0:T(8,128)S(1)}, f32[256,128]{1,0:T(8,128)S(1)}) custom-call(bf16[1024,2304]{1,0:T(8,128)(2,1)} %convolution_convert_fusion.p_ref, bf16[1024,128]{1,0:T(8,128)(2,1)S(1)} %pad.76.q_ref), custom_call_target="tpu_custom_call" | custom-call | tf_op jit(solution)/shard_map/tensor_scatter/pallas_call | solution.py:282
  215.9 41.0 %chunk_gather.1.x_hbm = bf16[4,256,2304]{2,1,0:T(8,128)(2,1)S(1)} custom-call(bf16[256,2304]{1,0:T(8,128)(2,1)S(1)} %multiply_convert_fusion.5.x_ref.normed_ref), custom_call_target="tpu_custom_call" | custom-call | tf_op jit(solution)/shard_map/chunk_gather/pallas_call | solution.py:936
  256.9 2.2 copy-done
  261.6 2.0 fusion.116
  267.1 18.4 %all-gather.6.cloned.1.call-done.gu_hbm = bf16[2304,4608]{1,0:T(8,128)(2,1)} async-done(((bf16[288,4608]{1,0:T(8,128)(2,1)}), bf16[2304,4608]{1,0:T(8,128)(2,1)}) %all-gather.6.cloned.1.call-update) | async-done | bytes 21233680 | tf_op jit(solution)/shard_map/all_gather | solution.py:1584
  285.6 116.8 %mlp.1 = (f32[256,2304]{1,0:T(8,128)}, f32[256,128]{1,0:T(8,128)}, bf16[4,256,2304]{2,1,0:T(8,128)(2,1)}, bf16[4,256,2304]{2,1,0:T(8,128)(2,1)}, bf16[4,256,2304...) custom-call(bf16[4,256,2304]{2,1,0:T(8,128)(2,1)} %copy-done, bf16[2304,4608]{1,0:T(8,128)(2,1)} %all-gather.6.cloned.1.call-done.gu_hbm, ...), custom_call_target="tpu_custom_call" | custom-call | tf_op jit(solution)/shard_map/mlp/pallas_call | solution.py:881
  402.4 1.5 broadcast_select_fusion.2
  403.9 2.4 multiply_reduce_fusion.3
  408.0 2.4 multiply_convert_fusion.3
  410.5 88.6 %mlp_back.1 = (f32[256,2304]{1,0:T(8,128)}, f32[256,128]{1,0:T(8,128)}, bf16[2304,128]{1,0:T(8,128)(2,1)}) custom-call(bf16[256,2304]{1,0:T(8,128)(2,1)} %get-tuple-element.104.g_ref.grad_mlp_ref, bf16[2304,2304]{1,0:T(8,128)(2,1)} %bitcast.86, bf16[2304,4608]{1,0:T(8,128)(2,1)} %all-gather.6.cloned.1.call-done.gu_hbm, ...), custom_call_target="tpu_custom_call" | custom-call | tf_op jit(solution)/shard_map/mlp_back/pallas_call | solution.py:563
  499.1 1.5 broadcast_select_fusion.4
  500.6 3.3 multiply_reduce_fusion.1
  505.8 1.8 multiply_convert_fusion.2.g_ref
  507.6 130.4 %attn_back.1 = (f32[256,2304]{1,0:T(8,128)}, f32[256,128]{1,0:T(8,128)}, f32[8,72,80]{2,1,0:T(8,128)}, f32[8,64,16]{2,1,0:T(8,128)}, f32[8,288,16]{2,1,0:T(8,128...) custom-call(s32[8]{0:T(128)} %copy-done.45, ...), custom_call_target="tpu_custom_call" | custom-call | tf_op jit(solution)/shard_map/attn_back/pallas_call | solution.py:1500
  638.0 3.9 fusion.12
  643.8 4.0 fusion.16
  (174 shorter events, 43.1 us)
Async XLA Ops:
  7.2 3.4 copy-start.24
  7.2 3.4 copy-start.23
  7.2 114.7 %all-gather.4.cloned.1.call-start = ((), (), s32[]{:S(2)}) async-start(), calls=%async_computation | async-start | bytes 7962624 | tf_op jit(solution)/shard_map/all_gather | solution.py:1578
  10.5 275.1 %all-gather.6.cloned.1.call-start = ((), (), s32[]{:S(2)}) async-start(), calls=%async_computation.1 | async-start | bytes 23887872 | tf_op jit(solution)/shard_map/all_gather | solution.py:1584
  12.2 12.8 %copy-start.40 = (f32[4,2304]{1,0:T(4,128)S(1)}, f32[4,2304]{1,0:T(4,128)}, u32[]{:S(2)}) copy-start(f32[4,2304]{1,0:T(4,128)} %param.23) | copy-start | bytes 110596
  12.2 12.9 %copy-start.9 = (bf16[256,2304]{1,0:T(8,128)(2,1)S(1)}, bf16[256,2304]{1,0:T(8,128)(2,1)}, u32[]{:S(2)}) copy-start(bf16[256,2304]{1,0:T(8,128)(2,1)} %param.19) | copy-start | bytes 3538948
  25.0 45.7 %copy-start.45 = (s32[8]{0:T(128)}, s32[8]{0:T(128)S(1)}, u32[]{:S(2)}) copy-start(s32[8]{0:T(128)S(1)} %all-reduce.14.ids_ref) | copy-start | bytes 100
  25.8 42.4 %copy-start.36 = (bf16[8,288,16]{1,2,0:T(8,128)(2,1)S(1)}, bf16[8,288,16]{1,2,0:T(8,128)(2,1)}, u32[]{:S(2)}) copy-start(bf16[8,288,16]{1,2,0:T(8,128)(2,1)} %param.33) | copy-start | bytes 221188
  25.8 42.7 %copy-start.32 = (bf16[8,2,16,288]{3,2,1,0:T(8,128)(2,1)S(1)}, bf16[8,2,16,288]{3,2,1,0:T(8,128)(2,1)}, u32[]{:S(2)}) copy-start(bf16[8,2,16,288]{3,2,1,0:T(8,128)(2,1)} %param.36) | copy-start | bytes 442372
  71.6 39.6 %copy-start.2 = (bf16[1024,2304]{1,0:T(8,128)(2,1)S(1)}, bf16[1024,2304]{1,0:T(8,128)(2,1)}, u32[]{:S(2)}) copy-start(bf16[1024,2304]{1,0:T(8,128)(2,1)} %copy-done.1) | copy-start | bytes 14155780
  117.9 28.4 %copy-start.13 = (f32[1024,128]{1,0:T(8,128)}, f32[1024,128]{1,0:T(8,128)S(1)}, u32[]{:S(2)}) copy-start(f32[1024,128]{1,0:T(8,128)S(1)} %get-tuple-element.118.cos_ref) | copy-start | bytes 1572868
  118.0 28.4 %copy-start.14 = (f32[1024,128]{1,0:T(8,128)}, f32[1024,128]{1,0:T(8,128)S(1)}, u32[]{:S(2)}) copy-start(f32[1024,128]{1,0:T(8,128)S(1)} %get-tuple-element.119.sin_ref) | copy-start | bytes 1572868
  141.7 4.7 copy-start.18
  141.7 4.7 copy-start.19
  146.7 5.1 copy-start.15
  146.7 5.1 copy-start.17
  148.3 3.5 copy-start.21
  151.8 3.9 copy-start.41
  152.2 3.5 copy-start.22
  215.8 41.0 %copy-start.3 = (bf16[256,2304]{1,0:T(8,128)(2,1)}, bf16[256,2304]{1,0:T(8,128)(2,1)S(1)}, u32[]{:S(2)}) copy-start(bf16[256,2304]{1,0:T(8,128)(2,1)S(1)} %multiply_convert_fusion.5.x_ref.normed_ref) | copy-start | bytes 3538948
  260.7 4.0 copy-start.16
  410.5 88.6 %copy-start.46 = (pred[128]{0:T(512)(128)(4,1)S(1)}, pred[128]{0:T(512)(128)(4,1)}, u32[]{:S(2)}) copy-start(pred[128]{0:T(512)(128)(4,1)} %constant.61.clone.1) | copy-start | bytes 388
  500.6 3.3 copy-start.6
  500.6 3.8 copy-start.8
  500.6 4.1 copy-start.12
  638.0 4.0 copy-start.25
  638.0 5.1 copy-start.31
  643.8 4.1 copy-start.30
  643.8 4.8 copy-start.39
  643.8 5.4 copy-start.35
  643.8 6.1 copy-start.29
  643.8 6.8 %copy-start.34 = (f32[8,2,16,72]{3,2,1,0:T(8,128)S(1)}, f32[8,2,16,72]{3,2,1,0:T(8,128)}, u32[]{:S(2)}) copy-start(f32[8,2,16,72]{3,2,1,0:T(8,128)} %get-tuple-element.149) | copy-start | bytes 221188
  (18 other events, 28.2 us)
Sparse Core Ops, SparseCore 0:
  10.6 85.8 all-gather.3
  98.2 187.3 all-gather.5

commit v5 on v4

--- a/solution.py
+++ b/solution.py
@@ -23,6 +23,7 @@
 BF16 = jnp.bfloat16
 F32 = jnp.float32
 VMEM_LIMIT = 48 * 1024 * 1024
+BLOCK = 32
 
 
 def rms_norm(values, gain_row):
@@ -81,11 +82,38 @@
     return jnp.pad(values, [(0, 0)] * (values.ndim - 1) + [(0, LANES - values.shape[-1])])
 
 
-def greet(peers):
+QUERY, KEY, VALUE, GATE, UP, OUT, DOWN = (
+    slice(i * RANK, (i + 1) * RANK) for i in range(7)
+)
+
+
+def band(values, first, last=None):
+    lane = lax.broadcasted_iota(jnp.int32, values.shape, 1)
+    keep = (lane >= first.start) & (lane < (last or first).stop)
+    return jnp.where(keep, values, 0.0)
+
+
+def lanes(*parts):
+    pieces, at = [], 0
+    for place, values in parts:
+        if place.start > at:
+            pieces.append(jnp.zeros(values.shape[:-1] + (place.start - at,), values.dtype))
+        pieces.append(values)
+        at = place.start + values.shape[-1]
+    last = parts[-1][1]
+    pieces.append(jnp.zeros(last.shape[:-1] + (LANES - at,), last.dtype))
+    return jnp.concatenate(pieces, axis=-1)
+
+
+def call(peers):
     barrier = pltpu.get_barrier_semaphore()
     for peer in peers:
         pl.semaphore_signal(barrier, inc=1, device_id=peer, device_id_type=MESH)
-    pl.semaphore_wait(barrier, len(peers))
+
+
+def greet(peers):
+    call(peers)
+    pl.semaphore_wait(pltpu.get_barrier_semaphore(), len(peers))
 
 
 def square_peers(index):
@@ -300,8 +328,22 @@
         self.across, self.down, self.far = square_peers(self.me)
         self.links = (self.across, self.down)
 
-    def greet(self):
-        greet([{"tensor": self.across}, {"tensor": self.down}])
+    def greet(self, far=False):
+        greet([{"tensor": peer} for peer in (self.across, self.down) + ((self.far,) if far else ())])
+
+    def spread(self, source_at, target, send_sem, recv_sem):
+        copies = [pltpu.make_async_copy(source_at(self.me), target.at[self.me], recv_sem.at[0])]
+        for which, peer in enumerate((self.across, self.down, self.far)):
+            copies.append(
+                remote(
+                    source_at(peer),
+                    target.at[self.me],
+                    send_sem.at[which],
+                    recv_sem.at[1 + which],
+                    peer,
+                )
+            )
+        return copies
 
 
 class ChunkGather:
@@ -431,13 +473,13 @@
     gelu_hbm,
     hidden_hbm,
     low_hbm,
-    lift_down_ref,
-    map_ref,
-    lift_gu_ref,
+    d_ref,
+    f_table,
     o_ref,
     l_ref,
     f_out,
     f_ref,
+    f_send,
     down_w,
     gu_w,
     buf,
@@ -451,6 +493,8 @@
     own_sem,
     gather_send,
     gather_recv,
+    spread_send,
+    spread_recv,
     *scratch,
 ):
     sq = Square(rows)
@@ -473,7 +517,7 @@
     own_load.start()
     for copy in loads(0):
         copy.start()
-    sq.greet()
+    sq.greet(far=True)
     gather = ChunkGather(sq, g_ref, buf, gather_send, gather_recv)
     gather.start()
     gu_load.start()
@@ -498,13 +542,13 @@
                         copy.start()
 
         incoming = buf.at[chunk]
-        low_down = nn(incoming[...], lift_down_ref[...]).astype(BF16)
+        low_down = band(nn(incoming[...], d_ref[...]), DOWN).astype(BF16)
         tile = tile_of(width)
 
         @pl.loop(0, width // tile)
         def _(step):
             here = columns(step, tile)
-            grad = nn(incoming[...], down_w[:, here]) + nt(low_down, map_ref[here, :])
+            grad = nn(incoming[...], down_w[:, here]) + nt(low_down, f_table[here, :])
             grads[:, here] = (grad * slope[slot, :, here].astype(F32)).astype(BF16)
             grads[:, columns(step, tile, width)] = (
                 grad * gelu[slot, :, here].astype(F32)
@@ -514,7 +558,10 @@
         def _():
             gu_load.wait()
 
-        part_low[chunk] = nn(grads[...], lift_gu_ref[...]).astype(BF16)
+        part_low[chunk] = (
+            band(nn(grads[:, :width], f_table[...]), GATE)
+            + band(nn(grads[:, width:], f_table[...]), UP)
+        ).astype(BF16)
         wide = tile_of(model)
 
         @pl.loop(0, model // wide)
@@ -532,19 +579,21 @@
             for scatter in scatters:
                 scatter.send_far()
 
-        low_turned = low_down.astype(F32).T[:RANK].astype(BF16)
+        low_turned = low_down.astype(F32).T.astype(BF16)
         gu_turned = low[slot].astype(F32).T.astype(BF16)
-        f_ref[:RANK, :] += nn(low_turned, hidden[slot])
-        f_ref[RANK : 2 * RANK, :] += nn(gu_turned[:RANK], grads[:, :width])
-        f_ref[2 * RANK : 3 * RANK, :] += nn(gu_turned[RANK : 2 * RANK], grads[:, width:])
-
-    @pl.loop(0, width // LANES)
-    def _(step):
-        here = columns(step, LANES)
-        f_out[here, :] = jnp.concatenate(
-            [f_ref[:, here], jnp.zeros((LANES - 4 * RANK, LANES), F32)], axis=0
-        ).T.astype(BF16)
-
+        f_ref[:RANK, :] += nn(low_turned[DOWN], hidden[slot])
+        f_ref[RANK : 2 * RANK, :] += nn(gu_turned[GATE], grads[:, :width])
+        f_ref[2 * RANK : 3 * RANK, :] += nn(gu_turned[UP], grads[:, width:])
+
+    cores, slices = f_send.shape[:2]
+    size = width // (cores * slices)
+    for core in range(cores):
+        for peer in range(slices):
+            first = (core * slices + peer) * size
+            f_send[core, peer] = f_ref[: 3 * RANK, first : first + size].astype(BF16)
+    spread = sq.spread(lambda peer: f_send.at[:, peer], f_out, spread_send, spread_recv)
+    for copy in spread:
+        copy.start()
     for link in range(2):
         for scatter in scatters:
             scatter.pass_on(link)
@@ -553,11 +602,14 @@
     scatters[1].collect(l_ref)
     for scatter in scatters:
         scatter.finish()
-
-
-def mlp_back_fused(grad, down_w, gu_w, slope, gelu, hidden, low, lift_down, map_hidden, lift_gu):
+    for copy in spread:
+        copy.wait()
+
+
+def mlp_back_fused(grad, down_w, gu_w, slope, gelu, hidden, low, d_tab, f_tab, dp):
     rows, model = grad.shape
     width = hidden.shape[2]
+    messages = (dp // 4, 4, 3 * RANK, width // dp)
     anywhere = pl.BlockSpec(memory_space=pl.ANY)
     vmem = pl.BlockSpec(memory_space=pltpu.VMEM)
     return pl.pallas_call(
@@ -565,12 +617,13 @@
         out_shape=(
             jax.ShapeDtypeStruct((rows, model), F32),
             jax.ShapeDtypeStruct((rows, LANES), F32),
-            jax.ShapeDtypeStruct((width, LANES), BF16),
+            jax.ShapeDtypeStruct((4, dp // 4, 3 * RANK, width // dp), BF16),
         ),
-        in_specs=[vmem] + [anywhere] * 6 + [vmem] * 3,
+        in_specs=[vmem] + [anywhere] * 6 + [vmem] * 2,
         out_specs=(vmem,) * 3,
         scratch_shapes=[
-            pltpu.VMEM((4 * RANK, width), F32),
+            pltpu.VMEM((3 * RANK, width), F32),
+            pltpu.VMEM(messages, BF16),
             pltpu.VMEM((model, width), BF16),
             pltpu.VMEM((model, 2 * width), BF16),
             pltpu.VMEM((4, rows, model), BF16),
@@ -584,6 +637,8 @@
             pltpu.SemaphoreType.DMA,
             pltpu.SemaphoreType.DMA((6,)),
             pltpu.SemaphoreType.DMA((6,)),
+            pltpu.SemaphoreType.DMA((3,)),
+            pltpu.SemaphoreType.DMA((4,)),
         ]
         + scatter_scratch(rows, model)
         + scatter_scratch(rows, LANES),
@@ -591,7 +646,7 @@
             collective_id=5, has_side_effects=True, vmem_limit_bytes=62 * 1024 * 1024
         ),
         name="mlp_back",
-    )(grad, down_w, gu_w, slope, gelu, hidden, low, lift_down, map_hidden, lift_gu)
+    )(grad, down_w, gu_w, slope, gelu, hidden, low, d_tab, f_tab)
 
 
 class Line:
@@ -691,18 +746,26 @@
 
 def mlp_kernel(
     rows,
+    length_ref,
     x_hbm,
     gu_hbm,
     shard_hbm,
+    d_ref,
+    f_table,
+    resid_ref,
+    cot_ref,
+    gains_ref,
+    layer_ref,
+    grad_ref,
     low_ref,
-    lift_gu_ref,
-    map_ref,
-    o_ref,
-    l_ref,
+    low_down_ref,
     hidden_out,
     slope_out,
     gelu_out,
     down_out,
+    work,
+    low_sum,
+    lows,
     seq,
     tiles,
     hidden,
@@ -758,6 +821,13 @@
     line.start()
     seq_load.wait()
 
+    @pl.loop(0, 4)
+    def _(chunk):
+        low = nn(seq[chunk], d_ref[...])
+        lows[0, chunk] = band(low, GATE).astype(BF16)
+        lows[1, chunk] = band(low, UP).astype(BF16)
+        low_ref[chunk] = band(low, GATE, UP).astype(BF16)
+
     @pl.loop(0, steps)
     def _(step):
         slot = lax.rem(step, 2)
@@ -779,8 +849,8 @@
         @pl.loop(0, 4)
         def _(chunk):
             both = nn(seq[chunk], tiles[slot])
-            gate = both[:, :tile] + nt(low_ref[chunk], lift_gu_ref[here, :])
-            up = both[:, tile:] + nt(low_ref[chunk], lift_gu_ref[columns(step, tile, width), :])
+            gate = both[:, :tile] + nt(lows[0, chunk], f_table[here, :])
+            up = both[:, tile:] + nt(lows[1, chunk], f_table[here, :])
             hidden[chunk, :, here], slope[slot, chunk], gelu[slot, chunk] = gelu_parts(gate, up)
 
         for copy in stores(step, slot):
@@ -812,7 +882,7 @@
 
     @pl.loop(0, 4)
     def _(chunk):
-        low_scratch[0][chunk] = nn(hidden[chunk], map_ref[...]).astype(BF16)
+        low_scratch[0][chunk] = band(nn(hidden[chunk], f_table[...]), DOWN).astype(BF16)
 
     low_scatter.send_far()
     low_scatter.send_own()
@@ -854,9 +924,24 @@
     for link in range(2):
         scatter_at(order[3]).pass_on(link)
     wide = part.shape[-1]
-    low_scatter.collect(l_ref)
+    low_scatter.collect(low_sum)
+    low_down_ref[...] = low_sum[...].astype(BF16)
     for place in range(4):
-        scatter_at(place).collect(o_ref, place * wide)
+        scatter_at(place).collect(work, place * wide)
+    add_lifted(work, low_down_ref, d_ref)
+
+    @pl.loop(0, rows // BLOCK)
+    def _(step):
+        here = pl.ds(pl.multiple_of(step * BLOCK, BLOCK), BLOCK)
+        at = sq.me * rows + step * BLOCK + lax.broadcasted_iota(jnp.int32, (BLOCK, 1), 0)
+        valid = (at < length_ref[0]).astype(F32)
+        total = work[here, :]
+        gain = gains_ref[3:4, :]
+        layer_ref[here, :] = (valid * (resid_ref[here, :] + rms_norm(total, gain))).astype(BF16)
+        grad_ref[here, :] = norm_back(total, gain, cot_ref[here, :].astype(F32) * valid).astype(
+            BF16
+        )
+
     for place in range(4):
         scatter_at(place).finish()
     low_scatter.finish()
@@ -869,7 +954,16 @@
         keep.wait()
 
 
-def mlp_fused(seq, gu_w, shard, low, lift_gu, map_hidden, dp):
+def add_lifted(work, low, table):
+    wide = tile_of(work.shape[1])
+
+    @pl.loop(0, work.shape[1] // wide)
+    def _(step):
+        here = columns(step, wide)
+        work[:, here] += nt(low[...], table[here, :])
+
+
+def mlp_fused(lengths, seq, gu_w, shard, d_tab, f_tab, resid, cotangent, gains, dp):
     chunks, rows, model = seq.shape
     width = shard.shape[1]
     tile = 384
@@ -881,16 +975,21 @@
     return pl.pallas_call(
         functools.partial(mlp_kernel, rows),
         out_shape=(
-            jax.ShapeDtypeStruct((rows, model), F32),
-            jax.ShapeDtypeStruct((rows, LANES), F32),
+            jax.ShapeDtypeStruct((rows, model), BF16),
+            jax.ShapeDtypeStruct((rows, model), BF16),
+            jax.ShapeDtypeStruct((4, rows, LANES), BF16),
+            jax.ShapeDtypeStruct((rows, LANES), BF16),
             saved,
             saved,
             saved,
             jax.ShapeDtypeStruct((dp,) + shard.shape, BF16),
         ),
-        in_specs=[anywhere] * 3 + [vmem] * 3,
-        out_specs=(vmem, vmem) + (anywhere,) * 4,
+        in_specs=[pl.BlockSpec(memory_space=pltpu.SMEM)] + [anywhere] * 3 + [vmem] * 5,
+        out_specs=(vmem,) * 4 + (anywhere,) * 4,
         scratch_shapes=[
+            pltpu.VMEM((rows, model), F32),
+            pltpu.VMEM((rows, LANES), F32),
+            pltpu.VMEM((2, 4, rows, LANES), BF16),
             pltpu.VMEM((4, rows, model), BF16),
             pltpu.VMEM((2, model, 2 * tile), BF16),
             pltpu.VMEM((4, rows, width), BF16),
@@ -914,7 +1013,7 @@
             collective_id=7, has_side_effects=True, vmem_limit_bytes=62 * 1024 * 1024
         ),
         name="mlp",
-    )(seq, gu_w, shard, low, lift_gu, map_hidden)
+    )(lengths, seq, gu_w, shard, d_tab, f_tab, resid, cotangent, gains)
 
 
 def chunk_gather_kernel(rows, x_ref, o_ref, own_sem, send_sem, recv_sem):
@@ -1180,7 +1279,13 @@
     rows,
     ids_ref,
     length_ref,
-    g_ref,
+    back_ref,
+    low_gu_ref,
+    resid_ref,
+    total_ref,
+    cot_ref,
+    layer_ref,
+    gains_ref,
     weight_hbm,
     seq_hbm,
     q_ref,
@@ -1192,17 +1297,15 @@
     cos_ref,
     sin_ref,
     low_ref,
-    lift_out_ref,
-    map_ref,
-    lift_qkv_ref,
+    d_table,
+    h_table,
+    k_table,
     normed_ref,
-    grad_gu_ref,
     low_out_ref,
     grad_mlp_ref,
     low_down_ref,
-    f_hbm,
+    f_ref,
     o_ref,
-    l_ref,
     in_out,
     heads_out,
     hidden_out,
@@ -1211,7 +1314,9 @@
     gateup_out,
     resid_out,
     weight,
-    seq,
+    work,
+    g_ref,
+    low_sum,
     buf,
     att,
     q_grad,
@@ -1223,69 +1328,98 @@
     h_turned,
     k_turned,
     d_send,
-    h_send,
-    k_send,
+    d_land,
+    d_sum,
     d_recv,
     f_recv,
-    h_recv,
-    k_recv,
+    hk_send,
+    hk_land,
+    hk_recv,
     load_sem,
     own_sem,
     gather_send,
     gather_recv,
+    f_sem,
     d_sem,
-    f_sem,
-    h_sem,
-    k_sem,
-    recv_sem,
+    hk_sem,
+    group_send,
+    group_recv,
+    line_recv,
     *scratch,
 ):
     sq = Square(rows)
-    lay = Layout()
+    dp = lax.axis_size("dp")
+    d = lax.axis_index("dp")
+    model = o_ref.shape[-1]
     half = sq.half
-    model = o_ref.shape[-1]
+    wide = tile_of(model)
     weight_load = pltpu.make_async_copy(weight_hbm, weight, load_sem.at[0])
-    seq_load = pltpu.make_async_copy(seq_hbm, seq, load_sem.at[1])
-    own_load = pltpu.make_async_copy(g_ref, buf.at[0], own_sem)
+    seq_load = pltpu.make_async_copy(seq_hbm, buf, load_sem.at[1])
     weight_load.start()
-    own_load.start()
-    greet_all(lay)
-    gather = ChunkGather(sq, g_ref, buf, gather_send, gather_recv)
-    gather.start()
-    seq_load.start()
-    sends = []
-    for step in range(lay.dp):
-        slot = lax.rem(lay.d + step, lay.dp)
-        flat = lay.t * lay.dp + slot
-        send_or_keep(
-            lay,
-            sends,
-            f_hbm.at[slot],
-            f_recv.at[lay.d],
-            f_sem.at[step],
-            recv_sem.at[0],
-            flat,
-            flat == lay.me,
-        )
-    part, part_low = scratch[0], scratch[5]
-    scatters = (ChunkScatter(sq, *scratch[:5]), ChunkScatter(sq, *scratch[5:10]))
+    peers = [{"tensor": peer} for peer in (sq.across, sq.down, sq.far)]
+    peers += [{"dp": lax.rem(d + step, dp)} for step in range(1, dp)]
+    call(peers)
 
     def turned(values):
         return values.astype(F32).T.astype(BF16)
 
-    d_turned[...] = jnp.zeros_like(d_turned)
-    wide = tile_of(model)
-    low_grads = (
-        (turned(grad_gu_ref[...]), normed_ref, 3 * RANK, 2 * RANK),
-        (turned(low_out_ref[...]), g_ref, 5 * RANK, RANK),
-        (turned(low_down_ref[...]), grad_mlp_ref, 6 * RANK, RANK),
-    )
+    low_gu = low_gu_ref[...].astype(BF16)
 
     @pl.loop(0, model // wide)
     def _(step):
         here = columns(step, wide)
-        for low, source, first, count in low_grads:
-            d_turned[pl.ds(first, count), here] = nn(low[:count], source[:, here])
+        work[:, here] = back_ref[:, here] + nt(low_gu, d_table[here, :])
+
+    @pl.loop(0, rows // BLOCK)
+    def _(step):
+        here = pl.ds(pl.multiple_of(step * BLOCK, BLOCK), BLOCK)
+        at = sq.me * rows + step * BLOCK + lax.broadcasted_iota(jnp.int32, (BLOCK, 1), 0)
+        valid = (at < length_ref[0]).astype(F32)
+        mid = cot_ref[here, :].astype(F32) * valid + norm_back(
+            resid_ref[here, :], gains_ref[2:3, :], work[here, :]
+        )
+        work[here, :] = mid
+        g_ref[here, :] = norm_back(total_ref[here, :], gains_ref[1:2, :], mid).astype(BF16)
+
+    own_load = pltpu.make_async_copy(g_ref, buf.at[0], own_sem)
+    own_load.start()
+    pl.semaphore_wait(pltpu.get_barrier_semaphore(), len(peers))
+    gather = ChunkGather(sq, g_ref, buf, gather_send, gather_recv)
+    gather.start()
+    line = []
+
+    def along(source_at, target, send_sem, recv_sem):
+        own = pltpu.make_async_copy(source_at(d), target.at[d], recv_sem)
+        own.start()
+        for step in range(1, dp):
+            peer = lax.rem(d + step, dp)
+            copy = pltpu.make_async_remote_copy(
+                src_ref=source_at(peer),
+                dst_ref=target.at[d],
+                send_sem=send_sem.at[step],
+                recv_sem=recv_sem,
+                device_id={"dp": peer},
+                device_id_type=MESH,
+            )
+            copy.start()
+            line.append(copy)
+
+    along(lambda k: f_ref.at[k // 2, lax.rem(k, 2)], f_recv, f_sem, line_recv.at[0])
+    part, part_low = scratch[0], scratch[5]
+    scatters = (ChunkScatter(sq, *scratch[:5]), ChunkScatter(sq, *scratch[5:10]))
+
+    d_turned[...] = jnp.zeros_like(d_turned)
+    low_grads = (
+        (turned(low_gu)[GATE.start : UP.stop], normed_ref, slice(GATE.start, UP.stop)),
+        (turned(low_out_ref[...])[OUT], g_ref, OUT),
+        (turned(low_down_ref[...])[DOWN], grad_mlp_ref, DOWN),
+    )
+
+    @pl.loop(0, model // wide)
+    def _(step):
+        here = columns(step, wide)
+        for low, source, place in low_grads:
+            d_turned[place, here] = nn(low, source[:, here])
 
     h_turned[...] = jnp.zeros_like(h_turned)
     k_turned[...] = jnp.zeros_like(k_turned)
@@ -1307,11 +1441,11 @@
                 gather.wait_chunk(step)
 
         incoming = buf.at[chunk]
-        low_out = nn(incoming[...], lift_out_ref[...]).astype(BF16)
+        low_out = band(nn(incoming[...], d_table[...]), OUT).astype(BF16)
         att[...] = (
-            nn(incoming[...], weight[:, qkv_width:]) + nt(low_out, map_ref[...])
+            nn(incoming[...], weight[:, qkv_width:]) + nt(low_out, h_table[...])
         ).astype(BF16)
-        low_turned = turned(low_out)[:RANK]
+        low_turned = turned(low_out)[OUT]
         for side in range(2):
             start = chunk_start(sq, chunk, side)
             here = pl.ds(start, half)
@@ -1342,6 +1476,8 @@
                     q_back[h * half : (h + 1) * half], cos_ref[here, :], sin_ref[here, :]
                 ).astype(BF16)
 
+    gather.finish()
+    seq_load.start()
     kv_grad[:, :HD] = rotate_back(k_sum[...], cos_ref[...], sin_ref[...]).astype(BF16)
     kv_grad[:, HD:] = v_sum[...].astype(BF16)
 
@@ -1352,7 +1488,11 @@
         for side in range(2):
             here = pl.ds(chunk_start(sq, chunk, side), half)
             joined[chunk, pl.ds(side * half, half), q_width:] = kv_grad[here, :]
-        part_low[chunk] = nn(joined[chunk], lift_qkv_ref[...]).astype(BF16)
+        part_low[chunk] = (
+            band(nn(joined[chunk, :, :q_width], h_table[...]), QUERY)
+            + band(nn(joined[chunk, :, q_width : q_width + HD], k_table[...]), KEY)
+            + band(nn(joined[chunk, :, q_width + HD :], k_table[...]), VALUE)
+        ).astype(BF16)
 
         @pl.loop(0, model // wide)
         def _(tile):
@@ -1373,130 +1513,147 @@
 
     @pl.loop(0, 4)
     def _(chunk):
-        grad_turned = turned(part_low[chunk])[: 3 * RANK]
+        grad_turned = turned(part_low[chunk])[: VALUE.stop]
         for side in range(2):
             here = pl.ds(chunk_start(sq, chunk, side), half)
             place = slice(side * half, (side + 1) * half)
             low_turned = turned(low_ref[here, :])
             mine = joined.at[chunk, pl.ds(side * half, half)]
-            h_turned[RANK : 2 * RANK, :] += nn(low_turned[:RANK], mine[:, :q_width])
-            k_turned[:RANK, :] += nn(
-                low_turned[RANK : 2 * RANK], mine[:, q_width : q_width + HD]
-            )
-            k_turned[RANK : 2 * RANK, :] += nn(
-                low_turned[2 * RANK : 3 * RANK], mine[:, q_width + HD :]
-            )
+            h_turned[RANK : 2 * RANK, :] += nn(low_turned[QUERY], mine[:, :q_width])
+            k_turned[:RANK, :] += nn(low_turned[KEY], mine[:, q_width : q_width + HD])
+            k_turned[RANK : 2 * RANK, :] += nn(low_turned[VALUE], mine[:, q_width + HD :])
+            where_from = chunk_start(sq, chunk, side)
+            block = where_from // rows
+            inside = pl.ds(pl.multiple_of(where_from - block * rows, half), half)
 
             @pl.loop(0, model // wide)
             def _(tile):
                 where = columns(tile, wide)
-                d_turned[: 3 * RANK, where] += nn(grad_turned[:, place], seq[here, where])
+                d_turned[: VALUE.stop, where] += nn(
+                    grad_turned[:, place],
+                    buf[block, inside, where],
+                )
 
     @pl.loop(0, model // LANES)
     def _(step):
         here = columns(step, LANES)
         d_send[here, :] = d_turned[:, here].T.astype(BF16)
 
-    h_send[...] = h_turned[...].T.astype(BF16)
-    k_send[...] = k_turned[...].T.astype(BF16)
-    d_rows, h_rows, k_rows = d_recv.shape[1], h_recv.shape[1], k_recv.shape[1]
-    for step in range(lay.dp):
-        slot = lax.rem(lay.d + step, lay.dp)
-        flat = lay.t * lay.dp + slot
-        for item, (source, size, target, sem) in enumerate(
-            ((h_send, h_rows, h_recv, h_sem), (k_send, k_rows, k_recv, k_sem))
-        ):
-            send_or_keep(
-                lay,
-                sends,
-                source.at[pl.ds(pl.multiple_of(slot * size, size), size)],
-                target.at[lay.d],
-                sem.at[step],
-                recv_sem.at[1 + item],
-                flat,
-                flat == lay.me,
+    d_rows = d_sum.shape[1]
+    spread = []
+    for k in range(dp):
+        spread.append(
+            sq.spread(
+                lambda peer, k=k: d_send.at[pl.ds(pl.multiple_of((k * 4 + peer) * d_rows, 8), d_rows)],
+                d_land.at[k],
+                group_send.at[k],
+                group_recv.at[k],
             )
-    pltpu.make_async_copy(
-        d_send.at[pl.ds(pl.multiple_of(lay.me * d_rows, 8), d_rows)],
-        d_recv.at[lay.me],
-        recv_sem.at[3],
-    ).start()
-    for step in range(1, lay.total):
-        flat = lax.rem(lay.me + step, lay.total)
-        send_or_keep(
-            lay,
-            sends,
-            d_send.at[pl.ds(pl.multiple_of(flat * d_rows, 8), d_rows)],
-            d_recv.at[lay.me],
-            d_sem.at[step],
-            recv_sem.at[3],
-            flat,
-            None,
         )
+    cores = hk_send.shape[0]
+    h_size, k_size = q_width // dp, HD // dp
+    hk_send[...] = jnp.zeros_like(hk_send)
+    for core in range(cores):
+        for peer in range(4):
+            at = core * 4 + peer
+            hk_send[core, peer, : 2 * RANK, :h_size] = h_turned[
+                : 2 * RANK, at * h_size : (at + 1) * h_size
+            ].astype(BF16)
+            hk_send[core, peer, 2 * RANK :, :k_size] = k_turned[
+                : 2 * RANK, at * k_size : (at + 1) * k_size
+            ].astype(BF16)
+    spread.append(
+        sq.spread(lambda peer: hk_send.at[:, peer], hk_land, group_send.at[dp], group_recv.at[dp])
+    )
+    for copies in spread:
+        for copy in copies:
+            copy.start()
     for link in range(2):
         for scatter in scatters:
             scatter.pass_on(link)
-    scatters[0].collect(o_ref)
-    scatters[1].collect(l_ref)
-    finish(
-        sends,
-        (
-            (f_recv, recv_sem.at[0]),
-            (h_recv, recv_sem.at[1]),
-            (k_recv, recv_sem.at[2]),
-            (d_recv, recv_sem.at[3]),
-        ),
-    )
+    for copies in spread:
+        copies[0].wait()
+        for copy in copies[1:]:
+            copy.wait_recv()
+    for k in range(dp):
+        d_sum[k] = sum(d_land[k, t].astype(F32) for t in range(4)).astype(BF16)
+    along(lambda k: d_sum.at[k], d_recv, d_sem, line_recv.at[1])
+    along(lambda k: hk_land.at[k // 2, lax.rem(k, 2)], hk_recv, hk_sem, line_recv.at[2])
+    scatters[1].collect(low_sum)
+    low_qkv = low_sum[...].astype(BF16)
+    for link in range(2):
+        scatters[0].copy(0, link).wait_recv()
+        scatters[0].copy(2, link).wait_recv()
+    landing = scratch[1]
+    low_sum[...] = low_qkv.astype(F32)
+
+    @pl.loop(0, rows // BLOCK)
+    def _(step):
+        here = pl.ds(pl.multiple_of(step * BLOCK, BLOCK), BLOCK)
+        link = (step * BLOCK) // half
+        there = pl.ds(pl.multiple_of(step * BLOCK - link * half, BLOCK), BLOCK)
+        total = (
+            part[0, here, :].astype(F32)
+            + landing[link, there, :].astype(F32)
+            + landing[4 + link, there, :].astype(F32)
+            + nt(low_sum[here, :].astype(BF16), d_table[...])
+        )
+        o_ref[here, :] = (
+            work[here, :] + norm_back(layer_ref[here, :].astype(F32), gains_ref[0:1, :], total)
+        ).astype(BF16)
+
+    for item, target in enumerate((f_recv, d_recv, hk_recv)):
+        pltpu.make_async_copy(target, target, line_recv.at[item]).wait()
 
     @pl.loop(0, NA)
     def _(adapter):
-        def pick(parts):
+        def pick(received):
             total = None
-            for group in range(lay.dp):
-                mine = jnp.where(ids_ref[group] == adapter, parts(group), 0.0)
+            for group in range(dp):
+                mine = jnp.where(
+                    ids_ref[group] == adapter, received[group].astype(F32), 0.0
+                )
                 total = mine if total is None else total + mine
             return total
 
-        def d_part(group):
-            return sum(
-                d_recv[group * lay.tensor + t].astype(F32) for t in range(lay.tensor)
-            )
-
-        d_all = pick(d_part)
+        d_all = pick(d_recv)
         in_out[adapter] = d_all[:, : 5 * RANK]
         d_flip = d_all.T
-        f_all = pick(lambda group: f_recv[group].astype(F32))
-        hidden_out[adapter] = f_all[:, :RANK]
-        f_flip = f_all.T
-        h_all = pick(lambda group: h_recv[group].astype(F32))
-        heads_out[adapter] = h_all[:, :RANK]
-        query_out[adapter] = h_all.T[RANK : 2 * RANK]
-        k_flip = pick(lambda group: k_recv[group].astype(F32)).T
+        f_all = pick(f_recv)
+        hidden_out[adapter] = f_all[:RANK].T
+        hk_all = pick(hk_recv)
+        heads_out[adapter] = hk_all[:RANK, :h_size].T
+        query_out[adapter] = hk_all[RANK : 2 * RANK, :h_size]
         for which in range(2):
-            band = slice(which * RANK, (which + 1) * RANK)
-            keyval_out[adapter, which] = k_flip[band]
-            gateup_out[adapter, which] = f_flip[RANK:][band]
-            resid_out[adapter, which] = d_flip[5 * RANK :][band]
-
-    gather.finish()
+            first = (which + 2) * RANK
+            keyval_out[adapter, which] = hk_all[first : first + RANK, :k_size]
+            first = (which + 1) * RANK
+            gateup_out[adapter, which] = f_all[first : first + RANK]
+            first = (which + 5) * RANK
+            resid_out[adapter, which] = d_flip[first : first + RANK]
+
+    for copies in spread:
+        for copy in copies[1:]:
+            copy.wait_send()
+    for copy in line:
+        copy.wait_send()
     for scatter in scatters:
         scatter.finish()
 
 
 def attn_back_fused(scalars, arrays, grad_shapes, dp, total):
-    (g, weight, seq, q) = arrays[:4]
-    rows, model = g.shape
-    f_send = arrays[-1]
     anywhere = pl.BlockSpec(memory_space=pl.ANY)
     vmem = pl.BlockSpec(memory_space=pltpu.VMEM)
     smem = pl.BlockSpec(memory_space=pltpu.SMEM)
+    rows, model = arrays[0].shape
+    weight, seq, q, f_in = arrays[7], arrays[8], arrays[9], arrays[-1]
     q_width = q.shape[1]
     specs = [smem, smem] + [vmem] * len(arrays)
-    specs[3] = specs[4] = specs[-1] = anywhere
-    outs = [jax.ShapeDtypeStruct((rows, model), F32), jax.ShapeDtypeStruct((rows, LANES), F32)]
+    specs[9] = specs[10] = anywhere
+    outs = [jax.ShapeDtypeStruct((rows, model), BF16)]
     outs += [jax.ShapeDtypeStruct(shape, F32) for shape in grad_shapes]
-    d_rows, h_rows = model // total, q_width // dp
-    k_rows = HD // dp
+    d_rows = model // total
+    messages = f_in.shape[2:]
     return pl.pallas_call(
         functools.partial(attn_back_kernel, rows),
         out_shape=tuple(outs),
@@ -1504,7 +1661,9 @@
         out_specs=(vmem,) * len(outs),
         scratch_shapes=[
             pltpu.VMEM(weight.shape, BF16),
-            pltpu.VMEM(seq.shape, BF16),
+            pltpu.VMEM((rows, model), F32),
+            pltpu.VMEM((rows, model), BF16),
+            pltpu.VMEM((rows, LANES), F32),
             pltpu.VMEM((4, rows, model), BF16),
             pltpu.VMEM((rows, q_width), BF16),
             pltpu.VMEM((4, rows, q_width), BF16),
@@ -1513,24 +1672,26 @@
             pltpu.VMEM((LEN, 2 * HD), BF16),
             pltpu.VMEM((4, rows, q_width + 2 * HD), BF16),
             pltpu.VMEM((LANES, model), F32),
-            pltpu.VMEM((LANES, q_width), F32),
-            pltpu.VMEM((LANES, HD), F32),
+            pltpu.VMEM((2 * RANK, q_width), F32),
+            pltpu.VMEM((2 * RANK, HD), F32),
             pltpu.VMEM((model, LANES), BF16),
-            pltpu.VMEM((q_width, LANES), BF16),
-            pltpu.VMEM((HD, LANES), BF16),
-            pltpu.VMEM((total, d_rows, LANES), BF16),
-            pltpu.VMEM(f_send.shape, BF16),
-            pltpu.VMEM((dp, h_rows, LANES), BF16),
-            pltpu.VMEM((dp, k_rows, LANES), BF16),
+            pltpu.VMEM((dp, 4, d_rows, LANES), BF16),
+            pltpu.VMEM((dp, d_rows, LANES), BF16),
+            pltpu.VMEM((dp, d_rows, LANES), BF16),
+            pltpu.VMEM((dp,) + messages, BF16),
+            pltpu.VMEM((dp // 4, 4, 4 * RANK, LANES), BF16),
+            pltpu.VMEM((4, dp // 4, 4 * RANK, LANES), BF16),
+            pltpu.VMEM((dp, 4 * RANK, LANES), BF16),
             pltpu.SemaphoreType.DMA((2,)),
             pltpu.SemaphoreType.DMA,
             pltpu.SemaphoreType.DMA((6,)),
             pltpu.SemaphoreType.DMA((6,)),
-            pltpu.SemaphoreType.DMA((total,)),
             pltpu.SemaphoreType.DMA((dp,)),
             pltpu.SemaphoreType.DMA((dp,)),
             pltpu.SemaphoreType.DMA((dp,)),
-            pltpu.SemaphoreType.DMA((4,)),
+            pltpu.SemaphoreType.DMA((dp + 1, 3)),
+            pltpu.SemaphoreType.DMA((dp + 1, 4)),
+            pltpu.SemaphoreType.DMA((3,)),
         ]
         + scatter_scratch(rows, model)
         + scatter_scratch(rows, LANES),
@@ -1592,15 +1753,15 @@
         return moved.reshape(NA, moved.shape[1], -1)
 
     def choose(*parts):
-        packed = pad_lanes(jnp.concatenate(parts, axis=-1))
+        packed = lanes(*parts)
         return lax.dot_general(
             group_hot, packed, (((1,), (0,)), ((), ())), preferred_element_type=F32
         ).astype(BF16)
 
-    d_send = choose(adapt_in, rows_of(lift_resid))
-    f_send = choose(adapt_hidden, rows_of(lift_gateup))
-    h_send = choose(adapt_heads, rows_of(lift_query))
-    k_send = choose(rows_of(lift_keyval))
+    d_send = choose((QUERY, adapt_in), (OUT, rows_of(lift_resid)))
+    f_send = choose((GATE, rows_of(lift_gateup)), (DOWN, adapt_hidden))
+    h_send = choose((QUERY, rows_of(lift_query)), (OUT, adapt_heads))
+    k_send = choose((KEY, rows_of(lift_keyval)))
     d_rows, f_rows, h_rows, k_rows = (item.shape[1] for item in (d_send, f_send, h_send, k_send))
     d_tab, f_tab, h_tab, k_tab = exchange(
         tables_kernel,
@@ -1622,10 +1783,10 @@
     h_tab = h_tab.reshape(head_width, LANES)
     k_tab = k_tab.reshape(HD, LANES)
     in_qkv, in_gu = d_tab[:, : 3 * RANK], d_tab[:, 3 * RANK : 5 * RANK]
-    lift_out, lift_down = d_tab[:, 5 * RANK : 6 * RANK], d_tab[:, 6 * RANK : 7 * RANK]
-    map_hidden, lift_gate, lift_up = (f_tab[:, i * RANK : (i + 1) * RANK] for i in range(3))
-    map_heads, lift_q = h_tab[:, :RANK], h_tab[:, RANK : 2 * RANK]
-    lift_k, lift_v = k_tab[:, :RANK], k_tab[:, RANK : 2 * RANK]
+    lift_out, lift_down = d_tab[:, OUT], d_tab[:, DOWN]
+    map_hidden, lift_gate, lift_up = f_tab[:, DOWN], f_tab[:, GATE], f_tab[:, UP]
+    map_heads, lift_q = h_tab[:, OUT], h_tab[:, QUERY]
+    lift_k, lift_v = k_tab[:, KEY], k_tab[:, VALUE]
 
     row_start = lay.t * rows
     length = lengths[0]
@@ -1667,147 +1828,141 @@
     resid_mid = resid_in + rms_norm(attn_total, norm_gains[1])
 
     normed_mlp = rms_norm(resid_mid, norm_gains[2]).astype(BF16)
-    line_of_four = count == 4 and lay.dp == 8
-    if line_of_four:
-        seq_mlp = chunk_gather(normed_mlp)
-        low_gu = pad_lanes(nn(seq_mlp.reshape(LEN, D), in_gu).astype(BF16)).reshape(4, rows, LANES)
-        lift_gu = jnp.concatenate(
-            [pad_lanes(lift_gate), jnp.pad(lift_up, ((0, 0), (RANK, LANES - 2 * RANK)))], axis=0
+    if count == 4 and lay.dp == 8:
+        layer_out, grad_mlp, low_gu, low_down, hidden, slope, gelu, down_w = mlp_fused(
+            lengths,
+            chunk_gather(normed_mlp),
+            gate_up_w,
+            down_shard,
+            d_tab,
+            f_tab,
+            resid_mid,
+            cotangent,
+            norm_gains,
+            lay.dp,
         )
-        mlp_main, low_down, hidden, slope, gelu, down_w = mlp_fused(
-            seq_mlp, gate_up_w, down_shard, low_gu, lift_gu, pad_lanes(map_hidden), lay.dp
-        )
-        down_w = down_w.reshape(D, hidden_here)
-    else:
-        seq_mlp = tensor_gather(normed_mlp, count)
-        low_gu = nn(seq_mlp, in_gu).astype(BF16)
-        low_g, low_u = low_gu[:, :RANK], low_gu[:, RANK:]
-        w_gate, w_up = gate_up_w[:, :hidden_here], gate_up_w[:, hidden_here:]
-        gate = nn(seq_mlp, w_gate) + nt(low_g, lift_gate)
-        up = nn(seq_mlp, w_up) + nt(low_u, lift_up)
-        hidden, slope, gelu = gelu_parts(gate, up)
-        down_w = lax.all_gather(down_shard, "dp", axis=0, tiled=True)
-        down_part = nt(hidden, down_w).astype(BF16)
-        low_down_part = pad_lanes(nn(hidden, map_hidden).astype(BF16))
-        mlp_main, low_down = tensor_scatter(down_part, low_down_part, count)
-    low_down = low_down[:, :RANK].astype(BF16)
-    mlp_total = mlp_main + nt(low_down, lift_down)
-    layer_out = (row_valid * (resid_mid + rms_norm(mlp_total, norm_gains[3]))).astype(BF16)
-
-    grad_out = cotangent.astype(F32) * row_valid
-    grad_mlp = norm_back(mlp_total, norm_gains[3], grad_out).astype(BF16)
-    if line_of_four:
         mlp_back, grad_low_gu, f_grad = mlp_back_fused(
             grad_mlp,
-            down_w,
+            down_w.reshape(D, hidden_here),
             gate_up_w,
             slope,
             gelu,
             hidden,
             low_gu,
-            pad_lanes(lift_down),
-            pad_lanes(map_hidden),
-            lift_gu,
+            d_tab,
+            f_tab,
+            lay.dp,
         )
-    else:
-        seq_grad_mlp = tensor_gather(grad_mlp, count)
-        grad_low_down = nn(seq_grad_mlp, lift_down).astype(BF16)
-        grad_hidden = nn(seq_grad_mlp, down_w) + nt(grad_low_down, map_hidden)
-        grad_gate = (grad_hidden * slope.astype(F32)).astype(BF16)
-        grad_up = (grad_hidden * gelu.astype(F32)).astype(BF16)
-        low_gu_part = pad_lanes(
-            jnp.concatenate([nn(grad_gate, lift_gate), nn(grad_up, lift_up)], axis=1).astype(BF16)
+        return (
+            layer_out,
+            *attn_back_fused(
+                (all_ids, lengths),
+                (
+                    mlp_back,
+                    grad_low_gu,
+                    resid_mid,
+                    attn_total,
+                    cotangent,
+                    layer_in,
+                    norm_gains,
+                    attn_w,
+                    seq_attn.reshape(count, rows, D),
+                    queries.reshape(LEN, head_width),
+                    keys,
+                    keys.T,
+                    values,
+                    attended,
+                    inverse_total.reshape(heads_here, LEN),
+                    cosine.reshape(LEN, HD // 2),
+                    sine.reshape(LEN, HD // 2),
+                    pad_lanes(low_qkv),
+                    d_tab,
+                    h_tab,
+                    k_tab,
+                    normed_mlp,
+                    lanes((OUT, low_out)),
+                    grad_mlp,
+                    low_down,
+                    f_grad,
+                ),
+                tuple(
+                    table.shape
+                    for table in (
+                        adapt_in,
+                        adapt_heads,
+                        adapt_hidden,
+                        lift_query,
+                        lift_keyval,
+                        lift_gateup,
+                        lift_resid,
+                    )
+                ),
+                lay.dp,
+                lay.total,
+            ),
         )
-        mlp_back_part = (nt(grad_gate, w_gate) + nt(grad_up, w_up)).astype(BF16)
-        mlp_back, grad_low_gu = tensor_scatter(mlp_back_part, low_gu_part, count)
-        f_parts = [tn(hidden, grad_low_down), tn(grad_gate, low_g), tn(grad_up, low_u)]
+
+    seq_mlp = tensor_gather(normed_mlp, count)
+    low_gu = nn(seq_mlp, in_gu).astype(BF16)
+    low_g, low_u = low_gu[:, :RANK], low_gu[:, RANK:]
+    w_gate, w_up = gate_up_w[:, :hidden_here], gate_up_w[:, hidden_here:]
+    gate = nn(seq_mlp, w_gate) + nt(low_g, lift_gate)
+    up = nn(seq_mlp, w_up) + nt(low_u, lift_up)
+    hidden, slope, gelu = gelu_parts(gate, up)
+    down_w = lax.all_gather(down_shard, "dp", axis=0, tiled=True)
+    down_part = nt(hidden, down_w).astype(BF16)
+    low_down_part = pad_lanes(nn(hidden, map_hidden).astype(BF16))
+    mlp_main, low_down = tensor_scatter(down_part, low_down_part, count)
+    low_down = low_down[:, :RANK].astype(BF16)
+    mlp_total = mlp_main + nt(low_down, lift_down)
+    layer_out = (row_valid * (resid_mid + rms_norm(mlp_total, norm_gains[3]))).astype(BF16)
+
+    grad_out = cotangent.astype(F32) * row_valid
+    grad_mlp = norm_back(mlp_total, norm_gains[3], grad_out).astype(BF16)
+    seq_grad_mlp = tensor_gather(grad_mlp, count)
+    grad_low_down = nn(seq_grad_mlp, lift_down).astype(BF16)
+    grad_hidden = nn(seq_grad_mlp, down_w) + nt(grad_low_down, map_hidden)
+    grad_gate = (grad_hidden * slope.astype(F32)).astype(BF16)
+    grad_up = (grad_hidden * gelu.astype(F32)).astype(BF16)
+    low_gu_part = pad_lanes(
+        jnp.concatenate([nn(grad_gate, lift_gate), nn(grad_up, lift_up)], axis=1).astype(BF16)
+    )
+    mlp_back_part = (nt(grad_gate, w_gate) + nt(grad_up, w_up)).astype(BF16)
+    mlp_back, grad_low_gu = tensor_scatter(mlp_back_part, low_gu_part, count)
+    f_parts = [tn(hidden, grad_low_down), tn(grad_gate, low_g), tn(grad_up, low_u)]
     grad_low_gu = grad_low_gu[:, : 2 * RANK].astype(BF16)
     grad_normed_mlp = mlp_back + nt(grad_low_gu, in_gu)
     grad_mid = grad_out + norm_back(resid_mid, norm_gains[2], grad_normed_mlp)
 
     grad_attn = norm_back(attn_total, norm_gains[1], grad_mid).astype(BF16)
-    grad_shapes = tuple(
-        table.shape
-        for table in (
-            adapt_in,
-            adapt_heads,
-            adapt_hidden,
-            lift_query,
-            lift_keyval,
-            lift_gateup,
-            lift_resid,
-        )
+    seq_grad_attn = tensor_gather(grad_attn, count)
+    grad_low_out = nn(seq_grad_attn, lift_out).astype(BF16)
+    grad_attended = (nn(seq_grad_attn, w_out) + nt(grad_low_out, map_heads)).astype(BF16)
+    grad_heads = grad_attended.reshape(LEN, heads_here, HD)
+    probs = weights * inverse_total
+    probs_low = probs.astype(BF16)
+    grad_probs = jnp.einsum("qhd,kd->hqk", grad_heads, values, preferred_element_type=F32)
+    grad_value = jnp.einsum("hqk,qhd->kd", probs_low, grad_heads, preferred_element_type=F32)
+    grad_capped = probs * (grad_probs - jnp.sum(probs * grad_probs, axis=-1, keepdims=True))
+    grad_raw = (grad_capped * (1.0 - squash * squash)).astype(BF16)
+    grad_query = jnp.einsum("hqk,kd->qhd", grad_raw, keys, preferred_element_type=F32)
+    grad_key = jnp.einsum("hqk,qhd->kd", grad_raw, queries, preferred_element_type=F32)
+    grad_q_pre = rotate(grad_query * HD ** (-0.5), cosine, -sine).astype(BF16)
+    grad_q_pre = grad_q_pre.reshape(LEN, head_width)
+    grad_k_pre = rotate(grad_key.reshape(LEN, 1, HD), cosine, -sine).astype(BF16)
+    grad_k_pre = grad_k_pre.reshape(LEN, HD)
+    grad_v_pre = grad_value.astype(BF16)
+    low_qkv_part = pad_lanes(
+        jnp.concatenate(
+            [nn(grad_q_pre, lift_q), nn(grad_k_pre, lift_k), nn(grad_v_pre, lift_v)], axis=1
+        ).astype(BF16)
     )
-    if line_of_four:
-        lift_qkv = jnp.concatenate(
-            [
-                pad_lanes(lift_q),
-                jnp.pad(lift_k, ((0, 0), (RANK, LANES - 2 * RANK))),
-                jnp.pad(lift_v, ((0, 0), (2 * RANK, LANES - 3 * RANK))),
-            ],
-            axis=0,
-        )
-        attn_back, grad_low_qkv, *adapter_grads = attn_back_fused(
-            (all_ids, lengths),
-            (
-                grad_attn,
-                attn_w,
-                seq_attn,
-                queries.reshape(LEN, head_width),
-                keys,
-                keys.T,
-                values,
-                attended,
-                inverse_total.reshape(heads_here, LEN),
-                cosine.reshape(LEN, HD // 2),
-                sine.reshape(LEN, HD // 2),
-                pad_lanes(low_qkv),
-                pad_lanes(lift_out),
-                pad_lanes(map_heads),
-                lift_qkv,
-                normed_mlp,
-                pad_lanes(grad_low_gu),
-                pad_lanes(low_out),
-                grad_mlp,
-                pad_lanes(low_down),
-                f_grad.reshape(lay.dp, -1, LANES),
-            ),
-            grad_shapes,
-            lay.dp,
-            lay.total,
-        )
-    else:
-        seq_grad_attn = tensor_gather(grad_attn, count)
-        grad_low_out = nn(seq_grad_attn, lift_out).astype(BF16)
-        grad_attended = (nn(seq_grad_attn, w_out) + nt(grad_low_out, map_heads)).astype(BF16)
-        grad_heads = grad_attended.reshape(LEN, heads_here, HD)
-        probs = weights * inverse_total
-        probs_low = probs.astype(BF16)
-        grad_probs = jnp.einsum("qhd,kd->hqk", grad_heads, values, preferred_element_type=F32)
-        grad_value = jnp.einsum("hqk,qhd->kd", probs_low, grad_heads, preferred_element_type=F32)
-        grad_capped = probs * (grad_probs - jnp.sum(probs * grad_probs, axis=-1, keepdims=True))
-        grad_raw = (grad_capped * (1.0 - squash * squash)).astype(BF16)
-        grad_query = jnp.einsum("hqk,kd->qhd", grad_raw, keys, preferred_element_type=F32)
-        grad_key = jnp.einsum("hqk,qhd->kd", grad_raw, queries, preferred_element_type=F32)
-        grad_q_pre = rotate(grad_query * HD ** (-0.5), cosine, -sine).astype(BF16)
-        grad_q_pre = grad_q_pre.reshape(LEN, head_width)
-        grad_k_pre = rotate(grad_key.reshape(LEN, 1, HD), cosine, -sine).astype(BF16)
-        grad_k_pre = grad_k_pre.reshape(LEN, HD)
-        grad_v_pre = grad_value.astype(BF16)
-        low_qkv_part = pad_lanes(
-            jnp.concatenate(
-                [nn(grad_q_pre, lift_q), nn(grad_k_pre, lift_k), nn(grad_v_pre, lift_v)], axis=1
-            ).astype(BF16)
-        )
-        grad_qkv = jnp.concatenate([grad_q_pre, grad_k_pre, grad_v_pre], axis=1)
-        attn_back_part = nt(grad_qkv, attn_w[:, :qkv_width]).astype(BF16)
-        attn_back, grad_low_qkv = tensor_scatter(attn_back_part, low_qkv_part, count)
+    grad_qkv = jnp.concatenate([grad_q_pre, grad_k_pre, grad_v_pre], axis=1)
+    attn_back_part = nt(grad_qkv, attn_w[:, :qkv_width]).astype(BF16)
+    attn_back, grad_low_qkv = tensor_scatter(attn_back_part, low_qkv_part, count)
     grad_low_qkv = grad_low_qkv[:, : 3 * RANK].astype(BF16)
     grad_normed_attn = attn_back + nt(grad_low_qkv, in_qkv)
     input_grad = (grad_mid + norm_back(resid_in, norm_gains[0], grad_normed_attn)).astype(BF16)
-
-    if line_of_four:
-        return (layer_out, input_grad, *adapter_grads)
 
     def packed(parts, blocks):
         return pad_lanes(jnp.concatenate(parts, axis=1).astype(BF16)).reshape(

time: 665 us -> 631 us (0.949)
  other arithmetic: 32.5 us -> 14.9 us
  Pallas kernels: 503 us -> 486 us
  matrix products: 38.7 us -> 30.8 us
    pallas_call x1, Pallas kernels: 130 us -> 114 us  [attn_back_fused(): pl.pallas_call(functools.partial(attn_back_kernel, rows), out_shape=tuple...]
    convert_element_type x4 -> x0, other arithmetic: 8.28 us -> none  [the longest x1 4.05 us: per_device(): (grad_mid + norm_back(resid_in, norm_gains[0], grad_normed_attn)).astype(...]
    dot_general x8 -> x5, matrix products: 19 us -> 10.7 us  [nt(): lax.dot_general(a, b, (((1,), (1,)), ((), ())), preferred_element_type=F32)]
    unnamed x114 -> x107, local copies, waits for them, and re-layouts: 25.9 us -> 26.7 us
  transfers between devices with their start and end apart: 2 -> 2, of which waited for: 1 -> 1; matrix products, arithmetic and copies ran while one was open for 10% -> 11% of each run, Pallas kernels for 25% -> 26%
where the time goes in v5:
time: 631 us; the launch traced here: 627 us
  Pallas kernels  486 us (77%)
  local copies, waits for them, and re-layouts  42.9 us (7%)
  matrix products  30.8 us (5%)
  waiting for transfers between devices  25.1 us (4%)
  between operations  16.5 us (3%)
  other arithmetic  14.9 us (2%)
  blocking collectives  10.7 us (2%)
    pallas_call x1, Pallas kernels, mlp_fused(): pl.pallas_call(functools.partial(mlp_kernel, rows), out_shape=(jax.ShapeD...  121 us
    pallas_call x1, Pallas kernels, attn_back_fused(): pl.pallas_call(functools.partial(attn_back_kernel, rows), out_shape=tuple...  114 us
    pallas_call x1, Pallas kernels, mlp_back_fused(): pl.pallas_call(functools.partial(mlp_back_kernel, rows), out_shape=(jax.S...  89.1 us
    pallas_call x1, Pallas kernels, tensor_scatter(): pl.pallas_call(functools.partial(scatter_kernel, count, rows), out_shape=...  45.7 us
    pallas_call x1, Pallas kernels, chunk_gather(): pl.pallas_call(functools.partial(chunk_gather_kernel, rows), out_shape=ja...  41.9 us
    pallas_call x1, Pallas kernels, tensor_gather(): pl.pallas_call(functools.partial(gather_kernel, count, rows), out_shape=j...  40.1 us
    pallas_call x1, Pallas kernels, exchange(): pl.pallas_call(kernel, out_shape=tuple((jax.ShapeDtypeStruct(shape, BF16)...  33.6 us
    unnamed x107, local copies, waits for them, and re-layouts  26.7 us
  transfers between devices with their start and end apart: 2, of which 1 were waited for; matrix products, arithmetic and copies ran while one was open for 11% of the time, Pallas kernels for 26%

profile of v5, /device:TPU:0, one launch (start us, length us, event | category | flops | bytes accessed | tf_op | source)
XLA Modules:
  0.0 626.7 jit_solution(981787737168917340)
XLA Ops:
  8.4 2.0 pad_maximum_fusion.1
  10.5 1.7 pad_maximum_fusion
  14.3 10.7 %all-reduce.2.ids_ref = s32[8]{0:T(128)S(1)} all-reduce(s32[8]{0:T(128)S(1)} %bitcast_dynamic-update-slice_fusion), channel_id=2, replica_groups=mesh['dp'=8,'tensor'=4] {'dp'}, use_global_device_ids=true, to_apply=%add.2 | all-reduce | flops 8 | bytes 64 | tf_op jit(solution)/shard_map/all_gather | solution.py:1748
  30.4 3.0 concatenate.37
  35.3 40.1 %tensor_gather.1 = bf16[1024,2304]{1,0:T(8,128)(2,1)S(1)} custom-call(bf16[256,2304]{1,0:T(8,128)(2,1)S(1)} %fusion.8.x_ref), custom_call_target="tpu_custom_call" | custom-call | tf_op jit(solution)/shard_map/tensor_gather/pallas_call | solution.py:200
  75.4 33.6 %adapter_tables.1 = (bf16[32,72,128]{2,1,0:T(8,128)(2,1)S(1)}, bf16[8,288,128]{2,1,0:T(8,128)(2,1)S(1)}, bf16[8,64,128]{2,1,0:T(8,128)(2,1)S(1)}, bf16[8,32,128]{2,1,0:T(8,128)(2,1)S(1)}) custom-call(bf16[8,72,128]{2,1,0:T(8,128)(2,1)S(1)} %copy.106.d_ref, bf16[8,288,128]{2,1,0:T(8,128)(2,1)S(1)} %copy.105.f_ref, bf16[8,64,128]{2,1,0:T(8,128)(2,1)S(1)} %copy.107.h_ref, ...), custom_call_target="tpu_custom_call" | custom-call | tf_op jit(solution)/shard_map/adapter_tables/pallas_call | solution.py:1243
  109.1 1.4 convolution_convert_fusion.1
  111.3 1.9 fusion.20
  114.6 8.4 %fusion.1 = f32[1024,1024]{0,1:T(8,128)S(1)} fusion(bf16[1024,2304]{1,0:T(8,128)(2,1)} %copy-done.1, bf16[2304,1536]{1,0:T(8,128)(2,1)} %all-gather.4.cloned.1.call-done.weight_hbm), kind=kOutput, calls=%fused_computation.4 | convolution fusion | flops 4831838208 | bytes 13631488 | tf_op jit(solution)/shard_map/dot_general | solution.py:70
  123.0 2.0 copy-done.15
  126.0 2.6 copy.97
  128.7 2.0 slice_add_fusion
  130.7 1.5 fusion.73
  132.1 2.5 copy.99
  134.7 2.6 copy.98
  137.3 1.8 multiply_subtract_fusion
  140.8 1.6 fusion.12
  142.4 2.5 fusion.26
  146.8 2.0 copy.91.k_ref
  148.8 5.3 fusion
  154.6 3.5 fusion.11
  160.1 6.1 convolution_convert_fusion.p_ref
  166.2 45.7 %tensor_scatter.1 = (f32[256,2304]{1,0:T(8,128)S(1)}, f32[256,128]{1,0:T(8,128)S(1)}) custom-call(bf16[1024,2304]{1,0:T(8,128)(2,1)} %convolution_convert_fusion.p_ref, bf16[1024,128]{1,0:T(8,128)(2,1)S(1)} %pad.8.q_ref), custom_call_target="tpu_custom_call" | custom-call | tf_op jit(solution)/shard_map/tensor_scatter/pallas_call | solution.py:310
  214.0 1.4 copy-done.7
  215.7 41.9 %chunk_gather.1.x_hbm = bf16[4,256,2304]{2,1,0:T(8,128)(2,1)S(1)} custom-call(bf16[256,2304]{1,0:T(8,128)(2,1)S(1)} %multiply_convert_fusion.2.x_ref.normed_ref), custom_call_target="tpu_custom_call" | custom-call | tf_op jit(solution)/shard_map/chunk_gather/pallas_call | solution.py:1035
  257.6 2.1 copy-done
  260.5 25.0 %all-gather.6.cloned.1.call-done.gu_hbm = bf16[2304,4608]{1,0:T(8,128)(2,1)} async-done(((bf16[288,4608]{1,0:T(8,128)(2,1)}), bf16[2304,4608]{1,0:T(8,128)(2,1)}) %all-gather.6.cloned.1.call-update) | async-done | bytes 21233680 | tf_op jit(solution)/shard_map/all_gather | solution.py:1745
  285.5 121.2 %mlp.1 = (bf16[256,2304]{1,0:T(8,128)(2,1)}, bf16[256,2304]{1,0:T(8,128)(2,1)}, bf16[4,256,128]{2,1,0:T(8,128)(2,1)}, bf16[256,128]{1,0:T(8,128)(2,1)}, bf16[4,2...) custom-call(s32[1]{0:T(128)} %copy.117.length_ref, ...), custom_call_target="tpu_custom_call" | custom-call | tf_op jit(solution)/shard_map/mlp/pallas_call | solution.py:975
  406.7 89.1 %mlp_back.1 = (f32[256,2304]{1,0:T(8,128)}, f32[256,128]{1,0:T(8,128)}, bf16[4,2,48,288]{3,2,1,0:T(8,128)(2,1)}) custom-call(bf16[256,2304]{1,0:T(8,128)(2,1)} %get-tuple-element.45.g_ref.grad_mlp_ref, bf16[2304,2304]{1,0:T(8,128)(2,1)} %bitcast.80, bf16[2304,4608]{1,0:T(8,128)(2,1)} %all-gather.6.cloned.1.call-done.gu_hbm, ...), custom_call_target="tpu_custom_call" | custom-call | tf_op jit(solution)/shard_map/mlp_back/pallas_call | solution.py:615
  495.8 114.1 %attn_back.1 = (bf16[256,2304]{1,0:T(8,128)(2,1)}, f32[8,72,80]{2,1,0:T(8,128)}, f32[8,64,16]{2,1,0:T(8,128)}, f32[8,288,16]{2,1,0:T(8,128)}, f32[8,16,64]{2,1,0...) custom-call(s32[8]{0:T(128)} %copy-done.39, s32[1]{0:T(128)} %copy.117.length_ref, ...), custom_call_target="tpu_custom_call" | custom-call | tf_op jit(solution)/shard_map/attn_back/pallas_call | solution.py:1657
  609.9 1.9 copy.92
  611.7 2.4 copy.93
  (150 shorter events, 26.4 us)
Async XLA Ops:
  7.2 107.4 %all-gather.4.cloned.1.call-start = ((), (), s32[]{:S(2)}) async-start(), calls=%async_computation | async-start | bytes 7962624 | tf_op jit(solution)/shard_map/all_gather | solution.py:1739
  10.5 275.0 %all-gather.6.cloned.1.call-start = ((), (), s32[]{:S(2)}) async-start(), calls=%async_computation.1 | async-start | bytes 23887872 | tf_op jit(solution)/shard_map/all_gather | solution.py:1745
  12.2 13.7 %copy-start.32 = (bf16[8,2,16,32]{3,2,1,0:T(8,128)(2,1)S(1)}, bf16[8,2,16,32]{3,2,1,0:T(8,128)(2,1)}, u32[]{:S(2)}) copy-start(bf16[8,2,16,32]{3,2,1,0:T(8,128)(2,1)} %param.35) | copy-start | bytes 49156
  12.2 14.6 %copy-start.36 = (bf16[8,64,16]{1,2,0:T(8,128)(2,1)S(1)}, bf16[8,64,16]{1,2,0:T(8,128)(2,1)}, u32[]{:S(2)}) copy-start(bf16[8,64,16]{1,2,0:T(8,128)(2,1)} %param.32) | copy-start | bytes 49156
  12.2 14.7 %copy-start.37 = (bf16[8,16,64]{2,1,0:T(8,128)(2,1)S(1)}, bf16[8,16,64]{2,1,0:T(8,128)(2,1)}, u32[]{:S(2)}) copy-start(bf16[8,16,64]{2,1,0:T(8,128)(2,1)} %param.34) | copy-start | bytes 49156
  12.2 15.2 %copy-start.28 = (bf16[8,72,80]{2,1,0:T(8,128)(2,1)S(1)}, bf16[8,72,80]{2,1,0:T(8,128)(2,1)}, u32[]{:S(2)}) copy-start(bf16[8,72,80]{2,1,0:T(8,128)(2,1)} %param.31) | copy-start | bytes 276484
  12.2 15.2 %copy-start.33 = (bf16[8,2,16,72]{3,2,1,0:T(8,128)(2,1)S(1)}, bf16[8,2,16,72]{3,2,1,0:T(8,128)(2,1)}, u32[]{:S(2)}) copy-start(bf16[8,2,16,72]{3,2,1,0:T(8,128)(2,1)} %param.37) | copy-start | bytes 110596
  12.2 15.6 %copy-start.31 = (bf16[8,288,16]{1,2,0:T(8,128)(2,1)S(1)}, bf16[8,288,16]{1,2,0:T(8,128)(2,1)}, u32[]{:S(2)}) copy-start(bf16[8,288,16]{1,2,0:T(8,128)(2,1)} %param.33) | copy-start | bytes 221188
  12.2 16.0 %copy-start.27 = (bf16[8,2,16,288]{3,2,1,0:T(8,128)(2,1)S(1)}, bf16[8,2,16,288]{3,2,1,0:T(8,128)(2,1)}, u32[]{:S(2)}) copy-start(bf16[8,2,16,288]{3,2,1,0:T(8,128)(2,1)} %param.36) | copy-start | bytes 442372
  25.1 8.4 %copy-start.39 = (s32[8]{0:T(128)}, s32[8]{0:T(128)S(1)}, u32[]{:S(2)}) copy-start(s32[8]{0:T(128)S(1)} %all-reduce.2.ids_ref) | copy-start | bytes 100
  25.8 3.7 copy-start.40
  30.4 3.5 copy-start.26
  30.4 4.1 copy-start.9
  75.4 35.1 %copy-start.1 = (bf16[1024,2304]{1,0:T(8,128)(2,1)}, bf16[1024,2304]{1,0:T(8,128)(2,1)S(1)}, u32[]{:S(2)}) copy-start(bf16[1024,2304]{1,0:T(8,128)(2,1)S(1)} %tensor_gather.1) | copy-start | bytes 14155780
  109.1 45.1 %copy-start.6 = (bf16[8,32,128]{2,1,0:T(8,128)(2,1)}, bf16[8,32,128]{2,1,0:T(8,128)(2,1)S(1)}, u32[]{:S(2)}) copy-start(bf16[8,32,128]{2,1,0:T(8,128)(2,1)S(1)} %get-tuple-element.37) | copy-start | bytes 196612
  109.1 50.4 %copy-start.5 = (bf16[8,64,128]{2,1,0:T(8,128)(2,1)}, bf16[8,64,128]{2,1,0:T(8,128)(2,1)S(1)}, u32[]{:S(2)}) copy-start(bf16[8,64,128]{2,1,0:T(8,128)(2,1)S(1)} %get-tuple-element.38) | copy-start | bytes 393220
  109.1 102.8 %copy-start.3 = (bf16[32,72,128]{2,1,0:T(8,128)(2,1)}, bf16[32,72,128]{2,1,0:T(8,128)(2,1)S(1)}, u32[]{:S(2)}) copy-start(bf16[32,72,128]{2,1,0:T(8,128)(2,1)S(1)} %get-tuple-element.36) | copy-start | bytes 1769476
  113.3 24.1 %copy-start.10 = (f32[1024,128]{1,0:T(8,128)}, f32[1024,128]{1,0:T(8,128)S(1)}, u32[]{:S(2)}) copy-start(f32[1024,128]{1,0:T(8,128)S(1)} %get-tuple-element.105.cos_ref) | copy-start | bytes 1572868
  113.3 24.1 %copy-start.11 = (f32[1024,128]{1,0:T(8,128)}, f32[1024,128]{1,0:T(8,128)S(1)}, u32[]{:S(2)}) copy-start(f32[1024,128]{1,0:T(8,128)S(1)} %get-tuple-element.106.sin_ref) | copy-start | bytes 1572868
  142.4 6.4 %copy-start.13 = (f32[1024,2,128]{2,0,1:T(8,128)S(1)}, f32[1024,2,128]{2,0,1:T(8,128)}, u32[]{:S(2)}) copy-start(f32[1024,2,128]{2,0,1:T(8,128)} %copy-done.12) | copy-start | bytes 3145732
  148.8 5.4 copy-start.16
  148.8 5.8 copy-start.22
  154.2 3.9 copy-start.38
  154.6 3.6 copy-start.17
  215.7 41.9 %copy-start.2 = (bf16[256,2304]{1,0:T(8,128)(2,1)}, bf16[256,2304]{1,0:T(8,128)(2,1)S(1)}, u32[]{:S(2)}) copy-start(bf16[256,2304]{1,0:T(8,128)(2,1)S(1)} %multiply_convert_fusion.2.x_ref.normed_ref) | copy-start | bytes 3538948
  215.7 44.0 %copy-start.41 = (bf16[128]{0:T(256)(128)(2,1)S(1)}, bf16[128]{0:T(256)(128)(2,1)}, u32[]{:S(2)}) copy-start(bf16[128]{0:T(256)(128)(2,1)} %copy-done.40) | copy-start | bytes 772
  215.7 44.0 %copy-start.42 = (bf16[128]{0:T(256)(128)(2,1)S(1)}, bf16[128]{0:T(256)(128)(2,1)}, u32[]{:S(2)}) copy-start(bf16[128]{0:T(256)(128)(2,1)} %get-tuple-element.103) | copy-start | bytes 772
  609.9 4.3 copy-start.20
  609.9 5.3 copy-start.21
  614.1 3.4 copy-start.30
  614.1 4.1 copy-start.24
  615.2 3.8 copy-start.29
  (14 other events, 25.4 us)
Sparse Core Ops, SparseCore 0:
  10.6 84.0 all-gather.3
  96.3 189.1 all-gather.5

commit v6 on v5

--- a/solution.py
+++ b/solution.py
@@ -131,48 +131,58 @@
     )
 
 
+class PlainGather:
+    def __init__(self, me, x_ref, o_ref, local_sem, send_sem, recv_sem):
+        rows = x_ref.shape[0]
+        half = rows // 2
+        links = square_peers(me)[:2]
+        self.own = pltpu.make_async_copy(x_ref, o_ref.at[pl.ds(me * rows, rows)], local_sem)
+        self.first, self.second, self.onward = [], [], []
+        for order, group in enumerate((self.first, self.second)):
+            for link in range(2):
+                part = link if order == 0 else 1 - link
+                group.append(
+                    remote(
+                        x_ref.at[pl.ds(part * half, half)],
+                        o_ref.at[pl.ds(me * rows + part * half, half)],
+                        send_sem.at[link, part],
+                        recv_sem.at[link, part],
+                        links[link],
+                    )
+                )
+        for link in range(2):
+            block = o_ref.at[pl.ds(links[link] * rows + link * half, half)]
+            self.onward.append(
+                remote(block, block, send_sem.at[2, link], recv_sem.at[2, link], links[1 - link])
+            )
+
+    def start(self):
+        self.own.start()
+        for copy in self.first + self.second:
+            copy.start()
+
+    def forward(self):
+        for copy, onward in zip(self.first, self.onward):
+            copy.wait_recv()
+            onward.start()
+
+    def finish(self):
+        for copy in self.second + self.onward:
+            copy.wait_recv()
+        self.own.wait()
+        for copy in self.first + self.second + self.onward:
+            copy.wait_send()
+
+
 def gather_kernel(count, rows, x_ref, o_ref, local_sem, send_sem, recv_sem):
     me = lax.axis_index("tensor")
     if count == 4:
         across, down, _ = square_peers(me)
         greet([{"tensor": across}, {"tensor": down}])
-        own = pltpu.make_async_copy(x_ref, o_ref.at[pl.ds(me * rows, rows)], local_sem)
-        own.start()
-        half = rows // 2
-        links = (across, down)
-        first = [[None, None], [None, None]]
-        for order in range(2):
-            for link in range(2):
-                part = order if link == 0 else 1 - order
-                target = o_ref.at[pl.ds(me * rows + part * half, half)]
-                copy = remote(
-                    x_ref.at[pl.ds(part * half, half)],
-                    target,
-                    send_sem.at[link, part],
-                    recv_sem.at[link, part],
-                    links[link],
-                )
-                copy.start()
-                first[link][part] = copy
-        second = []
-        for link in range(2):
-            first[link][link].wait_recv()
-            block = o_ref.at[pl.ds(links[link] * rows + link * half, half)]
-            copy = remote(
-                block, block, send_sem.at[2, link], recv_sem.at[2, link], links[1 - link]
-            )
-            copy.start()
-            second.append(copy)
-        for link in range(2):
-            first[link][1 - link].wait_recv()
-        for copy in second:
-            copy.wait_recv()
-        own.wait()
-        for link in range(2):
-            for part in range(2):
-                first[link][part].wait_send()
-        for copy in second:
-            copy.wait_send()
+        gather = PlainGather(me, x_ref, o_ref, local_sem, send_sem, recv_sem)
+        gather.start()
+        gather.forward()
+        gather.finish()
     else:
         peers = [lax.rem(me + step, count) for step in range(1, count)]
         greet([{"tensor": peer} for peer in peers])
@@ -346,6 +356,26 @@
         return copies
 
 
+def along(source_at, target, send_sem, recv_sem):
+    dp = lax.axis_size("dp")
+    d = lax.axis_index("dp")
+    pltpu.make_async_copy(source_at(d), target.at[d], recv_sem).start()
+    copies = []
+    for step in range(1, dp):
+        peer = lax.rem(d + step, dp)
+        copy = pltpu.make_async_remote_copy(
+            src_ref=source_at(peer),
+            dst_ref=target.at[d],
+            send_sem=send_sem.at[step],
+            recv_sem=recv_sem,
+            device_id={"dp": peer},
+            device_id_type=MESH,
+        )
+        copy.start()
+        copies.append(copy)
+    return copies
+
+
 class ChunkGather:
     def __init__(self, sq, source, buf, send_sem, recv_sem):
         half = sq.half
@@ -647,6 +677,189 @@
         ),
         name="mlp_back",
     )(grad, down_w, gu_w, slope, gelu, hidden, low, d_tab, f_tab)
+
+
+def front_kernel(
+    ids_ref,
+    layer_ref,
+    gains_ref,
+    f_all,
+    d_all,
+    hk_all,
+    seq_out,
+    ids_out,
+    d_out,
+    f_out,
+    h_out,
+    k_out,
+    normed,
+    ids_land,
+    f_pick,
+    d_pick,
+    hk_pick,
+    f_mid,
+    d_mid,
+    hk_mid,
+    d_join,
+    f_land,
+    d_land,
+    hk_land,
+    d_flip,
+    f_flip,
+    h_flip,
+    k_flip,
+    local_sem,
+    gather_send,
+    gather_recv,
+    line_send,
+    line_recv,
+    group_send,
+    group_recv,
+):
+    rows = layer_ref.shape[0]
+    sq = Square(rows)
+    dp = lax.axis_size("dp")
+    d = lax.axis_index("dp")
+    peers = [{"tensor": peer} for peer in (sq.across, sq.down, sq.far)]
+    peers += [{"dp": lax.rem(d + step, dp)} for step in range(1, dp)]
+    call(peers)
+
+    @pl.loop(0, rows // BLOCK)
+    def _(step):
+        here = pl.ds(pl.multiple_of(step * BLOCK, BLOCK), BLOCK)
+        normed[here, :] = rms_norm(layer_ref[here, :].astype(F32), gains_ref[0:1, :]).astype(BF16)
+
+    pl.semaphore_wait(pltpu.get_barrier_semaphore(), len(peers))
+    line = along(lambda k: ids_ref, ids_land, line_send.at[0], line_recv.at[0])
+    gather = PlainGather(sq.me, normed, seq_out, local_sem, gather_send, gather_recv)
+    gather.start()
+    pltpu.make_async_copy(ids_land, ids_land, line_recv.at[0]).wait()
+    ids_out[...] = ids_land[...]
+
+    @pl.loop(0, dp)
+    def _(k):
+        for source, target in ((f_all, f_pick), (d_all, d_pick), (hk_all, hk_pick)):
+            total = None
+            for adapter in range(NA):
+                hit = jnp.broadcast_to(ids_land[k, 0:1, 0:1], source.shape[1:]) == adapter
+                mine = jnp.where(hit, source[adapter].astype(F32), 0.0)
+                total = mine if total is None else total + mine
+            target[k] = total.astype(BF16)
+
+    lands = (f_mid, d_mid, hk_mid)
+    for item, (source, target) in enumerate(zip((f_pick, d_pick, hk_pick), lands)):
+        line += along(
+            lambda k, source=source: source.at[k],
+            target,
+            line_send.at[1 + item],
+            line_recv.at[1 + item],
+        )
+    gather.forward()
+    for flip in (d_flip, f_flip, h_flip, k_flip):
+        flip[...] = jnp.zeros_like(flip)
+    for item, target in enumerate(lands):
+        pltpu.make_async_copy(target, target, line_recv.at[1 + item]).wait()
+    size = d_mid.shape[2]
+    for k in range(dp):
+        d_join[:, k * size : (k + 1) * size] = d_mid[k]
+    per_user = dp // 4
+    spread = [
+        sq.spread(lambda peer: d_join, d_land, group_send.at[0], group_recv.at[0]),
+        sq.spread(
+            lambda peer: f_mid.at[pl.ds(peer * per_user, per_user)],
+            f_land,
+            group_send.at[1],
+            group_recv.at[1],
+        ),
+        sq.spread(
+            lambda peer: hk_mid.at[pl.ds(peer * per_user, per_user)],
+            hk_land,
+            group_send.at[2],
+            group_recv.at[2],
+        ),
+    ]
+    for copies in spread:
+        for copy in copies:
+            copy.start()
+    for copies in spread:
+        copies[0].wait()
+        for copy in copies[1:]:
+            copy.wait_recv()
+    f_size, h_size, k_size = f_mid.shape[2], h_out.shape[0] // dp, k_out.shape[0] // dp
+    for t in range(4):
+        for k in range(dp):
+            at = (k * 4 + t) * size
+            d_flip[: DOWN.stop, at : at + size] = d_land[
+                t, :, k * size : (k + 1) * size
+            ].astype(F32)
+        for core in range(per_user):
+            at = (core * 4 + t) * f_size
+            piece = f_land[t, core].astype(F32)
+            f_flip[GATE.start : UP.stop, at : at + f_size] = piece[: 2 * RANK]
+            f_flip[DOWN, at : at + f_size] = piece[2 * RANK :]
+            piece = hk_land[t, core].astype(F32)
+            at = (core * 4 + t) * h_size
+            h_flip[OUT, at : at + h_size] = piece[:RANK, :h_size]
+            h_flip[QUERY, at : at + h_size] = piece[RANK : 2 * RANK, :h_size]
+            at = (core * 4 + t) * k_size
+            k_flip[KEY.start : VALUE.stop, at : at + k_size] = piece[2 * RANK :, :k_size]
+    for flip, out in ((d_flip, d_out), (f_flip, f_out), (h_flip, h_out), (k_flip, k_out)):
+
+        @pl.loop(0, out.shape[0] // LANES)
+        def _(step, flip=flip, out=out):
+            here = columns(step, LANES)
+            out[here, :] = flip[:, here].T.astype(BF16)
+
+    gather.finish()
+    for copies in spread:
+        for copy in copies[1:]:
+            copy.wait_send()
+    for copy in line:
+        copy.wait_send()
+
+
+def front(ids, layer_in, gains, f_all, d_all, hk_all, dp, widths):
+    rows, model = layer_in.shape
+    anywhere = pl.BlockSpec(memory_space=pl.ANY)
+    vmem = pl.BlockSpec(memory_space=pltpu.VMEM)
+    tables_in = (f_all, d_all, hk_all)
+    shapes = [(dp,) + table.shape[1:] for table in tables_in]
+    joined = (shapes[1][1], dp * shapes[1][2])
+    return pl.pallas_call(
+        front_kernel,
+        out_shape=(
+            jax.ShapeDtypeStruct((4 * rows, model), BF16),
+            jax.ShapeDtypeStruct((dp,) + ids.shape, jnp.int32),
+        )
+        + tuple(jax.ShapeDtypeStruct((width, LANES), BF16) for width in widths),
+        in_specs=[vmem] * 6,
+        out_specs=(anywhere,) + (vmem,) * 5,
+        scratch_shapes=[
+            pltpu.VMEM((rows, model), BF16),
+            pltpu.VMEM((dp,) + ids.shape, jnp.int32),
+        ]
+        + [pltpu.VMEM(shape, BF16) for shape in shapes] * 2
+        + [
+            pltpu.VMEM(joined, BF16),
+            pltpu.VMEM((4, dp // 4) + shapes[0][1:], BF16),
+            pltpu.VMEM((4,) + joined, BF16),
+            pltpu.VMEM((4, dp // 4) + shapes[2][1:], BF16),
+        ]
+        + [pltpu.VMEM((LANES, width), F32) for width in widths]
+        + [
+            pltpu.SemaphoreType.DMA,
+            pltpu.SemaphoreType.DMA((3, 2)),
+            pltpu.SemaphoreType.DMA((3, 2)),
+            pltpu.SemaphoreType.DMA((4, dp)),
+            pltpu.SemaphoreType.DMA((4,)),
+            pltpu.SemaphoreType.DMA((3, 3)),
+            pltpu.SemaphoreType.DMA((3, 4)),
+        ],
+        compiler_params=pltpu.CompilerParams(
+            collective_id=9, has_side_effects=True, vmem_limit_bytes=VMEM_LIMIT
+        ),
+        name="front",
+    )(ids, layer_in, gains, *tables_in)
 
 
 class Line:
@@ -1016,39 +1229,6 @@
     )(lengths, seq, gu_w, shard, d_tab, f_tab, resid, cotangent, gains)
 
 
-def chunk_gather_kernel(rows, x_ref, o_ref, own_sem, send_sem, recv_sem):
-    sq = Square(rows)
-    sq.greet()
-    gather = ChunkGather(sq, x_ref, o_ref, send_sem, recv_sem)
-    gather.start()
-    own = pltpu.make_async_copy(x_ref, o_ref.at[0], own_sem)
-    own.start()
-    for chunk in range(1, 4):
-        gather.wait_chunk(chunk)
-    own.wait()
-    gather.finish()
-
-
-def chunk_gather(values):
-    rows, width = values.shape
-    anywhere = pl.BlockSpec(memory_space=pl.ANY)
-    return pl.pallas_call(
-        functools.partial(chunk_gather_kernel, rows),
-        out_shape=jax.ShapeDtypeStruct((4, rows, width), values.dtype),
-        in_specs=[anywhere],
-        out_specs=anywhere,
-        scratch_shapes=[
-            pltpu.SemaphoreType.DMA,
-            pltpu.SemaphoreType.DMA((6,)),
-            pltpu.SemaphoreType.DMA((6,)),
-        ],
-        compiler_params=pltpu.CompilerParams(
-            collective_id=8, has_side_effects=True, vmem_limit_bytes=VMEM_LIMIT
-        ),
-        name="chunk_gather",
-    )(values)
-
-
 class Layout:
     def __init__(self):
         self.dp = lax.axis_size("dp")
@@ -1275,6 +1455,270 @@
     return jnp.concatenate([first * cosine + second * sine, second * cosine - first * sine], axis=1)
 
 
+def turned(values):
+    return values.astype(F32).T.astype(BF16)
+
+
+def rotate_rows(values, cosine, sine):
+    first, second = values[:, : HD // 2], values[:, HD // 2 :]
+    return jnp.concatenate([first * cosine - second * sine, second * cosine + first * sine], axis=1)
+
+
+def softmax_weights(keys, queries, start, half, length):
+    shape = (keys.shape[0], queries.shape[0])
+    key_at = lax.broadcasted_iota(jnp.int32, shape, 0)
+    query_at = lax.rem(lax.broadcasted_iota(jnp.int32, shape, 1), half) + start
+    allowed = (key_at <= query_at) & (key_at < length)
+    squash = jnp.tanh(nt(keys, queries) * (1.0 / SOFT_CAP))
+    return squash, jnp.where(allowed, jnp.exp(SOFT_CAP * squash), 0.0)
+
+
+def stack_heads(ref, here, heads):
+    return jnp.concatenate([ref[here, h * HD : (h + 1) * HD] for h in range(heads)], axis=0)
+
+
+def far_first(step):
+    return step + 3 * ((3 - step) // 3) - 3 * (step // 3)
+
+
+def attn_kernel(
+    rows,
+    length_ref,
+    seq_hbm,
+    weight_hbm,
+    d_table,
+    h_table,
+    k_table,
+    cos_ref,
+    sin_ref,
+    layer_ref,
+    gains_ref,
+    q_ref,
+    k_ref,
+    kt_ref,
+    v_ref,
+    attended_ref,
+    inverse_ref,
+    low_ref,
+    low_out_ref,
+    total_ref,
+    resid_ref,
+    normed_ref,
+    mlp_out,
+    w_out_all,
+    h_all,
+    seq,
+    weight,
+    vt,
+    low_sum,
+    load_sem,
+    own_sem,
+    gather_send,
+    gather_recv,
+    w_send,
+    w_recv,
+    *scratch,
+):
+    sq = Square(rows)
+    half = sq.half
+    model = total_ref.shape[-1]
+    q_width = q_ref.shape[1]
+    qkv_width = q_width + 2 * HD
+    heads = q_width // HD
+    wide = tile_of(model)
+    core = lax.rem(lax.axis_index("dp"), 2)
+    sibling = lax.axis_index("dp") + 1 - 2 * core
+    weight_load = pltpu.make_async_copy(weight_hbm, weight, load_sem.at[0])
+    seq_load = pltpu.make_async_copy(seq_hbm, seq, load_sem.at[1])
+    weight_load.start()
+    seq_load.start()
+    greet([{"tensor": peer} for peer in (sq.across, sq.down, sq.far)] + [{"dp": sibling}])
+
+    share = model // 2
+    mine = pl.ds(pl.multiple_of(core * share, 8), share)
+    own_h = pltpu.make_async_copy(h_table, h_all.at[sq.me], own_sem.at[1])
+    own_h.start()
+    taken, passed_on = [], []
+    for which, peer in enumerate((sq.across, sq.down, sq.far)):
+        taken.append(
+            (
+                remote(
+                    weight_hbm.at[mine, pl.ds(qkv_width, q_width)],
+                    w_out_all.at[sq.me, mine],
+                    w_send.at[0, which],
+                    w_recv.at[0, which],
+                    peer,
+                ),
+                remote(
+                    h_table, h_all.at[sq.me], w_send.at[1, which], w_recv.at[1, which], peer
+                ),
+            )
+        )
+        block = w_out_all.at[peer, mine]
+        passed_on.append(
+            pltpu.make_async_remote_copy(
+                src_ref=block,
+                dst_ref=block,
+                send_sem=w_send.at[2, which],
+                recv_sem=w_recv.at[2, which],
+                device_id={"dp": sibling},
+                device_id_type=MESH,
+            )
+        )
+    weight_load.wait()
+    seq_load.wait()
+
+    @pl.loop(0, 4)
+    def _(block):
+        here = pl.ds(pl.multiple_of(block * rows, rows), rows)
+        low = band(nn(seq[block], d_table[...]), QUERY, VALUE).astype(BF16)
+        low_ref[here, :] = low
+        cosine, sine = cos_ref[here, :], sin_ref[here, :]
+        for h in range(heads):
+            column = slice(h * HD, (h + 1) * HD)
+            query = nn(seq[block], weight[:, column]) + nt(
+                band(low.astype(F32), QUERY).astype(BF16), h_table[column, :]
+            )
+            q_ref[here, column] = (rotate_rows(query, cosine, sine) * HD ** (-0.5)).astype(BF16)
+        key = nn(seq[block], weight[:, q_width : q_width + HD]) + nt(
+            band(low.astype(F32), KEY).astype(BF16), k_table[...]
+        )
+        key = rotate_rows(key, cosine, sine)
+        k_ref[here, :] = key.astype(BF16)
+        kt_ref[:, here] = key.T.astype(BF16)
+        value = nn(seq[block], weight[:, q_width + HD : qkv_width]) + nt(
+            band(low.astype(F32), VALUE).astype(BF16), k_table[...]
+        )
+        v_ref[here, :] = value.astype(BF16)
+        vt[:, here] = value.T.astype(BF16)
+
+    for copies in taken:
+        for copy in copies:
+            copy.start()
+    part, part_low = scratch[0], scratch[5]
+    scatters = (ChunkScatter(sq, *scratch[:5]), ChunkScatter(sq, *scratch[5:10]))
+
+    @pl.loop(0, 4)
+    def _(step):
+        chunk = far_first(step)
+        for side in range(2):
+            start = chunk_start(sq, chunk, side)
+            here = pl.ds(start, half)
+            unused, weights = softmax_weights(
+                k_ref[...], stack_heads(q_ref, here, heads), start, half, length_ref[0]
+            )
+            inverse = 1.0 / jnp.sum(weights, axis=0, keepdims=True)
+            mixed = nn(vt[...], (weights * inverse).astype(BF16)).T.astype(BF16)
+            for h in range(heads):
+                inverse_ref[h : h + 1, here] = inverse[:, h * half : (h + 1) * half]
+                attended_ref[here, h * HD : (h + 1) * HD] = mixed[h * half : (h + 1) * half]
+
+        attended = jnp.concatenate(
+            [attended_ref[pl.ds(chunk_start(sq, chunk, side), half), :] for side in range(2)],
+            axis=0,
+        )
+        part_low[chunk] = band(nn(attended, h_table[...]), OUT).astype(BF16)
+
+        @pl.loop(0, model // wide)
+        def _(tile):
+            here = columns(tile, wide)
+            part[chunk, :, here] = nt(attended, weight[here, qkv_width:]).astype(BF16)
+
+        @pl.when(step == 0)
+        def _():
+            for scatter in scatters:
+                scatter.send_far()
+
+        @pl.when(step == 1)
+        def _():
+            for scatter in scatters:
+                scatter.send_own()
+
+    for link in range(2):
+        for scatter in scatters:
+            scatter.pass_on(link)
+    scatters[1].collect(low_sum)
+    low_out_ref[...] = low_sum[...].astype(BF16)
+    scatters[0].collect(total_ref)
+    add_lifted(total_ref, low_out_ref, d_table)
+
+    @pl.loop(0, rows // BLOCK)
+    def _(step):
+        here = pl.ds(pl.multiple_of(step * BLOCK, BLOCK), BLOCK)
+        resid = layer_ref[here, :].astype(F32) + rms_norm(total_ref[here, :], gains_ref[1:2, :])
+        resid_ref[here, :] = resid
+        normed_ref[here, :] = rms_norm(resid, gains_ref[2:3, :]).astype(BF16)
+
+    gather = ChunkGather(sq, normed_ref, mlp_out, gather_send, gather_recv)
+    gather.start()
+    own = pltpu.make_async_copy(normed_ref, mlp_out.at[0], own_sem.at[0])
+    own.start()
+    for chunk in range(1, 4):
+        gather.wait_chunk(chunk)
+    for copies, onward in zip(taken, passed_on):
+        for copy in copies:
+            copy.wait_recv()
+        onward.start()
+    for copies, onward in zip(taken, passed_on):
+        for copy in copies:
+            copy.wait_send()
+        onward.wait()
+    own.wait()
+    own_h.wait()
+    gather.finish()
+    for scatter in scatters:
+        scatter.finish()
+
+
+def attn_fused(lengths, seq, weight, d_tab, h_tab, k_tab, cosine, sine, layer_in, gains):
+    rows, model = layer_in.shape
+    q_width = weight.shape[1] - 2 * HD
+    q_width //= 2
+    qkv_width = q_width + 2 * HD
+    anywhere = pl.BlockSpec(memory_space=pl.ANY)
+    vmem = pl.BlockSpec(memory_space=pltpu.VMEM)
+    narrow = jax.ShapeDtypeStruct((LEN, HD), BF16)
+    return pl.pallas_call(
+        functools.partial(attn_kernel, rows),
+        out_shape=(
+            jax.ShapeDtypeStruct((LEN, q_width), BF16),
+            narrow,
+            jax.ShapeDtypeStruct((HD, LEN), BF16),
+            narrow,
+            jax.ShapeDtypeStruct((LEN, q_width), BF16),
+            jax.ShapeDtypeStruct((q_width // HD, LEN), F32),
+            jax.ShapeDtypeStruct((LEN, LANES), BF16),
+            jax.ShapeDtypeStruct((rows, LANES), BF16),
+            jax.ShapeDtypeStruct((rows, model), F32),
+            jax.ShapeDtypeStruct((rows, model), F32),
+            jax.ShapeDtypeStruct((rows, model), BF16),
+            jax.ShapeDtypeStruct((4, rows, model), BF16),
+            jax.ShapeDtypeStruct((4, model, q_width), BF16),
+            jax.ShapeDtypeStruct((4, q_width, LANES), BF16),
+        ),
+        in_specs=[pl.BlockSpec(memory_space=pltpu.SMEM)] + [anywhere] * 2 + [vmem] * 7,
+        out_specs=(vmem,) * 11 + (anywhere,) * 3,
+        scratch_shapes=[
+            pltpu.VMEM((4, rows, model), BF16),
+            pltpu.VMEM(weight.shape, BF16),
+            pltpu.VMEM((HD, LEN), BF16),
+            pltpu.VMEM((rows, LANES), F32),
+            pltpu.SemaphoreType.DMA((2,)),
+            pltpu.SemaphoreType.DMA((2,)),
+            pltpu.SemaphoreType.DMA((6,)),
+            pltpu.SemaphoreType.DMA((6,)),
+            pltpu.SemaphoreType.DMA((3, 3)),
+            pltpu.SemaphoreType.DMA((3, 3)),
+        ]
+        + scatter_scratch(rows, model)
+        + scatter_scratch(rows, LANES),
+        compiler_params=pltpu.CompilerParams(
+            collective_id=8, has_side_effects=True, vmem_limit_bytes=62 * 1024 * 1024
+        ),
+        name="attn",
+    )(lengths, seq, weight, d_tab, h_tab, k_tab, cosine, sine, layer_in, gains)
+
+
 def attn_back_kernel(
     rows,
     ids_ref,
@@ -1287,6 +1731,7 @@
     layer_ref,
     gains_ref,
     weight_hbm,
+    w_out_hbm,
     seq_hbm,
     q_ref,
     k_ref,
@@ -1298,7 +1743,7 @@
     sin_ref,
     low_ref,
     d_table,
-    h_table,
+    h_all,
     k_table,
     normed_ref,
     low_out_ref,
@@ -1314,11 +1759,15 @@
     gateup_out,
     resid_out,
     weight,
+    w_out,
     work,
     g_ref,
     low_sum,
     buf,
+    att_send,
     att,
+    low_own,
+    low_all,
     q_grad,
     k_sum,
     v_sum,
@@ -1336,9 +1785,8 @@
     hk_land,
     hk_recv,
     load_sem,
-    own_sem,
-    gather_send,
-    gather_recv,
+    att_sends,
+    att_recvs,
     f_sem,
     d_sem,
     hk_sem,
@@ -1353,15 +1801,26 @@
     model = o_ref.shape[-1]
     half = sq.half
     wide = tile_of(model)
-    weight_load = pltpu.make_async_copy(weight_hbm, weight, load_sem.at[0])
+    q_width = q_ref.shape[1]
+    qkv_width = q_width + 2 * HD
+    others = (sq.far, sq.across, sq.down)
+    sources = [w_out_hbm.at[peer] for peer in others]
+    sources.append(weight_hbm.at[:, pl.ds(qkv_width, q_width)])
+    loads = [
+        pltpu.make_async_copy(source, w_out.at[which % 2], load_sem.at[2 + which])
+        for which, source in enumerate(sources)
+    ]
+    weight_load = pltpu.make_async_copy(
+        weight_hbm.at[:, pl.ds(0, qkv_width)], weight, load_sem.at[0]
+    )
     seq_load = pltpu.make_async_copy(seq_hbm, buf, load_sem.at[1])
+    loads[0].start()
+    loads[1].start()
     weight_load.start()
+    seq_load.start()
     peers = [{"tensor": peer} for peer in (sq.across, sq.down, sq.far)]
     peers += [{"dp": lax.rem(d + step, dp)} for step in range(1, dp)]
     call(peers)
-
-    def turned(values):
-        return values.astype(F32).T.astype(BF16)
 
     low_gu = low_gu_ref[...].astype(BF16)
 
@@ -1381,30 +1840,40 @@
         work[here, :] = mid
         g_ref[here, :] = norm_back(total_ref[here, :], gains_ref[1:2, :], mid).astype(BF16)
 
-    own_load = pltpu.make_async_copy(g_ref, buf.at[0], own_sem)
-    own_load.start()
+    low_own[...] = band(nn(g_ref[...], d_table[...]), OUT).astype(BF16)
     pl.semaphore_wait(pltpu.get_barrier_semaphore(), len(peers))
-    gather = ChunkGather(sq, g_ref, buf, gather_send, gather_recv)
-    gather.start()
+    heads_out_copies = []
+    for which, peer in enumerate(others + (sq.me,)):
+        loads[which].wait()
+        grads = (nn(g_ref[...], w_out[which % 2]) + nt(low_own[...], h_all[peer])).astype(BF16)
+        if which < 2:
+            loads[which + 2].start()
+        if which == 3:
+            att[sq.me] = grads
+            low_all[sq.me] = low_own[...]
+            continue
+        att_send[which] = grads
+        copies = (
+            remote(
+                att_send.at[which],
+                att.at[sq.me],
+                att_sends.at[which, 0],
+                att_recvs.at[which, 0],
+                peer,
+            ),
+            remote(
+                low_own,
+                low_all.at[sq.me],
+                att_sends.at[which, 1],
+                att_recvs.at[which, 1],
+                peer,
+            ),
+        )
+        for copy in copies:
+            copy.start()
+        heads_out_copies.append(copies)
     line = []
-
-    def along(source_at, target, send_sem, recv_sem):
-        own = pltpu.make_async_copy(source_at(d), target.at[d], recv_sem)
-        own.start()
-        for step in range(1, dp):
-            peer = lax.rem(d + step, dp)
-            copy = pltpu.make_async_remote_copy(
-                src_ref=source_at(peer),
-                dst_ref=target.at[d],
-                send_sem=send_sem.at[step],
-                recv_sem=recv_sem,
-                device_id={"dp": peer},
-                device_id_type=MESH,
-            )
-            copy.start()
-            line.append(copy)
-
-    along(lambda k: f_ref.at[k // 2, lax.rem(k, 2)], f_recv, f_sem, line_recv.at[0])
+    line += along(lambda k: f_ref.at[k // 2, lax.rem(k, 2)], f_recv, f_sem, line_recv.at[0])
     part, part_low = scratch[0], scratch[5]
     scatters = (ChunkScatter(sq, *scratch[:5]), ChunkScatter(sq, *scratch[5:10]))
 
@@ -1425,46 +1894,41 @@
     k_turned[...] = jnp.zeros_like(k_turned)
     k_sum[...] = jnp.zeros_like(k_sum)
     v_sum[...] = jnp.zeros_like(v_sum)
-    own_load.wait()
-    weight_load.wait()
-    q_width = q_ref.shape[1]
-    qkv_width = q_width + 2 * HD
     heads = q_width // HD
     stacked = heads * half
 
     @pl.loop(0, 4)
-    def _(chunk):
-        for step in range(4):
-
-            @pl.when(chunk == step)
-            def _(step=step):
-                gather.wait_chunk(step)
-
-        incoming = buf.at[chunk]
-        low_out = band(nn(incoming[...], d_table[...]), OUT).astype(BF16)
-        att[...] = (
-            nn(incoming[...], weight[:, qkv_width:]) + nt(low_out, h_table[...])
-        ).astype(BF16)
-        low_turned = turned(low_out)[OUT]
+    def _(turn):
+        for step, which in ((1, 1), (2, 2), (3, 0)):
+
+            @pl.when(turn == step)
+            def _(which=which):
+                for copy in heads_out_copies[which]:
+                    copy.wait_recv()
+
+        is_own, is_far = (3 - turn) // 3, turn // 3
+        is_down = turn // 2 - is_far
+        block = (
+            sq.me * is_own
+            + sq.far * is_far
+            + sq.down * is_down
+            + sq.across * (1 - is_own - is_far - is_down)
+        )
+        low_turned = turned(low_all[block])[OUT]
         for side in range(2):
-            start = chunk_start(sq, chunk, side)
+            start = pl.multiple_of(block * rows + side * half, half)
             here = pl.ds(start, half)
             place = pl.ds(side * half, half)
             h_turned[:RANK, :] += nn(
                 low_turned[:, side * half : (side + 1) * half], attended_ref[here, :]
             )
-            queries = jnp.concatenate(
-                [q_ref[here, h * HD : (h + 1) * HD] for h in range(heads)], axis=0
-            )
+            queries = stack_heads(q_ref, here, heads)
             grads = jnp.concatenate(
-                [att[place, h * HD : (h + 1) * HD] for h in range(heads)], axis=0
+                [att[block, place, h * HD : (h + 1) * HD] for h in range(heads)], axis=0
             )
             inverse = jnp.concatenate([inverse_ref[h : h + 1, here] for h in range(heads)], axis=1)
-            key_at = lax.broadcasted_iota(jnp.int32, (LEN, stacked), 0)
-            query_at = lax.rem(lax.broadcasted_iota(jnp.int32, (LEN, stacked), 1), half) + start
-            allowed = (key_at <= query_at) & (key_at < length_ref[0])
-            squash = jnp.tanh(nt(k_ref[...], queries) * (1.0 / SOFT_CAP))
-            probs = jnp.where(allowed, jnp.exp(SOFT_CAP * squash) * inverse, 0.0)
+            squash, weights = softmax_weights(k_ref[...], queries, start, half, length_ref[0])
+            probs = weights * inverse
             grad_probs = nt(v_ref[...], grads)
             mean = jnp.sum(probs * grad_probs, axis=0, keepdims=True)
             grad_raw = (probs * (grad_probs - mean) * (1.0 - squash * squash)).astype(BF16)
@@ -1472,24 +1936,24 @@
             v_sum[...] += nn(probs.astype(BF16), grads)
             q_back = nn(kt_ref[...], grad_raw).T * HD ** (-0.5)
             for h in range(heads):
-                q_grad[chunk, place, h * HD : (h + 1) * HD] = rotate_back(
+                q_grad[here, h * HD : (h + 1) * HD] = rotate_back(
                     q_back[h * half : (h + 1) * half], cos_ref[here, :], sin_ref[here, :]
                 ).astype(BF16)
 
-    gather.finish()
-    seq_load.start()
+    weight_load.wait()
     kv_grad[:, :HD] = rotate_back(k_sum[...], cos_ref[...], sin_ref[...]).astype(BF16)
     kv_grad[:, HD:] = v_sum[...].astype(BF16)
 
     @pl.loop(0, 4)
     def _(step):
-        chunk = step + 3 * ((3 - step) // 3) - 3 * (step // 3)
-        joined[chunk, :, :q_width] = q_grad[chunk]
+        chunk = far_first(step)
         for side in range(2):
             here = pl.ds(chunk_start(sq, chunk, side), half)
-            joined[chunk, pl.ds(side * half, half), q_width:] = kv_grad[here, :]
+            place = pl.ds(side * half, half)
+            joined[chunk, place, :q_width] = q_grad[here, :]
+            joined[chunk, place, q_width:] = kv_grad[here, :]
         part_low[chunk] = (
-            band(nn(joined[chunk, :, :q_width], h_table[...]), QUERY)
+            band(nn(joined[chunk, :, :q_width], h_all[sq.me]), QUERY)
             + band(nn(joined[chunk, :, q_width : q_width + HD], k_table[...]), KEY)
             + band(nn(joined[chunk, :, q_width + HD :], k_table[...]), VALUE)
         ).astype(BF16)
@@ -1497,7 +1961,7 @@
         @pl.loop(0, model // wide)
         def _(tile):
             here = columns(tile, wide)
-            part[chunk, :, here] = nt(joined[chunk], weight[here, :qkv_width]).astype(BF16)
+            part[chunk, :, here] = nt(joined[chunk], weight[here, :]).astype(BF16)
 
         @pl.when(step == 0)
         def _():
@@ -1577,8 +2041,8 @@
             copy.wait_recv()
     for k in range(dp):
         d_sum[k] = sum(d_land[k, t].astype(F32) for t in range(4)).astype(BF16)
-    along(lambda k: d_sum.at[k], d_recv, d_sem, line_recv.at[1])
-    along(lambda k: hk_land.at[k // 2, lax.rem(k, 2)], hk_recv, hk_sem, line_recv.at[2])
+    line += along(lambda k: d_sum.at[k], d_recv, d_sem, line_recv.at[1])
+    line += along(lambda k: hk_land.at[k // 2, lax.rem(k, 2)], hk_recv, hk_sem, line_recv.at[2])
     scatters[1].collect(low_sum)
     low_qkv = low_sum[...].astype(BF16)
     for link in range(2):
@@ -1620,9 +2084,9 @@
         in_out[adapter] = d_all[:, : 5 * RANK]
         d_flip = d_all.T
         f_all = pick(f_recv)
-        hidden_out[adapter] = f_all[:RANK].T
+        hidden_out[adapter] = f_all[:RANK]
         hk_all = pick(hk_recv)
-        heads_out[adapter] = hk_all[:RANK, :h_size].T
+        heads_out[adapter] = hk_all[:RANK, :h_size]
         query_out[adapter] = hk_all[RANK : 2 * RANK, :h_size]
         for which in range(2):
             first = (which + 2) * RANK
@@ -1635,6 +2099,9 @@
     for copies in spread:
         for copy in copies[1:]:
             copy.wait_send()
+    for copies in heads_out_copies:
+        for copy in copies:
+            copy.wait_send()
     for copy in line:
         copy.wait_send()
     for scatter in scatters:
@@ -1646,10 +2113,10 @@
     vmem = pl.BlockSpec(memory_space=pltpu.VMEM)
     smem = pl.BlockSpec(memory_space=pltpu.SMEM)
     rows, model = arrays[0].shape
-    weight, seq, q, f_in = arrays[7], arrays[8], arrays[9], arrays[-1]
+    weight, q, f_in = arrays[7], arrays[10], arrays[-1]
     q_width = q.shape[1]
     specs = [smem, smem] + [vmem] * len(arrays)
-    specs[9] = specs[10] = anywhere
+    specs[9] = specs[10] = specs[11] = anywhere
     outs = [jax.ShapeDtypeStruct((rows, model), BF16)]
     outs += [jax.ShapeDtypeStruct(shape, F32) for shape in grad_shapes]
     d_rows = model // total
@@ -1660,13 +2127,17 @@
         in_specs=specs,
         out_specs=(vmem,) * len(outs),
         scratch_shapes=[
-            pltpu.VMEM(weight.shape, BF16),
+            pltpu.VMEM((model, q_width + 2 * HD), BF16),
+            pltpu.VMEM((2, model, q_width), BF16),
             pltpu.VMEM((rows, model), F32),
             pltpu.VMEM((rows, model), BF16),
             pltpu.VMEM((rows, LANES), F32),
             pltpu.VMEM((4, rows, model), BF16),
-            pltpu.VMEM((rows, q_width), BF16),
+            pltpu.VMEM((3, rows, q_width), BF16),
             pltpu.VMEM((4, rows, q_width), BF16),
+            pltpu.VMEM((rows, LANES), BF16),
+            pltpu.VMEM((4, rows, LANES), BF16),
+            pltpu.VMEM((LEN, q_width), BF16),
             pltpu.VMEM((LEN, HD), F32),
             pltpu.VMEM((LEN, HD), F32),
             pltpu.VMEM((LEN, 2 * HD), BF16),
@@ -1682,10 +2153,9 @@
             pltpu.VMEM((dp // 4, 4, 4 * RANK, LANES), BF16),
             pltpu.VMEM((4, dp // 4, 4 * RANK, LANES), BF16),
             pltpu.VMEM((dp, 4 * RANK, LANES), BF16),
-            pltpu.SemaphoreType.DMA((2,)),
-            pltpu.SemaphoreType.DMA,
             pltpu.SemaphoreType.DMA((6,)),
-            pltpu.SemaphoreType.DMA((6,)),
+            pltpu.SemaphoreType.DMA((3, 2)),
+            pltpu.SemaphoreType.DMA((3, 2)),
             pltpu.SemaphoreType.DMA((dp,)),
             pltpu.SemaphoreType.DMA((dp,)),
             pltpu.SemaphoreType.DMA((dp,)),
@@ -1745,6 +2215,143 @@
     gate_up_w = lax.all_gather(gate_up_shard, "dp", axis=0, tiled=True)
     qkv_width = head_width + 2 * HD
 
+    cosine, sine = tables(LEN, HD)
+    if count == 4 and lay.dp == 8:
+        seq_attn, all_ids, d_tab, f_tab, h_tab, k_tab = front(
+            jnp.broadcast_to(adapter_ids, (8, LANES)),
+            layer_in,
+            norm_gains,
+            jnp.concatenate(
+                [
+                    lift_gateup.reshape(NA, 2 * RANK, -1),
+                    jnp.swapaxes(adapt_hidden, 1, 2),
+                ],
+                axis=1,
+            ),
+            jnp.concatenate(
+                [jnp.swapaxes(adapt_in, 1, 2), lift_resid.reshape(NA, 2 * RANK, -1)], axis=1
+            ),
+            jnp.concatenate(
+                [
+                    jnp.swapaxes(adapt_heads, 1, 2),
+                    lift_query,
+                    jnp.pad(
+                        lift_keyval.reshape(NA, 2 * RANK, -1),
+                        ((0, 0), (0, 0), (0, lift_query.shape[2] - lift_keyval.shape[3])),
+                    ),
+                ],
+                axis=1,
+            ),
+            lay.dp,
+            (D, hidden_here, head_width, HD),
+        )
+        (
+            queries,
+            keys,
+            keys_turned,
+            values,
+            attended,
+            inverse,
+            low_qkv,
+            low_out,
+            attn_total,
+            resid_mid,
+            normed_mlp,
+            seq_mlp,
+            w_out_all,
+            h_all,
+        ) = attn_fused(
+            lengths,
+            seq_attn.reshape(count, rows, D),
+            attn_w,
+            d_tab,
+            h_tab,
+            k_tab,
+            cosine.reshape(LEN, HD // 2),
+            sine.reshape(LEN, HD // 2),
+            layer_in,
+            norm_gains,
+        )
+        layer_out, grad_mlp, low_gu, low_down, hidden, slope, gelu, down_w = mlp_fused(
+            lengths,
+            seq_mlp,
+            gate_up_w,
+            down_shard,
+            d_tab,
+            f_tab,
+            resid_mid,
+            cotangent,
+            norm_gains,
+            lay.dp,
+        )
+        mlp_back, grad_low_gu, f_grad = mlp_back_fused(
+            grad_mlp,
+            down_w.reshape(D, hidden_here),
+            gate_up_w,
+            slope,
+            gelu,
+            hidden,
+            low_gu,
+            d_tab,
+            f_tab,
+            lay.dp,
+        )
+        grad_shapes = [
+            table.shape
+            for table in (
+                adapt_in,
+                adapt_heads,
+                adapt_hidden,
+                lift_query,
+                lift_keyval,
+                lift_gateup,
+                lift_resid,
+            )
+        ]
+        for which in (1, 2):
+            shape = grad_shapes[which]
+            grad_shapes[which] = (shape[0], shape[2], shape[1])
+        grads = list(
+            attn_back_fused(
+                (all_ids[:, 0, 0], lengths),
+                (
+                    mlp_back,
+                    grad_low_gu,
+                    resid_mid,
+                    attn_total,
+                    cotangent,
+                    layer_in,
+                    norm_gains,
+                    attn_w,
+                    w_out_all,
+                    seq_attn.reshape(count, rows, D),
+                    queries,
+                    keys,
+                    keys_turned,
+                    values,
+                    attended,
+                    inverse,
+                    cosine.reshape(LEN, HD // 2),
+                    sine.reshape(LEN, HD // 2),
+                    low_qkv,
+                    d_tab,
+                    h_all,
+                    k_tab,
+                    normed_mlp,
+                    low_out,
+                    grad_mlp,
+                    low_down,
+                    f_grad,
+                ),
+                tuple(grad_shapes),
+                lay.dp,
+                lay.total,
+            )
+        )
+        for which in (2, 3):
+            grads[which] = jnp.swapaxes(grads[which], 1, 2)
+        return (layer_out, *grads)
+
     all_ids = lax.all_gather(adapter_ids[:, 0], "dp", axis=0, tiled=True)
     group_hot = (all_ids[:, None] == jnp.arange(NA, dtype=jnp.int32)[None, :]).astype(BF16)
 
@@ -1791,7 +2398,6 @@
     row_start = lay.t * rows
     length = lengths[0]
     row_valid = ((row_start + jnp.arange(rows, dtype=jnp.int32)) < length).astype(F32)[:, None]
-    cosine, sine = tables(LEN, HD)
     place = jnp.arange(LEN, dtype=jnp.int32)
     allowed = (place[:, None] >= place[None, :]) & (place[None, :] < length)
 
@@ -1828,80 +2434,6 @@
     resid_mid = resid_in + rms_norm(attn_total, norm_gains[1])
 
     normed_mlp = rms_norm(resid_mid, norm_gains[2]).astype(BF16)
-    if count == 4 and lay.dp == 8:
-        layer_out, grad_mlp, low_gu, low_down, hidden, slope, gelu, down_w = mlp_fused(
-            lengths,
-            chunk_gather(normed_mlp),
-            gate_up_w,
-            down_shard,
-            d_tab,
-            f_tab,
-            resid_mid,
-            cotangent,
-            norm_gains,
-            lay.dp,
-        )
-        mlp_back, grad_low_gu, f_grad = mlp_back_fused(
-            grad_mlp,
-            down_w.reshape(D, hidden_here),
-            gate_up_w,
-            slope,
-            gelu,
-            hidden,
-            low_gu,
-            d_tab,
-            f_tab,
-            lay.dp,
-        )
-        return (
-            layer_out,
-            *attn_back_fused(
-                (all_ids, lengths),
-                (
-                    mlp_back,
-                    grad_low_gu,
-                    resid_mid,
-                    attn_total,
-                    cotangent,
-                    layer_in,
-                    norm_gains,
-                    attn_w,
-                    seq_attn.reshape(count, rows, D),
-                    queries.reshape(LEN, head_width),
-                    keys,
-                    keys.T,
-                    values,
-                    attended,
-                    inverse_total.reshape(heads_here, LEN),
-                    cosine.reshape(LEN, HD // 2),
-                    sine.reshape(LEN, HD // 2),
-                    pad_lanes(low_qkv),
-                    d_tab,
-                    h_tab,
-                    k_tab,
-                    normed_mlp,
-                    lanes((OUT, low_out)),
-                    grad_mlp,
-                    low_down,
-                    f_grad,
-                ),
-                tuple(
-                    table.shape
-                    for table in (
-                        adapt_in,
-                        adapt_heads,
-                        adapt_hidden,
-                        lift_query,
-                        lift_keyval,
-                        lift_gateup,
-                        lift_resid,
-                    )
-                ),
-                lay.dp,
-                lay.total,
-            ),
-        )
-
     seq_mlp = tensor_gather(normed_mlp, count)
     low_gu = nn(seq_mlp, in_gu).astype(BF16)
     low_g, low_u = low_gu[:, :RANK], low_gu[:, RANK:]

time: 631 us -> 606 us (0.960)
  Pallas kernels: 486 us -> 535 us
  matrix products: 30.8 us -> 0 us
  local copies, waits for them, and re-layouts: 42.9 us -> 12.4 us
  blocking collectives: 10.7 us -> 0 us
  waiting for transfers between devices: 25.1 us -> 35.1 us
  other arithmetic: 14.9 us -> 6.7 us
    pallas_call x4 -> x2, Pallas kernels: 161 us -> 230 us  [the longest x1 168 us: attn_fused(): pl.pallas_call(functools.partial(attn_kernel, rows), out_shape=(jax.Shape...]
    dot_general x14 -> x0, matrix products: 30.8 us -> none  [the longest x5 10.7 us: nt(): lax.dot_general(a, b, (((1,), (1,)), ((), ())), preferred_element_type=F32)]
    pallas_call x1, Pallas kernels: 114 us -> 94 us  [attn_back_fused(): pl.pallas_call(functools.partial(attn_back_kernel, rows), out_shape=tuple...]
    unnamed x107 -> x58, local copies, waits for them, and re-layouts: 26.7 us -> 10.5 us
    all_gather x1, waiting for transfers between devices: 0.01 us -> 15 us  [per_device(): attn_w = lax.all_gather(attn_shard, 'dp', axis=0, tiled=True)]
    all_gather x1 -> x0, blocking collectives: 10.7 us -> none  [per_device(): all_ids = lax.all_gather(adapter_ids[:, 0], 'dp', axis=0, tiled=True)]
  transfers between devices with their start and end apart: 2 -> 2, of which waited for: 1 -> 2; matrix products, arithmetic and copies ran while one was open for 11% -> 1% of each run, Pallas kernels for 26% -> 38%
where the time goes in v6:
time: 606 us; the launch traced here: 605 us
  Pallas kernels  535 us (88%)
  waiting for transfers between devices  35.1 us (6%)
  between operations  15.8 us (3%)
  local copies, waits for them, and re-layouts  12.4 us (2%)
  other arithmetic  6.7 us (1%)
    pallas_call x1, Pallas kernels, attn_fused(): pl.pallas_call(functools.partial(attn_kernel, rows), out_shape=(jax.Shape...  168 us
    pallas_call x1, Pallas kernels, mlp_fused(): pl.pallas_call(functools.partial(mlp_kernel, rows), out_shape=(jax.ShapeD...  121 us
    pallas_call x1, Pallas kernels, attn_back_fused(): pl.pallas_call(functools.partial(attn_back_kernel, rows), out_shape=tuple...  94 us
    pallas_call x1, Pallas kernels, mlp_back_fused(): pl.pallas_call(functools.partial(mlp_back_kernel, rows), out_shape=(jax.S...  89.6 us
    pallas_call x1, Pallas kernels, front(): pl.pallas_call(front_kernel, out_shape=(jax.ShapeDtypeStruct((4 * rows, m...  62.7 us
    all_gather x1, waiting for transfers between devices, per_device(): gate_up_w = lax.all_gather(gate_up_shard, 'dp', axis=0, tiled=True)  20.1 us
    all_gather x1, waiting for transfers between devices, per_device(): attn_w = lax.all_gather(attn_shard, 'dp', axis=0, tiled=True)  15 us
  transfers between devices with their start and end apart: 2, of which 2 were waited for; matrix products, arithmetic and copies ran while one was open for 1% of the time, Pallas kernels for 38%

profile of v6, /device:TPU:0, one launch (start us, length us, event | category | flops | bytes accessed | tf_op | source)
XLA Modules:
  0.0 605.2 jit_solution(6485647150794279421)
XLA Ops:
  7.2 0.0 all-gather.3.cloned.1.call-start
  7.3 1.2 constant_dynamic-slice_fusion
  8.4 2.0 pad_maximum_fusion.1
  10.4 0.0 all-gather.3.cloned.1.call-update
  10.5 0.0 all-gather.5.cloned.1.call-start
  10.5 1.7 pad_maximum_fusion
  12.3 0.0 copy-start.18
  12.3 0.0 all-gather.5.cloned.1.call-update
  13.8 0.1 copy.29
  14.2 62.7 %front.1 = (bf16[1024,2304]{1,0:T(8,128)(2,1)}, s32[8,8,128]{2,1,0:T(8,128)S(1)}, bf16[2304,128]{1,0:T(8,128)(2,1)S(1)}, bf16[2304,128]{1,0:T(8,128)(2,1)S(1)}, ...) custom-call(s32[8,128]{1,0:T(8,128)S(1)} %broadcast_in_dim.10.ids_ref, bf16[256,2304]{1,0:T(8,128)(2,1)S(1)} %copy-done, ...), custom_call_target="tpu_custom_call" | custom-call | tf_op jit(solution)/shard_map/front/pallas_call | solution.py:828
  76.9 0.8 copy-done.1
  77.7 0.8 copy-done.2
  78.5 0.6 copy-done.4
  79.1 0.7 copy-done.5
  79.8 0.8 slice_reduce_fusion.ids_ref
  80.5 2.8 fusion
  83.3 15.0 %all-gather.3.cloned.1.call-done.weight_hbm = bf16[2304,1536]{1,0:T(8,128)(2,1)} async-done(((bf16[288,1536]{1,0:T(8,128)(2,1)}), bf16[2304,1536]{1,0:T(8,128)(2,1)}) %all-gather.3.cloned.1.call-update) | async-done | bytes 7077904 | tf_op jit(solution)/shard_map/all_gather | solution.py:2209
  98.3 167.8 %attn.1 = (bf16[1024,512]{1,0:T(8,128)(2,1)}, bf16[1024,256]{1,0:T(8,128)(2,1)}, bf16[256,1024]{1,0:T(8,128)(2,1)}, bf16[1024,256]{1,0:T(8,128)(2,1)}, bf16[1024...) custom-call(s32[1]{0:T(128)S(6)} %copy.39.length_ref, ...), custom_call_target="tpu_custom_call" | custom-call | tf_op jit(solution)/shard_map/attn/pallas_call | solution.py:1681
  266.1 20.1 %all-gather.5.cloned.1.call-done.gu_hbm = bf16[2304,4608]{1,0:T(8,128)(2,1)} async-done(((bf16[288,4608]{1,0:T(8,128)(2,1)}), bf16[2304,4608]{1,0:T(8,128)(2,1)}) %all-gather.5.cloned.1.call-update) | async-done | bytes 21233680 | tf_op jit(solution)/shard_map/all_gather | solution.py:2215
  286.2 121.1 %mlp.1 = (bf16[256,2304]{1,0:T(8,128)(2,1)}, bf16[256,2304]{1,0:T(8,128)(2,1)}, bf16[4,256,128]{2,1,0:T(8,128)(2,1)}, bf16[256,128]{1,0:T(8,128)(2,1)}, bf16[4,2...) custom-call(s32[1]{0:T(128)S(6)} %copy.39.length_ref, ...), custom_call_target="tpu_custom_call" | custom-call | tf_op jit(solution)/shard_map/mlp/pallas_call | solution.py:1188
  407.3 89.6 %mlp_back.1 = (f32[256,2304]{1,0:T(8,128)}, f32[256,128]{1,0:T(8,128)}, bf16[4,2,48,288]{3,2,1,0:T(8,128)(2,1)}) custom-call(bf16[256,2304]{1,0:T(8,128)(2,1)} %get-tuple-element.61.g_ref.grad_mlp_ref, bf16[2304,2304]{1,0:T(8,128)(2,1)} %bitcast.16, bf16[2304,4608]{1,0:T(8,128)(2,1)} %all-gather.5.cloned.1.call-done.gu_hbm, ...), custom_call_target="tpu_custom_call" | custom-call | tf_op jit(solution)/shard_map/mlp_back/pallas_call | solution.py:645
  496.9 94.0 %attn_back.1 = (bf16[256,2304]{1,0:T(8,128)(2,1)}, f32[8,72,80]{2,1,0:T(8,128)}, f32[8,16,64]{2,1,0:T(8,128)}, f32[8,16,288]{2,1,0:T(8,128)}, f32[8,16,64]{2,1,0...) custom-call(s32[8]{0:T(128)} %slice_reduce_fusion.ids_ref, ...), custom_call_target="tpu_custom_call" | custom-call | tf_op jit(solution)/shard_map/attn_back/pallas_call | solution.py:2124
  590.9 1.0 copy.41
  591.9 0.7 copy-done.9
  592.6 1.0 copy.42
  593.6 0.7 copy.43
  594.3 0.6 copy.44
  594.9 0.7 copy.45
  595.6 0.6 copy.46
  596.3 0.7 copy.47
  596.9 0.7 copy.48
  597.7 0.7 copy.49
  (47 shorter events, 0.2 us)
Async XLA Ops:
  7.2 3.3 copy-start.6
  7.2 3.3 copy-start.7
  7.2 91.1 %all-gather.3.cloned.1.call-start = ((), (), s32[]{:S(2)}) async-start(), calls=%async_computation | async-start | bytes 7962624 | tf_op jit(solution)/shard_map/all_gather | solution.py:2209
  10.5 275.7 %all-gather.5.cloned.1.call-start = ((), (), s32[]{:S(2)}) async-start(), calls=%async_computation.1 | async-start | bytes 23887872 | tf_op jit(solution)/shard_map/all_gather | solution.py:2215
  12.3 1.5 copy-start.14
  12.3 1.7 copy-start.21
  12.3 1.7 copy-start.22
  12.3 1.7 copy-start.23
  12.3 1.7 copy-start.18
  12.3 1.8 copy-start.13
  12.3 1.8 copy-start.17
  12.3 1.8 copy-start
  12.3 1.8 copy-start.3
  76.8 0.8 copy-start.1
  77.7 0.8 copy-start.2
  78.5 0.6 copy-start.4
  79.1 0.7 copy-start.5
  496.9 94.0 %copy-start.8 = (bf16[256,2304]{1,0:T(8,128)(2,1)S(1)}, bf16[256,2304]{1,0:T(8,128)(2,1)}, u32[]{:S(2)}) copy-start(bf16[256,2304]{1,0:T(8,128)(2,1)} %get-tuple-element.104) | copy-start | bytes 3538948
  590.8 1.7 copy-start.9
  592.5 1.1 copy-start.11
  592.5 1.8 copy-start.20
  592.5 2.4 copy-start.12
  592.5 3.1 copy-start.19
  592.5 3.7 copy-start.16
  592.6 4.4 copy-start.10
  592.6 5.1 copy-start.15
Sparse Core Ops, SparseCore 0:
  10.6 87.6 all-gather.2
  100.0 186.1 all-gather.4

commit v7 on v6

--- a/solution.py
+++ b/solution.py
@@ -428,61 +428,89 @@
         self.sq, self.half = sq, sq.half
         self.part, self.landing, self.passed = part, landing, passed
         self.send_sem, self.recv_sem = send_sem, recv_sem
-
-    def copy(self, kind, link):
+        self.tiles = send_sem.shape[-1]
+        self.width = part.shape[-1] // self.tiles
+
+    def columns(self, tile):
+        if self.tiles == 1:
+            return pl.ds(0, self.width)
+        return columns(tile, self.width)
+
+    def copy(self, kind, link, tile):
         rows = pl.ds(link * self.half, self.half)
+        cols = self.columns(tile)
         source = (
-            self.passed.at[link] if kind == 2 else self.part.at[1 + 2 * kind, rows]
+            self.passed.at[link, :, cols]
+            if kind == 2
+            else self.part.at[1 + 2 * kind, rows, cols]
         )
         slot = 2 * kind + link
         return remote(
             source,
-            self.landing.at[slot],
-            self.send_sem.at[slot],
-            self.recv_sem.at[slot],
+            self.landing.at[slot, :, cols],
+            self.send_sem.at[slot, tile],
+            self.recv_sem.at[slot, tile],
             self.sq.links[1 - link if kind == 2 else link],
         )
 
+    def send(self, kind, tile):
+        for link in range(2):
+            self.copy(kind, link, tile).start()
+
     def send_own(self):
+        for tile in range(self.tiles):
+            self.send(0, tile)
+
+    def send_far(self):
+        for tile in range(self.tiles):
+            self.send(1, tile)
+
+    def pass_on(self):
+        for tile in range(self.tiles):
+            cols = self.columns(tile)
+            for link in range(2):
+                self.copy(1, link, tile).wait_recv()
+                rows = pl.ds((1 - link) * self.half, self.half)
+                mine = self.part[2, rows, cols].astype(F32)
+                self.passed[link, :, cols] = (
+                    mine + self.landing[2 + link, :, cols].astype(F32)
+                ).astype(BF16)
+                self.copy(2, link, tile).start()
+
+    def arrived(self):
+        for kind in (0, 2):
+            for tile in range(self.tiles):
+                for link in range(2):
+                    self.copy(kind, link, tile).wait_recv()
+
+    def collect(self, out_ref, places=((0, 0),)):
+        self.arrived()
         for link in range(2):
-            self.copy(0, link).start()
-
-    def send_far(self):
-        for link in range(2):
-            self.copy(1, link).start()
-
-    def pass_on(self, link):
-        self.copy(1, link).wait_recv()
-        rows = pl.ds((1 - link) * self.half, self.half)
-        mine = self.part[2, rows, :].astype(F32)
-        self.passed[link] = (mine + self.landing[2 + link].astype(F32)).astype(BF16)
-        self.copy(2, link).start()
-
-    def collect(self, out_ref, first=0):
-        for link in range(2):
-            self.copy(0, link).wait_recv()
-            self.copy(2, link).wait_recv()
             rows = pl.ds(link * self.half, self.half)
-            out_ref[rows, first : first + self.part.shape[-1]] = (
+            total = (
                 self.part[0, rows, :].astype(F32)
                 + self.landing[link].astype(F32)
                 + self.landing[4 + link].astype(F32)
             )
+            size = self.part.shape[-1] // len(places)
+            for source, target in places:
+                out_ref[rows, target : target + size] = total[:, source : source + size]
 
     def finish(self):
         for kind in range(3):
-            for link in range(2):
-                self.copy(kind, link).wait_send()
-
-
-def scatter_scratch(rows, width):
+            for tile in range(self.tiles):
+                for link in range(2):
+                    self.copy(kind, link, tile).wait_send()
+
+
+def scatter_scratch(rows, width, tiles=1):
     half = rows // 2
     return [
         pltpu.VMEM((4, rows, width), BF16),
         pltpu.VMEM((6, half, width), BF16),
         pltpu.VMEM((2, half, width), BF16),
-        pltpu.SemaphoreType.DMA((6,)),
-        pltpu.SemaphoreType.DMA((6,)),
+        pltpu.SemaphoreType.DMA((6, tiles)),
+        pltpu.SemaphoreType.DMA((6, tiles)),
     ]
 
 
@@ -599,15 +627,21 @@
             here = columns(step, wide)
             part[chunk, :, here] = nt(grads[...], gu_w[here, :]).astype(BF16)
 
+            @pl.when(chunk == 1)
+            def _():
+                scatters[0].send(0, step)
+
+            @pl.when(chunk == 3)
+            def _():
+                scatters[0].send(1, step)
+
         @pl.when(chunk == 1)
         def _():
-            for scatter in scatters:
-                scatter.send_own()
+            scatters[1].send_own()
 
         @pl.when(chunk == 3)
         def _():
-            for scatter in scatters:
-                scatter.send_far()
+            scatters[1].send_far()
 
         low_turned = low_down.astype(F32).T.astype(BF16)
         gu_turned = low[slot].astype(F32).T.astype(BF16)
@@ -624,9 +658,8 @@
     spread = sq.spread(lambda peer: f_send.at[:, peer], f_out, spread_send, spread_recv)
     for copy in spread:
         copy.start()
-    for link in range(2):
-        for scatter in scatters:
-            scatter.pass_on(link)
+    for scatter in scatters:
+        scatter.pass_on()
     gather.finish()
     scatters[0].collect(o_ref)
     scatters[1].collect(l_ref)
@@ -670,7 +703,7 @@
             pltpu.SemaphoreType.DMA((3,)),
             pltpu.SemaphoreType.DMA((4,)),
         ]
-        + scatter_scratch(rows, model)
+        + scatter_scratch(rows, model, model // tile_of(model))
         + scatter_scratch(rows, LANES),
         compiler_params=pltpu.CompilerParams(
             collective_id=5, has_side_effects=True, vmem_limit_bytes=62 * 1024 * 1024
@@ -892,66 +925,70 @@
         ends = (last - self.z) // last + self.z // last
         pl.semaphore_wait(barrier, len(others) + 3 - ends)
 
-    def copy(self, place, kind):
+    def copy(self, place, kind, part):
         target = (self.d + 2, self.d - 2, self.sibling)[kind]
         slot = 2 * place + self.core
+        half = self.slots.shape[1] // 2
+        block = self.slots.at[slot, pl.ds(part * half, half)]
         return pltpu.make_async_remote_copy(
-            src_ref=self.slots.at[slot],
-            dst_ref=self.slots.at[slot],
-            send_sem=self.send_sem.at[kind, place],
-            recv_sem=self.recv_sem.at[slot],
+            src_ref=block,
+            dst_ref=block,
+            send_sem=self.send_sem.at[kind, place, part],
+            recv_sem=self.recv_sem.at[slot, part],
             device_id={"dp": target},
             device_id_type=MESH,
         )
 
-    def send_up(self, place):
+    def send_up(self, place, part):
         @pl.when(self.z < self.places - 1)
         def _():
-            self.copy(place, 0).start()
-
-    def send_down(self, place):
+            self.copy(place, 0, part).start()
+
+    def send_down(self, place, part):
         @pl.when(self.z > 0)
         def _():
-            self.copy(place, 1).start()
+            self.copy(place, 1, part).start()
 
     def start(self):
-        self.send_up(self.z)
-        self.send_down(self.z)
-        self.copy(self.z, 2).start()
-
-    def arrive(self, distance):
+        for part in range(2):
+            self.send_up(self.z, part)
+            self.send_down(self.z, part)
+            self.copy(self.z, 2, part).start()
+
+    def arrive(self, distance, part):
         @pl.when(self.z >= distance)
         def _():
             place = self.z - distance
-            self.copy(place, 2).wait_recv()
-            self.send_up(place)
-            self.copy(place, 2).start()
+            self.copy(place, 2, part).wait_recv()
+            self.send_up(place, part)
+            self.copy(place, 2, part).start()
 
         @pl.when(self.z + distance < self.places)
         def _():
             place = self.z + distance
-            self.copy(place, 2).wait_recv()
-            self.send_down(place)
-            self.copy(place, 2).start()
-
-    def wait_sibling(self, place):
-        slot = self.slots.at[2 * place + 1 - self.core]
-        pltpu.make_async_copy(
-            slot, slot, self.recv_sem.at[2 * place + 1 - self.core]
-        ).wait()
+            self.copy(place, 2, part).wait_recv()
+            self.send_down(place, part)
+            self.copy(place, 2, part).start()
+
+    def wait_sibling(self, place, part):
+        half = self.slots.shape[1] // 2
+        other = 2 * place + 1 - self.core
+        block = self.slots.at[other, pl.ds(part * half, half)]
+        pltpu.make_async_copy(block, block, self.recv_sem.at[other, part]).wait()
 
     def finish(self):
         for place in range(self.places):
-
-            @pl.when((self.z >= place) & (self.z < self.places - 1))
-            def _(place=place):
-                self.copy(place, 0).wait_send()
-
-            @pl.when((self.z <= place) & (self.z > 0))
-            def _(place=place):
-                self.copy(place, 1).wait_send()
-
-            self.copy(place, 2).wait_send()
+            for part in range(2):
+
+                @pl.when((self.z >= place) & (self.z < self.places - 1))
+                def _(place=place, part=part):
+                    self.copy(place, 0, part).wait_send()
+
+                @pl.when((self.z <= place) & (self.z > 0))
+                def _(place=place, part=part):
+                    self.copy(place, 1, part).wait_send()
+
+                self.copy(place, 2, part).wait_send()
 
 
 ARRIVALS = ((0, 1, 2, 3), (1, 0, 2, 3), (2, 1, 3, 0), (3, 2, 1, 0))
@@ -1069,9 +1106,11 @@
         for copy in stores(step, slot):
             copy.start()
 
-        @pl.when(step == steps - 2)
-        def _():
-            line.arrive(1)
+        for part_at, part_of in ((steps // 2 - 1, 0), (steps - 2, 1)):
+
+            @pl.when(step == part_at)
+            def _(part_of=part_of):
+                line.arrive(1, part_of)
 
     keep_hidden = pltpu.make_async_copy(hidden, hidden_out, keep_sem.at[0])
     keep_hidden.start()
@@ -1081,14 +1120,10 @@
     is_here = (is_first, 1 - is_first - is_third - is_last, is_third, is_last)
     order = [sum(flag * ARRIVALS[z][i] for z, flag in enumerate(is_here)) for i in range(4)]
 
-    def scatter_at(place):
+    def scatter_at(place, half):
+        at = 2 * place + half
         return ChunkScatter(
-            sq,
-            part.at[place],
-            landing.at[place],
-            passed.at[place],
-            part_send.at[place],
-            part_recv.at[place],
+            sq, part.at[at], landing.at[at], passed.at[at], part_send.at[at], part_recv.at[at]
         )
 
     low_scatter = ChunkScatter(sq, *low_scratch)
@@ -1100,47 +1135,51 @@
     low_scatter.send_far()
     low_scatter.send_own()
     keeps = []
-    for step in range(4):
-        if step >= 2:
-            line.arrive(step)
-        place = order[step]
-        line.wait_sibling(place)
+    earlier = low_scatter
+    half_rows = down.shape[1] // 2
+    arrivals = {(1, 0): ((2, 0),), (2, 0): ((2, 1),), (3, 0): ((3, 0),), (3, 1): ((3, 1),)}
+    for turn in range(4):
+        place = order[turn]
+        for half in range(2):
+            for distance, piece in arrivals.get((turn, half), ()):
+                line.arrive(distance, piece)
+            line.wait_sibling(place, half)
+            scatter = scatter_at(place, half)
+
+            @pl.loop(0, 4)
+            def _(step, place=place, half=half, scatter=scatter):
+                chunk = far_first(step)
+                for core in range(2):
+                    part[
+                        2 * place + half, chunk, :, core * half_rows : (core + 1) * half_rows
+                    ] = nt(
+                        hidden[chunk],
+                        down[2 * place + core, half * half_rows : (half + 1) * half_rows],
+                    ).astype(BF16)
+
+                @pl.when(step == 0)
+                def _():
+                    scatter.send_far()
+
+                @pl.when(step == 1)
+                def _():
+                    scatter.send_own()
+
+            earlier.pass_on()
+            earlier = scatter
         pair = pl.ds(2 * place, 2)
-        keep = pltpu.make_async_copy(down.at[pair], down_out.at[pair], keep_sem.at[1 + step])
+        keep = pltpu.make_async_copy(down.at[pair], down_out.at[pair], keep_sem.at[1 + turn])
         keep.start()
         keeps.append(keep)
-        scatter = scatter_at(place)
-        shard_rows = down.shape[1]
-
-        @pl.loop(0, 4)
-        def _(turn, place=place, scatter=scatter):
-            chunk = turn + 3 * ((3 - turn) // 3) - 3 * (turn // 3)
-            for core in range(2):
-                part[place, chunk, :, core * shard_rows : (core + 1) * shard_rows] = nt(
-                    hidden[chunk], down[2 * place + core]
-                ).astype(BF16)
-
-            @pl.when(turn == 0)
-            def _():
-                scatter.send_far()
-
-            @pl.when(turn == 1)
-            def _():
-                scatter.send_own()
-
-        if step > 0:
-            for link in range(2):
-                scatter_at(order[step - 1]).pass_on(link)
-        else:
-            for link in range(2):
-                low_scatter.pass_on(link)
-    for link in range(2):
-        scatter_at(order[3]).pass_on(link)
-    wide = part.shape[-1]
     low_scatter.collect(low_sum)
     low_down_ref[...] = low_sum[...].astype(BF16)
-    for place in range(4):
-        scatter_at(place).collect(work, place * wide)
+    earlier.pass_on()
+    everything = [(place, half) for place in range(4) for half in range(2)]
+    for place, half in everything:
+        first = 2 * place * down.shape[1] + half * half_rows
+        scatter_at(place, half).collect(
+            work, ((0, first), (half_rows, first + down.shape[1]))
+        )
     add_lifted(work, low_down_ref, d_ref)
 
     @pl.loop(0, rows // BLOCK)
@@ -1155,8 +1194,8 @@
             BF16
         )
 
-    for place in range(4):
-        scatter_at(place).finish()
+    for place, half in everything:
+        scatter_at(place, half).finish()
     low_scatter.finish()
     line.finish()
     for step in (steps - 2, steps - 1):
@@ -1180,7 +1219,7 @@
     chunks, rows, model = seq.shape
     width = shard.shape[1]
     tile = 384
-    wide = model // (dp // 2)
+    wide = model // dp
     half = rows // 2
     anywhere = pl.BlockSpec(memory_space=pl.ANY)
     vmem = pl.BlockSpec(memory_space=pltpu.VMEM)
@@ -1213,13 +1252,13 @@
             pltpu.SemaphoreType.DMA((2, 2)),
             pltpu.SemaphoreType.DMA((2, 2)),
             pltpu.SemaphoreType.DMA((5,)),
-            pltpu.SemaphoreType.DMA((3, dp // 2)),
-            pltpu.SemaphoreType.DMA((dp,)),
-            pltpu.VMEM((4, 4, rows, wide), BF16),
-            pltpu.VMEM((4, 6, half, wide), BF16),
-            pltpu.VMEM((4, 2, half, wide), BF16),
-            pltpu.SemaphoreType.DMA((4, 6)),
-            pltpu.SemaphoreType.DMA((4, 6)),
+            pltpu.SemaphoreType.DMA((3, dp // 2, 2)),
+            pltpu.SemaphoreType.DMA((dp, 2)),
+            pltpu.VMEM((dp, 4, rows, wide), BF16),
+            pltpu.VMEM((dp, 6, half, wide), BF16),
+            pltpu.VMEM((dp, 2, half, wide), BF16),
+            pltpu.SemaphoreType.DMA((dp, 6, 1)),
+            pltpu.SemaphoreType.DMA((dp, 6, 1)),
         ]
         + scatter_scratch(rows, LANES),
         compiler_params=pltpu.CompilerParams(
@@ -1624,19 +1663,24 @@
             here = columns(tile, wide)
             part[chunk, :, here] = nt(attended, weight[here, qkv_width:]).astype(BF16)
 
+            @pl.when(step == 0)
+            def _():
+                scatters[0].send(1, tile)
+
+            @pl.when(step == 1)
+            def _():
+                scatters[0].send(0, tile)
+
         @pl.when(step == 0)
         def _():
-            for scatter in scatters:
-                scatter.send_far()
+            scatters[1].send_far()
 
         @pl.when(step == 1)
         def _():
-            for scatter in scatters:
-                scatter.send_own()
-
-    for link in range(2):
-        for scatter in scatters:
-            scatter.pass_on(link)
+            scatters[1].send_own()
+
+    for scatter in scatters:
+        scatter.pass_on()
     scatters[1].collect(low_sum)
     low_out_ref[...] = low_sum[...].astype(BF16)
     scatters[0].collect(total_ref)
@@ -1710,7 +1754,7 @@
             pltpu.SemaphoreType.DMA((3, 3)),
             pltpu.SemaphoreType.DMA((3, 3)),
         ]
-        + scatter_scratch(rows, model)
+        + scatter_scratch(rows, model, model // tile_of(model))
         + scatter_scratch(rows, LANES),
         compiler_params=pltpu.CompilerParams(
             collective_id=8, has_side_effects=True, vmem_limit_bytes=62 * 1024 * 1024
@@ -1915,30 +1959,41 @@
             + sq.across * (1 - is_own - is_far - is_down)
         )
         low_turned = turned(low_all[block])[OUT]
-        for side in range(2):
-            start = pl.multiple_of(block * rows + side * half, half)
-            here = pl.ds(start, half)
-            place = pl.ds(side * half, half)
-            h_turned[:RANK, :] += nn(
-                low_turned[:, side * half : (side + 1) * half], attended_ref[here, :]
-            )
-            queries = stack_heads(q_ref, here, heads)
-            grads = jnp.concatenate(
-                [att[block, place, h * HD : (h + 1) * HD] for h in range(heads)], axis=0
-            )
-            inverse = jnp.concatenate([inverse_ref[h : h + 1, here] for h in range(heads)], axis=1)
-            squash, weights = softmax_weights(k_ref[...], queries, start, half, length_ref[0])
-            probs = weights * inverse
-            grad_probs = nt(v_ref[...], grads)
-            mean = jnp.sum(probs * grad_probs, axis=0, keepdims=True)
-            grad_raw = (probs * (grad_probs - mean) * (1.0 - squash * squash)).astype(BF16)
-            k_sum[...] += nn(grad_raw, queries)
-            v_sum[...] += nn(probs.astype(BF16), grads)
-            q_back = nn(kt_ref[...], grad_raw).T * HD ** (-0.5)
-            for h in range(heads):
-                q_grad[here, h * HD : (h + 1) * HD] = rotate_back(
-                    q_back[h * half : (h + 1) * half], cos_ref[here, :], sin_ref[here, :]
-                ).astype(BF16)
+        h_turned[:RANK, :] += nn(
+            low_turned, attended_ref[pl.ds(pl.multiple_of(block * rows, rows), rows), :]
+        )
+        for last in range(4):
+
+            @pl.when(block == last)
+            def _(last=last):
+                seen = slice(0, (last + 1) * rows)
+
+                @pl.loop(0, 2)
+                def _(side):
+                    start = pl.multiple_of(last * rows + side * half, half)
+                    here = pl.ds(start, half)
+                    place = pl.ds(pl.multiple_of(side * half, half), half)
+                    queries = stack_heads(q_ref, here, heads)
+                    grads = jnp.concatenate(
+                        [att[last, place, h * HD : (h + 1) * HD] for h in range(heads)], axis=0
+                    )
+                    inverse = jnp.concatenate(
+                        [inverse_ref[h : h + 1, here] for h in range(heads)], axis=1
+                    )
+                    squash, weights = softmax_weights(
+                        k_ref[seen, :], queries, start, half, length_ref[0]
+                    )
+                    probs = weights * inverse
+                    grad_probs = nt(v_ref[seen, :], grads)
+                    mean = jnp.sum(probs * grad_probs, axis=0, keepdims=True)
+                    grad_raw = (probs * (grad_probs - mean) * (1.0 - squash * squash)).astype(BF16)
+                    k_sum[seen, :] += nn(grad_raw, queries)
+                    v_sum[seen, :] += nn(probs.astype(BF16), grads)
+                    q_back = nn(kt_ref[:, seen], grad_raw).T * HD ** (-0.5)
+                    for h in range(heads):
+                        q_grad[here, h * HD : (h + 1) * HD] = rotate_back(
+                            q_back[h * half : (h + 1) * half], cos_ref[here, :], sin_ref[here, :]
+                        ).astype(BF16)
 
     weight_load.wait()
     kv_grad[:, :HD] = rotate_back(k_sum[...], cos_ref[...], sin_ref[...]).astype(BF16)
@@ -1963,15 +2018,21 @@
             here = columns(tile, wide)
             part[chunk, :, here] = nt(joined[chunk], weight[here, :]).astype(BF16)
 
+            @pl.when(step == 0)
+            def _():
+                scatters[0].send(1, tile)
+
+            @pl.when(step == 1)
+            def _():
+                scatters[0].send(0, tile)
+
         @pl.when(step == 0)
         def _():
-            for scatter in scatters:
-                scatter.send_far()
+            scatters[1].send_far()
 
         @pl.when(step == 1)
         def _():
-            for scatter in scatters:
-                scatter.send_own()
+            scatters[1].send_own()
 
     seq_load.wait()
 
@@ -2032,9 +2093,8 @@
     for copies in spread:
         for copy in copies:
             copy.start()
-    for link in range(2):
-        for scatter in scatters:
-            scatter.pass_on(link)
+    for scatter in scatters:
+        scatter.pass_on()
     for copies in spread:
         copies[0].wait()
         for copy in copies[1:]:
@@ -2045,9 +2105,7 @@
     line += along(lambda k: hk_land.at[k // 2, lax.rem(k, 2)], hk_recv, hk_sem, line_recv.at[2])
     scatters[1].collect(low_sum)
     low_qkv = low_sum[...].astype(BF16)
-    for link in range(2):
-        scatters[0].copy(0, link).wait_recv()
-        scatters[0].copy(2, link).wait_recv()
+    scatters[0].arrived()
     landing = scratch[1]
     low_sum[...] = low_qkv.astype(F32)
 
@@ -2163,7 +2221,7 @@
             pltpu.SemaphoreType.DMA((dp + 1, 4)),
             pltpu.SemaphoreType.DMA((3,)),
         ]
-        + scatter_scratch(rows, model)
+        + scatter_scratch(rows, model, model // tile_of(model))
         + scatter_scratch(rows, LANES),
         compiler_params=pltpu.CompilerParams(
             collective_id=6, has_side_effects=True, vmem_limit_bytes=62 * 1024 * 1024

time: 606 us -> 594 us (0.980)
  Pallas kernels: 535 us -> 524 us
    pallas_call x1, Pallas kernels: 121 us -> 110 us  [mlp_fused(): pl.pallas_call(functools.partial(mlp_kernel, rows), out_shape=(jax.ShapeD...]
  transfers between devices with their start and end apart: 2 -> 2, of which waited for: 2 -> 2; matrix products, arithmetic and copies ran while one was open for 1% -> 1% of each run, Pallas kernels for 38% -> 39%
where the time goes in v7:
time: 594 us; the launch traced here: 593 us
  Pallas kernels  524 us (88%)
  waiting for transfers between devices  34.8 us (6%)
  between operations  15.8 us (3%)
  local copies, waits for them, and re-layouts  12.4 us (2%)
  other arithmetic  6.7 us (1%)
    pallas_call x1, Pallas kernels, attn_fused(): pl.pallas_call(functools.partial(attn_kernel, rows), out_shape=(jax.Shape...  168 us
    pallas_call x1, Pallas kernels, mlp_fused(): pl.pallas_call(functools.partial(mlp_kernel, rows), out_shape=(jax.ShapeD...  110 us
    pallas_call x1, Pallas kernels, attn_back_fused(): pl.pallas_call(functools.partial(attn_back_kernel, rows), out_shape=tuple...  93.8 us
    pallas_call x1, Pallas kernels, mlp_back_fused(): pl.pallas_call(functools.partial(mlp_back_kernel, rows), out_shape=(jax.S...  89 us
    pallas_call x1, Pallas kernels, front(): pl.pallas_call(front_kernel, out_shape=(jax.ShapeDtypeStruct((4 * rows, m...  62.7 us
    all_gather x1, waiting for transfers between devices, per_device(): gate_up_w = lax.all_gather(gate_up_shard, 'dp', axis=0, tiled=True)  19.8 us
    all_gather x1, waiting for transfers between devices, per_device(): attn_w = lax.all_gather(attn_shard, 'dp', axis=0, tiled=True)  15 us
  transfers between devices with their start and end apart: 2, of which 2 were waited for; matrix products, arithmetic and copies ran while one was open for 1% of the time, Pallas kernels for 39%

profile of v7, /device:TPU:0, one launch (start us, length us, event | category | flops | bytes accessed | tf_op | source)
XLA Modules:
  0.0 593.4 jit_solution(16529636186858394050)
XLA Ops:
  7.2 0.0 all-gather.3.cloned.1.call-start
  7.3 1.2 constant_dynamic-slice_fusion
  8.4 2.0 pad_maximum_fusion.1
  10.4 0.0 all-gather.3.cloned.1.call-update
  10.5 0.0 all-gather.5.cloned.1.call-start
  10.5 1.7 pad_maximum_fusion
  12.3 0.0 copy-start.18
  12.3 0.0 all-gather.5.cloned.1.call-update
  13.8 0.1 copy.29
  14.2 62.7 %front.1 = (bf16[1024,2304]{1,0:T(8,128)(2,1)}, s32[8,8,128]{2,1,0:T(8,128)S(1)}, bf16[2304,128]{1,0:T(8,128)(2,1)S(1)}, bf16[2304,128]{1,0:T(8,128)(2,1)S(1)}, ...) custom-call(s32[8,128]{1,0:T(8,128)S(1)} %broadcast_in_dim.10.ids_ref, bf16[256,2304]{1,0:T(8,128)(2,1)S(1)} %copy-done, ...), custom_call_target="tpu_custom_call" | custom-call | tf_op jit(solution)/shard_map/front/pallas_call | solution.py:861
  76.9 0.8 copy-done.1
  77.7 0.8 copy-done.2
  78.5 0.6 copy-done.4
  79.1 0.7 copy-done.5
  79.8 0.8 slice_reduce_fusion.ids_ref
  80.5 2.8 fusion
  83.3 15.0 %all-gather.3.cloned.1.call-done.weight_hbm = bf16[2304,1536]{1,0:T(8,128)(2,1)} async-done(((bf16[288,1536]{1,0:T(8,128)(2,1)}), bf16[2304,1536]{1,0:T(8,128)(2,1)}) %all-gather.3.cloned.1.call-update) | async-done | bytes 7077904 | tf_op jit(solution)/shard_map/all_gather | solution.py:2267
  98.3 168.0 %attn.1 = (bf16[1024,512]{1,0:T(8,128)(2,1)}, bf16[1024,256]{1,0:T(8,128)(2,1)}, bf16[256,1024]{1,0:T(8,128)(2,1)}, bf16[1024,256]{1,0:T(8,128)(2,1)}, bf16[1024...) custom-call(s32[1]{0:T(128)S(6)} %copy.39.length_ref, ...), custom_call_target="tpu_custom_call" | custom-call | tf_op jit(solution)/shard_map/attn/pallas_call | solution.py:1725
  266.4 19.8 %all-gather.5.cloned.1.call-done.gu_hbm = bf16[2304,4608]{1,0:T(8,128)(2,1)} async-done(((bf16[288,4608]{1,0:T(8,128)(2,1)}), bf16[2304,4608]{1,0:T(8,128)(2,1)}) %all-gather.5.cloned.1.call-update) | async-done | bytes 21233680 | tf_op jit(solution)/shard_map/all_gather | solution.py:2273
  286.2 110.0 %mlp.1 = (bf16[256,2304]{1,0:T(8,128)(2,1)}, bf16[256,2304]{1,0:T(8,128)(2,1)}, bf16[4,256,128]{2,1,0:T(8,128)(2,1)}, bf16[256,128]{1,0:T(8,128)(2,1)}, bf16[4,2...) custom-call(s32[1]{0:T(128)S(6)} %copy.39.length_ref, ...), custom_call_target="tpu_custom_call" | custom-call | tf_op jit(solution)/shard_map/mlp/pallas_call | solution.py:1227
  396.2 89.0 %mlp_back.1 = (f32[256,2304]{1,0:T(8,128)}, f32[256,128]{1,0:T(8,128)}, bf16[4,2,48,288]{3,2,1,0:T(8,128)(2,1)}) custom-call(bf16[256,2304]{1,0:T(8,128)(2,1)} %get-tuple-element.61.g_ref.grad_mlp_ref, bf16[2304,2304]{1,0:T(8,128)(2,1)} %bitcast.16, bf16[2304,4608]{1,0:T(8,128)(2,1)} %all-gather.5.cloned.1.call-done.gu_hbm, ...), custom_call_target="tpu_custom_call" | custom-call | tf_op jit(solution)/shard_map/mlp_back/pallas_call | solution.py:678
  485.3 93.8 %attn_back.1 = (bf16[256,2304]{1,0:T(8,128)(2,1)}, f32[8,72,80]{2,1,0:T(8,128)}, f32[8,16,64]{2,1,0:T(8,128)}, f32[8,16,288]{2,1,0:T(8,128)}, f32[8,16,64]{2,1,0...) custom-call(s32[8]{0:T(128)} %slice_reduce_fusion.ids_ref, ...), custom_call_target="tpu_custom_call" | custom-call | tf_op jit(solution)/shard_map/attn_back/pallas_call | solution.py:2182
  579.1 1.0 copy.41
  580.1 0.7 copy-done.9
  580.8 1.0 copy.42
  581.8 0.7 copy.43
  582.5 0.6 copy.44
  583.2 0.7 copy.45
  583.8 0.6 copy.46
  584.5 0.7 copy.47
  585.1 0.7 copy.48
  585.9 0.7 copy.49
  (47 shorter events, 0.2 us)
Async XLA Ops:
  7.2 3.3 copy-start.6
  7.2 3.3 copy-start.7
  7.2 91.1 %all-gather.3.cloned.1.call-start = ((), (), s32[]{:S(2)}) async-start(), calls=%async_computation | async-start | bytes 7962624 | tf_op jit(solution)/shard_map/all_gather | solution.py:2267
  10.5 275.7 %all-gather.5.cloned.1.call-start = ((), (), s32[]{:S(2)}) async-start(), calls=%async_computation.1 | async-start | bytes 23887872 | tf_op jit(solution)/shard_map/all_gather | solution.py:2273
  12.3 1.5 copy-start.14
  12.3 1.7 copy-start.21
  12.3 1.7 copy-start.22
  12.3 1.7 copy-start.23
  12.3 1.7 copy-start.18
  12.3 1.8 copy-start.13
  12.3 1.8 copy-start.17
  12.3 1.8 copy-start
  12.3 1.8 copy-start.3
  76.8 0.8 copy-start.1
  77.7 0.8 copy-start.2
  78.5 0.6 copy-start.4
  79.1 0.7 copy-start.5
  485.3 93.8 %copy-start.8 = (bf16[256,2304]{1,0:T(8,128)(2,1)S(1)}, bf16[256,2304]{1,0:T(8,128)(2,1)}, u32[]{:S(2)}) copy-start(bf16[256,2304]{1,0:T(8,128)(2,1)} %get-tuple-element.104) | copy-start | bytes 3538948
  579.1 1.7 copy-start.9
  580.8 1.1 copy-start.11
  580.8 1.8 copy-start.20
  580.8 2.4 copy-start.12
  580.8 3.1 copy-start.19
  580.8 3.7 copy-start.16
  580.8 4.4 copy-start.10
  580.8 5.1 copy-start.15
Sparse Core Ops, SparseCore 0:
  10.6 87.6 all-gather.2
  100.0 186.1 all-gather.4

commit v8 on v7

--- a/solution.py
+++ b/solution.py
@@ -719,12 +719,14 @@
     f_all,
     d_all,
     hk_all,
+    shard_hbm,
     seq_out,
     ids_out,
     d_out,
     f_out,
     h_out,
     k_out,
+    weight_out,
     normed,
     ids_land,
     f_pick,
@@ -748,6 +750,9 @@
     line_recv,
     group_send,
     group_recv,
+    shard_sem,
+    shard_send,
+    shard_recv,
 ):
     rows = layer_ref.shape[0]
     sq = Square(rows)
@@ -756,6 +761,9 @@
     peers = [{"tensor": peer} for peer in (sq.across, sq.down, sq.far)]
     peers += [{"dp": lax.rem(d + step, dp)} for step in range(1, dp)]
     call(peers)
+    shards = Line(weight_out, shard_send, shard_recv)
+    own_shard = pltpu.make_async_copy(shard_hbm, weight_out.at[d], shard_sem)
+    own_shard.start()
 
     @pl.loop(0, rows // BLOCK)
     def _(step):
@@ -764,6 +772,8 @@
 
     pl.semaphore_wait(pltpu.get_barrier_semaphore(), len(peers))
     line = along(lambda k: ids_ref, ids_land, line_send.at[0], line_recv.at[0])
+    own_shard.wait()
+    shards.start()
     gather = PlainGather(sq.me, normed, seq_out, local_sem, gather_send, gather_recv)
     gather.start()
     pltpu.make_async_copy(ids_land, ids_land, line_recv.at[0]).wait()
@@ -787,11 +797,13 @@
             line_send.at[1 + item],
             line_recv.at[1 + item],
         )
+    shards.arrive(1, 0)
     gather.forward()
     for flip in (d_flip, f_flip, h_flip, k_flip):
         flip[...] = jnp.zeros_like(flip)
     for item, target in enumerate(lands):
         pltpu.make_async_copy(target, target, line_recv.at[1 + item]).wait()
+    shards.arrive(1, 1)
     size = d_mid.shape[2]
     for k in range(dp):
         d_join[:, k * size : (k + 1) * size] = d_mid[k]
@@ -814,10 +826,12 @@
     for copies in spread:
         for copy in copies:
             copy.start()
+    shards.arrive(2, 0)
     for copies in spread:
         copies[0].wait()
         for copy in copies[1:]:
             copy.wait_recv()
+    shards.arrive(2, 1)
     f_size, h_size, k_size = f_mid.shape[2], h_out.shape[0] // dp, k_out.shape[0] // dp
     for t in range(4):
         for k in range(dp):
@@ -843,7 +857,13 @@
             here = columns(step, LANES)
             out[here, :] = flip[:, here].T.astype(BF16)
 
+    shards.arrive(3, 0)
     gather.finish()
+    shards.arrive(3, 1)
+    for place in range(dp // 2):
+        for part in range(2):
+            shards.wait_sibling(place, part)
+    shards.finish()
     for copies in spread:
         for copy in copies[1:]:
             copy.wait_send()
@@ -851,7 +871,7 @@
         copy.wait_send()
 
 
-def front(ids, layer_in, gains, f_all, d_all, hk_all, dp, widths):
+def front(ids, layer_in, gains, f_all, d_all, hk_all, shard, dp, widths):
     rows, model = layer_in.shape
     anywhere = pl.BlockSpec(memory_space=pl.ANY)
     vmem = pl.BlockSpec(memory_space=pltpu.VMEM)
@@ -864,9 +884,10 @@
             jax.ShapeDtypeStruct((4 * rows, model), BF16),
             jax.ShapeDtypeStruct((dp,) + ids.shape, jnp.int32),
         )
-        + tuple(jax.ShapeDtypeStruct((width, LANES), BF16) for width in widths),
-        in_specs=[vmem] * 6,
-        out_specs=(anywhere,) + (vmem,) * 5,
+        + tuple(jax.ShapeDtypeStruct((width, LANES), BF16) for width in widths)
+        + (jax.ShapeDtypeStruct((dp,) + shard.shape, BF16),),
+        in_specs=[vmem] * 6 + [anywhere],
+        out_specs=(anywhere,) + (vmem,) * 5 + (anywhere,),
         scratch_shapes=[
             pltpu.VMEM((rows, model), BF16),
             pltpu.VMEM((dp,) + ids.shape, jnp.int32),
@@ -887,12 +908,15 @@
             pltpu.SemaphoreType.DMA((4,)),
             pltpu.SemaphoreType.DMA((3, 3)),
             pltpu.SemaphoreType.DMA((3, 4)),
+            pltpu.SemaphoreType.DMA,
+            pltpu.SemaphoreType.DMA((3, dp // 2, 2)),
+            pltpu.SemaphoreType.DMA((dp, 2)),
         ],
         compiler_params=pltpu.CompilerParams(
             collective_id=9, has_side_effects=True, vmem_limit_bytes=VMEM_LIMIT
         ),
         name="front",
-    )(ids, layer_in, gains, *tables_in)
+    )(ids, layer_in, gains, *tables_in, shard)
 
 
 class Line:
@@ -989,6 +1013,58 @@
                     self.copy(place, 1, part).wait_send()
 
                 self.copy(place, 2, part).wait_send()
+
+
+class WeightSpread:
+    def __init__(self, sq, line, weight_hbm, h_table, w_out_all, h_all, own_sem, send_sem, recv_sem):
+        model, q_width = w_out_all.shape[1:]
+        share = model // 2
+        mine = pl.ds(pl.multiple_of(line.core * share, 8), share)
+        first = weight_hbm.shape[1] - q_width
+        self.own = pltpu.make_async_copy(h_table, h_all.at[sq.me], own_sem)
+        self.taken, self.onward = [], []
+        for which, peer in enumerate((sq.across, sq.down, sq.far)):
+            pairs = (
+                (weight_hbm.at[mine, pl.ds(first, q_width)], w_out_all.at[sq.me, mine]),
+                (h_table, h_all.at[sq.me]),
+            )
+            self.taken.append(
+                [
+                    remote(
+                        source, target, send_sem.at[item, which], recv_sem.at[item, which], peer
+                    )
+                    for item, (source, target) in enumerate(pairs)
+                ]
+            )
+            block = w_out_all.at[peer, mine]
+            self.onward.append(
+                pltpu.make_async_remote_copy(
+                    src_ref=block,
+                    dst_ref=block,
+                    send_sem=send_sem.at[2, which],
+                    recv_sem=recv_sem.at[2, which],
+                    device_id={"dp": line.sibling},
+                    device_id_type=MESH,
+                )
+            )
+
+    def start(self):
+        self.own.start()
+        for copies in self.taken:
+            for copy in copies:
+                copy.start()
+
+    def pass_on(self, which):
+        for copy in self.taken[which]:
+            copy.wait_recv()
+        self.onward[which].start()
+
+    def finish(self):
+        self.own.wait()
+        for copies, onward in zip(self.taken, self.onward):
+            for copy in copies:
+                copy.wait_send()
+            onward.wait()
 
 
 ARRIVALS = ((0, 1, 2, 3), (1, 0, 2, 3), (2, 1, 3, 0), (3, 2, 1, 0))
@@ -1554,6 +1630,7 @@
     own_sem,
     gather_send,
     gather_recv,
+    w_own,
     w_send,
     w_recv,
     *scratch,
@@ -1565,45 +1642,14 @@
     qkv_width = q_width + 2 * HD
     heads = q_width // HD
     wide = tile_of(model)
-    core = lax.rem(lax.axis_index("dp"), 2)
-    sibling = lax.axis_index("dp") + 1 - 2 * core
     weight_load = pltpu.make_async_copy(weight_hbm, weight, load_sem.at[0])
     seq_load = pltpu.make_async_copy(seq_hbm, seq, load_sem.at[1])
     weight_load.start()
     seq_load.start()
-    greet([{"tensor": peer} for peer in (sq.across, sq.down, sq.far)] + [{"dp": sibling}])
-
-    share = model // 2
-    mine = pl.ds(pl.multiple_of(core * share, 8), share)
-    own_h = pltpu.make_async_copy(h_table, h_all.at[sq.me], own_sem.at[1])
-    own_h.start()
-    taken, passed_on = [], []
-    for which, peer in enumerate((sq.across, sq.down, sq.far)):
-        taken.append(
-            (
-                remote(
-                    weight_hbm.at[mine, pl.ds(qkv_width, q_width)],
-                    w_out_all.at[sq.me, mine],
-                    w_send.at[0, which],
-                    w_recv.at[0, which],
-                    peer,
-                ),
-                remote(
-                    h_table, h_all.at[sq.me], w_send.at[1, which], w_recv.at[1, which], peer
-                ),
-            )
-        )
-        block = w_out_all.at[peer, mine]
-        passed_on.append(
-            pltpu.make_async_remote_copy(
-                src_ref=block,
-                dst_ref=block,
-                send_sem=w_send.at[2, which],
-                recv_sem=w_recv.at[2, which],
-                device_id={"dp": sibling},
-                device_id_type=MESH,
-            )
-        )
+    line = Line(None, None, None)
+    greet(
+        [{"tensor": peer} for peer in (sq.across, sq.down, sq.far)] + [{"dp": line.sibling}]
+    )
     weight_load.wait()
     seq_load.wait()
 
@@ -1631,9 +1677,6 @@
         v_ref[here, :] = value.astype(BF16)
         vt[:, here] = value.T.astype(BF16)
 
-    for copies in taken:
-        for copy in copies:
-            copy.start()
     part, part_low = scratch[0], scratch[5]
     scatters = (ChunkScatter(sq, *scratch[:5]), ChunkScatter(sq, *scratch[5:10]))
 
@@ -1695,20 +1738,19 @@
 
     gather = ChunkGather(sq, normed_ref, mlp_out, gather_send, gather_recv)
     gather.start()
-    own = pltpu.make_async_copy(normed_ref, mlp_out.at[0], own_sem.at[0])
+    own = pltpu.make_async_copy(normed_ref, mlp_out.at[0], own_sem)
     own.start()
-    for chunk in range(1, 4):
+    gather.wait_chunk(1)
+    weights = WeightSpread(
+        sq, line, weight_hbm, h_table, w_out_all, h_all, w_own, w_send, w_recv
+    )
+    weights.start()
+    for chunk in range(2, 4):
         gather.wait_chunk(chunk)
-    for copies, onward in zip(taken, passed_on):
-        for copy in copies:
-            copy.wait_recv()
-        onward.start()
-    for copies, onward in zip(taken, passed_on):
-        for copy in copies:
-            copy.wait_send()
-        onward.wait()
     own.wait()
-    own_h.wait()
+    for which in range(3):
+        weights.pass_on(which)
+    weights.finish()
     gather.finish()
     for scatter in scatters:
         scatter.finish()
@@ -1748,9 +1790,10 @@
             pltpu.VMEM((HD, LEN), BF16),
             pltpu.VMEM((rows, LANES), F32),
             pltpu.SemaphoreType.DMA((2,)),
-            pltpu.SemaphoreType.DMA((2,)),
+            pltpu.SemaphoreType.DMA,
             pltpu.SemaphoreType.DMA((6,)),
             pltpu.SemaphoreType.DMA((6,)),
+            pltpu.SemaphoreType.DMA,
             pltpu.SemaphoreType.DMA((3, 3)),
             pltpu.SemaphoreType.DMA((3, 3)),
         ]
@@ -1772,26 +1815,26 @@
     resid_ref,
     total_ref,
     cot_ref,
-    layer_ref,
+    layer_hbm,
     gains_ref,
     weight_hbm,
     w_out_hbm,
     seq_hbm,
-    q_ref,
-    k_ref,
-    kt_ref,
-    v_ref,
-    attended_ref,
+    q_hbm,
+    k_hbm,
+    kt_hbm,
+    v_hbm,
+    attended_hbm,
     inverse_ref,
-    cos_ref,
-    sin_ref,
-    low_ref,
+    cos_hbm,
+    sin_hbm,
+    low_hbm,
     d_table,
     h_all,
     k_table,
-    normed_ref,
+    normed_hbm,
     low_out_ref,
-    grad_mlp_ref,
+    grad_mlp_hbm,
     low_down_ref,
     f_ref,
     o_ref,
@@ -1802,6 +1845,17 @@
     keyval_out,
     gateup_out,
     resid_out,
+    q_ref,
+    k_ref,
+    kt_ref,
+    v_ref,
+    attended_ref,
+    cos_ref,
+    sin_ref,
+    low_ref,
+    normed_ref,
+    grad_mlp_ref,
+    layer_ref,
     weight,
     w_out,
     work,
@@ -1829,6 +1883,7 @@
     hk_land,
     hk_recv,
     load_sem,
+    late_sem,
     att_sends,
     att_recvs,
     f_sem,
@@ -1858,8 +1913,28 @@
         weight_hbm.at[:, pl.ds(0, qkv_width)], weight, load_sem.at[0]
     )
     seq_load = pltpu.make_async_copy(seq_hbm, buf, load_sem.at[1])
+    late = [
+        pltpu.make_async_copy(source, target, late_sem.at[which])
+        for which, (source, target) in enumerate(
+            (
+                (q_hbm, q_ref),
+                (k_hbm, k_ref),
+                (kt_hbm, kt_ref),
+                (v_hbm, v_ref),
+                (attended_hbm, attended_ref),
+                (cos_hbm, cos_ref),
+                (sin_hbm, sin_ref),
+                (low_hbm, low_ref),
+                (normed_hbm, normed_ref),
+                (grad_mlp_hbm, grad_mlp_ref),
+                (layer_hbm, layer_ref),
+            )
+        )
+    ]
     loads[0].start()
     loads[1].start()
+    for copy in late:
+        copy.start()
     weight_load.start()
     seq_load.start()
     peers = [{"tensor": peer} for peer in (sq.across, sq.down, sq.far)]
@@ -1921,6 +1996,8 @@
     part, part_low = scratch[0], scratch[5]
     scatters = (ChunkScatter(sq, *scratch[:5]), ChunkScatter(sq, *scratch[5:10]))
 
+    for copy in late:
+        copy.wait()
     d_turned[...] = jnp.zeros_like(d_turned)
     low_grads = (
         (turned(low_gu)[GATE.start : UP.stop], normed_ref, slice(GATE.start, UP.stop)),
@@ -2166,6 +2243,9 @@
         scatter.finish()
 
 
+LATE = (10, 11, 12, 13, 14, 16, 17, 18, 22, 24, 5)
+
+
 def attn_back_fused(scalars, arrays, grad_shapes, dp, total):
     anywhere = pl.BlockSpec(memory_space=pl.ANY)
     vmem = pl.BlockSpec(memory_space=pltpu.VMEM)
@@ -2174,7 +2254,9 @@
     weight, q, f_in = arrays[7], arrays[10], arrays[-1]
     q_width = q.shape[1]
     specs = [smem, smem] + [vmem] * len(arrays)
-    specs[9] = specs[10] = specs[11] = anywhere
+    late = [arrays[which] for which in LATE]
+    for which in LATE + (7, 8, 9):
+        specs[2 + which] = anywhere
     outs = [jax.ShapeDtypeStruct((rows, model), BF16)]
     outs += [jax.ShapeDtypeStruct(shape, F32) for shape in grad_shapes]
     d_rows = model // total
@@ -2185,6 +2267,7 @@
         in_specs=specs,
         out_specs=(vmem,) * len(outs),
         scratch_shapes=[
+            *(pltpu.VMEM(array.shape, array.dtype) for array in late),
             pltpu.VMEM((model, q_width + 2 * HD), BF16),
             pltpu.VMEM((2, model, q_width), BF16),
             pltpu.VMEM((rows, model), F32),
@@ -2212,6 +2295,7 @@
             pltpu.VMEM((4, dp // 4, 4 * RANK, LANES), BF16),
             pltpu.VMEM((dp, 4 * RANK, LANES), BF16),
             pltpu.SemaphoreType.DMA((6,)),
+            pltpu.SemaphoreType.DMA((len(late),)),
             pltpu.SemaphoreType.DMA((3, 2)),
             pltpu.SemaphoreType.DMA((3, 2)),
             pltpu.SemaphoreType.DMA((dp,)),
@@ -2264,18 +2348,16 @@
     key_cols = lax.dynamic_slice_in_dim(key_weight, lay.kv_head * HD, HD, 1)
     value_cols = lax.dynamic_slice_in_dim(value_weight, lay.kv_head * HD, HD, 1)
     attn_shard = jnp.concatenate([query_weight, key_cols, value_cols, out_weight.T], axis=1)
-    attn_w = lax.all_gather(attn_shard, "dp", axis=0, tiled=True)
     gate_up_shard = jnp.concatenate([gate_weight, up_weight], axis=1)
     down_shard = down_weight.T
     attn_shard, gate_up_shard, down_shard = lax.optimization_barrier(
         (attn_shard, gate_up_shard, down_shard)
     )
-    gate_up_w = lax.all_gather(gate_up_shard, "dp", axis=0, tiled=True)
     qkv_width = head_width + 2 * HD
 
     cosine, sine = tables(LEN, HD)
     if count == 4 and lay.dp == 8:
-        seq_attn, all_ids, d_tab, f_tab, h_tab, k_tab = front(
+        seq_attn, all_ids, d_tab, f_tab, h_tab, k_tab, attn_w = front(
             jnp.broadcast_to(adapter_ids, (8, LANES)),
             layer_in,
             norm_gains,
@@ -2300,9 +2382,13 @@
                 ],
                 axis=1,
             ),
+            attn_shard,
             lay.dp,
             (D, hidden_here, head_width, HD),
         )
+        attn_w = attn_w.reshape(D, -1)
+        gate_up_shard, attn_w = lax.optimization_barrier((gate_up_shard, attn_w))
+        gate_up_w = lax.all_gather(gate_up_shard, "dp", axis=0, tiled=True)
         (
             queries,
             keys,
@@ -2330,7 +2416,16 @@
             layer_in,
             norm_gains,
         )
-        layer_out, grad_mlp, low_gu, low_down, hidden, slope, gelu, down_w = mlp_fused(
+        (
+            layer_out,
+            grad_mlp,
+            low_gu,
+            low_down,
+            hidden,
+            slope,
+            gelu,
+            down_w,
+        ) = mlp_fused(
             lengths,
             seq_mlp,
             gate_up_w,
@@ -2410,6 +2505,9 @@
             grads[which] = jnp.swapaxes(grads[which], 1, 2)
         return (layer_out, *grads)
 
+    attn_w = lax.all_gather(attn_shard, "dp", axis=0, tiled=True)
+    gate_up_w = lax.all_gather(gate_up_shard, "dp", axis=0, tiled=True)
+
     all_ids = lax.all_gather(adapter_ids[:, 0], "dp", axis=0, tiled=True)
     group_hot = (all_ids[:, None] == jnp.arange(NA, dtype=jnp.int32)[None, :]).astype(BF16)
 

time: 594 us -> 587 us (0.988)
  waiting for transfers between devices: 34.8 us -> 14.2 us
  Pallas kernels: 524 us -> 537 us
    all_gather x1 -> x0, waiting for transfers between devices: 15 us -> none  [per_device(): attn_w = lax.all_gather(attn_shard, 'dp', axis=0, tiled=True)]
    pallas_call x1, Pallas kernels: 62.7 us -> 77.6 us  [front(): pl.pallas_call(front_kernel, out_shape=(jax.ShapeDtypeStruct((4 * rows, m...]
  transfers between devices with their start and end apart: 2 -> 1, of which waited for: 2 -> 1; matrix products, arithmetic and copies ran while one was open for 1% -> 1% of each run, Pallas kernels for 39% -> 29%
where the time goes in v8:
time: 587 us; the launch traced here: 586 us
  Pallas kernels  537 us (91%)
  between operations  15.6 us (3%)
  waiting for transfers between devices  14.2 us (2%)
  local copies, waits for them, and re-layouts  13.5 us (2%)
  other arithmetic  6.52 us (1%)
    pallas_call x1, Pallas kernels, attn_fused(): pl.pallas_call(functools.partial(attn_kernel, rows), out_shape=(jax.Shape...  168 us
    pallas_call x1, Pallas kernels, mlp_fused(): pl.pallas_call(functools.partial(mlp_kernel, rows), out_shape=(jax.ShapeD...  110 us
    pallas_call x1, Pallas kernels, attn_back_fused(): pl.pallas_call(functools.partial(attn_back_kernel, rows), out_shape=tuple...  91.5 us
    pallas_call x1, Pallas kernels, mlp_back_fused(): pl.pallas_call(functools.partial(mlp_back_kernel, rows), out_shape=(jax.S...  89 us
    pallas_call x1, Pallas kernels, front(): pl.pallas_call(front_kernel, out_shape=(jax.ShapeDtypeStruct((4 * rows, m...  77.6 us
    all_gather x1, waiting for transfers between devices, per_device(): gate_up_w = lax.all_gather(gate_up_shard, 'dp', axis=0, tiled=True)  14.2 us
  transfers between devices with their start and end apart: 1, of which 1 were waited for; matrix products, arithmetic and copies ran while one was open for 1% of the time, Pallas kernels for 29%

profile of v8, /device:TPU:0, one launch (start us, length us, event | category | flops | bytes accessed | tf_op | source)
XLA Modules:
  0.0 586.4 jit_solution(18343305865383282005)
XLA Ops:
  7.2 0.0 all-gather.2.cloned.1.call-start
  7.9 1.0 copy.29
  9.0 3.5 pad_maximum_fusion
  12.5 0.0 copy-start.21
  12.5 0.0 copy-start.3
  12.5 1.1 constant_dynamic-slice_fusion
  13.7 0.1 pad_maximum_fusion.1.shard_hbm
  13.9 0.2 copy-done
  14.1 77.6 %front.1 = (bf16[1024,2304]{1,0:T(8,128)(2,1)}, s32[8,8,128]{2,1,0:T(8,128)S(1)}, bf16[2304,128]{1,0:T(8,128)(2,1)S(1)}, bf16[2304,128]{1,0:T(8,128)(2,1)S(1)}, ...) custom-call(s32[8,128]{1,0:T(8,128)S(1)} %broadcast_in_dim.10.ids_ref, ...), custom_call_target="tpu_custom_call" | custom-call | tf_op jit(solution)/shard_map/front/pallas_call | solution.py:881
  91.8 0.0 copy-start.1
  91.8 0.8 copy-done.1
  92.6 0.8 copy-done.2
  93.4 0.6 copy-done.4
  94.0 0.7 copy-done.5
  94.7 0.0 all-gather.2.cloned.1.call-update
  95.4 2.8 fusion
  98.2 168.5 %attn.1 = (bf16[1024,512]{1,0:T(8,128)(2,1)}, bf16[1024,256]{1,0:T(8,128)(2,1)}, bf16[256,1024]{1,0:T(8,128)(2,1)}, bf16[1024,256]{1,0:T(8,128)(2,1)}, bf16[1024...) custom-call(s32[1]{0:T(128)S(6)} %copy.39.length_ref, ...), custom_call_target="tpu_custom_call" | custom-call | tf_op jit(solution)/shard_map/attn/pallas_call | solution.py:1767
  266.7 0.8 slice_reduce_fusion.ids_ref
  267.4 14.2 %all-gather.2.cloned.1.call-done.gu_hbm = bf16[2304,4608]{1,0:T(8,128)(2,1)} async-done(((bf16[288,4608]{1,0:T(8,128)(2,1)}), bf16[2304,4608]{1,0:T(8,128)(2,1)}) %all-gather.2.cloned.1.call-update) | async-done | bytes 21233680 | tf_op jit(solution)/shard_map/all_gather | solution.py:2391
  281.6 110.0 %mlp.1 = (bf16[256,2304]{1,0:T(8,128)(2,1)}, bf16[256,2304]{1,0:T(8,128)(2,1)}, bf16[4,256,128]{2,1,0:T(8,128)(2,1)}, bf16[256,128]{1,0:T(8,128)(2,1)}, bf16[4,2...) custom-call(s32[1]{0:T(128)S(6)} %copy.39.length_ref, ...), custom_call_target="tpu_custom_call" | custom-call | tf_op jit(solution)/shard_map/mlp/pallas_call | solution.py:1303
  391.6 89.0 %mlp_back.1 = (f32[256,2304]{1,0:T(8,128)}, f32[256,128]{1,0:T(8,128)}, bf16[4,2,48,288]{3,2,1,0:T(8,128)(2,1)}) custom-call(bf16[256,2304]{1,0:T(8,128)(2,1)} %get-tuple-element.69.g_ref.grad_mlp_hbm, bf16[2304,2304]{1,0:T(8,128)(2,1)} %bitcast.19, bf16[2304,4608]{1,0:T(8,128)(2,1)} %all-gather.2.cloned.1.call-done.gu_hbm, ...), custom_call_target="tpu_custom_call" | custom-call | tf_op jit(solution)/shard_map/mlp_back/pallas_call | solution.py:678
  480.6 91.5 %attn_back.1 = (bf16[256,2304]{1,0:T(8,128)(2,1)}, f32[8,72,80]{2,1,0:T(8,128)}, f32[8,16,64]{2,1,0:T(8,128)}, f32[8,16,288]{2,1,0:T(8,128)}, f32[8,16,64]{2,1,0...) custom-call(s32[8]{0:T(128)} %slice_reduce_fusion.ids_ref, ...), custom_call_target="tpu_custom_call" | custom-call | tf_op jit(solution)/shard_map/attn_back/pallas_call | solution.py:2264
  572.1 1.0 copy.41
  573.1 0.7 copy-done.7
  573.8 1.0 copy.42
  574.9 0.7 copy.43
  575.6 0.6 copy.44
  576.2 0.7 copy.45
  576.9 0.6 copy.46
  577.5 0.7 copy.47
  578.2 0.7 copy.48
  578.9 0.7 copy.49
  (42 shorter events, 0.2 us)
Async XLA Ops:
  7.2 274.5 %all-gather.2.cloned.1.call-start = ((), (), s32[]{:S(2)}) async-start(), calls=%async_computation | async-start | bytes 23887872 | tf_op jit(solution)/shard_map/all_gather | solution.py:2391
  8.9 4.7 copy-start.9
  8.9 4.7 copy-start.10
  12.4 1.3 copy-start.17
  12.4 1.3 copy-start.13
  12.5 1.4 copy-start.16
  12.5 1.4 copy-start.20
  12.5 1.4 copy-start.21
  12.5 1.4 copy-start.22
  12.5 1.6 copy-start
  12.5 1.6 copy-start.3
  91.8 0.8 copy-start.1
  92.6 0.8 copy-start.2
  93.4 0.6 copy-start.4
  94.0 0.7 copy-start.5
  480.6 91.5 %copy-start.6 = (bf16[256,2304]{1,0:T(8,128)(2,1)S(1)}, bf16[256,2304]{1,0:T(8,128)(2,1)}, u32[]{:S(2)}) copy-start(bf16[256,2304]{1,0:T(8,128)(2,1)} %get-tuple-element.112) | copy-start | bytes 3538948
  572.1 1.7 copy-start.7
  573.8 1.1 copy-start.11
  573.8 1.8 copy-start.19
  573.8 2.4 copy-start.12
  573.8 3.1 copy-start.18
  573.8 3.7 copy-start.15
  573.8 4.4 copy-start.8
  573.8 5.1 copy-start.14
Sparse Core Ops, SparseCore 0:
  94.8 186.7 all-gather.1

commit v9 on v8

--- a/solution.py
+++ b/solution.py
@@ -1015,56 +1015,70 @@
                 self.copy(place, 2, part).wait_send()
 
 
-class WeightSpread:
-    def __init__(self, sq, line, weight_hbm, h_table, w_out_all, h_all, own_sem, send_sem, recv_sem):
-        model, q_width = w_out_all.shape[1:]
-        share = model // 2
+class HalfSpread:
+    def __init__(self, sq, line, weight, columns_from, target, send_sem, recv_sem):
+        model, width = target.shape[1:]
+        share, part_rows = model // 2, model // 4
+        cols = pl.ds(columns_from, width)
+
+        def rows(part):
+            return pl.ds(pl.multiple_of(line.core * share + part * part_rows, 8), part_rows)
+
+        self.first, self.second, self.onward, self.sibling = [], [], [], []
+        for order, group in enumerate((self.first, self.second)):
+            for link in range(2):
+                part = link if order == 0 else 1 - link
+                sem = 2 * order + link
+                group.append(
+                    remote(
+                        weight.at[rows(part), cols],
+                        target.at[sq.me, rows(part)],
+                        send_sem.at[sem],
+                        recv_sem.at[sem],
+                        sq.links[link],
+                    )
+                )
+        for link in range(2):
+            block = target.at[sq.links[link], rows(link)]
+            self.onward.append(
+                remote(
+                    block, block, send_sem.at[4 + link], recv_sem.at[4 + link], sq.links[1 - link]
+                )
+            )
         mine = pl.ds(pl.multiple_of(line.core * share, 8), share)
-        first = weight_hbm.shape[1] - q_width
-        self.own = pltpu.make_async_copy(h_table, h_all.at[sq.me], own_sem)
-        self.taken, self.onward = [], []
         for which, peer in enumerate((sq.across, sq.down, sq.far)):
-            pairs = (
-                (weight_hbm.at[mine, pl.ds(first, q_width)], w_out_all.at[sq.me, mine]),
-                (h_table, h_all.at[sq.me]),
-            )
-            self.taken.append(
-                [
-                    remote(
-                        source, target, send_sem.at[item, which], recv_sem.at[item, which], peer
-                    )
-                    for item, (source, target) in enumerate(pairs)
-                ]
-            )
-            block = w_out_all.at[peer, mine]
-            self.onward.append(
+            block = target.at[peer, mine]
+            self.sibling.append(
                 pltpu.make_async_remote_copy(
                     src_ref=block,
                     dst_ref=block,
-                    send_sem=send_sem.at[2, which],
-                    recv_sem=recv_sem.at[2, which],
+                    send_sem=send_sem.at[6 + which],
+                    recv_sem=recv_sem.at[6 + which],
                     device_id={"dp": line.sibling},
                     device_id_type=MESH,
                 )
             )
 
     def start(self):
-        self.own.start()
-        for copies in self.taken:
-            for copy in copies:
-                copy.start()
-
-    def pass_on(self, which):
-        for copy in self.taken[which]:
+        for copy in self.first + self.second:
+            copy.start()
+
+    def forward(self):
+        for copy, onward in zip(self.first, self.onward):
             copy.wait_recv()
-        self.onward[which].start()
+            onward.start()
+
+    def share(self):
+        for copy in self.second + self.onward:
+            copy.wait_recv()
+        for copy in self.sibling:
+            copy.start()
 
     def finish(self):
-        self.own.wait()
-        for copies, onward in zip(self.taken, self.onward):
-            for copy in copies:
-                copy.wait_send()
-            onward.wait()
+        for copy in self.first + self.second + self.onward:
+            copy.wait_send()
+        for copy in self.sibling:
+            copy.wait()
 
 
 ARRIVALS = ((0, 1, 2, 3), (1, 0, 2, 3), (2, 1, 3, 0), (3, 2, 1, 0))
@@ -1076,6 +1090,7 @@
     x_hbm,
     gu_hbm,
     shard_hbm,
+    weight_hbm,
     d_ref,
     f_table,
     resid_ref,
@@ -1089,6 +1104,7 @@
     slope_out,
     gelu_out,
     down_out,
+    w_kv_all,
     work,
     low_sum,
     lows,
@@ -1109,6 +1125,8 @@
     passed,
     part_send,
     part_recv,
+    w_send,
+    w_recv,
     *low_scratch,
 ):
     sq = Square(rows)
@@ -1145,6 +1163,9 @@
     line.greet([{"tensor": sq.across}, {"tensor": sq.down}])
     own_shard.wait()
     line.start()
+    keys_from = (weight_hbm.shape[1] - w_kv_all.shape[2]) // 2
+    spread = HalfSpread(sq, line, weight_hbm, keys_from, w_kv_all, w_send, w_recv)
+    spread.start()
     seq_load.wait()
 
     @pl.loop(0, 4)
@@ -1187,6 +1208,8 @@
             @pl.when(step == part_at)
             def _(part_of=part_of):
                 line.arrive(1, part_of)
+                if part_of == 0:
+                    spread.forward()
 
     keep_hidden = pltpu.make_async_copy(hidden, hidden_out, keep_sem.at[0])
     keep_hidden.start()
@@ -1219,6 +1242,8 @@
         for half in range(2):
             for distance, piece in arrivals.get((turn, half), ()):
                 line.arrive(distance, piece)
+            if (turn, half) == (1, 0):
+                spread.share()
             line.wait_sibling(place, half)
             scatter = scatter_at(place, half)
 
@@ -1274,6 +1299,7 @@
         scatter_at(place, half).finish()
     low_scatter.finish()
     line.finish()
+    spread.finish()
     for step in (steps - 2, steps - 1):
         for copy in stores(step, step % 2):
             copy.wait()
@@ -1291,7 +1317,7 @@
         work[:, here] += nt(low[...], table[here, :])
 
 
-def mlp_fused(lengths, seq, gu_w, shard, d_tab, f_tab, resid, cotangent, gains, dp):
+def mlp_fused(lengths, seq, gu_w, shard, attn_w, d_tab, f_tab, resid, cotangent, gains, dp):
     chunks, rows, model = seq.shape
     width = shard.shape[1]
     tile = 384
@@ -1311,9 +1337,10 @@
             saved,
             saved,
             jax.ShapeDtypeStruct((dp,) + shard.shape, BF16),
+            jax.ShapeDtypeStruct((4, model, 2 * HD), BF16),
         ),
-        in_specs=[pl.BlockSpec(memory_space=pltpu.SMEM)] + [anywhere] * 3 + [vmem] * 5,
-        out_specs=(vmem,) * 4 + (anywhere,) * 4,
+        in_specs=[pl.BlockSpec(memory_space=pltpu.SMEM)] + [anywhere] * 4 + [vmem] * 5,
+        out_specs=(vmem,) * 4 + (anywhere,) * 5,
         scratch_shapes=[
             pltpu.VMEM((rows, model), F32),
             pltpu.VMEM((rows, LANES), F32),
@@ -1335,13 +1362,15 @@
             pltpu.VMEM((dp, 2, half, wide), BF16),
             pltpu.SemaphoreType.DMA((dp, 6, 1)),
             pltpu.SemaphoreType.DMA((dp, 6, 1)),
+            pltpu.SemaphoreType.DMA((9,)),
+            pltpu.SemaphoreType.DMA((9,)),
         ]
         + scatter_scratch(rows, LANES),
         compiler_params=pltpu.CompilerParams(
             collective_id=7, has_side_effects=True, vmem_limit_bytes=62 * 1024 * 1024
         ),
         name="mlp",
-    )(lengths, seq, gu_w, shard, d_tab, f_tab, resid, cotangent, gains)
+    )(lengths, seq, gu_w, shard, attn_w, d_tab, f_tab, resid, cotangent, gains)
 
 
 class Layout:
@@ -1621,6 +1650,7 @@
     normed_ref,
     mlp_out,
     w_out_all,
+    w_q_all,
     h_all,
     seq,
     weight,
@@ -1630,7 +1660,8 @@
     own_sem,
     gather_send,
     gather_recv,
-    w_own,
+    h_send,
+    h_recv,
     w_send,
     w_recv,
     *scratch,
@@ -1650,6 +1681,14 @@
     greet(
         [{"tensor": peer} for peer in (sq.across, sq.down, sq.far)] + [{"dp": line.sibling}]
     )
+    out_spread = HalfSpread(
+        sq, line, weight_hbm, qkv_width, w_out_all, w_send.at[0], w_recv.at[0]
+    )
+    q_spread = HalfSpread(sq, line, weight_hbm, 0, w_q_all, w_send.at[1], w_recv.at[1])
+    out_spread.start()
+    h_spread = sq.spread(lambda peer: h_table, h_all, h_send, h_recv)
+    for copy in h_spread:
+        copy.start()
     weight_load.wait()
     seq_load.wait()
 
@@ -1677,6 +1716,7 @@
         v_ref[here, :] = value.astype(BF16)
         vt[:, here] = value.T.astype(BF16)
 
+    out_spread.forward()
     part, part_low = scratch[0], scratch[5]
     scatters = (ChunkScatter(sq, *scratch[:5]), ChunkScatter(sq, *scratch[5:10]))
 
@@ -1741,16 +1781,17 @@
     own = pltpu.make_async_copy(normed_ref, mlp_out.at[0], own_sem)
     own.start()
     gather.wait_chunk(1)
-    weights = WeightSpread(
-        sq, line, weight_hbm, h_table, w_out_all, h_all, w_own, w_send, w_recv
-    )
-    weights.start()
+    q_spread.start()
+    out_spread.share()
     for chunk in range(2, 4):
         gather.wait_chunk(chunk)
     own.wait()
-    for which in range(3):
-        weights.pass_on(which)
-    weights.finish()
+    q_spread.forward()
+    for copy in h_spread:
+        copy.wait()
+    out_spread.finish()
+    q_spread.share()
+    q_spread.finish()
     gather.finish()
     for scatter in scatters:
         scatter.finish()
@@ -1780,10 +1821,11 @@
             jax.ShapeDtypeStruct((rows, model), BF16),
             jax.ShapeDtypeStruct((4, rows, model), BF16),
             jax.ShapeDtypeStruct((4, model, q_width), BF16),
+            jax.ShapeDtypeStruct((4, model, q_width), BF16),
             jax.ShapeDtypeStruct((4, q_width, LANES), BF16),
         ),
         in_specs=[pl.BlockSpec(memory_space=pltpu.SMEM)] + [anywhere] * 2 + [vmem] * 7,
-        out_specs=(vmem,) * 11 + (anywhere,) * 3,
+        out_specs=(vmem,) * 11 + (anywhere,) * 4,
         scratch_shapes=[
             pltpu.VMEM((4, rows, model), BF16),
             pltpu.VMEM(weight.shape, BF16),
@@ -1793,9 +1835,10 @@
             pltpu.SemaphoreType.DMA,
             pltpu.SemaphoreType.DMA((6,)),
             pltpu.SemaphoreType.DMA((6,)),
-            pltpu.SemaphoreType.DMA,
-            pltpu.SemaphoreType.DMA((3, 3)),
-            pltpu.SemaphoreType.DMA((3, 3)),
+            pltpu.SemaphoreType.DMA((3,)),
+            pltpu.SemaphoreType.DMA((4,)),
+            pltpu.SemaphoreType.DMA((2, 9)),
+            pltpu.SemaphoreType.DMA((2, 9)),
         ]
         + scatter_scratch(rows, model, model // tile_of(model))
         + scatter_scratch(rows, LANES),
@@ -1819,6 +1862,8 @@
     gains_ref,
     weight_hbm,
     w_out_hbm,
+    w_q_hbm,
+    w_kv_hbm,
     seq_hbm,
     q_hbm,
     k_hbm,
@@ -1856,8 +1901,8 @@
     normed_ref,
     grad_mlp_ref,
     layer_ref,
-    weight,
-    w_out,
+    slots,
+    total,
     work,
     g_ref,
     low_sum,
@@ -1866,11 +1911,14 @@
     att,
     low_own,
     low_all,
+    part_low,
+    q_land,
+    kv_land,
+    low_land,
     q_grad,
     k_sum,
     v_sum,
     kv_grad,
-    joined,
     d_turned,
     h_turned,
     k_turned,
@@ -1886,13 +1934,14 @@
     late_sem,
     att_sends,
     att_recvs,
+    back_sends,
+    back_recvs,
     f_sem,
     d_sem,
     hk_sem,
     group_send,
     group_recv,
     line_recv,
-    *scratch,
 ):
     sq = Square(rows)
     dp = lax.axis_size("dp")
@@ -1903,16 +1952,18 @@
     q_width = q_ref.shape[1]
     qkv_width = q_width + 2 * HD
     others = (sq.far, sq.across, sq.down)
+    arrivals = ((sq.down, 2), (sq.far, 0), (sq.across, 1))
     sources = [w_out_hbm.at[peer] for peer in others]
     sources.append(weight_hbm.at[:, pl.ds(qkv_width, q_width)])
+    sources.append(weight_hbm.at[:, pl.ds(0, q_width)])
+    sources.append(weight_hbm.at[:, pl.ds(q_width, 2 * HD)])
+    for peer, unused in arrivals:
+        sources += [w_q_hbm.at[peer], w_kv_hbm.at[peer]]
     loads = [
-        pltpu.make_async_copy(source, w_out.at[which % 2], load_sem.at[2 + which])
+        pltpu.make_async_copy(source, slots.at[which % 4], load_sem.at[1 + which])
         for which, source in enumerate(sources)
     ]
-    weight_load = pltpu.make_async_copy(
-        weight_hbm.at[:, pl.ds(0, qkv_width)], weight, load_sem.at[0]
-    )
-    seq_load = pltpu.make_async_copy(seq_hbm, buf, load_sem.at[1])
+    seq_load = pltpu.make_async_copy(seq_hbm, buf, load_sem.at[0])
     late = [
         pltpu.make_async_copy(source, target, late_sem.at[which])
         for which, (source, target) in enumerate(
@@ -1931,11 +1982,10 @@
             )
         )
     ]
-    loads[0].start()
-    loads[1].start()
+    for copy in loads[:4]:
+        copy.start()
     for copy in late:
         copy.start()
-    weight_load.start()
     seq_load.start()
     peers = [{"tensor": peer} for peer in (sq.across, sq.down, sq.far)]
     peers += [{"dp": lax.rem(d + step, dp)} for step in range(1, dp)]
@@ -1959,42 +2009,53 @@
         work[here, :] = mid
         g_ref[here, :] = norm_back(total_ref[here, :], gains_ref[1:2, :], mid).astype(BF16)
 
-    low_own[...] = band(nn(g_ref[...], d_table[...]), OUT).astype(BF16)
+    low_out = band(nn(g_ref[...], d_table[...]), OUT).astype(BF16)
+    low_own[...] = turned(low_out)[OUT]
     pl.semaphore_wait(pltpu.get_barrier_semaphore(), len(peers))
     heads_out_copies = []
     for which, peer in enumerate(others + (sq.me,)):
         loads[which].wait()
-        grads = (nn(g_ref[...], w_out[which % 2]) + nt(low_own[...], h_all[peer])).astype(BF16)
-        if which < 2:
-            loads[which + 2].start()
+        grads = (nn(g_ref[...], slots[which]) + nt(low_out, h_all[peer])).astype(BF16)
+        loads[which + 4].start()
         if which == 3:
             att[sq.me] = grads
             low_all[sq.me] = low_own[...]
             continue
         att_send[which] = grads
-        copies = (
+        copies = tuple(
             remote(
-                att_send.at[which],
-                att.at[sq.me],
-                att_sends.at[which, 0],
-                att_recvs.at[which, 0],
-                peer,
-            ),
-            remote(
-                low_own,
-                low_all.at[sq.me],
-                att_sends.at[which, 1],
-                att_recvs.at[which, 1],
-                peer,
-            ),
+                source, target.at[sq.me], att_sends.at[which, item], att_recvs.at[which, item], peer
+            )
+            for item, (source, target) in enumerate(
+                ((att_send.at[which], att), (low_own, low_all))
+            )
         )
         for copy in copies:
             copy.start()
         heads_out_copies.append(copies)
     line = []
     line += along(lambda k: f_ref.at[k // 2, lax.rem(k, 2)], f_recv, f_sem, line_recv.at[0])
-    part, part_low = scratch[0], scratch[5]
-    scatters = (ChunkScatter(sq, *scratch[:5]), ChunkScatter(sq, *scratch[5:10]))
+    back = []
+    for which, peer in enumerate(others):
+        here = pl.ds(pl.multiple_of(peer * rows, rows), rows)
+        back.append(
+            tuple(
+                remote(
+                    source,
+                    target.at[sq.me],
+                    back_sends.at[which, item],
+                    back_recvs.at[which, item],
+                    peer,
+                )
+                for item, (source, target) in enumerate(
+                    (
+                        (q_grad.at[here], q_land),
+                        (kv_grad.at[here], kv_land),
+                        (part_low.at[peer], low_land),
+                    )
+                )
+            )
+        )
 
     for copy in late:
         copy.wait()
@@ -2020,22 +2081,22 @@
 
     @pl.loop(0, 4)
     def _(turn):
-        for step, which in ((1, 1), (2, 2), (3, 0)):
-
-            @pl.when(turn == step)
+        for step, (unused, which) in enumerate(arrivals):
+
+            @pl.when(turn == step + 1)
             def _(which=which):
                 for copy in heads_out_copies[which]:
                     copy.wait_recv()
 
-        is_own, is_far = (3 - turn) // 3, turn // 3
-        is_down = turn // 2 - is_far
+        is_own, is_across = (3 - turn) // 3, turn // 3
+        is_far = turn // 2 - is_across
         block = (
             sq.me * is_own
             + sq.far * is_far
-            + sq.down * is_down
-            + sq.across * (1 - is_own - is_far - is_down)
-        )
-        low_turned = turned(low_all[block])[OUT]
+            + sq.across * is_across
+            + sq.down * (1 - is_own - is_far - is_across)
+        )
+        low_turned = low_all[block]
         h_turned[:RANK, :] += nn(
             low_turned, attended_ref[pl.ds(pl.multiple_of(block * rows, rows), rows), :]
         )
@@ -2072,69 +2133,61 @@
                             q_back[h * half : (h + 1) * half], cos_ref[here, :], sin_ref[here, :]
                         ).astype(BF16)
 
-    weight_load.wait()
+        for step, (unused, which) in enumerate(arrivals):
+
+            @pl.when(turn == step + 1)
+            def _(which=which):
+                back[which][0].start()
+
     kv_grad[:, :HD] = rotate_back(k_sum[...], cos_ref[...], sin_ref[...]).astype(BF16)
     kv_grad[:, HD:] = v_sum[...].astype(BF16)
+    for copies in back:
+        copies[1].start()
 
     @pl.loop(0, 4)
-    def _(step):
-        chunk = far_first(step)
-        for side in range(2):
-            here = pl.ds(chunk_start(sq, chunk, side), half)
-            place = pl.ds(side * half, half)
-            joined[chunk, place, :q_width] = q_grad[here, :]
-            joined[chunk, place, q_width:] = kv_grad[here, :]
-        part_low[chunk] = (
-            band(nn(joined[chunk, :, :q_width], h_all[sq.me]), QUERY)
-            + band(nn(joined[chunk, :, q_width : q_width + HD], k_table[...]), KEY)
-            + band(nn(joined[chunk, :, q_width + HD :], k_table[...]), VALUE)
+    def _(block):
+        here = pl.ds(pl.multiple_of(block * rows, rows), rows)
+        part_low[block] = (
+            band(nn(q_grad[here, :], h_all[sq.me]), QUERY)
+            + band(nn(kv_grad[here, :HD], k_table[...]), KEY)
+            + band(nn(kv_grad[here, HD:], k_table[...]), VALUE)
         ).astype(BF16)
 
+    for copies in back:
+        copies[2].start()
+
+    def add_block(queries, keys_values, which, first):
+        for item in range(2):
+            loads[which + item].wait()
+        low_q, low_kv = which % 4, (which + 1) % 4
+
         @pl.loop(0, model // wide)
-        def _(tile):
-            here = columns(tile, wide)
-            part[chunk, :, here] = nt(joined[chunk], weight[here, :]).astype(BF16)
-
-            @pl.when(step == 0)
-            def _():
-                scatters[0].send(1, tile)
-
-            @pl.when(step == 1)
-            def _():
-                scatters[0].send(0, tile)
-
-        @pl.when(step == 0)
-        def _():
-            scatters[1].send_far()
-
-        @pl.when(step == 1)
-        def _():
-            scatters[1].send_own()
-
+        def _(step):
+            here = columns(step, wide)
+            grad = nt(queries, slots[low_q, here, :]) + nt(keys_values, slots[low_kv, here, :])
+            total[:, here] = grad if first else total[:, here] + grad
+
+        for item in range(2):
+            if which + item + 4 < len(loads):
+                loads[which + item + 4].start()
+
+    own = pl.ds(pl.multiple_of(sq.me * rows, rows), rows)
+    add_block(q_grad[own, :], kv_grad[own, :], 4, True)
     seq_load.wait()
 
     @pl.loop(0, 4)
-    def _(chunk):
-        grad_turned = turned(part_low[chunk])[: VALUE.stop]
-        for side in range(2):
-            here = pl.ds(chunk_start(sq, chunk, side), half)
-            place = slice(side * half, (side + 1) * half)
-            low_turned = turned(low_ref[here, :])
-            mine = joined.at[chunk, pl.ds(side * half, half)]
-            h_turned[RANK : 2 * RANK, :] += nn(low_turned[QUERY], mine[:, :q_width])
-            k_turned[:RANK, :] += nn(low_turned[KEY], mine[:, q_width : q_width + HD])
-            k_turned[RANK : 2 * RANK, :] += nn(low_turned[VALUE], mine[:, q_width + HD :])
-            where_from = chunk_start(sq, chunk, side)
-            block = where_from // rows
-            inside = pl.ds(pl.multiple_of(where_from - block * rows, half), half)
-
-            @pl.loop(0, model // wide)
-            def _(tile):
-                where = columns(tile, wide)
-                d_turned[: VALUE.stop, where] += nn(
-                    grad_turned[:, place],
-                    buf[block, inside, where],
-                )
+    def _(block):
+        here = pl.ds(pl.multiple_of(block * rows, rows), rows)
+        grad_turned = turned(part_low[block])[: VALUE.stop]
+        low_turned = turned(low_ref[here, :])
+        h_turned[RANK : 2 * RANK, :] += nn(low_turned[QUERY], q_grad[here, :])
+        k_turned[:RANK, :] += nn(low_turned[KEY], kv_grad[here, :HD])
+        k_turned[RANK : 2 * RANK, :] += nn(low_turned[VALUE], kv_grad[here, HD:])
+
+        @pl.loop(0, model // wide)
+        def _(step):
+            where = columns(step, wide)
+            d_turned[: VALUE.stop, where] += nn(grad_turned, buf[block, :, where])
 
     @pl.loop(0, model // LANES)
     def _(step):
@@ -2170,8 +2223,10 @@
     for copies in spread:
         for copy in copies:
             copy.start()
-    for scatter in scatters:
-        scatter.pass_on()
+    for step, (peer, which) in enumerate(arrivals):
+        for copy in back[which]:
+            copy.wait_recv()
+        add_block(q_land[peer], kv_land[peer], 6 + 2 * step, False)
     for copies in spread:
         copies[0].wait()
         for copy in copies[1:]:
@@ -2180,25 +2235,22 @@
         d_sum[k] = sum(d_land[k, t].astype(F32) for t in range(4)).astype(BF16)
     line += along(lambda k: d_sum.at[k], d_recv, d_sem, line_recv.at[1])
     line += along(lambda k: hk_land.at[k // 2, lax.rem(k, 2)], hk_recv, hk_sem, line_recv.at[2])
-    scatters[1].collect(low_sum)
+    low_sum[...] = sum(
+        low_land[peer].astype(F32) for peer, unused in arrivals
+    ) + part_low[sq.me].astype(F32)
     low_qkv = low_sum[...].astype(BF16)
-    scatters[0].arrived()
-    landing = scratch[1]
-    low_sum[...] = low_qkv.astype(F32)
+
+    @pl.loop(0, model // wide)
+    def _(step):
+        here = columns(step, wide)
+        total[:, here] += nt(low_qkv, d_table[here, :])
 
     @pl.loop(0, rows // BLOCK)
     def _(step):
         here = pl.ds(pl.multiple_of(step * BLOCK, BLOCK), BLOCK)
-        link = (step * BLOCK) // half
-        there = pl.ds(pl.multiple_of(step * BLOCK - link * half, BLOCK), BLOCK)
-        total = (
-            part[0, here, :].astype(F32)
-            + landing[link, there, :].astype(F32)
-            + landing[4 + link, there, :].astype(F32)
-            + nt(low_sum[here, :].astype(BF16), d_table[...])
-        )
         o_ref[here, :] = (
-            work[here, :] + norm_back(layer_ref[here, :].astype(F32), gains_ref[0:1, :], total)
+            work[here, :]
+            + norm_back(layer_ref[here, :].astype(F32), gains_ref[0:1, :], total[here, :])
         ).astype(BF16)
 
     for item, target in enumerate((f_recv, d_recv, hk_recv)):
@@ -2234,16 +2286,14 @@
     for copies in spread:
         for copy in copies[1:]:
             copy.wait_send()
-    for copies in heads_out_copies:
+    for copies in heads_out_copies + back:
         for copy in copies:
             copy.wait_send()
     for copy in line:
         copy.wait_send()
-    for scatter in scatters:
-        scatter.finish()
-
-
-LATE = (10, 11, 12, 13, 14, 16, 17, 18, 22, 24, 5)
+
+
+LATE = (12, 13, 14, 15, 16, 18, 19, 20, 24, 26, 5)
 
 
 def attn_back_fused(scalars, arrays, grad_shapes, dp, total):
@@ -2251,11 +2301,11 @@
     vmem = pl.BlockSpec(memory_space=pltpu.VMEM)
     smem = pl.BlockSpec(memory_space=pltpu.SMEM)
     rows, model = arrays[0].shape
-    weight, q, f_in = arrays[7], arrays[10], arrays[-1]
+    q, f_in = arrays[12], arrays[-1]
     q_width = q.shape[1]
     specs = [smem, smem] + [vmem] * len(arrays)
     late = [arrays[which] for which in LATE]
-    for which in LATE + (7, 8, 9):
+    for which in LATE + (7, 8, 9, 10, 11):
         specs[2 + which] = anywhere
     outs = [jax.ShapeDtypeStruct((rows, model), BF16)]
     outs += [jax.ShapeDtypeStruct(shape, F32) for shape in grad_shapes]
@@ -2268,21 +2318,24 @@
         out_specs=(vmem,) * len(outs),
         scratch_shapes=[
             *(pltpu.VMEM(array.shape, array.dtype) for array in late),
-            pltpu.VMEM((model, q_width + 2 * HD), BF16),
-            pltpu.VMEM((2, model, q_width), BF16),
+            pltpu.VMEM((4, model, q_width), BF16),
+            pltpu.VMEM((rows, model), F32),
             pltpu.VMEM((rows, model), F32),
             pltpu.VMEM((rows, model), BF16),
             pltpu.VMEM((rows, LANES), F32),
             pltpu.VMEM((4, rows, model), BF16),
             pltpu.VMEM((3, rows, q_width), BF16),
             pltpu.VMEM((4, rows, q_width), BF16),
-            pltpu.VMEM((rows, LANES), BF16),
+            pltpu.VMEM((RANK, rows), BF16),
+            pltpu.VMEM((4, RANK, rows), BF16),
+            pltpu.VMEM((4, rows, LANES), BF16),
+            pltpu.VMEM((4, rows, q_width), BF16),
+            pltpu.VMEM((4, rows, 2 * HD), BF16),
             pltpu.VMEM((4, rows, LANES), BF16),
             pltpu.VMEM((LEN, q_width), BF16),
             pltpu.VMEM((LEN, HD), F32),
             pltpu.VMEM((LEN, HD), F32),
             pltpu.VMEM((LEN, 2 * HD), BF16),
-            pltpu.VMEM((4, rows, q_width + 2 * HD), BF16),
             pltpu.VMEM((LANES, model), F32),
             pltpu.VMEM((2 * RANK, q_width), F32),
             pltpu.VMEM((2 * RANK, HD), F32),
@@ -2294,19 +2347,19 @@
             pltpu.VMEM((dp // 4, 4, 4 * RANK, LANES), BF16),
             pltpu.VMEM((4, dp // 4, 4 * RANK, LANES), BF16),
             pltpu.VMEM((dp, 4 * RANK, LANES), BF16),
-            pltpu.SemaphoreType.DMA((6,)),
+            pltpu.SemaphoreType.DMA((13,)),
             pltpu.SemaphoreType.DMA((len(late),)),
             pltpu.SemaphoreType.DMA((3, 2)),
             pltpu.SemaphoreType.DMA((3, 2)),
+            pltpu.SemaphoreType.DMA((3, 3)),
+            pltpu.SemaphoreType.DMA((3, 3)),
             pltpu.SemaphoreType.DMA((dp,)),
             pltpu.SemaphoreType.DMA((dp,)),
             pltpu.SemaphoreType.DMA((dp,)),
             pltpu.SemaphoreType.DMA((dp + 1, 3)),
             pltpu.SemaphoreType.DMA((dp + 1, 4)),
             pltpu.SemaphoreType.DMA((3,)),
-        ]
-        + scatter_scratch(rows, model, model // tile_of(model))
-        + scatter_scratch(rows, LANES),
+        ],
         compiler_params=pltpu.CompilerParams(
             collective_id=6, has_side_effects=True, vmem_limit_bytes=62 * 1024 * 1024
         ),
@@ -2403,6 +2456,7 @@
             normed_mlp,
             seq_mlp,
             w_out_all,
+            w_q_all,
             h_all,
         ) = attn_fused(
             lengths,
@@ -2425,11 +2479,13 @@
             slope,
             gelu,
             down_w,
+            w_kv_all,
         ) = mlp_fused(
             lengths,
             seq_mlp,
             gate_up_w,
             down_shard,
+            attn_w,
             d_tab,
             f_tab,
             resid_mid,
@@ -2477,6 +2533,8 @@
                     norm_gains,
                     attn_w,
                     w_out_all,
+                    w_q_all,
+                    w_kv_all,
                     seq_attn.reshape(count, rows, D),
                     queries,
                     keys,

time: 587 us -> 570 us (0.971)
  waiting for transfers between devices: 14.2 us -> 0.51 us
    pallas_call x1, Pallas kernels: 91.5 us -> 75 us  [attn_back_fused(): pl.pallas_call(functools.partial(attn_back_kernel, rows), out_shape=tuple...]
    pallas_call x1, Pallas kernels: 168 us -> 182 us  [attn_fused(): pl.pallas_call(functools.partial(attn_kernel, rows), out_shape=(jax.Shape...]
    all_gather x1, waiting for transfers between devices: 14.2 us -> 0.49 us  [per_device(): gate_up_w = lax.all_gather(gate_up_shard, 'dp', axis=0, tiled=True)]
  transfers between devices with their start and end apart: 1 -> 1, of which waited for: 1 -> 1; matrix products, arithmetic and copies ran while one was open for 1% -> 1% of each run, Pallas kernels for 29% -> 32%
where the time goes in v9:
time: 570 us
  Pallas kernels  534 us (94%)
  between operations  15.6 us (3%)
  local copies, waits for them, and re-layouts  13.5 us (2%)
  other arithmetic  6.43 us (1%)
    pallas_call x1, Pallas kernels, attn_fused(): pl.pallas_call(functools.partial(attn_kernel, rows), out_shape=(jax.Shape...  182 us
    pallas_call x1, Pallas kernels, mlp_fused(): pl.pallas_call(functools.partial(mlp_kernel, rows), out_shape=(jax.ShapeD...  110 us
    pallas_call x1, Pallas kernels, mlp_back_fused(): pl.pallas_call(functools.partial(mlp_back_kernel, rows), out_shape=(jax.S...  89 us
    pallas_call x1, Pallas kernels, front(): pl.pallas_call(front_kernel, out_shape=(jax.ShapeDtypeStruct((4 * rows, m...  77.6 us
    pallas_call x1, Pallas kernels, attn_back_fused(): pl.pallas_call(functools.partial(attn_back_kernel, rows), out_shape=tuple...  75 us
    unnamed x56, local copies, waits for them, and re-layouts  11.6 us
  transfers between devices with their start and end apart: 1, of which 1 were waited for; matrix products, arithmetic and copies ran while one was open for 1% of the time, Pallas kernels for 32%

profile of v9, /device:TPU:0, one launch (start us, length us, event | category | flops | bytes accessed | tf_op | source)
XLA Modules:
  0.0 570.0 jit_solution(10825489387853130600)
XLA Ops:
  7.2 0.0 all-gather.2.cloned.1.call-start
  7.9 1.0 copy.29
  8.9 0.0 copy-start.9
  8.9 0.0 copy-start.10
  9.0 3.5 pad_maximum_fusion
  12.4 0.0 copy-start.22
  12.5 1.1 constant_dynamic-slice_fusion
  13.6 0.1 pad_maximum_fusion.1.shard_hbm
  13.9 0.2 copy-done
  14.1 77.6 %front.1 = (bf16[1024,2304]{1,0:T(8,128)(2,1)}, s32[8,8,128]{2,1,0:T(8,128)S(1)}, bf16[2304,128]{1,0:T(8,128)(2,1)S(1)}, bf16[2304,128]{1,0:T(8,128)(2,1)S(1)}, ...) custom-call(s32[8,128]{1,0:T(8,128)S(1)} %broadcast_in_dim.10.ids_ref, ...), custom_call_target="tpu_custom_call" | custom-call | tf_op jit(solution)/shard_map/front/pallas_call | solution.py:881
  91.7 0.8 copy-done.1
  92.6 0.8 copy-done.2
  93.4 0.6 copy-done.4
  94.0 0.7 copy-done.5
  94.7 0.0 all-gather.2.cloned.1.call-update
  95.3 2.8 fusion
  98.1 182.2 %attn.1 = (bf16[1024,512]{1,0:T(8,128)(2,1)}, bf16[1024,256]{1,0:T(8,128)(2,1)}, bf16[256,1024]{1,0:T(8,128)(2,1)}, bf16[1024,256]{1,0:T(8,128)(2,1)}, bf16[1024...) custom-call(s32[1]{0:T(128)S(6)} %copy.39.length_ref, ...), custom_call_target="tpu_custom_call" | custom-call | tf_op jit(solution)/shard_map/attn/pallas_call | solution.py:1808
  280.4 0.8 slice_reduce_fusion.ids_ref
  281.1 0.5 all-gather.2.cloned.1.call-done.gu_hbm
  281.6 110.1 %mlp.1 = (bf16[256,2304]{1,0:T(8,128)(2,1)}, bf16[256,2304]{1,0:T(8,128)(2,1)}, bf16[4,256,128]{2,1,0:T(8,128)(2,1)}, bf16[256,128]{1,0:T(8,128)(2,1)}, bf16[4,2...) custom-call(s32[1]{0:T(128)S(6)} %copy.39.length_ref, ...), custom_call_target="tpu_custom_call" | custom-call | tf_op jit(solution)/shard_map/mlp/pallas_call | solution.py:1329
  391.7 89.0 %mlp_back.1 = (f32[256,2304]{1,0:T(8,128)}, f32[256,128]{1,0:T(8,128)}, bf16[4,2,48,288]{3,2,1,0:T(8,128)(2,1)}) custom-call(bf16[256,2304]{1,0:T(8,128)(2,1)} %get-tuple-element.71.g_ref.grad_mlp_hbm, bf16[2304,2304]{1,0:T(8,128)(2,1)} %bitcast.20, bf16[2304,4608]{1,0:T(8,128)(2,1)} %all-gather.2.cloned.1.call-done.gu_hbm, ...), custom_call_target="tpu_custom_call" | custom-call | tf_op jit(solution)/shard_map/mlp_back/pallas_call | solution.py:678
  480.7 75.0 %attn_back.1 = (bf16[256,2304]{1,0:T(8,128)(2,1)}, f32[8,72,80]{2,1,0:T(8,128)}, f32[8,16,64]{2,1,0:T(8,128)}, f32[8,16,288]{2,1,0:T(8,128)}, f32[8,16,64]{2,1,0...) custom-call(s32[8]{0:T(128)} %slice_reduce_fusion.ids_ref, ...), custom_call_target="tpu_custom_call" | custom-call | tf_op jit(solution)/shard_map/attn_back/pallas_call | solution.py:2314
  555.8 1.0 copy.41
  556.8 0.6 copy-done.7
  557.4 1.0 copy.42
  558.4 0.7 copy.43
  559.1 0.6 copy.44
  559.8 0.7 copy.45
  560.4 0.6 copy.46
  561.1 0.7 copy.47
  561.7 0.7 copy.48
  562.5 0.7 copy.49
  (42 shorter events, 0.2 us)
Async XLA Ops:
  7.2 274.4 %all-gather.2.cloned.1.call-start = ((), (), s32[]{:S(2)}) async-start(), calls=%async_computation | async-start | bytes 23887872 | tf_op jit(solution)/shard_map/all_gather | solution.py:2444
  8.9 4.7 copy-start.9
  8.9 4.7 copy-start.10
  12.4 1.3 copy-start.17
  12.4 1.3 copy-start.13
  12.4 1.4 copy-start.16
  12.4 1.4 copy-start.20
  12.4 1.4 copy-start.21
  12.4 1.4 copy-start.22
  12.4 1.6 copy-start
  12.5 1.6 copy-start.3
  91.7 0.8 copy-start.1
  92.6 0.8 copy-start.2
  93.4 0.6 copy-start.4
  94.0 0.7 copy-start.5
  480.7 75.0 %copy-start.6 = (bf16[256,2304]{1,0:T(8,128)(2,1)S(1)}, bf16[256,2304]{1,0:T(8,128)(2,1)}, u32[]{:S(2)}) copy-start(bf16[256,2304]{1,0:T(8,128)(2,1)} %get-tuple-element.116) | copy-start | bytes 3538948
  555.7 1.7 copy-start.7
  555.7 2.7 copy-start.11
  555.7 3.4 copy-start.19
  555.7 4.0 copy-start.12
  555.7 4.7 copy-start.18
  557.4 3.7 copy-start.15
  557.4 4.3 copy-start.8
  557.4 5.1 copy-start.14
Sparse Core Ops, SparseCore 0:
  94.8 186.7 all-gather.1

commit v10 on v9

--- a/solution.py
+++ b/solution.py
@@ -425,7 +425,7 @@
 
 class ChunkScatter:
     def __init__(self, sq, part, landing, passed, send_sem, recv_sem):
-        self.sq, self.half = sq, sq.half
+        self.sq, self.half = sq, landing.shape[-2]
         self.part, self.landing, self.passed = part, landing, passed
         self.send_sem, self.recv_sem = send_sem, recv_sem
         self.tiles = send_sem.shape[-1]
@@ -520,6 +520,39 @@
 
 def columns(step, tile, base=0):
     return pl.ds(pl.multiple_of(base + step * tile, LANES), tile)
+
+
+def pack_rows(low):
+    size = low.shape[0] // 8
+    return jnp.concatenate(
+        [
+            jnp.concatenate(
+                [
+                    low[(4 * half + i) * size : (4 * half + i + 1) * size, GATE.start : UP.stop]
+                    for i in range(4)
+                ],
+                axis=1,
+            )
+            for half in range(2)
+        ],
+        axis=0,
+    )
+
+
+def unpack_rows(packed):
+    size = packed.shape[0] // 2
+    width = UP.stop - GATE.start
+    low = jnp.concatenate(
+        [
+            packed[half * size : (half + 1) * size, i * width : (i + 1) * width]
+            for half in range(2)
+            for i in range(4)
+        ],
+        axis=0,
+    )
+    before = jnp.zeros((low.shape[0], GATE.start), low.dtype)
+    after = jnp.zeros((low.shape[0], LANES - UP.stop), low.dtype)
+    return jnp.concatenate([before, low, after], axis=1)
 
 
 def mlp_back_kernel(
@@ -535,9 +568,8 @@
     f_table,
     o_ref,
     l_ref,
-    f_out,
+    f_send,
     f_ref,
-    f_send,
     down_w,
     gu_w,
     buf,
@@ -551,8 +583,6 @@
     own_sem,
     gather_send,
     gather_recv,
-    spread_send,
-    spread_recv,
     *scratch,
 ):
     sq = Square(rows)
@@ -575,7 +605,7 @@
     own_load.start()
     for copy in loads(0):
         copy.start()
-    sq.greet(far=True)
+    sq.greet()
     gather = ChunkGather(sq, g_ref, buf, gather_send, gather_recv)
     gather.start()
     gu_load.start()
@@ -616,10 +646,6 @@
         def _():
             gu_load.wait()
 
-        part_low[chunk] = (
-            band(nn(grads[:, :width], f_table[...]), GATE)
-            + band(nn(grads[:, width:], f_table[...]), UP)
-        ).astype(BF16)
         wide = tile_of(model)
 
         @pl.loop(0, model // wide)
@@ -634,6 +660,11 @@
             @pl.when(chunk == 3)
             def _():
                 scatters[0].send(1, step)
+
+        part_low[chunk] = pack_rows(
+            band(nn(grads[:, :width], f_table[...]), GATE)
+            + band(nn(grads[:, width:], f_table[...]), UP)
+        ).astype(BF16)
 
         @pl.when(chunk == 1)
         def _():
@@ -649,24 +680,19 @@
         f_ref[RANK : 2 * RANK, :] += nn(gu_turned[GATE], grads[:, :width])
         f_ref[2 * RANK : 3 * RANK, :] += nn(gu_turned[UP], grads[:, width:])
 
+    for scatter in scatters:
+        scatter.pass_on()
     cores, slices = f_send.shape[:2]
     size = width // (cores * slices)
     for core in range(cores):
         for peer in range(slices):
             first = (core * slices + peer) * size
             f_send[core, peer] = f_ref[: 3 * RANK, first : first + size].astype(BF16)
-    spread = sq.spread(lambda peer: f_send.at[:, peer], f_out, spread_send, spread_recv)
-    for copy in spread:
-        copy.start()
-    for scatter in scatters:
-        scatter.pass_on()
     gather.finish()
     scatters[0].collect(o_ref)
     scatters[1].collect(l_ref)
     for scatter in scatters:
         scatter.finish()
-    for copy in spread:
-        copy.wait()
 
 
 def mlp_back_fused(grad, down_w, gu_w, slope, gelu, hidden, low, d_tab, f_tab, dp):
@@ -679,14 +705,13 @@
         functools.partial(mlp_back_kernel, rows),
         out_shape=(
             jax.ShapeDtypeStruct((rows, model), F32),
-            jax.ShapeDtypeStruct((rows, LANES), F32),
-            jax.ShapeDtypeStruct((4, dp // 4, 3 * RANK, width // dp), BF16),
+            jax.ShapeDtypeStruct((rows // 4, LANES), F32),
+            jax.ShapeDtypeStruct(messages, BF16),
         ),
         in_specs=[vmem] + [anywhere] * 6 + [vmem] * 2,
         out_specs=(vmem,) * 3,
         scratch_shapes=[
             pltpu.VMEM((3 * RANK, width), F32),
-            pltpu.VMEM(messages, BF16),
             pltpu.VMEM((model, width), BF16),
             pltpu.VMEM((model, 2 * width), BF16),
             pltpu.VMEM((4, rows, model), BF16),
@@ -700,11 +725,9 @@
             pltpu.SemaphoreType.DMA,
             pltpu.SemaphoreType.DMA((6,)),
             pltpu.SemaphoreType.DMA((6,)),
-            pltpu.SemaphoreType.DMA((3,)),
-            pltpu.SemaphoreType.DMA((4,)),
         ]
         + scatter_scratch(rows, model, model // tile_of(model))
-        + scatter_scratch(rows, LANES),
+        + scatter_scratch(rows // 4, LANES),
         compiler_params=pltpu.CompilerParams(
             collective_id=5, has_side_effects=True, vmem_limit_bytes=62 * 1024 * 1024
         ),
@@ -716,10 +739,19 @@
     ids_ref,
     layer_ref,
     gains_ref,
-    f_all,
-    d_all,
-    hk_all,
-    shard_hbm,
+    gate_up_all,
+    hidden_all,
+    in_all,
+    resid_all,
+    heads_all,
+    query_all,
+    key_value_all,
+    query_hbm,
+    key_hbm,
+    value_hbm,
+    output_hbm,
+    gate_hbm,
+    up_hbm,
     seq_out,
     ids_out,
     d_out,
@@ -727,7 +759,11 @@
     h_out,
     k_out,
     weight_out,
+    gate_up_out,
     normed,
+    shard_pack,
+    gate_up_pack,
+    ids_own,
     ids_land,
     f_pick,
     d_pick,
@@ -762,8 +798,32 @@
     peers += [{"dp": lax.rem(d + step, dp)} for step in range(1, dp)]
     call(peers)
     shards = Line(weight_out, shard_send, shard_recv)
-    own_shard = pltpu.make_async_copy(shard_hbm, weight_out.at[d], shard_sem)
-    own_shard.start()
+    q_width, width = query_hbm.shape[1], gate_hbm.shape[1]
+    kv_first = pl.multiple_of(sq.me * (q_width // HD) // (HQ // KV) * HD, HD)
+    packs = [
+        pltpu.make_async_copy(source, target, shard_sem.at[which])
+        for which, (source, target) in enumerate(
+            (
+                (query_hbm, shard_pack.at[:, pl.ds(0, q_width)]),
+                (key_hbm.at[:, pl.ds(kv_first, HD)], shard_pack.at[:, pl.ds(q_width, HD)]),
+                (
+                    value_hbm.at[:, pl.ds(kv_first, HD)],
+                    shard_pack.at[:, pl.ds(q_width + HD, HD)],
+                ),
+                (output_hbm, shard_pack.at[:, pl.ds(q_width + 2 * HD, q_width)]),
+                (gate_hbm, gate_up_pack.at[:, pl.ds(0, width)]),
+                (up_hbm, gate_up_pack.at[:, pl.ds(width, width)]),
+            )
+        )
+    ]
+    for copy in packs:
+        copy.start()
+    keep_shard = pltpu.make_async_copy(shard_pack, weight_out.at[d], shard_sem.at[6])
+    keep_gate_up = pltpu.make_async_copy(gate_up_pack, gate_up_out, shard_sem.at[7])
+    ids_own[...] = jnp.full(ids_own.shape, ids_ref[0, 0], jnp.int32)
+    for copy in packs[:4]:
+        copy.wait()
+    keep_shard.start()
 
     @pl.loop(0, rows // BLOCK)
     def _(step):
@@ -771,23 +831,36 @@
         normed[here, :] = rms_norm(layer_ref[here, :].astype(F32), gains_ref[0:1, :]).astype(BF16)
 
     pl.semaphore_wait(pltpu.get_barrier_semaphore(), len(peers))
-    line = along(lambda k: ids_ref, ids_land, line_send.at[0], line_recv.at[0])
-    own_shard.wait()
+    keep_shard.wait()
     shards.start()
+    line = along(lambda k: ids_own, ids_land, line_send.at[0], line_recv.at[0])
+    for copy in packs[4:]:
+        copy.wait()
+    keep_gate_up.start()
     gather = PlainGather(sq.me, normed, seq_out, local_sem, gather_send, gather_recv)
     gather.start()
     pltpu.make_async_copy(ids_land, ids_land, line_recv.at[0]).wait()
     ids_out[...] = ids_land[...]
 
+    def pick(source, group):
+        total = None
+        for adapter in range(NA):
+            hit = jnp.broadcast_to(ids_land[group, 0:1, 0:1], source.shape[1:]) == adapter
+            mine = jnp.where(hit, source[adapter].astype(F32), 0.0)
+            total = mine if total is None else total + mine
+        return total
+
     @pl.loop(0, dp)
-    def _(k):
-        for source, target in ((f_all, f_pick), (d_all, d_pick), (hk_all, hk_pick)):
-            total = None
-            for adapter in range(NA):
-                hit = jnp.broadcast_to(ids_land[k, 0:1, 0:1], source.shape[1:]) == adapter
-                mine = jnp.where(hit, source[adapter].astype(F32), 0.0)
-                total = mine if total is None else total + mine
-            target[k] = total.astype(BF16)
+    def _(group):
+        f_pick[group, : 2 * RANK, :] = pick(gate_up_all, group).astype(BF16)
+        f_pick[group, 2 * RANK :, :] = pick(hidden_all, group).astype(BF16)
+        d_pick[group, : UP.stop, :] = pick(in_all, group).T.astype(BF16)
+        d_pick[group, UP.stop :, :] = pick(resid_all, group).astype(BF16)
+        hk_pick[group, :RANK, :] = pick(heads_all, group).astype(BF16)
+        hk_pick[group, RANK : 2 * RANK, :] = pick(query_all, group).astype(BF16)
+        hk_pick[group, 2 * RANK :, : key_value_all.shape[2]] = pick(key_value_all, group).astype(
+            BF16
+        )
 
     lands = (f_mid, d_mid, hk_mid)
     for item, (source, target) in enumerate(zip((f_pick, d_pick, hk_pick), lands)):
@@ -864,6 +937,7 @@
         for part in range(2):
             shards.wait_sibling(place, part)
     shards.finish()
+    keep_gate_up.wait()
     for copies in spread:
         for copy in copies[1:]:
             copy.wait_send()
@@ -871,26 +945,40 @@
         copy.wait_send()
 
 
-def front(ids, layer_in, gains, f_all, d_all, hk_all, shard, dp, widths):
+def front(ids, layer_in, gains, adapters, weights, dp, widths):
     rows, model = layer_in.shape
     anywhere = pl.BlockSpec(memory_space=pl.ANY)
     vmem = pl.BlockSpec(memory_space=pltpu.VMEM)
-    tables_in = (f_all, d_all, hk_all)
-    shapes = [(dp,) + table.shape[1:] for table in tables_in]
+    gate_up_all, hidden_all, in_all, resid_all, heads_all, query_all, key_value_all = adapters
+    tile = (8, LANES)
+    shapes = [
+        (dp, gate_up_all.shape[1] + RANK, gate_up_all.shape[2]),
+        (dp, in_all.shape[2] + resid_all.shape[1], in_all.shape[1]),
+        (dp, 2 * RANK + key_value_all.shape[1], query_all.shape[2]),
+    ]
+    query, key, value, output, gate, up = weights
+    shard = (query.shape[0], 2 * query.shape[1] + 2 * HD)
+    gate_up = (gate.shape[0], 2 * gate.shape[1])
     joined = (shapes[1][1], dp * shapes[1][2])
     return pl.pallas_call(
         front_kernel,
         out_shape=(
             jax.ShapeDtypeStruct((4 * rows, model), BF16),
-            jax.ShapeDtypeStruct((dp,) + ids.shape, jnp.int32),
+            jax.ShapeDtypeStruct((dp,) + tile, jnp.int32),
         )
         + tuple(jax.ShapeDtypeStruct((width, LANES), BF16) for width in widths)
-        + (jax.ShapeDtypeStruct((dp,) + shard.shape, BF16),),
-        in_specs=[vmem] * 6 + [anywhere],
-        out_specs=(anywhere,) + (vmem,) * 5 + (anywhere,),
+        + (
+            jax.ShapeDtypeStruct((dp,) + shard, BF16),
+            jax.ShapeDtypeStruct(gate_up, BF16),
+        ),
+        in_specs=[pl.BlockSpec(memory_space=pltpu.SMEM)] + [vmem] * 9 + [anywhere] * 6,
+        out_specs=(anywhere,) + (vmem,) * 5 + (anywhere,) * 2,
         scratch_shapes=[
             pltpu.VMEM((rows, model), BF16),
-            pltpu.VMEM((dp,) + ids.shape, jnp.int32),
+            pltpu.VMEM(shard, BF16),
+            pltpu.VMEM(gate_up, BF16),
+            pltpu.VMEM(tile, jnp.int32),
+            pltpu.VMEM((dp,) + tile, jnp.int32),
         ]
         + [pltpu.VMEM(shape, BF16) for shape in shapes] * 2
         + [
@@ -908,15 +996,15 @@
             pltpu.SemaphoreType.DMA((4,)),
             pltpu.SemaphoreType.DMA((3, 3)),
             pltpu.SemaphoreType.DMA((3, 4)),
-            pltpu.SemaphoreType.DMA,
+            pltpu.SemaphoreType.DMA((8,)),
             pltpu.SemaphoreType.DMA((3, dp // 2, 2)),
             pltpu.SemaphoreType.DMA((dp, 2)),
         ],
         compiler_params=pltpu.CompilerParams(
-            collective_id=9, has_side_effects=True, vmem_limit_bytes=VMEM_LIMIT
+            collective_id=9, has_side_effects=True, vmem_limit_bytes=62 * 1024 * 1024
         ),
         name="front",
-    )(ids, layer_in, gains, *tables_in, shard)
+    )(ids, layer_in, gains, *adapters, *weights)
 
 
 class Line:
@@ -1905,7 +1993,6 @@
     total,
     work,
     g_ref,
-    low_sum,
     buf,
     att_send,
     att,
@@ -1926,6 +2013,7 @@
     d_land,
     d_sum,
     d_recv,
+    f_land,
     f_recv,
     hk_send,
     hk_land,
@@ -1937,6 +2025,8 @@
     back_sends,
     back_recvs,
     f_sem,
+    f_send_sem,
+    f_recv_sem,
     d_sem,
     hk_sem,
     group_send,
@@ -1991,7 +2081,7 @@
     peers += [{"dp": lax.rem(d + step, dp)} for step in range(1, dp)]
     call(peers)
 
-    low_gu = low_gu_ref[...].astype(BF16)
+    low_gu = unpack_rows(low_gu_ref[...]).astype(BF16)
 
     @pl.loop(0, model // wide)
     def _(step):
@@ -2034,7 +2124,9 @@
             copy.start()
         heads_out_copies.append(copies)
     line = []
-    line += along(lambda k: f_ref.at[k // 2, lax.rem(k, 2)], f_recv, f_sem, line_recv.at[0])
+    f_spread = sq.spread(lambda peer: f_ref.at[:, peer], f_land, f_send_sem, f_recv_sem)
+    for copy in f_spread:
+        copy.start()
     back = []
     for which, peer in enumerate(others):
         here = pl.ds(pl.multiple_of(peer * rows, rows), rows)
@@ -2143,15 +2235,20 @@
     kv_grad[:, HD:] = v_sum[...].astype(BF16)
     for copies in back:
         copies[1].start()
+    f_spread[0].wait()
+    for copy in f_spread[1:]:
+        copy.wait_recv()
+    line += along(lambda k: f_land.at[k // 2, lax.rem(k, 2)], f_recv, f_sem, line_recv.at[0])
 
     @pl.loop(0, 4)
     def _(block):
         here = pl.ds(pl.multiple_of(block * rows, rows), rows)
-        part_low[block] = (
+        low = (
             band(nn(q_grad[here, :], h_all[sq.me]), QUERY)
             + band(nn(kv_grad[here, :HD], k_table[...]), KEY)
             + band(nn(kv_grad[here, HD:], k_table[...]), VALUE)
-        ).astype(BF16)
+        )
+        part_low[block] = turned(low)[: VALUE.stop]
 
     for copies in back:
         copies[2].start()
@@ -2178,7 +2275,7 @@
     @pl.loop(0, 4)
     def _(block):
         here = pl.ds(pl.multiple_of(block * rows, rows), rows)
-        grad_turned = turned(part_low[block])[: VALUE.stop]
+        grad_turned = part_low[block]
         low_turned = turned(low_ref[here, :])
         h_turned[RANK : 2 * RANK, :] += nn(low_turned[QUERY], q_grad[here, :])
         k_turned[:RANK, :] += nn(low_turned[KEY], kv_grad[here, :HD])
@@ -2235,10 +2332,11 @@
         d_sum[k] = sum(d_land[k, t].astype(F32) for t in range(4)).astype(BF16)
     line += along(lambda k: d_sum.at[k], d_recv, d_sem, line_recv.at[1])
     line += along(lambda k: hk_land.at[k // 2, lax.rem(k, 2)], hk_recv, hk_sem, line_recv.at[2])
-    low_sum[...] = sum(
+    low_total = sum(
         low_land[peer].astype(F32) for peer, unused in arrivals
     ) + part_low[sq.me].astype(F32)
-    low_qkv = low_sum[...].astype(BF16)
+    rest = jnp.zeros((LANES - VALUE.stop, rows), F32)
+    low_qkv = turned(jnp.concatenate([low_total, rest], axis=0))
 
     @pl.loop(0, model // wide)
     def _(step):
@@ -2283,7 +2381,7 @@
             first = (which + 5) * RANK
             resid_out[adapter, which] = d_flip[first : first + RANK]
 
-    for copies in spread:
+    for copies in spread + [f_spread]:
         for copy in copies[1:]:
             copy.wait_send()
     for copies in heads_out_copies + back:
@@ -2311,6 +2409,7 @@
     outs += [jax.ShapeDtypeStruct(shape, F32) for shape in grad_shapes]
     d_rows = model // total
     messages = f_in.shape[2:]
+    landed = (4, f_in.shape[0]) + messages
     return pl.pallas_call(
         functools.partial(attn_back_kernel, rows),
         out_shape=tuple(outs),
@@ -2322,16 +2421,15 @@
             pltpu.VMEM((rows, model), F32),
             pltpu.VMEM((rows, model), F32),
             pltpu.VMEM((rows, model), BF16),
-            pltpu.VMEM((rows, LANES), F32),
             pltpu.VMEM((4, rows, model), BF16),
             pltpu.VMEM((3, rows, q_width), BF16),
             pltpu.VMEM((4, rows, q_width), BF16),
             pltpu.VMEM((RANK, rows), BF16),
             pltpu.VMEM((4, RANK, rows), BF16),
-            pltpu.VMEM((4, rows, LANES), BF16),
+            pltpu.VMEM((4, 3 * RANK, rows), BF16),
             pltpu.VMEM((4, rows, q_width), BF16),
             pltpu.VMEM((4, rows, 2 * HD), BF16),
-            pltpu.VMEM((4, rows, LANES), BF16),
+            pltpu.VMEM((4, 3 * RANK, rows), BF16),
             pltpu.VMEM((LEN, q_width), BF16),
             pltpu.VMEM((LEN, HD), F32),
             pltpu.VMEM((LEN, HD), F32),
@@ -2343,6 +2441,7 @@
             pltpu.VMEM((dp, 4, d_rows, LANES), BF16),
             pltpu.VMEM((dp, d_rows, LANES), BF16),
             pltpu.VMEM((dp, d_rows, LANES), BF16),
+            pltpu.VMEM(landed, BF16),
             pltpu.VMEM((dp,) + messages, BF16),
             pltpu.VMEM((dp // 4, 4, 4 * RANK, LANES), BF16),
             pltpu.VMEM((4, dp // 4, 4 * RANK, LANES), BF16),
@@ -2354,6 +2453,8 @@
             pltpu.SemaphoreType.DMA((3, 3)),
             pltpu.SemaphoreType.DMA((3, 3)),
             pltpu.SemaphoreType.DMA((dp,)),
+            pltpu.SemaphoreType.DMA((3,)),
+            pltpu.SemaphoreType.DMA((4,)),
             pltpu.SemaphoreType.DMA((dp,)),
             pltpu.SemaphoreType.DMA((dp,)),
             pltpu.SemaphoreType.DMA((dp + 1, 3)),
@@ -2398,49 +2499,29 @@
     hidden_here = FF // count
     assert lay.ratio % heads_here == 0
 
-    key_cols = lax.dynamic_slice_in_dim(key_weight, lay.kv_head * HD, HD, 1)
-    value_cols = lax.dynamic_slice_in_dim(value_weight, lay.kv_head * HD, HD, 1)
-    attn_shard = jnp.concatenate([query_weight, key_cols, value_cols, out_weight.T], axis=1)
-    gate_up_shard = jnp.concatenate([gate_weight, up_weight], axis=1)
-    down_shard = down_weight.T
-    attn_shard, gate_up_shard, down_shard = lax.optimization_barrier(
-        (attn_shard, gate_up_shard, down_shard)
-    )
     qkv_width = head_width + 2 * HD
-
     cosine, sine = tables(LEN, HD)
     if count == 4 and lay.dp == 8:
-        seq_attn, all_ids, d_tab, f_tab, h_tab, k_tab, attn_w = front(
-            jnp.broadcast_to(adapter_ids, (8, LANES)),
+        adapters = (
+            lift_gateup.reshape(NA, 2 * RANK, -1),
+            jnp.swapaxes(adapt_hidden, 1, 2),
+            adapt_in,
+            lift_resid.reshape(NA, 2 * RANK, -1),
+            jnp.swapaxes(adapt_heads, 1, 2),
+            lift_query,
+            lift_keyval.reshape(NA, 2 * RANK, -1),
+        )
+        seq_attn, all_ids, d_tab, f_tab, h_tab, k_tab, attn_w, gate_up_shard = front(
+            adapter_ids,
             layer_in,
             norm_gains,
-            jnp.concatenate(
-                [
-                    lift_gateup.reshape(NA, 2 * RANK, -1),
-                    jnp.swapaxes(adapt_hidden, 1, 2),
-                ],
-                axis=1,
-            ),
-            jnp.concatenate(
-                [jnp.swapaxes(adapt_in, 1, 2), lift_resid.reshape(NA, 2 * RANK, -1)], axis=1
-            ),
-            jnp.concatenate(
-                [
-                    jnp.swapaxes(adapt_heads, 1, 2),
-                    lift_query,
-                    jnp.pad(
-                        lift_keyval.reshape(NA, 2 * RANK, -1),
-                        ((0, 0), (0, 0), (0, lift_query.shape[2] - lift_keyval.shape[3])),
-                    ),
-                ],
-                axis=1,
-            ),
-            attn_shard,
+            adapters,
+            (query_weight, key_weight, value_weight, out_weight.T, gate_weight, up_weight),
             lay.dp,
             (D, hidden_here, head_width, HD),
         )
         attn_w = attn_w.reshape(D, -1)
-        gate_up_shard, attn_w = lax.optimization_barrier((gate_up_shard, attn_w))
+        down_shard = down_weight.T
         gate_up_w = lax.all_gather(gate_up_shard, "dp", axis=0, tiled=True)
         (
             queries,
@@ -2563,6 +2644,11 @@
             grads[which] = jnp.swapaxes(grads[which], 1, 2)
         return (layer_out, *grads)
 
+    key_cols = lax.dynamic_slice_in_dim(key_weight, lay.kv_head * HD, HD, 1)
+    value_cols = lax.dynamic_slice_in_dim(value_weight, lay.kv_head * HD, HD, 1)
+    attn_shard = jnp.concatenate([query_weight, key_cols, value_cols, out_weight.T], axis=1)
+    gate_up_shard = jnp.concatenate([gate_weight, up_weight], axis=1)
+    down_shard = down_weight.T
     attn_w = lax.all_gather(attn_shard, "dp", axis=0, tiled=True)
     gate_up_w = lax.all_gather(gate_up_shard, "dp", axis=0, tiled=True)
 

time: 570 us -> 562 us (0.986)
    pallas_call x1, Pallas kernels: 77.6 us -> 84.9 us  [front(): pl.pallas_call(front_kernel, out_shape=(jax.ShapeDtypeStruct((4 * rows, m...]
    unnamed x56 -> x27, local copies, waits for them, and re-layouts: 11.6 us -> 7.39 us
  transfers between devices with their start and end apart: 1 -> 1, of which waited for: 1 -> 0; matrix products, arithmetic and copies ran while one was open for 1% -> 1% of each run, Pallas kernels for 32% -> 32%
where the time goes in v10:
time: 562 us
  Pallas kernels  535 us (95%)
  between operations  15.4 us (3%)
  local copies, waits for them, and re-layouts  8.91 us (2%)
    pallas_call x1, Pallas kernels, attn_fused(): pl.pallas_call(functools.partial(attn_kernel, rows), out_shape=(jax.Shape...  182 us
    pallas_call x1, Pallas kernels, mlp_fused(): pl.pallas_call(functools.partial(mlp_kernel, rows), out_shape=(jax.ShapeD...  110 us
    pallas_call x1, Pallas kernels, front(): pl.pallas_call(front_kernel, out_shape=(jax.ShapeDtypeStruct((4 * rows, m...  84.9 us
    pallas_call x1, Pallas kernels, mlp_back_fused(): pl.pallas_call(functools.partial(mlp_back_kernel, rows), out_shape=(jax.S...  83.4 us
    pallas_call x1, Pallas kernels, attn_back_fused(): pl.pallas_call(functools.partial(attn_back_kernel, rows), out_shape=tuple...  74.1 us
  transfers between devices with their start and end apart: 1, of which 0 were waited for; matrix products, arithmetic and copies ran while one was open for 1% of the time, Pallas kernels for 32%

profile of v10, /device:TPU:0, one launch (start us, length us, event | category | flops | bytes accessed | tf_op | source)
XLA Modules:
  0.0 562.1 jit_solution(1823597528130469416)
XLA Ops:
  7.2 0.0 all-gather.2.cloned.1.call-start
  7.9 84.9 %front.1 = (bf16[1024,2304]{1,0:T(8,128)(2,1)}, s32[8,8,128]{2,1,0:T(8,128)}, bf16[2304,128]{1,0:T(8,128)(2,1)}, bf16[2304,128]{1,0:T(8,128)(2,1)}, bf16[512,128...) custom-call(s32[1,1]{1,0:T(1,128)S(6)} %copy.38.ids_ref, ...), custom_call_target="tpu_custom_call" | custom-call | tf_op jit(solution)/shard_map/front/pallas_call | solution.py:963
  92.8 0.0 all-gather.2.cloned.1.call-update
  93.4 2.8 fusion
  96.2 182.3 %attn.1 = (bf16[1024,512]{1,0:T(8,128)(2,1)}, bf16[1024,256]{1,0:T(8,128)(2,1)}, bf16[256,1024]{1,0:T(8,128)(2,1)}, bf16[1024,256]{1,0:T(8,128)(2,1)}, bf16[1024...) custom-call(s32[1]{0:T(128)S(6)} %copy.37.length_ref, ...), custom_call_target="tpu_custom_call" | custom-call | tf_op jit(solution)/shard_map/attn/pallas_call | solution.py:1896
  278.6 1.5 slice_reduce_fusion.ids_ref
  280.1 110.1 %mlp.1 = (bf16[256,2304]{1,0:T(8,128)(2,1)}, bf16[256,2304]{1,0:T(8,128)(2,1)}, bf16[4,256,128]{2,1,0:T(8,128)(2,1)}, bf16[256,128]{1,0:T(8,128)(2,1)}, bf16[4,2...) custom-call(s32[1]{0:T(128)S(6)} %copy.37.length_ref, ...), custom_call_target="tpu_custom_call" | custom-call | tf_op jit(solution)/shard_map/mlp/pallas_call | solution.py:1417
  390.2 83.4 %mlp_back.1 = (f32[256,2304]{1,0:T(8,128)}, f32[64,128]{1,0:T(8,128)}, bf16[2,4,48,288]{3,2,1,0:T(8,128)(2,1)}) custom-call(bf16[256,2304]{1,0:T(8,128)(2,1)} %get-tuple-element.63.g_ref.grad_mlp_hbm, bf16[2304,2304]{1,0:T(8,128)(2,1)} %bitcast.17, bf16[2304,4608]{1,0:T(8,128)(2,1)} %all-gather.2.cloned.1.call-done.gu_hbm, ...), custom_call_target="tpu_custom_call" | custom-call | tf_op jit(solution)/shard_map/mlp_back/pallas_call | solution.py:704
  473.6 0.0 copy-start
  473.7 74.1 %attn_back.1 = (bf16[256,2304]{1,0:T(8,128)(2,1)}, f32[8,72,80]{2,1,0:T(8,128)}, f32[8,16,64]{2,1,0:T(8,128)}, f32[8,16,288]{2,1,0:T(8,128)}, f32[8,16,64]{2,1,0...) custom-call(s32[8]{0:T(128)} %slice_reduce_fusion.ids_ref, ...), custom_call_target="tpu_custom_call" | custom-call | tf_op jit(solution)/shard_map/attn_back/pallas_call | solution.py:2413
  547.8 0.0 copy-start.1
  547.8 0.0 copy-done
  547.8 0.0 copy-start.3
  547.8 0.0 copy-start.8
  547.8 0.0 copy-start.4
  547.8 0.0 copy-start.7
  547.8 1.0 copy.39
  548.9 0.6 copy-done.1
  549.5 1.0 copy.40
  550.5 0.0 copy-done.3
  550.5 0.7 copy.41
  551.2 0.0 copy-done.8
  551.2 0.6 copy.42
  551.8 0.0 copy-done.4
  551.8 0.7 copy.43
  552.5 0.0 copy-done.7
  552.5 0.6 copy.44
  553.2 0.0 copy-done.6
  553.2 0.7 copy.45
  553.8 0.0 copy-done.2
  553.8 0.7 copy.46
  554.6 0.7 copy.47
  (6 shorter events, 0.0 us)
Async XLA Ops:
  7.2 272.9 %all-gather.2.cloned.1.call-start = ((), (), s32[]{:S(2)}) async-start(), calls=%async_computation | async-start | bytes 23887872 | tf_op jit(solution)/shard_map/all_gather | solution.py:2525
  473.6 74.1 %copy-start = (bf16[256,2304]{1,0:T(8,128)(2,1)S(1)}, bf16[256,2304]{1,0:T(8,128)(2,1)}, u32[]{:S(2)}) copy-start(bf16[256,2304]{1,0:T(8,128)(2,1)} %get-tuple-element.106) | copy-start | bytes 3538948
  547.8 1.7 copy-start.1
  547.8 2.7 copy-start.3
  547.8 3.4 copy-start.8
  547.8 4.0 copy-start.4
  547.8 4.7 copy-start.7
  549.5 3.7 copy-start.6
  549.5 4.3 copy-start.2
  549.5 5.1 copy-start.5
Sparse Core Ops, SparseCore 0:
  92.9 187.1 all-gather.1

commit v11 on v10

--- a/solution.py
+++ b/solution.py
@@ -739,13 +739,13 @@
     ids_ref,
     layer_ref,
     gains_ref,
-    gate_up_all,
-    hidden_all,
-    in_all,
-    resid_all,
-    heads_all,
-    query_all,
-    key_value_all,
+    gate_up_table_hbm,
+    hidden_table_hbm,
+    in_table_hbm,
+    resid_table_hbm,
+    heads_table_hbm,
+    query_table_hbm,
+    key_value_table_hbm,
     query_hbm,
     key_hbm,
     value_hbm,
@@ -760,6 +760,13 @@
     k_out,
     weight_out,
     gate_up_out,
+    gate_up_all,
+    hidden_all,
+    in_all,
+    resid_all,
+    heads_all,
+    query_all,
+    key_value_all,
     normed,
     shard_pack,
     gate_up_pack,
@@ -787,6 +794,7 @@
     group_send,
     group_recv,
     shard_sem,
+    table_sem,
     shard_send,
     shard_recv,
 ):
@@ -816,7 +824,21 @@
             )
         )
     ]
-    for copy in packs:
+    table_loads = [
+        pltpu.make_async_copy(source, target, table_sem.at[which])
+        for which, (source, target) in enumerate(
+            (
+                (gate_up_table_hbm, gate_up_all),
+                (hidden_table_hbm, hidden_all),
+                (in_table_hbm, in_all),
+                (resid_table_hbm, resid_all),
+                (heads_table_hbm, heads_all),
+                (query_table_hbm, query_all),
+                (key_value_table_hbm, key_value_all),
+            )
+        )
+    ]
+    for copy in packs + table_loads:
         copy.start()
     keep_shard = pltpu.make_async_copy(shard_pack, weight_out.at[d], shard_sem.at[6])
     keep_gate_up = pltpu.make_async_copy(gate_up_pack, gate_up_out, shard_sem.at[7])
@@ -841,6 +863,9 @@
     gather.start()
     pltpu.make_async_copy(ids_land, ids_land, line_recv.at[0]).wait()
     ids_out[...] = ids_land[...]
+
+    for copy in table_loads:
+        copy.wait()
 
     def pick(source, group):
         total = None
@@ -971,9 +996,10 @@
             jax.ShapeDtypeStruct((dp,) + shard, BF16),
             jax.ShapeDtypeStruct(gate_up, BF16),
         ),
-        in_specs=[pl.BlockSpec(memory_space=pltpu.SMEM)] + [vmem] * 9 + [anywhere] * 6,
+        in_specs=[pl.BlockSpec(memory_space=pltpu.SMEM)] + [vmem] * 2 + [anywhere] * 13,
         out_specs=(anywhere,) + (vmem,) * 5 + (anywhere,) * 2,
         scratch_shapes=[
+            *(pltpu.VMEM(table.shape, BF16) for table in adapters),
             pltpu.VMEM((rows, model), BF16),
             pltpu.VMEM(shard, BF16),
             pltpu.VMEM(gate_up, BF16),
@@ -997,6 +1023,7 @@
             pltpu.SemaphoreType.DMA((3, 3)),
             pltpu.SemaphoreType.DMA((3, 4)),
             pltpu.SemaphoreType.DMA((8,)),
+            pltpu.SemaphoreType.DMA((7,)),
             pltpu.SemaphoreType.DMA((3, dp // 2, 2)),
             pltpu.SemaphoreType.DMA((dp, 2)),
         ],
@@ -1179,10 +1206,10 @@
     gu_hbm,
     shard_hbm,
     weight_hbm,
-    d_ref,
-    f_table,
-    resid_ref,
-    cot_ref,
+    d_hbm,
+    f_hbm,
+    resid_hbm,
+    cot_hbm,
     gains_ref,
     layer_ref,
     grad_ref,
@@ -1193,6 +1220,10 @@
     gelu_out,
     down_out,
     w_kv_all,
+    d_ref,
+    f_table,
+    resid_ref,
+    cot_ref,
     work,
     low_sum,
     lows,
@@ -1244,8 +1275,16 @@
             for which, (source, target) in enumerate(((slope, slope_out), (gelu, gelu_out)))
         ]
 
+    late = [
+        pltpu.make_async_copy(source, target, load_sem.at[2 + which])
+        for which, (source, target) in enumerate(
+            ((d_hbm, d_ref), (f_hbm, f_table), (resid_hbm, resid_ref), (cot_hbm, cot_ref))
+        )
+    ]
     own_shard.start()
     seq_load.start()
+    for copy in late:
+        copy.start()
     for copy in tile_loads(0, 0):
         copy.start()
     line.greet([{"tensor": sq.across}, {"tensor": sq.down}])
@@ -1255,6 +1294,8 @@
     spread = HalfSpread(sq, line, weight_hbm, keys_from, w_kv_all, w_send, w_recv)
     spread.start()
     seq_load.wait()
+    for copy in late:
+        copy.wait()
 
     @pl.loop(0, 4)
     def _(chunk):
@@ -1427,9 +1468,10 @@
             jax.ShapeDtypeStruct((dp,) + shard.shape, BF16),
             jax.ShapeDtypeStruct((4, model, 2 * HD), BF16),
         ),
-        in_specs=[pl.BlockSpec(memory_space=pltpu.SMEM)] + [anywhere] * 4 + [vmem] * 5,
+        in_specs=[pl.BlockSpec(memory_space=pltpu.SMEM)] + [anywhere] * 8 + [vmem],
         out_specs=(vmem,) * 4 + (anywhere,) * 5,
         scratch_shapes=[
+            *(pltpu.VMEM(array.shape, array.dtype) for array in (d_tab, f_tab, resid, cotangent)),
             pltpu.VMEM((rows, model), F32),
             pltpu.VMEM((rows, LANES), F32),
             pltpu.VMEM((2, 4, rows, LANES), BF16),
@@ -1439,7 +1481,7 @@
             pltpu.VMEM((2, 4, rows, tile), BF16),
             pltpu.VMEM((2, 4, rows, tile), BF16),
             pltpu.VMEM((dp,) + shard.shape, BF16),
-            pltpu.SemaphoreType.DMA((2,)),
+            pltpu.SemaphoreType.DMA((6,)),
             pltpu.SemaphoreType.DMA((2, 2)),
             pltpu.SemaphoreType.DMA((2, 2)),
             pltpu.SemaphoreType.DMA((5,)),

time: 562 us -> 560 us (level)
  transfers between devices with their start and end apart: 1 -> 1, of which waited for: 0 -> 0; matrix products, arithmetic and copies ran while one was open for 1% -> 1% of each run, Pallas kernels for 32% -> 33%
where the time goes in v11:
time: 560 us
  Pallas kernels  533 us (95%)
  between operations  15.4 us (3%)
  local copies, waits for them, and re-layouts  8.9 us (2%)
    pallas_call x1, Pallas kernels, attn_fused(): pl.pallas_call(functools.partial(attn_kernel, rows), out_shape=(jax.Shape...  182 us
    pallas_call x1, Pallas kernels, mlp_fused(): pl.pallas_call(functools.partial(mlp_kernel, rows), out_shape=(jax.ShapeD...  108 us
    pallas_call x1, Pallas kernels, front(): pl.pallas_call(front_kernel, out_shape=(jax.ShapeDtypeStruct((4 * rows, m...  84.9 us
    pallas_call x1, Pallas kernels, mlp_back_fused(): pl.pallas_call(functools.partial(mlp_back_kernel, rows), out_shape=(jax.S...  83.5 us
    pallas_call x1, Pallas kernels, attn_back_fused(): pl.pallas_call(functools.partial(attn_back_kernel, rows), out_shape=tuple...  73.6 us
  transfers between devices with their start and end apart: 1, of which 0 were waited for; matrix products, arithmetic and copies ran while one was open for 1% of the time, Pallas kernels for 33%

profile of v11, /device:TPU:0, one launch (start us, length us, event | category | flops | bytes accessed | tf_op | source)
XLA Modules:
  0.0 559.9 jit_solution(8612761311368369585)
XLA Ops:
  7.2 0.0 all-gather.2.cloned.1.call-start
  7.9 84.9 %front.1 = (bf16[1024,2304]{1,0:T(8,128)(2,1)}, s32[8,8,128]{2,1,0:T(8,128)}, bf16[2304,128]{1,0:T(8,128)(2,1)}, bf16[2304,128]{1,0:T(8,128)(2,1)}, bf16[512,128...) custom-call(s32[1,1]{1,0:T(1,128)S(6)} %copy.38.ids_ref, ...), custom_call_target="tpu_custom_call" | custom-call | tf_op jit(solution)/shard_map/front/pallas_call | solution.py:988
  92.8 0.0 all-gather.2.cloned.1.call-update
  93.5 2.8 fusion
  96.3 182.3 %attn.1 = (bf16[1024,512]{1,0:T(8,128)(2,1)}, bf16[1024,256]{1,0:T(8,128)(2,1)}, bf16[256,1024]{1,0:T(8,128)(2,1)}, bf16[1024,256]{1,0:T(8,128)(2,1)}, bf16[1024...) custom-call(s32[1]{0:T(128)S(6)} %copy.37.length_ref, ...), custom_call_target="tpu_custom_call" | custom-call | tf_op jit(solution)/shard_map/attn/pallas_call | solution.py:1938
  278.7 1.5 slice_reduce_fusion.ids_ref
  280.2 108.4 %mlp.1 = (bf16[256,2304]{1,0:T(8,128)(2,1)}, bf16[256,2304]{1,0:T(8,128)(2,1)}, bf16[4,256,128]{2,1,0:T(8,128)(2,1)}, bf16[256,128]{1,0:T(8,128)(2,1)}, bf16[4,2...) custom-call(s32[1]{0:T(128)S(6)} %copy.37.length_ref, ...), custom_call_target="tpu_custom_call" | custom-call | tf_op jit(solution)/shard_map/mlp/pallas_call | solution.py:1458
  388.6 83.5 %mlp_back.1 = (f32[256,2304]{1,0:T(8,128)}, f32[64,128]{1,0:T(8,128)}, bf16[2,4,48,288]{3,2,1,0:T(8,128)(2,1)}) custom-call(bf16[256,2304]{1,0:T(8,128)(2,1)} %get-tuple-element.63.g_ref.grad_mlp_hbm, bf16[2304,2304]{1,0:T(8,128)(2,1)} %bitcast.17, bf16[2304,4608]{1,0:T(8,128)(2,1)} %all-gather.2.cloned.1.call-done.gu_hbm, ...), custom_call_target="tpu_custom_call" | custom-call | tf_op jit(solution)/shard_map/mlp_back/pallas_call | solution.py:704
  472.0 0.0 copy-start
  472.0 73.6 %attn_back.1 = (bf16[256,2304]{1,0:T(8,128)(2,1)}, f32[8,72,80]{2,1,0:T(8,128)}, f32[8,16,64]{2,1,0:T(8,128)}, f32[8,16,288]{2,1,0:T(8,128)}, f32[8,16,64]{2,1,0...) custom-call(s32[8]{0:T(128)} %slice_reduce_fusion.ids_ref, ...), custom_call_target="tpu_custom_call" | custom-call | tf_op jit(solution)/shard_map/attn_back/pallas_call | solution.py:2455
  545.6 0.0 copy-start.1
  545.6 0.0 copy-done
  545.6 0.0 copy-start.3
  545.6 0.0 copy-start.8
  545.6 0.0 copy-start.4
  545.7 0.0 copy-start.7
  545.7 1.0 copy.39
  546.7 0.6 copy-done.1
  547.3 1.0 copy.40
  548.3 0.0 copy-done.3
  548.3 0.7 copy.41
  549.0 0.0 copy-done.8
  549.0 0.6 copy.42
  549.7 0.0 copy-done.4
  549.7 0.7 copy.43
  550.3 0.0 copy-done.7
  550.4 0.6 copy.44
  551.0 0.0 copy-done.6
  551.0 0.7 copy.45
  551.6 0.0 copy-done.2
  551.6 0.7 copy.46
  552.4 0.7 copy.47
  (6 shorter events, 0.0 us)
Async XLA Ops:
  7.2 273.0 %all-gather.2.cloned.1.call-start = ((), (), s32[]{:S(2)}) async-start(), calls=%async_computation | async-start | bytes 23887872 | tf_op jit(solution)/shard_map/all_gather | solution.py:2567
  472.0 73.6 %copy-start = (bf16[256,2304]{1,0:T(8,128)(2,1)S(1)}, bf16[256,2304]{1,0:T(8,128)(2,1)}, u32[]{:S(2)}) copy-start(bf16[256,2304]{1,0:T(8,128)(2,1)} %get-tuple-element.106) | copy-start | bytes 3538948
  545.6 1.7 copy-start.1
  545.6 2.7 copy-start.3
  545.6 3.4 copy-start.8
  545.6 4.0 copy-start.4
  545.7 4.7 copy-start.7
  547.3 3.7 copy-start.6
  547.3 4.3 copy-start.2
  547.3 5.1 copy-start.5
Sparse Core Ops, SparseCore 0:
  93.0 187.0 all-gather.1
